TPU v7x, 32 devices: a whole 2x2x4 slice. The times are simulated.
32 devices in a mesh: dp: 4 (over y, x), seq: 8 (over z, core).
Axes of the slice: x: 2, y: 2, z: 4, core: 2. Of those that a mesh axis runs over, the one named last changes fastest.
Arguments:
- layer_input: bfloat16 [8, 2048, 2048], P('dp', 'seq'), may hold values from -6 to 6
- doc_lengths: int32 [8, 8], P('dp'), may hold values from 1 to 1024, 2048 in all within a row
- attn_norm: float32 [2048], replicated, may hold values from 0.5 to 1.5
- q_norm: float32 [128], replicated, may hold values from 0.5 to 1.5
- k_norm: float32 [128], replicated, may hold values from 0.5 to 1.5
- ffn_norm: float32 [2048], replicated, may hold values from 0.5 to 1.5
- w_qkv: bfloat16 [4096, 2048], P('dp'), may hold values from -0.125 to 0.125
- w_gate: bfloat16 [16, 2048], P('dp'), may hold values from -0.125 to 0.125
- w_out: bfloat16 [2048, 2048], P('dp'), may hold values from -1.5 to 1.5
- w_gu: bfloat16 [12288, 2048], P('dp'), may hold values from -0.125 to 0.125
- w_down: bfloat16 [2048, 6144], P('dp'), may hold values from -0.078125 to 0.078125
- cotangent: bfloat16 [8, 2048, 2048], P('dp', 'seq'), may hold values from -6 to 6
Outputs:
- output: bfloat16 [8, 2048, 2048], P('dp', 'seq')
- grad_input: bfloat16 [8, 2048, 2048], P('dp', 'seq')
- grad_attn_norm: float32 [2048], replicated
- grad_q_norm: float32 [128], replicated
- grad_k_norm: float32 [128], replicated
- grad_ffn_norm: float32 [2048], replicated
- grad_w_qkv: float32 [4096, 2048], P('dp')
- grad_w_gate: float32 [16, 2048], P('dp')
- grad_w_out: float32 [2048, 2048], P('dp')
- grad_w_gu: float32 [12288, 2048], P('dp')
- grad_w_down: float32 [2048, 6144], P('dp')
Inputs may be any that keep to these rules, and one draw needn't show every extreme that they name: `doc_lengths`: each row's 8 lengths add up to 2048, and the longest one of each row is exactly 1024.
All inputs are finite; a program needn't handle non-finite values.
Results may differ from a plain program's by a relative error of at most 0.02.
Values may be sent and summed in bfloat16 or wider, within the bound.
No kernel may reach another device: no remote copies, remote signals or barrier semaphores. Data moves between devices by JAX's collectives and lax.ppermute only.
A program may use at most 512 MiB of HBM per device.

v0:
```python
import math

import jax
import jax.numpy as jnp
from jax import lax
from jax.sharding import PartitionSpec as P

QUERY_HEADS = 16
KEY_VALUE_HEADS = 8
HEAD_SIZE = 128
FF = 6144


epsilon = 1e-06
theta_base = 1000000.0
masked_score = -1e30


def dot_trans(left, right):
    return lax.dot_general(
        left, right, (((1,), (1,)), ((), ())), preferred_element_type=jnp.float32
    )


def dot_plain(left, right):
    return jnp.dot(left, right, preferred_element_type=jnp.float32)


def dot_first(left, right):
    return lax.dot_general(
        left, right, (((0,), (0,)), ((), ())), preferred_element_type=jnp.float32
    )


def normalize(value, gain):
    factor = lax.rsqrt(jnp.mean(value * value, axis=-1, keepdims=True) + epsilon)
    return (value * factor * gain, factor)


def norm_back(value, factor, gain, grad):
    weighted = grad * gain
    inner = jnp.mean(weighted * value, axis=-1, keepdims=True)
    return factor * weighted - value * factor**3 * inner


def rotate(value, cosine, sine):
    half = value.shape[-1] // 2
    turned = jnp.concatenate([-value[..., half:], value[..., :half]], axis=-1)
    return value * cosine + turned * sine


def rotate_back(grad, cosine, sine):
    half = grad.shape[-1] // 2
    scaled = grad * sine
    turned = jnp.concatenate([scaled[..., half:], -scaled[..., :half]], axis=-1)
    return grad * cosine + turned


def doc_positions(lengths, row_length_tokens):
    ends = jnp.cumsum(lengths, axis=-1)
    starts = ends - lengths
    places = jnp.arange(row_length_tokens, dtype=jnp.int32)
    segment = jnp.sum((places[:, None] >= ends[..., None, :]).astype(jnp.int32), axis=-1)
    owners = segment[..., None] == jnp.arange(lengths.shape[-1], dtype=jnp.int32)
    first = jnp.sum(jnp.where(owners, starts[..., None, :], 0), axis=-1)
    return (segment, places - first)


def rope_tables(position):
    freq = jnp.power(theta_base, -(jnp.arange(HEAD_SIZE // 2, dtype=jnp.float32) * 2.0) / HEAD_SIZE)
    angle = position.astype(jnp.float32)[..., None] * freq
    both = jnp.concatenate([angle, angle], axis=-1)
    return (jnp.cos(both), jnp.sin(both))


def block_mask(segment, places, start, block):
    segment_block = lax.dynamic_slice_in_dim(segment, start, block, 0)
    place_block = start + jnp.arange(block, dtype=jnp.int32)
    return (segment_block[:, None] == segment[None, :]) & (place_block[:, None] >= places[None, :])


def attend(queries, keys, values, segment, block, scale):
    row_length_tokens = queries.shape[0]
    places = jnp.arange(row_length_tokens, dtype=jnp.int32)

    def one_block(index):
        start = index * block
        query_block = lax.dynamic_slice_in_dim(queries, start, block, 0)
        allowed = block_mask(segment, places, start, block)
        scores = (
            jnp.einsum("qhd,khd->hqk", query_block, keys, preferred_element_type=jnp.float32)
            * scale
        )
        scores = jnp.where(allowed[None], scores, masked_score)
        peak = jnp.max(scores, axis=-1, keepdims=True)
        weights = jnp.exp(scores - peak)
        total = jnp.sum(weights, axis=-1, keepdims=True)
        probs = (weights / total).astype(jnp.bfloat16)
        result = jnp.einsum("hqk,khd->qhd", probs, values, preferred_element_type=jnp.float32)
        return (result, (peak + jnp.log(total))[..., 0])

    results, logsum = lax.map(one_block, jnp.arange(row_length_tokens // block))
    return (results.reshape(row_length_tokens, results.shape[2], results.shape[3]), logsum)


def attend_back(queries, keys, values, d_attn, logsum, segment, block, scale):
    row_length_tokens, heads, width = keys.shape
    places = jnp.arange(row_length_tokens, dtype=jnp.int32)
    zeros = jnp.zeros((row_length_tokens, heads, width), jnp.float32)

    def one_block(carry, index):
        key_sum, value_sum = carry
        start = index * block
        query_block = lax.dynamic_slice_in_dim(queries, start, block, 0)
        grad_block = lax.dynamic_slice_in_dim(d_attn, start, block, 0)
        allowed = block_mask(segment, places, start, block)
        scores = (
            jnp.einsum("qhd,khd->hqk", query_block, keys, preferred_element_type=jnp.float32)
            * scale
        )
        scores = jnp.where(allowed[None], scores, masked_score)
        probs = jnp.exp(scores - logsum[index][..., None])
        d_probs = jnp.einsum("qhd,khd->hqk", grad_block, values, preferred_element_type=jnp.float32)
        inner = jnp.sum(probs * d_probs, axis=-1, keepdims=True)
        d_scores = (probs * (d_probs - inner)).astype(jnp.bfloat16)
        d_query = (
            jnp.einsum("hqk,khd->qhd", d_scores, keys, preferred_element_type=jnp.float32) * scale
        )
        key_sum = (
            key_sum
            + jnp.einsum("hqk,qhd->khd", d_scores, query_block, preferred_element_type=jnp.float32)
            * scale
        )
        value_sum = value_sum + jnp.einsum(
            "hqk,qhd->khd",
            probs.astype(jnp.bfloat16),
            grad_block,
            preferred_element_type=jnp.float32,
        )
        return ((key_sum, value_sum), d_query)

    sums, d_queries = lax.scan(one_block, (zeros, zeros), jnp.arange(row_length_tokens // block))
    return (d_queries.reshape(row_length_tokens, heads, width), sums[0], sums[1])


def rows_data(left, right):
    return lax.psum_scatter(
        dot_first(left, right).astype(jnp.bfloat16), "dp", scatter_dimension=0, tiled=True
    ).astype(jnp.float32)


def shards(
    layer_input,
    doc_lengths,
    attn_norm,
    q_norm,
    k_norm,
    ffn_norm,
    w_qkv,
    w_gate,
    w_out,
    w_gu,
    w_down,
    cotangent,
):
    rows_dev, tok_dev, width = layer_input.shape
    seq_size = lax.axis_size("seq")
    row_length_tokens = tok_dev * seq_size
    heads_dev = QUERY_HEADS // seq_size
    group_repeat_count = QUERY_HEADS // KEY_VALUE_HEADS
    token_count_total = rows_dev * tok_dev
    block = min(512, row_length_tokens)
    scale = 1.0 / math.sqrt(HEAD_SIZE)
    segment, position = doc_positions(doc_lengths, row_length_tokens)
    local_pos = lax.dynamic_slice_in_dim(
        position, lax.axis_index("seq") * tok_dev, tok_dev, 1
    ).reshape(token_count_total)
    cosine, sine = rope_tables(local_pos)
    cosine = cosine[:, None, :]
    sine = sine[:, None, :]
    inputs = layer_input.reshape(token_count_total, width).astype(jnp.float32)
    normed_a, factor_a = normalize(inputs, attn_norm)
    normed_a = normed_a.astype(jnp.bfloat16)
    qkv_full, gate_full, out_full = (
        lax.all_gather(w_qkv, "dp", axis=0, tiled=True),
        lax.all_gather(w_gate, "dp", axis=0, tiled=True),
        lax.all_gather(w_out, "dp", axis=0, tiled=True),
    )
    projected_rows = dot_trans(normed_a, qkv_full)
    gate_logit = dot_trans(normed_a, gate_full)
    query_raw = projected_rows[:, : QUERY_HEADS * HEAD_SIZE].reshape(
        token_count_total, QUERY_HEADS, HEAD_SIZE
    )
    unnormed_key = projected_rows[
        :, QUERY_HEADS * HEAD_SIZE : (QUERY_HEADS + KEY_VALUE_HEADS) * HEAD_SIZE
    ].reshape(token_count_total, KEY_VALUE_HEADS, HEAD_SIZE)
    unnormed_value = projected_rows[:, (QUERY_HEADS + KEY_VALUE_HEADS) * HEAD_SIZE :].reshape(
        token_count_total, KEY_VALUE_HEADS, HEAD_SIZE
    )
    query_normed, query_factor = normalize(query_raw, q_norm)
    key_normed, key_factor = normalize(unnormed_key, k_norm)
    token_shape = (rows_dev, tok_dev, QUERY_HEADS * HEAD_SIZE)
    queries = rotate(query_normed, cosine, sine).astype(jnp.bfloat16).reshape(token_shape)
    keys = (
        jnp.repeat(rotate(key_normed, cosine, sine), group_repeat_count, axis=1)
        .astype(jnp.bfloat16)
        .reshape(token_shape)
    )
    values = (
        jnp.repeat(unnormed_value, group_repeat_count, axis=1)
        .astype(jnp.bfloat16)
        .reshape(token_shape)
    )
    head_q, head_k, head_v = (
        lax.all_to_all(queries, "seq", split_axis=2, concat_axis=1, tiled=True),
        lax.all_to_all(keys, "seq", split_axis=2, concat_axis=1, tiled=True),
        lax.all_to_all(values, "seq", split_axis=2, concat_axis=1, tiled=True),
    )
    head_shape = (rows_dev, row_length_tokens, heads_dev, HEAD_SIZE)
    head_q = head_q.reshape(head_shape)
    head_k = head_k.reshape(head_shape)
    head_v = head_v.reshape(head_shape)
    results = []
    logsums = []
    for row in range(rows_dev):
        result_row, logsum_row = attend(
            head_q[row], head_k[row], head_v[row], segment[row], block, scale
        )
        results.append(result_row)
        logsums.append(logsum_row)
    head_out = (
        jnp.stack(results)
        .astype(jnp.bfloat16)
        .reshape(rows_dev, row_length_tokens, heads_dev * HEAD_SIZE)
    )
    attn_tok = lax.all_to_all(head_out, "seq", split_axis=1, concat_axis=2, tiled=True)
    attn_values = attn_tok.reshape(token_count_total, QUERY_HEADS, HEAD_SIZE).astype(jnp.float32)
    gate_sig = jax.nn.sigmoid(gate_logit)
    gated = (
        (attn_values * gate_sig[:, :, None])
        .reshape(token_count_total, QUERY_HEADS * HEAD_SIZE)
        .astype(jnp.bfloat16)
    )
    mid = inputs + dot_trans(gated, out_full)
    normed_f, factor_f = normalize(mid, ffn_norm)
    normed_f = normed_f.astype(jnp.bfloat16)
    gu_full, down_full = (
        lax.all_gather(w_gu, "dp", axis=0, tiled=True),
        lax.all_gather(w_down, "dp", axis=0, tiled=True),
    )
    gate_up = dot_trans(normed_f, gu_full)
    gate_part = gate_up[:, :FF]
    up_part = gate_up[:, FF:]
    gate_act = jax.nn.sigmoid(gate_part)
    silu_part = gate_part * gate_act
    hidden = (silu_part * up_part).astype(jnp.bfloat16)
    result = mid + dot_trans(hidden, down_full)
    output = result.astype(jnp.bfloat16).reshape(rows_dev, tok_dev, width)
    d_out = cotangent.reshape(token_count_total, width)
    d_hidden = dot_plain(d_out, down_full)
    d_gate = d_hidden * up_part * gate_act * (1.0 + gate_part * (1.0 - gate_act))
    d_up = d_hidden * silu_part
    d_gate_up = jnp.concatenate([d_gate, d_up], axis=1).astype(jnp.bfloat16)
    d_normed = dot_plain(d_gate_up, gu_full)
    part_ffn_norm = jnp.sum(d_normed * mid * factor_f, axis=0)
    d_mid = d_out.astype(jnp.float32) + norm_back(mid, factor_f, ffn_norm, d_normed)
    d_mid_low = d_mid.astype(jnp.bfloat16)
    qkv_back, gate_back, out_back = (
        lax.all_gather(w_qkv, "dp", axis=0, tiled=True),
        lax.all_gather(w_gate, "dp", axis=0, tiled=True),
        lax.all_gather(w_out, "dp", axis=0, tiled=True),
    )
    d_gated = dot_plain(d_mid_low, out_back).reshape(token_count_total, QUERY_HEADS, HEAD_SIZE)
    d_attn = (d_gated * gate_sig[:, :, None]).astype(jnp.bfloat16).reshape(token_shape)
    d_gate_logit = (jnp.sum(d_gated * attn_values, axis=-1) * gate_sig * (1.0 - gate_sig)).astype(
        jnp.bfloat16
    )
    head_grad = lax.all_to_all(d_attn, "seq", split_axis=2, concat_axis=1, tiled=True).reshape(
        head_shape
    )
    grads_q = []
    grads_k = []
    grads_v = []
    for row in range(rows_dev):
        d_q, d_k, d_v = attend_back(
            head_q[row],
            head_k[row],
            head_v[row],
            head_grad[row],
            logsums[row],
            segment[row],
            block,
            scale,
        )
        grads_q.append(d_q)
        grads_k.append(d_k)
        grads_v.append(d_v)
    flat_shape = (rows_dev, row_length_tokens, heads_dev * HEAD_SIZE)
    send_q = jnp.stack(grads_q).astype(jnp.bfloat16).reshape(flat_shape)
    send_k = jnp.stack(grads_k).astype(jnp.bfloat16).reshape(flat_shape)
    send_v = jnp.stack(grads_v).astype(jnp.bfloat16).reshape(flat_shape)
    back_q, backward_key_rows, backward_value_rows = (
        lax.all_to_all(send_q, "seq", split_axis=1, concat_axis=2, tiled=True),
        lax.all_to_all(send_k, "seq", split_axis=1, concat_axis=2, tiled=True),
        lax.all_to_all(send_v, "seq", split_axis=1, concat_axis=2, tiled=True),
    )
    d_query = back_q.reshape(token_count_total, QUERY_HEADS, HEAD_SIZE).astype(jnp.float32)
    key_gradient = jnp.sum(
        backward_key_rows.reshape(
            token_count_total, KEY_VALUE_HEADS, group_repeat_count, HEAD_SIZE
        ).astype(jnp.float32),
        axis=2,
    )
    value_gradient = jnp.sum(
        backward_value_rows.reshape(
            token_count_total, KEY_VALUE_HEADS, group_repeat_count, HEAD_SIZE
        ).astype(jnp.float32),
        axis=2,
    )
    d_query_n = rotate_back(d_query, cosine, sine)
    d_key_n = rotate_back(key_gradient, cosine, sine)
    part_q_norm = jnp.sum(d_query_n * query_raw * query_factor, axis=(0, 1))
    part_k_norm = jnp.sum(d_key_n * unnormed_key * key_factor, axis=(0, 1))
    d_query_raw = norm_back(query_raw, query_factor, q_norm, d_query_n)
    unnormed_key_gradient = norm_back(unnormed_key, key_factor, k_norm, d_key_n)
    d_proj = jnp.concatenate(
        [
            d_query_raw.reshape(token_count_total, QUERY_HEADS * HEAD_SIZE),
            unnormed_key_gradient.reshape(token_count_total, KEY_VALUE_HEADS * HEAD_SIZE),
            value_gradient.reshape(token_count_total, KEY_VALUE_HEADS * HEAD_SIZE),
        ],
        axis=1,
    ).astype(jnp.bfloat16)
    d_normed_a = dot_plain(d_proj, qkv_back) + dot_plain(d_gate_logit, gate_back)
    part_attn_norm = jnp.sum(d_normed_a * inputs * factor_a, axis=0)
    grad_input = (
        (d_mid + norm_back(inputs, factor_a, attn_norm, d_normed_a))
        .astype(jnp.bfloat16)
        .reshape(rows_dev, tok_dev, width)
    )
    part_gate = dot_first(d_gate_logit, normed_a)
    totals = lax.psum(
        (part_attn_norm, part_q_norm, part_k_norm, part_ffn_norm, part_gate), ("dp", "seq")
    )
    gate_rows = QUERY_HEADS // lax.axis_size("dp")
    grad_w_gate = lax.dynamic_slice_in_dim(
        totals[4], lax.axis_index("dp") * gate_rows, gate_rows, 0
    )
    shard_qkv = rows_data(d_proj, normed_a)
    shard_out = rows_data(d_mid_low, gated)
    shard_gu = rows_data(d_gate_up, normed_f)
    shard_down = rows_data(d_out, hidden)
    grad_qkv, grad_out, grad_gu, grad_down = (
        lax.psum(shard_qkv.astype(jnp.bfloat16), "seq").astype(jnp.float32),
        lax.psum(shard_out.astype(jnp.bfloat16), "seq").astype(jnp.float32),
        lax.psum(shard_gu.astype(jnp.bfloat16), "seq").astype(jnp.float32),
        lax.psum(shard_down.astype(jnp.bfloat16), "seq").astype(jnp.float32),
    )
    return (
        output,
        grad_input,
        totals[0],
        totals[1],
        totals[2],
        totals[3],
        grad_qkv,
        grad_w_gate,
        grad_out,
        grad_gu,
        grad_down,
    )


def solution(mesh):
    in_specs = (
        P("dp", "seq", None),
        P("dp", None),
        P(),
        P(),
        P(),
        P(),
        P("dp", None),
        P("dp", None),
        P("dp", None),
        P("dp", None),
        P("dp", None),
        P("dp", "seq", None),
    )
    out_specs = (
        P("dp", "seq", None),
        P("dp", "seq", None),
        P(),
        P(),
        P(),
        P(),
        P("dp", None),
        P("dp", None),
        P("dp", None),
        P("dp", None),
        P("dp", None),
    )
    return jax.shard_map(shards, mesh=mesh, in_specs=in_specs, out_specs=out_specs, check_vma=False)
```

profile of v0, /device:TPU:0, one launch (start us, length us, event | category | flops | bytes accessed | tf_op | source)
XLA Modules:
  0.0 3050.6 jit_solution(15980742591610796726)
XLA Ops:
  21.7 148.2 %all-gather.6.cloned.1.call-done = bf16[4096,2048]{1,0:T(8,128)(2,1)} async-done(((bf16[1024,2048]{1,0:T(8,128)(2,1)}), bf16[4096,2048]{1,0:T(8,128)(2,1)}) %all-gather.6.cloned.1.call-update) | async-done | bytes 16777232 | tf_op jit(solution)/shard_map/all_gather | solution.py:185
  169.9 13.0 fusion.131
  209.8 9.2 add_convert_fusion.1
  238.4 6.1 copy.378
  244.5 32.0 %all-to-all-done = bf16[2,256,2048]{1,0,2:T(2,128)(2,1)} async-done(((bf16[2,256,2048]{1,0,2:T(2,128)(2,1)}), bf16[2,256,2048]{1,0,2:T(2,128)(2,1)}, u32[]{:S(2)}, u32[]{:S(2)}) %all-to-all-start) | async-done | bytes 2097184 | tf_op jit(solution)/shard_map/all_to_all | solution.py:215
  290.4 6.3 copy.381
  296.6 32.6 %all-to-all-done.1 = bf16[2,256,2048]{1,0,2:T(2,128)(2,1)S(1)} async-done(((bf16[2,256,2048]{1,0,2:T(2,128)(2,1)}), bf16[2,256,2048]{1,0,2:T(2,128)(2,1)S(1)}, u32[]{:S(2)}, u32[]{:S(2)}) %all-to-all-start.1) | async-done | bytes 2097184 | tf_op jit(solution)/shard_map/all_to_all | solution.py:216
  344.4 38.3 %all-to-all-done.2 = bf16[2,256,2048]{1,0,2:T(2,128)(2,1)} async-done(((bf16[2,256,2048]{1,0,2:T(2,128)(2,1)}), bf16[2,256,2048]{1,0,2:T(2,128)(2,1)}, u32[]{:S(2)}, u32[]{:S(2)}) %all-to-all-start.2) | async-done | bytes 2097184 | tf_op jit(solution)/shard_map/all_to_all | solution.py:217
  390.3 44.0 %while.57 = (s32[]{:T(128)}, bf16[4,512,2,128]{3,1,2,0:T(8,128)(2,1)}, f32[4,2,512]{2,1,0:T(2,128)S(1)}, s32[4]{0:T(128)S(1)}, s32[2048]{0:T(1024)S(1)}, /*index...) while((s32[]{:T(128)}, ...), condition=%wide.region_13.14_spmd.clone, body=%wide.region_10.13_spmd.clone.sunk | while | flops 1102052864 | bytes 40683784 | solution.py:102
  454.2 44.0 %while.56 = (s32[]{:T(128)}, bf16[4,512,2,128]{3,1,2,0:T(8,128)(2,1)S(1)}, f32[4,2,512]{2,1,0:T(2,128)S(1)}, s32[4]{0:T(128)S(1)}, s32[2048]{0:T(1024)S(1)}, /*i...) while((s32[]{:T(128)}, ...), condition=%wide.region_9.10_spmd.clone, body=%wide.region_6.9_spmd.clone.sunk | while | flops 1102052864 | bytes 32295124 | solution.py:102
  503.5 14.0 copy.395
  522.0 8.9 all-gather
  539.5 31.5 %all-to-all-done.3 = bf16[2,2048,256]{2,0,1:T(2,128)(2,1)} async-done(((bf16[2,2048,256]{2,0,1:T(2,128)(2,1)}), bf16[2,2048,256]{2,0,1:T(2,128)(2,1)}, u32[]{:S(2)}, u32[]{:S(2)}) %all-to-all-start.3) | async-done | bytes 2097184 | tf_op jit(solution)/shard_map/all_to_all | solution.py:236
  582.2 10.6 multiply_reduce_fusion.6
  593.5 105.2 %all-gather.10.cloned.1.call-done = bf16[12288,2048]{1,0:T(8,128)(2,1)} async-done(((bf16[3072,2048]{1,0:T(8,128)(2,1)}), bf16[12288,2048]{1,0:T(8,128)(2,1)}) %all-gather.10.cloned.1.call-update) | async-done | bytes 50331664 | tf_op jit(solution)/shard_map/all_gather | solution.py:248
  698.6 38.5 %fusion.122 = f32[512,12288]{1,0:T(8,128)} fusion(bf16[12288,2048]{1,0:T(8,128)(2,1)} %all-gather.10.cloned.1.call-done, f32[512,2048]{1,0:T(8,128)} %get-tuple-element.966, f32[2048]{0:T(1024)S(1)} %copy-done.77, f32[512]{0:T(512)S(1)} %get-tuple-element.964), kind=kOutput, calls=%fused_computation.226 | convolution fusion | flops 25772949504 | bytes 79702016 | tf_op jit(solution)/shard_map/dot_general | solution.py:20
  737.1 190.9 %all-gather.12.cloned.1.call-done = bf16[2048,6144]{1,0:T(8,128)(2,1)} async-done(((bf16[512,6144]{1,0:T(8,128)(2,1)}), bf16[2048,6144]{1,0:T(8,128)(2,1)}) %all-gather.12.cloned.1.call-update) | async-done | bytes 25165840 | tf_op jit(solution)/shard_map/all_gather | solution.py:249
  927.9 31.6 %multiply_convert_fusion.3 = (bf16[512,6144]{1,0:T(8,128)(2,1)}, bf16[512,6144]{1,0:T(8,128)(2,1)}, bf16[512,6144]{1,0:T(8,128)(2,1)}) fusion(f32[512,12288]{1,0:T(8,128)} %fusion.122, bf16[512,2048]{1,0:T(8,128)(2,1)S(1)} %bitcast.416, bf16[2048,6144]{1,0:T(8,128)(2,1)} %all-gather.12.cloned.1.call-done), kind=kOutput, calls=%fused_computation.103 | convolution fusion | flops 12932087808 | bytes 71303168 | tf_op jit(solution)/shard_map/dot_general | solution.py:26
  959.6 37.2 %multiply_reduce_fusion.2 = (f32[2048]{0:T(1024)}, f32[512]{0:T(512)S(1)}, f32[512,2048]{1,0:T(8,128)}) fusion(f32[512,2048]{1,0:T(8,128)} %get-tuple-element.966, f32[512]{0:T(512)S(1)} %get-tuple-element.964, f32[2048]{0:T(1024)S(1)} %copy-done.77, bf16[12288,2048]{1,0:T(8,128)(2,1)} %all-gather.10.cloned.1.call-done, ...), kind=kOutput, calls=%fused_computation.144 | convolution fusion | flops 25801259008 | bytes 71323648 | tf_op jit(solution)/shard_map/dot_general | solution.py:26
  1019.0 49.0 %all-to-all-done.4 = bf16[2,256,2048]{1,0,2:T(2,128)(2,1)S(1)} async-done(((bf16[2,256,2048]{1,0,2:T(2,128)(2,1)}), bf16[2,256,2048]{1,0,2:T(2,128)(2,1)S(1)}, u32[]{:S(2)}, u32[]{:S(2)}) %all-to-all-start.4) | async-done | bytes 2097184 | tf_op jit(solution)/shard_map/all_to_all | solution.py:278
  1072.5 134.4 %while.59 = (s32[]{:T(128)}, f32[2048,2,128]{0,2,1:T(8,128)}, f32[2048,2,128]{0,2,1:T(8,128)}, bf16[4,512,2,128]{3,1,2,0:T(8,128)(2,1)}, s32[4]{0:T(128)S(1)}, /...) while((s32[]{:T(128)}, f32[2048,2,128]{0,2,1:T(8,128)}, ...), condition=%wide.region_21.22_spmd.clone, body=%wide.region_19.21_spmd.clone.sunk | while | flops 2721709568 | bytes 147372528 | solution.py:142
  1073.7 5.6 fusion.245
  1083.2 5.9 multiply_reduce_fusion.13
  1106.8 5.6 fusion.245
  1116.4 5.9 multiply_reduce_fusion.13
  1140.6 5.6 fusion.245
  1150.1 5.9 multiply_reduce_fusion.13
  1174.4 5.6 fusion.245
  1183.9 5.9 multiply_reduce_fusion.13
  1214.1 135.0 %while.58 = (s32[]{:T(128)}, f32[2048,2,128]{0,2,1:T(8,128)}, f32[2048,2,128]{0,2,1:T(8,128)}, bf16[4,512,2,128]{3,1,2,0:T(8,128)(2,1)}, s32[4]{0:T(128)S(1)}, /...) while((s32[]{:T(128)}, f32[2048,2,128]{0,2,1:T(8,128)}, ...), condition=%wide.region_18.19_spmd.clone, body=%wide.region_16.18_spmd.clone.sunk | while | flops 2721709568 | bytes 147372528 | solution.py:142
  1215.7 5.6 fusion.231
  1225.3 5.9 multiply_reduce_fusion.12
  1239.8 5.4 fusion.234
  1248.9 5.6 fusion.231
  1258.4 5.9 multiply_reduce_fusion.12
  1273.6 5.4 fusion.234
  1282.7 5.6 fusion.231
  1292.2 5.9 multiply_reduce_fusion.12
  1316.5 5.6 fusion.231
  1326.1 5.9 multiply_reduce_fusion.12
  1341.3 5.4 fusion.234
  1360.6 9.2 convolution_convert_fusion.2
  1376.2 33.4 %all-to-all-done.7 = bf16[2,2048,256]{2,0,1:T(2,128)(2,1)} async-done(((bf16[2,2048,256]{2,0,1:T(2,128)(2,1)}), bf16[2,2048,256]{2,0,1:T(2,128)(2,1)}, u32[]{:S(2)}, u32[]{:S(2)}) %all-to-all-start.7) | async-done | bytes 2097184 | tf_op jit(solution)/shard_map/all_to_all | solution.py:305
  1423.4 14.0 copy.413
  1437.5 24.8 all-to-all-done.6
  1487.5 28.1 all-to-all-done.5
  1527.4 6.4 copy.443
  1539.2 6.2 multiply_reduce_fusion.4
  1557.1 12.6 fusion.88
  1569.7 14.8 convolution_convert_fusion.1
  1586.1 19.4 convert_bitcast_fusion
  1606.2 35.2 %convolution_convert_fusion = bf16[12288,2048]{1,0:T(8,128)(2,1)} fusion(bf16[512,6144]{1,0:T(8,128)(2,1)} %get-tuple-element.931, bf16[512,6144]{1,0:T(8,128)(2,1)} %get-tuple-element.930, f32[512,2048]{1,0:T(8,128)} %get-tuple-element.966, f32[2048]{0:T(1024)S(1)} %copy-done.78, f32[512]{0:T(512)S(1)} %copy-done.82), kind=kOutput, calls=%fused_computation.98 | convolution fusion | flops 25823281152 | bytes 67119104 | tf_op jit(solution)/shard_map/dot_general | solution.py:30
  1652.8 83.6 %reduce-scatter.5.cloned.1.call-done = bf16[1024,2048]{1,0:T(8,128)(2,1)} async-done(((bf16[4096,2048]{1,0:T(8,128)(2,1)}), bf16[1024,2048]{1,0:T(8,128)(2,1)}) %reduce-scatter.5.cloned.1.call-update) | async-done | bytes 4194320 | tf_op jit(solution)/shard_map/reduce_scatter | solution.py:147
  1736.3 225.4 %reduce-scatter.11.cloned.1.call-done = bf16[512,6144]{0,1:T(8,128)(2,1)} async-done(((bf16[2048,6144]{0,1:T(8,128)(2,1)}), bf16[512,6144]{0,1:T(8,128)(2,1)}) %reduce-scatter.11.cloned.1.call-update) | async-done | bytes 6291472 | tf_op jit(solution)/shard_map/reduce_scatter | solution.py:147
  1961.7 427.1 %reduce-scatter.9.cloned.1.call-done = bf16[3072,2048]{1,0:T(8,128)(2,1)} async-done(((bf16[12288,2048]{1,0:T(8,128)(2,1)}), bf16[3072,2048]{1,0:T(8,128)(2,1)}) %reduce-scatter.9.cloned.1.call-update) | async-done | bytes 12582928 | tf_op jit(solution)/shard_map/reduce_scatter | solution.py:147
  2392.6 19.9 add_convert_fusion
  2412.5 107.0 %all-reduce.5.cloned.1.call-done = f32[16,2048]{1,0:T(8,128)} async-done(((f32[16,2048]{1,0:T(8,128)}), f32[16,2048]{1,0:T(8,128)}) %all-reduce.5.cloned.1.call-update) | async-done | bytes 131088 | tf_op jit(solution)/shard_map/psum | solution.py:342
  2521.0 16.0 fusion.99
  2536.9 41.0 %all-reduce = (f32[2048]{0:T(1024)}, f32[128]{0:T(128)}, f32[128]{0:T(128)}, f32[2048]{0:T(1024)}) all-reduce(f32[2048]{0:T(1024)S(1)} %get-tuple-element.824, f32[128]{0:T(128)S(1)} %bitcast_reduce_fusion, f32[128]{0:T(128)S(1)} %bitcast_reduce_fusion.1, f32[2048]{0:T(1024)S(1)} %copy-done.84), channel_id=1, replica_groups=mesh['dp'=4,'seq'=8] {'dp','seq'}, use_global_device_ids=true, to_apply=%region_29.30 | all-reduce | flops 4352 | bytes 34816 | tf_op jit(solution)/shard_map/psum | solution.py:342
  2578.0 6.1 fusion.96
  2584.1 428.8 %all-reduce.7.cloned.1.call-done = (bf16[512,6144]{0,1:T(8,128)(2,1)}, bf16[1024,2048]{1,0:T(8,128)(2,1)}, bf16[512,2048]{1,0:T(8,128)(2,1)}, bf16[3072,2048]{1,0:T(8,128)(2,1)}) async-done(((bf16[512,6144]{0,1:T(8,128)(2,1)}, bf16[1024,2048]{1,0:T(8,128)(2,1)}, bf16[512,2048]{1,0:T(8,128)(2,1)}, bf16[3072,2048]{1,0:T(8,128)(2,1)}), (bf16[512,6144]{0,1:T(8,128)(2,1)}, bf16[1024,2048]{1,0:T(8,128)(2,1)}, ...) | async-done | bytes 25165840 | tf_op jit(solution)/shard_map/psum | solution.py:357
  3012.8 7.7 convert_element_type.244
  3024.8 9.0 convert_element_type.248
  3033.8 9.5 copy.428
  (621 shorter events, 510.4 us)
Async XLA Ops:
  7.2 162.7 %all-gather.6.cloned.1.call-start = ((), (), s32[]{:S(2)}) async-start(), calls=%async_computation.12 | async-start | bytes 20971520 | tf_op jit(solution)/shard_map/all_gather | solution.py:185
  7.9 574.3 %all-gather.8.cloned.1.call-start = ((), (), s32[]{:S(2)}) async-start(), calls=%async_computation.13 | async-start | bytes 10485760 | tf_op jit(solution)/shard_map/all_gather | solution.py:187
  8.7 689.9 %all-gather.10.cloned.1.call-start = ((), (), s32[]{:S(2)}) async-start(), calls=%async_computation.14 | async-start | bytes 62914560 | tf_op jit(solution)/shard_map/all_gather | solution.py:248
  10.8 9.0 copy-start.73
  12.5 220.2 %copy-start.34 = (f32[512,128]{1,0:T(8,128)}, f32[512,128]{1,0:T(8,128)S(1)}, u32[]{:S(2)}) copy-start(f32[512,128]{1,0:T(8,128)S(1)} %get-tuple-element.957) | copy-start | bytes 786436
  12.5 220.2 %copy-start.36 = (f32[512,128]{1,0:T(8,128)}, f32[512,128]{1,0:T(8,128)S(1)}, u32[]{:S(2)}) copy-start(f32[512,128]{1,0:T(8,128)S(1)} %get-tuple-element.958) | copy-start | bytes 786436
  19.8 190.0 %copy-start.67 = (f32[2048]{0:T(1024)}, f32[2048]{0:T(1024)S(1)}, u32[]{:S(2)}) copy-start(f32[2048]{0:T(1024)S(1)} %broadcast_bitcast_fusion) | copy-start | bytes 24580
  222.9 53.7 %all-to-all-start = ((bf16[2,256,2048]{1,0,2:T(2,128)(2,1)}), bf16[2,256,2048]{1,0,2:T(2,128)(2,1)}, u32[]{:S(2)}, u32[]{:S(2)}) async-start(bf16[2,256,2048]{1,0,2:T(2,128)(2,1)} %copy.373), calls=%async_computation | async-start | bytes 4194304 | tf_op jit(solution)/shard_map/all_to_all | solution.py:215
  276.6 52.7 %all-to-all-start.1 = ((bf16[2,256,2048]{1,0,2:T(2,128)(2,1)}), bf16[2,256,2048]{1,0,2:T(2,128)(2,1)S(1)}, u32[]{:S(2)}, u32[]{:S(2)}) async-start(bf16[2,256,2048]{1,0,2:T(2,128)(2,1)} %copy.378), calls=%async_computation.1 | async-start | bytes 4194304 | tf_op jit(solution)/shard_map/all_to_all | solution.py:216
  329.3 53.4 %all-to-all-start.2 = ((bf16[2,256,2048]{1,0,2:T(2,128)(2,1)}), bf16[2,256,2048]{1,0,2:T(2,128)(2,1)}, u32[]{:S(2)}, u32[]{:S(2)}) async-start(bf16[2,256,2048]{1,0,2:T(2,128)(2,1)} %copy.381), calls=%async_computation.2 | async-start | bytes 4194304 | tf_op jit(solution)/shard_map/all_to_all | solution.py:217
  333.6 594.3 %all-gather.12.cloned.1.call-start = ((), (), s32[]{:S(2)}) async-start(), calls=%async_computation.15 | async-start | bytes 31457280 | tf_op jit(solution)/shard_map/all_gather | solution.py:249
  434.3 12.5 copy-start.4
  434.3 12.5 copy-start.13
  434.3 12.5 copy-start.31
  434.3 12.5 copy-start.58
  434.3 12.5 copy-start.65
  503.5 18.5 copy-start.76
  517.5 13.5 copy-start.24
  517.5 53.5 %all-to-all-start.3 = ((bf16[2,2048,256]{2,0,1:T(2,128)(2,1)}), bf16[2,2048,256]{2,0,1:T(2,128)(2,1)}, u32[]{:S(2)}, u32[]{:S(2)}) async-start(bf16[2,2048,256]{2,0,1:T(2,128)(2,1)} %copy.395), calls=%async_computation.3 | async-start | bytes 4194304 | tf_op jit(solution)/shard_map/all_to_all | solution.py:236
  531.0 8.6 copy-start.61
  531.7 7.9 copy-start.63
  582.2 116.4 %copy-start.77 = (f32[2048]{0:T(1024)S(1)}, f32[2048]{0:T(1024)}, u32[]{:S(2)}) copy-start(f32[2048]{0:T(1024)} %param.25) | copy-start | bytes 24580
  593.5 403.3 %copy-start.81 = (f32[512]{0:T(512)}, f32[512]{0:T(512)S(1)}, u32[]{:S(2)}) copy-start(f32[512]{0:T(512)S(1)} %get-tuple-element.964) | copy-start | bytes 6148
  698.6 229.3 %copy-start.54 = (bf16[2,256,2048]{2,1,0:T(8,128)(2,1)S(1)}, bf16[2,256,2048]{2,1,0:T(8,128)(2,1)}, u32[]{:S(2)}) copy-start(bf16[2,256,2048]{2,1,0:T(8,128)(2,1)} %param.31) | copy-start | bytes 6291460
  959.6 37.2 %copy-start.83 = (f32[512]{0:T(512)S(1)}, f32[512]{0:T(512)}, u32[]{:S(2)}) copy-start(f32[512]{0:T(512)} %get-tuple-element.963) | copy-start | bytes 6148
  1002.6 6.7 copy-start.28
  1014.1 53.8 %all-to-all-start.4 = ((bf16[2,256,2048]{1,0,2:T(2,128)(2,1)}), bf16[2,256,2048]{1,0,2:T(2,128)(2,1)S(1)}, u32[]{:S(2)}, u32[]{:S(2)}) async-start(bf16[2,256,2048]{1,0,2:T(2,128)(2,1)} %copy.399), calls=%async_computation.4 | async-start | bytes 4194304 | tf_op jit(solution)/shard_map/all_to_all | solution.py:278
  1083.2 6.0 slice-start.1
  1116.4 6.0 slice-start.1
  1150.1 6.0 slice-start.1
  1183.9 6.0 slice-start.1
  1206.9 7.2 copy-start.3
  1206.9 7.2 copy-start.12
  1206.9 7.2 copy-start.57
  1225.3 6.0 slice-start.3
  1258.4 6.0 slice-start.3
  1292.2 6.0 slice-start.2
  1292.2 6.0 slice-start.3
  1326.0 6.0 slice-start.3
  1356.1 53.5 %all-to-all-start.7 = ((bf16[2,2048,256]{2,0,1:T(2,128)(2,1)}), bf16[2,2048,256]{2,0,1:T(2,128)(2,1)}, u32[]{:S(2)}, u32[]{:S(2)}) async-start(bf16[2,2048,256]{2,0,1:T(2,128)(2,1)} %copy.423), calls=%async_computation.7 | async-start | bytes 4194304 | tf_op jit(solution)/shard_map/all_to_all | solution.py:305
  1360.6 292.2 %reduce-scatter.7.cloned.1.call-start = ((), (), s32[]{:S(2)}) async-start(), calls=%async_computation.18 | async-start | bytes 10485760 | tf_op jit(solution)/shard_map/reduce_scatter | solution.py:147
  1372.4 40.9 %copy-start.42 = (bf16[4,512,2,128]{3,1,2,0:T(8,128)(2,1)S(1)}, bf16[4,512,2,128]{3,1,2,0:T(8,128)(2,1)}, u32[]{:S(2)}) copy-start(bf16[4,512,2,128]{3,1,2,0:T(8,128)(2,1)} %get-tuple-element.260) | copy-start | bytes 3145732
  1409.6 52.6 %all-to-all-start.6 = ((bf16[2,2048,256]{2,0,1:T(2,128)(2,1)}), bf16[2,2048,256]{2,0,1:T(2,128)(2,1)S(1)}, u32[]{:S(2)}, u32[]{:S(2)}) async-start(bf16[2,2048,256]{2,0,1:T(2,128)(2,1)} %copy.417), calls=%async_computation.6 | async-start | bytes 4194304 | tf_op jit(solution)/shard_map/all_to_all | solution.py:304
  1423.4 43.4 %copy-start.80 = (f32[128]{0:T(128)S(1)}, f32[128]{0:T(128)}, u32[]{:S(2)}) copy-start(f32[128]{0:T(128)} %param.24) | copy-start | bytes 1540
  1423.4 43.4 %copy-start.69 = (f32[512,8]{0,1:T(8,128)S(1)}, f32[512,8]{0,1:T(8,128)}, u32[]{:S(2)}) copy-start(f32[512,8]{0,1:T(8,128)} %get-tuple-element.959) | copy-start | bytes 49156
  1462.2 53.4 %all-to-all-start.5 = ((bf16[2,2048,256]{2,0,1:T(2,128)(2,1)}), bf16[2,2048,256]{2,0,1:T(2,128)(2,1)}, u32[]{:S(2)}, u32[]{:S(2)}) async-start(bf16[2,2048,256]{2,0,1:T(2,128)(2,1)} %copy.413), calls=%async_computation.5 | async-start | bytes 4194304 | tf_op jit(solution)/shard_map/all_to_all | solution.py:303
  1466.6 269.8 %reduce-scatter.5.cloned.1.call-start = ((), (), s32[]{:S(2)}) async-start(), calls=%async_computation.16 | async-start | bytes 20971520 | tf_op jit(solution)/shard_map/reduce_scatter | solution.py:147
  1527.4 6.4 copy-start.19
  1539.1 8.0 slice-start.4
  1539.1 6.2 copy-start.39
  1539.2 8.0 slice-start.5
  1547.5 8.6 copy-start.26
  1550.6 6.6 copy-start.16
  1550.6 6.6 copy-start.68
  1584.5 377.2 %reduce-scatter.11.cloned.1.call-start = ((), (), s32[]{:S(2)}) async-start(), calls=%async_computation.20 | async-start | bytes 31457280 | tf_op jit(solution)/shard_map/reduce_scatter | solution.py:147
  1605.5 783.3 %reduce-scatter.9.cloned.1.call-start = ((), (), s32[]{:S(2)}) async-start(), calls=%async_computation.19 | async-start | bytes 62914560 | tf_op jit(solution)/shard_map/reduce_scatter | solution.py:147
  1641.5 878.0 %all-reduce.5.cloned.1.call-start = ((), (), s32[]{:S(2)}) async-start(), calls=%async_computation.17 | async-start | bytes 262144 | tf_op jit(solution)/shard_map/psum | solution.py:342
  1652.7 1360.1 %all-reduce.7.cloned.1.call-start = ((), (), s32[]{:S(2)}) async-start(), calls=%async_computation.21 | async-start | bytes 50331648 | tf_op jit(solution)/shard_map/psum | solution.py:357
  2392.6 128.3 %copy-start.75 = (f32[1024]{0:T(1024)S(1)}, f32[1024]{0:T(1024)}, u32[]{:S(2)}) copy-start(f32[1024]{0:T(1024)} %get-tuple-element.935) | copy-start | bytes 12292
  2392.6 128.4 %copy-start.70 = (f32[2048]{0:T(1024)S(1)}, f32[2048]{0:T(1024)}, u32[]{:S(2)}) copy-start(f32[2048]{0:T(1024)} %get-tuple-element.932) | copy-start | bytes 24580
  2392.6 128.4 %copy-start.23 = (bf16[2,256,2048]{2,1,0:T(8,128)(2,1)S(1)}, bf16[2,256,2048]{2,1,0:T(8,128)(2,1)}, u32[]{:S(2)}) copy-start(bf16[2,256,2048]{2,1,0:T(8,128)(2,1)} %param.20) | copy-start | bytes 6291460
  2392.6 128.4 %copy-start.72 = (f32[2048]{0:T(1024)S(1)}, f32[2048]{0:T(1024)}, u32[]{:S(2)}) copy-start(f32[2048]{0:T(1024)} %param.22) | copy-start | bytes 24580
  2521.0 16.0 copy-start.84
  3012.8 12.0 copy-start.32
  (97 other events, 335.8 us)
Sparse Core Ops, SparseCore 0:
  9.8 160.0 all-gather.5
  171.8 87.4 all-gather.7
  261.1 437.4 all-gather.9
  700.3 227.5 all-gather.11
  1370.0 86.6 reduce-scatter.6
  1584.6 151.6 reduce-scatter.4
  1740.0 221.6 reduce-scatter.10
  1964.8 423.9 reduce-scatter.8
  2395.0 124.4 all-reduce.4
  2522.2 490.6 all-reduce.6
where the time goes:
time: 3060 us; the launch traced here: 3050 us
  waiting for transfers between devices  1990 us (65%)
  matrix products  486 us (16%)
  local copies, waits for them, and re-layouts  266 us (9%)
  other arithmetic  182 us (6%)
  blocking collectives  49.9 us (2%)
  starting transfers between devices  35 us (1%)
    reduce_scatter x4, waiting for transfers between devices, rows_data(): lax.psum_scatter(dot_first(left, right).astype(jnp.bfloat16), 'dp', scatt...  736 us
    psum x1, waiting for transfers between devices, shards(): lax.psum(shard_down.astype(jnp.bfloat16), 'seq').astype(jnp.float32)  429 us
    all_gather x1, waiting for transfers between devices, shards(): lax.all_gather(w_down, 'dp', axis=0, tiled=True)  191 us
    all_gather x1, waiting for transfers between devices, shards(): lax.all_gather(w_qkv, 'dp', axis=0, tiled=True)  148 us
    psum x1, waiting for transfers between devices, shards(): lax.psum((part_attn_norm, part_q_norm, part_k_norm, part_ffn_norm, part_g...  107 us
    all_gather x1, waiting for transfers between devices, shards(): lax.all_gather(w_gu, 'dp', axis=0, tiled=True)  105 us
    dot_general x5, matrix products, dot_plain(): return jnp.dot(left, right, preferred_element_type=jnp.float32)  92.1 us
    dot_general x5, matrix products, dot_trans(): lax.dot_general(left, right, (((1,), (1,)), ((), ())), preferred_element_...  82.6 us
  transfers between devices with their start and end apart: 18, of which 16 were waited for; matrix products, arithmetic and copies ran while one was open for 18% of the time, Pallas kernels for 0%

commit v1 on v0

v1 whole, which is shorter than its diff:
```python
import functools
import math

import jax
import jax.numpy as jnp
from jax import lax
from jax.experimental import pallas as pl
from jax.experimental.pallas import tpu as pltpu
from jax.sharding import PartitionSpec as P

QUERY_HEADS = 16
KEY_VALUE_HEADS = 8
HEAD = 128
FF = 6144
CORES = 2

GROUP = QUERY_HEADS // KEY_VALUE_HEADS
CORE_Q = QUERY_HEADS // CORES
CORE_KV = KEY_VALUE_HEADS // CORES
epsilon = 1e-06
theta_base = 1000000.0
SCALE = 1.0 / math.sqrt(HEAD)
SCALE2 = SCALE * math.log2(math.e)
BF = jnp.bfloat16
F32 = jnp.float32


def dot_nt(left, right, out=F32):
    return lax.dot_general(left, right, (((1,), (1,)), ((), ())), preferred_element_type=F32).astype(out)


def dot_nn(left, right, out=F32):
    return lax.dot_general(left, right, (((1,), (0,)), ((), ())), preferred_element_type=F32).astype(out)


def dot_tn(left, right, out=F32):
    return lax.dot_general(left, right, (((0,), (0,)), ((), ())), preferred_element_type=F32).astype(out)


def doc_positions(lengths, total):
    ends = jnp.cumsum(lengths, axis=-1)
    starts = ends - lengths
    places = jnp.arange(total, dtype=jnp.int32)
    segment = jnp.sum((places[:, None] >= ends[..., None, :]).astype(jnp.int32), axis=-1)
    owners = segment[..., None] == jnp.arange(lengths.shape[-1], dtype=jnp.int32)
    first = jnp.sum(jnp.where(owners, starts[..., None, :], 0), axis=-1)
    return first, places - first


def pack_kernel(chips, proj_ref, cos_ref, sin_ref, qg_ref, kg_ref, out_ref):
    per = CORE_Q // chips
    copies = max(1, chips // CORE_KV)
    cos = cos_ref[...]
    sin = sin_ref[...]

    def head(index, gain):
        u = proj_ref[:, index * HEAD : (index + 1) * HEAD]
        factor = lax.rsqrt(jnp.mean(u * u, axis=-1, keepdims=True) + epsilon)
        n = u * factor * gain
        return (n * cos + pltpu.roll(n, HEAD // 2, 1) * sin).astype(BF)

    for z in range(chips):
        for h in range(per):
            out_ref[z, :, h * HEAD : (h + 1) * HEAD] = head(z * per + h, qg_ref[...])
        if z % copies == 0:
            kv = z // copies
            key = head(CORE_Q + kv, kg_ref[...])
            base = (CORE_Q + CORE_KV + kv) * HEAD
            value = proj_ref[:, base : base + HEAD].astype(BF)
        out_ref[z, :, per * HEAD : (per + 1) * HEAD] = key
        out_ref[z, :, (per + 1) * HEAD : (per + 2) * HEAD] = value


def pack_heads(proj, cos, sin, q_gain, k_gain, row, chips, chip_tok):
    per = CORE_Q // chips
    lanes = (per + 2) * HEAD
    block = min(256, chip_tok)
    steps = chip_tok // block
    width = proj.shape[1]
    tok = lambda i: (row * steps + i, 0)
    return pl.pallas_call(
        functools.partial(pack_kernel, chips),
        grid=(steps,),
        in_specs=[
            pl.BlockSpec((block, width), tok),
            pl.BlockSpec((block, HEAD), tok),
            pl.BlockSpec((block, HEAD), tok),
            pl.BlockSpec((1, HEAD), lambda i: (0, 0)),
            pl.BlockSpec((1, HEAD), lambda i: (0, 0)),
        ],
        out_specs=pl.BlockSpec((chips, block, lanes), lambda i: (0, i, 0)),
        out_shape=jax.ShapeDtypeStruct((chips, chip_tok, lanes), BF),
        name="pack_heads",
    )(proj, cos, sin, q_gain, k_gain)


def unpack_kernel(chips, grad_ref, proj_ref, cos_ref, sin_ref, qg_ref, kg_ref, out_ref, qs_ref, ks_ref):
    per = CORE_Q // chips
    copies = max(1, chips // CORE_KV)
    cos = cos_ref[...]
    sin = sin_ref[...]

    @pl.when(pl.program_id(0) == 0)
    def _():
        qs_ref[...] = jnp.zeros_like(qs_ref)
        ks_ref[...] = jnp.zeros_like(ks_ref)

    def head(e, index, gain, sum_ref):
        e = e * cos + pltpu.roll(e * sin, HEAD // 2, 1)
        u = proj_ref[:, index * HEAD : (index + 1) * HEAD]
        factor = lax.rsqrt(jnp.mean(u * u, axis=-1, keepdims=True) + epsilon)
        n = u * factor
        sum_ref[...] += jnp.sum((e * n).reshape(-1, 8, HEAD), axis=0)
        weighted = e * gain
        inner = jnp.mean(weighted * n, axis=-1, keepdims=True)
        out_ref[:, index * HEAD : (index + 1) * HEAD] = (factor * (weighted - n * inner)).astype(BF)

    def part(z, lane):
        return grad_ref[z, :, lane * HEAD : (lane + 1) * HEAD].astype(F32)

    for z in range(chips):
        for h in range(per):
            head(part(z, h), z * per + h, qg_ref[...], qs_ref)
    for kv in range(CORE_KV):
        spread = range(kv * copies, (kv + 1) * copies)
        head(sum(part(z, per) for z in spread), CORE_Q + kv, kg_ref[...], ks_ref)
        base = (CORE_Q + CORE_KV + kv) * HEAD
        out_ref[:, base : base + HEAD] = sum(part(z, per + 1) for z in spread).astype(BF)


def unpack_heads(grads, proj, cos, sin, q_gain, k_gain, row, chips, chip_tok):
    lanes = grads.shape[2]
    block = min(256, chip_tok)
    steps = chip_tok // block
    width = proj.shape[1]
    tok = lambda i: (row * steps + i, 0)
    small = pl.BlockSpec((8, HEAD), lambda i: (0, 0))
    return pl.pallas_call(
        functools.partial(unpack_kernel, chips),
        grid=(steps,),
        in_specs=[
            pl.BlockSpec((chips, block, lanes), lambda i: (0, i, 0)),
            pl.BlockSpec((block, width), tok),
            pl.BlockSpec((block, HEAD), tok),
            pl.BlockSpec((block, HEAD), tok),
            pl.BlockSpec((1, HEAD), lambda i: (0, 0)),
            pl.BlockSpec((1, HEAD), lambda i: (0, 0)),
        ],
        out_specs=[pl.BlockSpec((block, width), lambda i: (i, 0)), small, small],
        out_shape=[
            jax.ShapeDtypeStruct((chip_tok, width), BF),
            jax.ShapeDtypeStruct((8, HEAD), F32),
            jax.ShapeDtypeStruct((8, HEAD), F32),
        ],
        name="unpack_heads",
    )(grads, proj, cos, sin, q_gain, k_gain)


def visible(j, size, start, diagonal):
    inner = lax.broadcasted_iota(jnp.int32, (size, size), 0)
    allowed = inner >= start - j * size
    if diagonal:
        allowed = allowed & (inner <= lax.broadcasted_iota(jnp.int32, (size, size), 1))
    return allowed


def attend_kernel(per, low_ref, q_ref, k_ref, v_ref, start_ref, out_ref, log_ref, acc_ref, sum_ref):
    i = pl.program_id(0)
    size = q_ref.shape[1]
    start = start_ref[...]
    acc_ref[...] = jnp.zeros_like(acc_ref)
    sum_ref[...] = jnp.zeros_like(sum_ref)

    def one(j, diagonal):
        key = k_ref[j]
        value = v_ref[j]
        allowed = visible(j, size, start, diagonal)
        for h in range(per):
            scores = dot_nt(key, q_ref[0, :, h * HEAD : (h + 1) * HEAD])
            p = jnp.where(allowed, jnp.exp2(scores * SCALE2), 0.0)
            sum_ref[h : h + 1, :] += jnp.sum(p, axis=0, keepdims=True)
            acc_ref[h] += dot_tn(value, p.astype(BF))

    def step(j, carry):
        one(j, False)
        return carry

    lax.fori_loop(low_ref[i], i, step, 0)
    one(i, True)
    for h in range(per):
        total = sum_ref[h : h + 1, :]
        out_ref[0, :, h * HEAD : (h + 1) * HEAD] = (acc_ref[h] / total).T.astype(BF)
        log_ref[h : h + 1, :] = jnp.log2(total)


def attend(packed, start, low):
    chips, size, lanes = packed.shape
    per = lanes // HEAD - 2
    return pl.pallas_call(
        functools.partial(attend_kernel, per),
        grid_spec=pltpu.PrefetchScalarGridSpec(
            num_scalar_prefetch=1,
            grid=(chips,),
            in_specs=[
                pl.BlockSpec((1, size, per * HEAD), lambda i, low: (i, 0, 0)),
                pl.BlockSpec((chips, size, HEAD), lambda i, low: (0, 0, per)),
                pl.BlockSpec((chips, size, HEAD), lambda i, low: (0, 0, per + 1)),
                pl.BlockSpec((1, size), lambda i, low: (0, i)),
            ],
            out_specs=[
                pl.BlockSpec((1, size, per * HEAD), lambda i, low: (i, 0, 0)),
                pl.BlockSpec((per, size), lambda i, low: (0, i)),
            ],
            scratch_shapes=[pltpu.VMEM((per, HEAD, size), F32), pltpu.VMEM((per, size), F32)],
        ),
        out_shape=[
            jax.ShapeDtypeStruct((chips, size, per * HEAD), BF),
            jax.ShapeDtypeStruct((per, chips * size), F32),
        ],
        name="attend",
    )(low, packed, packed, packed, start)


def attend_back_kernel(
    per, low_ref, q_ref, k_ref, v_ref, grad_ref, res_ref, log_ref, start_ref, out_ref, dq_ref, dk_ref, dv_ref
):
    i = pl.program_id(0)
    size = q_ref.shape[1]
    start = start_ref[...]

    @pl.when(i == 0)
    def _():
        dk_ref[...] = jnp.zeros_like(dk_ref)
        dv_ref[...] = jnp.zeros_like(dv_ref)

    dq_ref[...] = jnp.zeros_like(dq_ref)
    ones = jnp.ones((8, HEAD), F32)
    inner = []
    for h in range(per):
        cols = slice(h * HEAD, (h + 1) * HEAD)
        both = grad_ref[0, :, cols].astype(F32) * res_ref[0, :, cols].astype(F32)
        sums = lax.dot_general(
            ones, both, (((1,), (1,)), ((), ())), precision=lax.Precision.HIGHEST, preferred_element_type=F32
        )
        inner.append(sums[0:1, :])

    def one(j, diagonal):
        key = k_ref[j]
        value = v_ref[j]
        allowed = visible(j, size, start, diagonal)
        for h in range(per):
            query = q_ref[0, :, h * HEAD : (h + 1) * HEAD]
            grad = grad_ref[0, :, h * HEAD : (h + 1) * HEAD]
            scores = dot_nt(key, query)
            p = jnp.where(allowed, jnp.exp2(scores * SCALE2 - log_ref[h : h + 1, :]), 0.0)
            dp = dot_nt(value, grad)
            ds = (p * (dp - inner[h])).astype(BF)
            dv_ref[j] += dot_nn(p.astype(BF), grad)
            dk_ref[j] += dot_nn(ds, query)
            dq_ref[h] += dot_tn(ds, key)

    def step(j, carry):
        one(j, False)
        return carry

    lax.fori_loop(low_ref[i], i, step, 0)
    one(i, True)
    for h in range(per):
        out_ref[i, :, h * HEAD : (h + 1) * HEAD] = (dq_ref[h] * SCALE).astype(BF)

    @pl.when(i == pl.num_programs(0) - 1)
    def _():
        out_ref[:, :, per * HEAD : (per + 1) * HEAD] = (dk_ref[...] * SCALE).astype(BF)
        out_ref[:, :, (per + 1) * HEAD : (per + 2) * HEAD] = dv_ref[...].astype(BF)


def attend_back(packed, grad, result, logs, start, low):
    chips, size, lanes = packed.shape
    per = lanes // HEAD - 2
    one = pl.BlockSpec((1, size, per * HEAD), lambda i, low: (i, 0, 0))
    return pl.pallas_call(
        functools.partial(attend_back_kernel, per),
        grid_spec=pltpu.PrefetchScalarGridSpec(
            num_scalar_prefetch=1,
            grid=(chips,),
            in_specs=[
                one,
                pl.BlockSpec((chips, size, HEAD), lambda i, low: (0, 0, per)),
                pl.BlockSpec((chips, size, HEAD), lambda i, low: (0, 0, per + 1)),
                one,
                one,
                pl.BlockSpec((per, size), lambda i, low: (0, i)),
                pl.BlockSpec((1, size), lambda i, low: (0, i)),
            ],
            out_specs=pl.BlockSpec((chips, size, lanes), lambda i, low: (0, 0, 0)),
            scratch_shapes=[
                pltpu.VMEM((per, size, HEAD), F32),
                pltpu.VMEM((chips, size, HEAD), F32),
                pltpu.VMEM((chips, size, HEAD), F32),
            ],
        ),
        out_shape=jax.ShapeDtypeStruct((chips, size, lanes), BF),
        name="attend_back",
    )(low, packed, packed, packed, grad, result, logs, start)


def gate_kernel(res_ref, logit_ref, out_ref):
    chips, _, lanes = res_ref.shape
    per = lanes // HEAD
    sig = jax.nn.sigmoid(logit_ref[...])
    for z in range(chips):
        for h in range(per):
            head = z * per + h
            value = res_ref[z, :, h * HEAD : (h + 1) * HEAD].astype(F32)
            out_ref[:, head * HEAD : (head + 1) * HEAD] = (value * sig[:, head : head + 1]).astype(BF)


def gate_rows(result, logits, row):
    chips, size, lanes = result.shape
    block = min(256, size)
    steps = size // block
    return pl.pallas_call(
        gate_kernel,
        grid=(steps,),
        in_specs=[
            pl.BlockSpec((chips, block, lanes), lambda i: (0, i, 0)),
            pl.BlockSpec((block, HEAD), lambda i: (row * steps + i, 0)),
        ],
        out_specs=pl.BlockSpec((block, chips * lanes), lambda i: (i, 0)),
        out_shape=jax.ShapeDtypeStruct((size, chips * lanes), BF),
        name="gate_rows",
    )(result, logits)


def gate_back_kernel(grad_ref, res_ref, logit_ref, out_ref, dlogit_ref):
    chips, size, lanes = res_ref.shape
    per = lanes // HEAD
    sig = jax.nn.sigmoid(logit_ref[...])
    lane = lax.broadcasted_iota(jnp.int32, sig.shape, 1)
    sums = jnp.zeros(sig.shape, F32)
    for z in range(chips):
        for h in range(per):
            head = z * per + h
            e = grad_ref[:, head * HEAD : (head + 1) * HEAD]
            value = res_ref[z, :, h * HEAD : (h + 1) * HEAD].astype(F32)
            out_ref[z, :, h * HEAD : (h + 1) * HEAD] = (e * sig[:, head : head + 1]).astype(BF)
            sums = jnp.where(lane == head, jnp.sum(e * value, axis=-1, keepdims=True), sums)
    dlogit_ref[...] = (sums * sig * (1.0 - sig)).astype(BF)


def gate_back(grad, result, logits, row):
    chips, size, lanes = result.shape
    block = min(256, size)
    steps = size // block
    return pl.pallas_call(
        gate_back_kernel,
        grid=(steps,),
        in_specs=[
            pl.BlockSpec((block, chips * lanes), lambda i: (i, 0)),
            pl.BlockSpec((chips, block, lanes), lambda i: (0, i, 0)),
            pl.BlockSpec((block, HEAD), lambda i: (row * steps + i, 0)),
        ],
        out_specs=[
            pl.BlockSpec((chips, block, lanes), lambda i: (0, i, 0)),
            pl.BlockSpec((block, HEAD), lambda i: (i, 0)),
        ],
        out_shape=[jax.ShapeDtypeStruct((chips, size, lanes), BF), jax.ShapeDtypeStruct((size, HEAD), BF)],
        name="gate_back",
    )(grad, result, logits)


def shards(
    layer_input,
    doc_lengths,
    attn_norm,
    q_norm,
    k_norm,
    ffn_norm,
    w_qkv,
    w_gate,
    w_out,
    w_gu,
    w_down,
    cotangent,
):
    rows, tok, width = layer_input.shape
    seq = lax.axis_size("seq")
    dp = lax.axis_size("dp")
    chips = seq // CORES
    place = lax.axis_index("seq")
    core = place % CORES
    chip = place // CORES
    first = core == 0
    chip_tok = tok * CORES
    length = tok * seq
    tokens = rows * chip_tok
    pair = [(s, s ^ 1) for s in range(seq)]
    groups = [[z * CORES + c for z in range(chips)] for c in range(CORES)]
    q_shard = lax.axis_index("dp") * w_qkv.shape[0] < QUERY_HEADS * HEAD

    def swap(x):
        return lax.ppermute(x, "seq", pair)

    def pick(a, b):
        return jnp.where(first, a, b)

    def both(x):
        other = swap(x)
        return jnp.concatenate([pick(x, other), pick(other, x)], axis=1).reshape(tokens, width)

    def own(x):
        x = x.reshape(rows, CORES, tok, width)
        return pick(x[:, 0], x[:, 1])

    def pair_sum(x):
        return x.astype(F32) + swap(x).astype(F32)

    def exchange(x):
        return lax.all_to_all(x, "seq", 0, 0, axis_index_groups=groups, tiled=True)

    def chip_sum(x):
        if chips != 4:
            return lax.psum(x, "seq", axis_index_groups=groups)
        inward = [(c, 2 + c) for c in range(CORES)] + [(6 + c, 4 + c) for c in range(CORES)]
        middle = [(2 + c, 4 + c) for c in range(CORES)] + [(4 + c, 2 + c) for c in range(CORES)]
        outward = [(2 + c, c) for c in range(CORES)] + [(4 + c, 6 + c) for c in range(CORES)]
        half = x + lax.ppermute(x, "seq", inward)
        full = half + lax.ppermute(half, "seq", middle)
        spread = lax.ppermute(full, "seq", outward)
        return jnp.where((chip == 1) | (chip == 2), full, spread)

    def total_sum(x):
        for name, size in (("seq", seq), ("dp", dp)):
            step = 1
            while step < size:
                x = x + lax.ppermute(x, name, [(s, s ^ step) for s in range(size)])
                step *= 2
        return x

    def scatter(x):
        return lax.psum_scatter(x, "dp", scatter_dimension=0, tiled=True)

    def gather(x):
        return lax.all_gather(x, "dp", axis=0, tiled=True)

    def core_rows(w, unit):
        return jnp.concatenate(
            [pick(w[a : a + unit], w[a + unit : a + 2 * unit]) for a in range(0, w.shape[0], 2 * unit)], axis=0
        )

    def core_cols(w, unit):
        return jnp.concatenate(
            [pick(w[:, a : a + unit], w[:, a + unit : a + 2 * unit]) for a in range(0, w.shape[1], 2 * unit)],
            axis=1,
        )

    def join_rows(low, high, unit):
        parts = []
        for a in range(0, low.shape[0], unit):
            parts += [low[a : a + unit], high[a : a + unit]]
        return jnp.concatenate(parts, axis=0)

    def join_cols(low, high, unit):
        parts = []
        for a in range(0, low.shape[1], unit):
            parts += [low[:, a : a + unit], high[:, a : a + unit]]
        return jnp.concatenate(parts, axis=1)

    ff_unit = w_gu.shape[0] // CORES
    qkv_half = jnp.where(q_shard, core_rows(w_qkv, GROUP * HEAD), core_rows(w_qkv, HEAD))
    qkv_full = gather(qkv_half)
    gate_full = gather(w_gate)
    out_full = gather(core_cols(w_out, GROUP * HEAD))
    gu_full = gather(core_rows(w_gu, ff_unit))
    down_full = gather(core_cols(w_down, ff_unit))
    gate_core = jnp.pad(core_rows(gate_full, GROUP), ((0, HEAD - CORE_Q), (0, 0)))

    start, position = doc_positions(doc_lengths, length)
    low = start.reshape(rows, chips, chip_tok)[:, :, 0] // chip_tok
    local = lax.dynamic_slice_in_dim(position, chip * chip_tok, chip_tok, 1).reshape(tokens)
    freq = jnp.power(theta_base, -(jnp.arange(HEAD // 2, dtype=F32) * 2.0) / HEAD)
    angle = local.astype(F32)[:, None] * freq
    cos = jnp.cos(angle)
    sin = jnp.sin(angle)
    cos = jnp.concatenate([cos, cos], axis=1)
    sin = jnp.concatenate([-sin, sin], axis=1)

    inputs_low = both(layer_input)
    d_out = both(cotangent)
    inputs = inputs_low.astype(F32)
    factor_a = lax.rsqrt(jnp.mean(inputs * inputs, axis=-1, keepdims=True) + epsilon)
    normed_a = (inputs * factor_a * attn_norm).astype(BF)
    logits = dot_nt(normed_a, gate_core)
    proj = dot_nt(normed_a, qkv_full)
    q_gain = q_norm[None, :]
    k_gain = k_norm[None, :]

    packed, results, logs, gated, partial = [], [], [], [], []
    for row in range(rows):
        packed.append(exchange(pack_heads(proj, cos, sin, q_gain, k_gain, row, chips, chip_tok)))
    for row in range(rows):
        head_out, log = attend(packed[row], start[row : row + 1], low[row])
        results.append(head_out)
        logs.append(log)
    tok_results = [exchange(r) for r in results]
    for row in range(rows):
        gated.append(gate_rows(tok_results[row], logits, row))
        partial.append(pair_sum(dot_nt(gated[row], out_full, BF)))
    mid = inputs + jnp.concatenate(partial, axis=0)
    gated = jnp.concatenate(gated, axis=0)

    factor_f = lax.rsqrt(jnp.mean(mid * mid, axis=-1, keepdims=True) + epsilon)
    normed_f = (mid * factor_f * ffn_norm).astype(BF)
    gate_up = dot_nt(normed_f, gu_full, BF)
    gate_part = gate_up[:, : FF // CORES].astype(F32)
    up_part = gate_up[:, FF // CORES :].astype(F32)
    gate_act = jax.nn.sigmoid(gate_part)
    silu = gate_part * gate_act
    hidden = (silu * up_part).astype(BF)
    shard_down = scatter(dot_tn(d_out, hidden, BF))
    d_hidden = dot_nn(d_out, down_full)
    d_gate = d_hidden * up_part * gate_act * (1.0 + gate_part * (1.0 - gate_act))
    d_up = d_hidden * silu
    d_gate_up = jnp.concatenate([d_gate.astype(BF), d_up.astype(BF)], axis=1)
    d_normed = pair_sum(dot_nn(d_gate_up, gu_full, BF))
    half_cols = width // 2
    shard_gu = [scatter(dot_tn(d_gate_up, normed_f[:, a : a + half_cols], BF)) for a in (0, half_cols)]
    out_part = dot_nt(hidden, down_full, BF).reshape(rows, CORES, tok, width)
    out_other = swap(pick(out_part[:, 1], out_part[:, 0]))
    output = (own(mid) + pick(out_part[:, 0], out_part[:, 1]).astype(F32) + out_other.astype(F32)).astype(BF)

    part_ffn = 0.5 * jnp.sum(d_normed * mid * factor_f, axis=0)
    weighted = d_normed * ffn_norm
    inner = jnp.mean(weighted * mid, axis=-1, keepdims=True)
    d_mid = d_out.astype(F32) + factor_f * weighted - mid * factor_f**3 * inner
    d_mid_low = d_mid.astype(BF)
    shard_out = scatter(dot_tn(d_mid_low, gated, BF))

    d_proj, d_logit, d_heads = [], [], []
    q_sum = 0.0
    k_sum = 0.0
    for row in range(rows):
        d_gated = dot_nn(d_mid_low[row * chip_tok : (row + 1) * chip_tok], out_full)
        d_attn, dl = gate_back(d_gated, tok_results[row], logits, row)
        d_logit.append(dl)
        d_heads.append(exchange(d_attn))
    for row in range(rows):
        grads = exchange(
            attend_back(packed[row], d_heads[row], results[row], logs[row], start[row : row + 1], low[row])
        )
        dpr, qs, ks = unpack_heads(grads, proj, cos, sin, q_gain, k_gain, row, chips, chip_tok)
        d_proj.append(dpr)
        q_sum = q_sum + qs
        k_sum = k_sum + ks
    d_proj = jnp.concatenate(d_proj, axis=0)
    d_logit = jnp.concatenate(d_logit, axis=0)
    shard_qkv = scatter(dot_tn(d_proj, normed_a, BF))
    d_norm_part = (dot_nn(d_proj, qkv_full) + dot_nn(d_logit, gate_core)).astype(BF)
    d_norm_part = d_norm_part.reshape(rows, CORES, tok, width)
    d_norm_other = swap(pick(d_norm_part[:, 1], d_norm_part[:, 0]))
    d_normed_a = pick(d_norm_part[:, 0], d_norm_part[:, 1]).astype(F32) + d_norm_other.astype(F32)
    own_in = layer_input.astype(F32)
    own_factor = lax.rsqrt(jnp.mean(own_in * own_in, axis=-1, keepdims=True) + epsilon)
    part_attn = jnp.sum(d_normed_a * own_in * own_factor, axis=(0, 1))
    weighted_a = d_normed_a * attn_norm
    inner_a = jnp.mean(weighted_a * own_in, axis=-1, keepdims=True)
    grad_input = (own(d_mid) + own_factor * weighted_a - own_in * own_factor**3 * inner_a).astype(BF)

    part_gate = dot_tn(d_logit, normed_a)[:CORE_Q]
    zero = jnp.zeros_like(part_gate)
    part_gate = join_rows(pick(part_gate, zero), pick(zero, part_gate), GROUP)
    heads = jnp.concatenate([jnp.sum(q_sum, axis=0), jnp.sum(k_sum, axis=0)])
    heads = jnp.pad(heads, (0, width - heads.shape[0]))
    early = total_sum(jnp.concatenate([part_gate, part_ffn[None], jnp.zeros((7, width), F32)], axis=0))
    late = total_sum(jnp.stack([part_attn, heads]))
    gate_count = w_gate.shape[0]
    grad_w_gate = lax.dynamic_slice_in_dim(early, lax.axis_index("dp") * gate_count, gate_count, 0)

    def halves(shard):
        mine = chip_sum(shard)
        other = swap(mine)
        return pick(mine, other).astype(F32), pick(other, mine).astype(F32)

    grad_down = join_cols(*halves(shard_down), ff_unit)
    gu_low, gu_high = zip(*[halves(s) for s in shard_gu])
    grad_gu = jnp.concatenate([jnp.concatenate(gu_low, axis=1), jnp.concatenate(gu_high, axis=1)], axis=0)
    grad_out = join_cols(*halves(shard_out), GROUP * HEAD)
    qkv_low, qkv_high = halves(shard_qkv)
    grad_qkv = jnp.where(
        q_shard, join_rows(qkv_low, qkv_high, GROUP * HEAD), join_rows(qkv_low, qkv_high, HEAD)
    )
    return (
        output,
        grad_input,
        late[0],
        late[1, :HEAD],
        late[1, HEAD : 2 * HEAD],
        early[QUERY_HEADS],
        grad_qkv,
        grad_w_gate,
        grad_out,
        grad_gu,
        grad_down,
    )


def solution(mesh):
    token = P("dp", "seq", None)
    shard = P("dp", None)
    in_specs = (token, shard, P(), P(), P(), P(), shard, shard, shard, shard, shard, token)
    out_specs = (token, token, P(), P(), P(), P(), shard, shard, shard, shard, shard)
    return jax.shard_map(shards, mesh=mesh, in_specs=in_specs, out_specs=out_specs, check_vma=False)
```

time: 3060 us -> 1770 us (0.58)
  waiting for transfers between devices: 1990 us -> 1040 us
  local copies, waits for them, and re-layouts: 266 us -> 30.6 us
  matrix products: 486 us -> 262 us
  Pallas kernels: 0 us -> 102 us
  starting transfers between devices: 35 us -> 83.8 us
  blocking collectives: 49.9 us -> 8.97 us
  other arithmetic: 182 us -> 220 us
    psum x2 -> x0, waiting for transfers between devices: 536 us -> none  [the longest x1 429 us: shards(): lax.psum(shard_down.astype(jnp.bfloat16), 'seq').astype(jnp.float32)]
    reduce_scatter x4 -> x5, waiting for transfers between devices: 736 us -> 286 us  [scatter(): return lax.psum_scatter(x, 'dp', scatter_dimension=0, tiled=True)]
    ppermute x0 -> x37, waiting for transfers between devices: none -> 344 us  [the longest x5 269 us: chip_sum(): spread = lax.ppermute(full, 'seq', outward)]
    dot_general x71 -> x18, matrix products: 486 us -> 262 us  [the longest x6 89.4 us: dot_tn(): lax.dot_general(left, right, (((0,), (0,)), ((), ())), preferred_element_...]
    all_gather x4, waiting for transfers between devices: 444 us -> 236 us  [gather(): return lax.all_gather(x, 'dp', axis=0, tiled=True)]
    pallas_call x0 -> x12, Pallas kernels: none -> 102 us  [the longest x2 39.6 us: attend_back(): pl.pallas_call(functools.partial(attend_back_kernel, per), grid_spec=pltp...]
    all_to_all x8, waiting for transfers between devices: 270 us -> 176 us  [exchange(): return lax.all_to_all(x, 'seq', 0, 0, axis_index_groups=groups, tiled=True)]
    concatenate x0 -> x7, other arithmetic: none -> 63.6 us  [the longest x1 51.4 us: shards(): jnp.concatenate([jnp.concatenate(gu_low, axis=1), jnp.concatenate(gu_high...]
  transfers between devices with their start and end apart: 18 -> 54, of which waited for: 16 -> 24; matrix products, arithmetic and copies ran while one was open for 18% -> 18% of each run, Pallas kernels for 0% -> 5%
where the time goes in v1:
time: 1770 us; the launch traced here: 1760 us
  waiting for transfers between devices  1040 us (59%)
  matrix products  262 us (15%)
  other arithmetic  220 us (12%)
  Pallas kernels  102 us (6%)
  starting transfers between devices  83.8 us (5%)
  local copies, waits for them, and re-layouts  30.6 us (2%)
    reduce_scatter x5, waiting for transfers between devices, scatter(): return lax.psum_scatter(x, 'dp', scatter_dimension=0, tiled=True)  286 us
    ppermute x5, waiting for transfers between devices, chip_sum(): spread = lax.ppermute(full, 'seq', outward)  269 us
    all_gather x4, waiting for transfers between devices, gather(): return lax.all_gather(x, 'dp', axis=0, tiled=True)  236 us
    all_to_all x8, waiting for transfers between devices, exchange(): return lax.all_to_all(x, 'seq', 0, 0, axis_index_groups=groups, tiled=True)  176 us
    dot_general x6, matrix products, dot_tn(): lax.dot_general(left, right, (((0,), (0,)), ((), ())), preferred_element_...  89.4 us
    dot_general x6, matrix products, dot_nn(): lax.dot_general(left, right, (((1,), (0,)), ((), ())), preferred_element_...  87.9 us
    dot_general x6, matrix products, dot_nt(): lax.dot_general(left, right, (((1,), (1,)), ((), ())), preferred_element_...  84.3 us
    concatenate x1, other arithmetic, shards(): jnp.concatenate([jnp.concatenate(gu_low, axis=1), jnp.concatenate(gu_high...  51.4 us
  transfers between devices with their start and end apart: 54, of which 24 were waited for; matrix products, arithmetic and copies ran while one was open for 18% of the time, Pallas kernels for 5%

profile of v1, /device:TPU:0, one launch (start us, length us, event | category | flops | bytes accessed | tf_op | source)
XLA Modules:
  0.0 1763.3 jit_solution(6451082587838168951)
XLA Ops:
  17.8 8.0 slice_select_fusion
  38.2 67.0 %all-gather.6.cloned.1.call-done = bf16[2048,2048]{1,0:T(8,128)(2,1)} async-done(((bf16[512,2048]{1,0:T(8,128)(2,1)}), bf16[2048,2048]{1,0:T(8,128)(2,1)}) %all-gather.6.cloned.1.call-update) | async-done | bytes 8388624 | tf_op jit(solution)/shard_map/all_gather | solution.py:444
  105.3 14.6 fusion.66.proj_ref
  119.8 6.2 pack_heads.3
  126.0 4.6 all-to-all-start.2
  136.2 6.2 pack_heads.2
  142.4 36.5 %all-to-all-done.2.q_ref.k_ref.v_ref = bf16[4,512,512]{2,1,0:T(8,128)(2,1)} async-done(((bf16[4,512,512]{2,1,0:T(8,128)(2,1)}), bf16[4,512,512]{2,1,0:T(8,128)(2,1)}, u32[]{:S(2)}, u32[]{:S(2)}) %all-to-all-start.2) | async-done | bytes 2097184 | tf_op jit(solution)/shard_map/all_to_all | solution.py:419
  178.9 4.6 all-to-all-start
  184.8 10.8 attend.3
  195.5 35.8 %all-to-all-done.q_ref.k_ref.v_ref = bf16[4,512,512]{2,1,0:T(8,128)(2,1)} async-done(((bf16[4,512,512]{2,1,0:T(8,128)(2,1)}), bf16[4,512,512]{2,1,0:T(8,128)(2,1)}, u32[]{:S(2)}, u32[]{:S(2)}) %all-to-all-start) | async-done | bytes 2097184 | tf_op jit(solution)/shard_map/all_to_all | solution.py:419
  234.9 10.9 attend.2
  245.8 14.3 all-to-all-done.3.res_ref
  260.1 4.2 all-to-all-start.1
  264.5 9.0 all-gather
  280.4 6.2 convolution_convert_fusion.8
  292.3 5.0 convolution_convert_fusion.9
  313.7 76.6 %all-gather.10.cloned.1.call-done = bf16[6144,2048]{1,0:T(8,128)(2,1)} async-done(((bf16[1536,2048]{1,0:T(8,128)(2,1)}), bf16[6144,2048]{1,0:T(8,128)(2,1)}) %all-gather.10.cloned.1.call-update) | async-done | bytes 25165840 | tf_op jit(solution)/shard_map/all_gather | solution.py:444
  390.3 32.6 %convolution_convert_fusion.3 = bf16[1024,6144]{1,0:T(8,128)(2,1)} fusion(bf16[1024,2048]{1,0:T(8,128)(2,1)} %multiply_convert_fusion.1, bf16[6144,2048]{1,0:T(8,128)(2,1)} %all-gather.10.cloned.1.call-done), kind=kOutput, calls=%fused_computation.20 | convolution fusion | flops 25776095232 | bytes 41943040 | tf_op jit(solution)/shard_map/dot_general | solution.py:29
  422.9 92.0 %all-gather.12.cloned.1.call-done = bf16[2048,3072]{1,0:T(8,128)(2,1)} async-done(((bf16[512,3072]{1,0:T(8,128)(2,1)}), bf16[2048,3072]{1,0:T(8,128)(2,1)}) %all-gather.12.cloned.1.call-update) | async-done | bytes 12582928 | tf_op jit(solution)/shard_map/all_gather | solution.py:444
  515.0 26.4 %fusion.3 = (bf16[1024,3072]{1,0:T(8,128)(2,1)}, bf16[1024,3072]{1,0:T(8,128)(2,1)}) fusion(bf16[1024,6144]{1,0:T(8,128)(2,1)} %convolution_convert_fusion.3, bf16[1024,2048]{1,0:T(8,128)(2,1)} %bitcast.154, bf16[2048,3072]{1,0:T(8,128)(2,1)} %all-gather.12.cloned.1.call-done), kind=kOutput, calls=%fused_computation.8 | convolution fusion | flops 12932087808 | bytes 41943040 | tf_op jit(solution)/shard_map/dot_general | solution.py:33
  541.5 34.4 %convolution_convert_fusion.5 = bf16[1024,2048]{1,0:T(8,128)(2,1)} fusion(bf16[6144,2048]{1,0:T(8,128)(2,1)} %all-gather.10.cloned.1.call-done, bf16[1024,3072]{1,0:T(8,128)(2,1)} %get-tuple-element.47, bf16[1024,3072]{1,0:T(8,128)(2,1)} %get-tuple-element.46), kind=kOutput, calls=%fused_computation.65 | convolution fusion | flops 25797066752 | bytes 41943040 | tf_op jit(solution)/shard_map/dot_general | solution.py:33
  575.8 7.4 collective-permute-done.5
  583.2 8.5 multiply_reduce_fusion
  591.8 14.8 fusion.58
  606.5 6.5 fusion.30.grad_ref
  617.0 5.0 all-to-all-start.4
  622.0 6.5 fusion.28.grad_ref
  632.5 15.6 all-to-all-done.4.grad_ref
  651.6 19.8 %attend_back.2 = bf16[4,512,512]{2,1,0:T(8,128)(2,1)} custom-call(s32[4]{0:T(128)} %get-tuple-element.108.low_ref, bf16[4,512,512]{2,1,0:T(8,128)(2,1)} %all-to-all-done.q_ref.k_ref.v_ref, bf16[4,512,512]{2,1,0:T(8,128)(2,1)} %all-to-all-done.q_ref.k_ref.v_ref, bf16[4,512,512]{2,1,0:T(8,128)(2,1)} %all-to-all-done.q_ref.k_ref.v_ref, ...), custom_call_target="tpu_custom_call" | custom-call | tf_op jit(solution)/shard_map/attend_back/pallas_call | solution.py:281
  671.3 5.5 all-to-all-done.6.grad_ref
  680.4 19.8 %attend_back.3 = bf16[4,512,512]{2,1,0:T(8,128)(2,1)} custom-call(s32[4]{0:T(128)} %get-tuple-element.109.low_ref, bf16[4,512,512]{2,1,0:T(8,128)(2,1)} %all-to-all-done.2.q_ref.k_ref.v_ref, bf16[4,512,512]{2,1,0:T(8,128)(2,1)} %all-to-all-done.2.q_ref.k_ref.v_ref, bf16[4,512,512]{2,1,0:T(8,128)(2,1)} %all-to-all-done.2.q_ref.k_ref.v_ref, ...), custom_call_target="tpu_custom_call" | custom-call | tf_op jit(solution)/shard_map/attend_back/pallas_call | solution.py:281
  700.2 27.9 %all-to-all-done.5.grad_ref = bf16[4,512,512]{2,1,0:T(8,128)(2,1)S(1)} async-done(((bf16[4,512,512]{2,1,0:T(8,128)(2,1)}), bf16[4,512,512]{2,1,0:T(8,128)(2,1)S(1)}, u32[]{:S(2)}, u32[]{:S(2)}) %all-to-all-start.5) | async-done | bytes 2097184 | tf_op jit(solution)/shard_map/all_to_all | solution.py:419
  728.1 4.5 all-to-all-start.7
  732.7 7.7 unpack_heads.2
  743.5 36.9 %all-to-all-done.7.grad_ref = bf16[4,512,512]{2,1,0:T(8,128)(2,1)} async-done(((bf16[4,512,512]{2,1,0:T(8,128)(2,1)}), bf16[4,512,512]{2,1,0:T(8,128)(2,1)}, u32[]{:S(2)}, u32[]{:S(2)}) %all-to-all-start.7) | async-done | bytes 2097184 | tf_op jit(solution)/shard_map/all_to_all | solution.py:419
  780.4 7.5 unpack_heads.3
  791.3 13.4 convolution_convert_fusion.4
  806.2 8.4 convolution_convert_fusion.7
  814.7 21.9 %convolution_convert_fusion.1 = bf16[6144,1024]{1,0:T(8,128)(2,1)} fusion(bf16[1024,3072]{1,0:T(8,128)(2,1)} %get-tuple-element.47, bf16[1024,3072]{1,0:T(8,128)(2,1)} %get-tuple-element.46, bf16[1024,2048]{1,0:T(8,128)(2,1)} %multiply_convert_fusion.1), kind=kOutput, calls=%fused_computation.18 | convolution fusion | flops 12916359168 | bytes 27262976 | tf_op jit(solution)/shard_map/dot_general | solution.py:37
  836.7 21.7 %convolution_convert_fusion.2 = bf16[6144,1024]{1,0:T(8,128)(2,1)} fusion(bf16[1024,3072]{1,0:T(8,128)(2,1)} %get-tuple-element.47, bf16[1024,3072]{1,0:T(8,128)(2,1)} %get-tuple-element.46, bf16[1024,2048]{1,0:T(8,128)(2,1)} %multiply_convert_fusion.1), kind=kOutput, calls=%fused_computation.19 | convolution fusion | flops 12916359168 | bytes 27262976 | tf_op jit(solution)/shard_map/dot_general | solution.py:37
  858.5 21.1 %convolution_convert_fusion = bf16[2048,3072]{1,0:T(8,128)(2,1)} fusion(bf16[1024,2048]{1,0:T(8,128)(2,1)} %bitcast.155, bf16[1024,6144]{1,0:T(8,128)(2,1)} %convolution_convert_fusion.3), kind=kOutput, calls=%fused_computation.17 | convolution fusion | flops 12916359168 | bytes 29360128 | tf_op jit(solution)/shard_map/dot_general | solution.py:37
  882.2 21.7 %convolution_convert_fusion.6 = bf16[1024,2048]{1,0:T(8,128)(2,1)} fusion(bf16[2048,3072]{1,0:T(8,128)(2,1)} %all-gather.12.cloned.1.call-done, bf16[1024,6144]{1,0:T(8,128)(2,1)} %convolution_convert_fusion.3), kind=kOutput, calls=%fused_computation.66 | convolution fusion | flops 12912164864 | bytes 29360128 | tf_op jit(solution)/shard_map/dot_general | solution.py:29
  904.0 12.9 fusion.67
  932.6 12.2 reduce-scatter.8.cloned.1.call-done
  948.6 20.9 %collective-permute-done.17 = bf16[512,2048]{1,0:T(8,128)(2,1)} collective-permute-done((bf16[512,2048]{1,0:T(8,128)(2,1)}, bf16[512,2048]{1,0:T(8,128)(2,1)}, u32[]{:S(2)}, u32[]{:S(2)}) %collective-permute-start.17) | collective-permute-done | bytes 2097184 | tf_op jit(solution)/shard_map/ppermute | solution.py:427
  969.5 4.5 add.204
  976.0 5.4 fusion.17
  981.6 4.3 collective-permute-start.14
  985.8 10.3 collective-permute-done.21
  1001.6 33.7 %collective-permute-done.14 = f32[24,2048]{1,0:T(8,128)S(1)} collective-permute-done((f32[24,2048]{1,0:T(8,128)S(1)}, f32[24,2048]{1,0:T(8,128)S(1)}, u32[]{:S(2)}, u32[]{:S(2)}) %collective-permute-start.14) | collective-permute-done | bytes 196640 | tf_op jit(solution)/shard_map/ppermute | solution.py:436
  1037.5 35.8 %reduce-scatter.12.cloned.1.call-done = bf16[1536,1024]{1,0:T(8,128)(2,1)} async-done(((bf16[6144,1024]{1,0:T(8,128)(2,1)}), bf16[1536,1024]{1,0:T(8,128)(2,1)}) %reduce-scatter.12.cloned.1.call-update) | async-done | bytes 3145744 | tf_op jit(solution)/shard_map/reduce_scatter | solution.py:441
  1073.3 4.5 collective-permute-start.29
  1077.8 119.2 %reduce-scatter.10.cloned.1.call-done = bf16[1536,1024]{1,0:T(8,128)(2,1)} async-done(((bf16[6144,1024]{1,0:T(8,128)(2,1)}), bf16[1536,1024]{1,0:T(8,128)(2,1)}) %reduce-scatter.10.cloned.1.call-update) | async-done | bytes 3145744 | tf_op jit(solution)/shard_map/reduce_scatter | solution.py:441
  1197.0 5.1 collective-permute-start.25
  1202.1 118.7 %reduce-scatter.14.cloned.1.call-done = bf16[512,3072]{1,0:T(8,128)(2,1)} async-done(((bf16[2048,3072]{1,0:T(8,128)(2,1)}), bf16[512,3072]{1,0:T(8,128)(2,1)}) %reduce-scatter.14.cloned.1.call-update) | async-done | bytes 3145744 | tf_op jit(solution)/shard_map/reduce_scatter | solution.py:441
  1320.7 5.4 collective-permute-start.33
  1330.5 5.9 fusion.55
  1336.3 12.0 add.177
  1363.0 19.2 %collective-permute-done.23 = bf16[512,1024]{1,0:T(8,128)(2,1)S(1)} collective-permute-done((bf16[512,1024]{1,0:T(8,128)(2,1)S(1)}, bf16[512,1024]{1,0:T(8,128)(2,1)S(1)}, u32[]{:S(2)}, u32[]{:S(2)}) %collective-permute-start.23) | collective-permute-done | bytes 1048608 | tf_op jit(solution)/shard_map/ppermute | solution.py:429
  1404.5 20.6 %collective-permute-done.19 = bf16[512,2048]{1,0:T(8,128)(2,1)} collective-permute-done((bf16[512,2048]{1,0:T(8,128)(2,1)S(1)}, bf16[512,2048]{1,0:T(8,128)(2,1)}, u32[]{:S(2)}, u32[]{:S(2)}) %collective-permute-start.19) | collective-permute-done | bytes 2097184 | tf_op jit(solution)/shard_map/ppermute | solution.py:429
  1443.2 229.1 %collective-permute-done.35 = bf16[512,3072]{1,0:T(8,128)(2,1)} collective-permute-done((bf16[512,3072]{1,0:T(8,128)(2,1)S(1)}, bf16[512,3072]{1,0:T(8,128)(2,1)}, u32[]{:S(2)}, u32[]{:S(2)}) %collective-permute-start.35) | collective-permute-done | bytes 3145760 | tf_op jit(solution)/shard_map/ppermute | solution.py:429
  1677.6 6.5 maximum_select_fusion
  1700.1 51.4 %maximum_convert_fusion = f32[3072,2048]{1,0:T(8,128)} fusion(bf16[1536,1024]{1,0:T(8,128)(2,1)S(1)} %get-tuple-element.58, bf16[1536,1024]{1,0:T(8,128)(2,1)S(1)} %get-tuple-element.56, bf16[1536,1024]{1,0:T(8,128)(2,1)S(1)} %get-tuple-element.57, bf16[1536,1024]{1,0:T(8,128)(2,1)S(1)} %get-tuple-element.55), kind=kLoop, calls=%fused_computation.14 | loop fusion | flops 50331648 | bytes 37748736 | tf_op jit(solution)/shard_map/concatenate | solution.py:586
  1751.5 5.0 pad_maximum_fusion.1
  (329 shorter events, 197.4 us)
Async XLA Ops:
  7.2 98.1 %all-gather.6.cloned.1.call-start = ((), (), s32[]{:S(2)}) async-start(), calls=%async_computation.13 | async-start | bytes 10485760 | tf_op jit(solution)/shard_map/all_gather | solution.py:444
  14.9 265.5 %all-gather.8.cloned.1.call-start = ((), (), s32[]{:S(2)}) async-start(), calls=%async_computation.14 | async-start | bytes 5242880 | tf_op jit(solution)/shard_map/all_gather | solution.py:444
  17.8 372.5 %all-gather.10.cloned.1.call-start = ((), (), s32[]{:S(2)}) async-start(), calls=%async_computation.15 | async-start | bytes 31457280 | tf_op jit(solution)/shard_map/all_gather | solution.py:444
  27.7 4.4 collective-permute-start
  34.2 276.1 %copy-start = (bf16[2,256,2048]{2,1,0:T(8,128)(2,1)}, bf16[2,256,2048]{2,1,0:T(8,128)(2,1)S(1)}, u32[]{:S(2)}) copy-start(bf16[2,256,2048]{2,1,0:T(8,128)(2,1)S(1)} %get-tuple-element.75) | copy-start | bytes 6291460
  126.0 52.8 %all-to-all-start.2 = ((bf16[4,512,512]{2,1,0:T(8,128)(2,1)}), bf16[4,512,512]{2,1,0:T(8,128)(2,1)}, u32[]{:S(2)}, u32[]{:S(2)}) async-start(bf16[4,512,512]{2,1,0:T(8,128)(2,1)} %pack_heads.3), calls=%async_computation.2 | async-start | bytes 4194304 | tf_op jit(solution)/shard_map/all_to_all | solution.py:419
  130.6 384.3 %all-gather.12.cloned.1.call-start = ((), (), s32[]{:S(2)}) async-start(), calls=%async_computation.16 | async-start | bytes 15728640 | tf_op jit(solution)/shard_map/all_gather | solution.py:444
  178.9 52.4 %all-to-all-start = ((bf16[4,512,512]{2,1,0:T(8,128)(2,1)}), bf16[4,512,512]{2,1,0:T(8,128)(2,1)}, u32[]{:S(2)}, u32[]{:S(2)}) async-start(bf16[4,512,512]{2,1,0:T(8,128)(2,1)} %pack_heads.2), calls=%async_computation | async-start | bytes 4194304 | tf_op jit(solution)/shard_map/all_to_all | solution.py:419
  231.3 28.8 %all-to-all-start.3 = ((bf16[4,512,256]{2,1,0:T(8,128)(2,1)}), bf16[4,512,256]{2,1,0:T(8,128)(2,1)S(1)}, u32[]{:S(2)}, u32[]{:S(2)}) async-start(bf16[4,512,256]{2,1,0:T(8,128)(2,1)} %get-tuple-element.26.res_ref), calls=%async_computation.3 | async-start | bytes 2097152 | tf_op jit(solution)/shard_map/all_to_all | solution.py:419
  260.1 29.6 %all-to-all-start.1 = ((bf16[4,512,256]{2,1,0:T(8,128)(2,1)}), bf16[4,512,256]{2,1,0:T(8,128)(2,1)}, u32[]{:S(2)}, u32[]{:S(2)}) async-start(bf16[4,512,256]{2,1,0:T(8,128)(2,1)} %get-tuple-element.25.res_ref), calls=%async_computation.1 | async-start | bytes 2097152 | tf_op jit(solution)/shard_map/all_to_all | solution.py:419
  264.4 33.0 %collective-permute-start.4 = (bf16[2,256,2048]{2,1,0:T(8,128)(2,1)}, bf16[2,256,2048]{2,1,0:T(8,128)(2,1)}, u32[]{:S(2)}, u32[]{:S(2)}) collective-permute-start(bf16[2,256,2048]{2,1,0:T(8,128)(2,1)} %param.23), channel_id=1, source_target_pairs={{0,1},{1,0},{2,3},{3,2},{4,5},{5,4},{6,7},{7,6},{8,9},{9,8},{10,11... | collective-permute-start | bytes 6291464 | tf_op jit(solution)/shard_map/ppermute | solution.py:402
  286.6 15.6 collective-permute-start.2
  297.3 8.0 collective-permute-start.1
  541.4 41.8 %copy-start.1 = (bf16[2,256,2048]{2,1,0:T(8,128)(2,1)S(1)}, bf16[2,256,2048]{2,1,0:T(8,128)(2,1)}, u32[]{:S(2)}) copy-start(bf16[2,256,2048]{2,1,0:T(8,128)(2,1)} %copy-done) | copy-start | bytes 6291460
  541.4 41.8 %copy-start.5 = (bf16[2,256,2048]{2,1,0:T(8,128)(2,1)S(1)}, bf16[2,256,2048]{2,1,0:T(8,128)(2,1)}, u32[]{:S(2)}) copy-start(bf16[2,256,2048]{2,1,0:T(8,128)(2,1)} %copy-done.3) | copy-start | bytes 6291460
  541.4 41.8 %copy-start.39 = (f32[2048]{0:T(1024)S(1)}, f32[2048]{0:T(1024)}, u32[]{:S(2)}) copy-start(f32[2048]{0:T(1024)} %param.17) | copy-start | bytes 24580
  541.4 41.8 %copy-start.42 = (f32[1024]{0:T(1024)S(1)}, f32[1024]{0:T(1024)}, u32[]{:S(2)}) copy-start(f32[1024]{0:T(1024)} %copy-done.41) | copy-start | bytes 12292
  575.8 7.4 collective-permute-start.5
  617.0 31.0 %all-to-all-start.4 = ((bf16[4,512,256]{2,1,0:T(8,128)(2,1)}), bf16[4,512,256]{2,1,0:T(8,128)(2,1)S(1)}, u32[]{:S(2)}, u32[]{:S(2)}) async-start(bf16[4,512,256]{2,1,0:T(8,128)(2,1)} %get-tuple-element.27), calls=%async_computation.4 | async-start | bytes 2097152 | tf_op jit(solution)/shard_map/all_to_all | solution.py:419
  648.0 28.8 %all-to-all-start.6 = ((bf16[4,512,256]{2,1,0:T(8,128)(2,1)}), bf16[4,512,256]{2,1,0:T(8,128)(2,1)S(1)}, u32[]{:S(2)}, u32[]{:S(2)}) async-start(bf16[4,512,256]{2,1,0:T(8,128)(2,1)} %get-tuple-element.30), calls=%async_computation.6 | async-start | bytes 2097152 | tf_op jit(solution)/shard_map/all_to_all | solution.py:419
  676.8 51.3 %all-to-all-start.5 = ((bf16[4,512,512]{2,1,0:T(8,128)(2,1)}), bf16[4,512,512]{2,1,0:T(8,128)(2,1)S(1)}, u32[]{:S(2)}, u32[]{:S(2)}) async-start(bf16[4,512,512]{2,1,0:T(8,128)(2,1)} %attend_back.2), calls=%async_computation.5 | async-start | bytes 4194304 | tf_op jit(solution)/shard_map/all_to_all | solution.py:419
  728.1 52.3 %all-to-all-start.7 = ((bf16[4,512,512]{2,1,0:T(8,128)(2,1)}), bf16[4,512,512]{2,1,0:T(8,128)(2,1)}, u32[]{:S(2)}, u32[]{:S(2)}) async-start(bf16[4,512,512]{2,1,0:T(8,128)(2,1)} %attend_back.3), calls=%async_computation.7 | async-start | bytes 4194304 | tf_op jit(solution)/shard_map/all_to_all | solution.py:419
  732.6 189.2 %reduce-scatter.6.cloned.1.call-start = ((), (), s32[]{:S(2)}) async-start(), calls=%async_computation.17 | async-start | bytes 10485760 | tf_op jit(solution)/shard_map/reduce_scatter | solution.py:441
  804.7 140.1 %reduce-scatter.8.cloned.1.call-start = ((), (), s32[]{:S(2)}) async-start(), calls=%async_computation.18 | async-start | bytes 5242880 | tf_op jit(solution)/shard_map/reduce_scatter | solution.py:441
  814.7 258.6 %reduce-scatter.12.cloned.1.call-start = ((), (), s32[]{:S(2)}) async-start(), calls=%async_computation.20 | async-start | bytes 15728640 | tf_op jit(solution)/shard_map/reduce_scatter | solution.py:441
  836.7 360.3 %reduce-scatter.10.cloned.1.call-start = ((), (), s32[]{:S(2)}) async-start(), calls=%async_computation.19 | async-start | bytes 15728640 | tf_op jit(solution)/shard_map/reduce_scatter | solution.py:441
  858.4 462.3 %reduce-scatter.14.cloned.1.call-start = ((), (), s32[]{:S(2)}) async-start(), calls=%async_computation.21 | async-start | bytes 15728640 | tf_op jit(solution)/shard_map/reduce_scatter | solution.py:441
  921.9 54.1 %collective-permute-start.6 = (bf16[2,256,2048]{2,1,0:T(8,128)(2,1)}, bf16[2,256,2048]{2,1,0:T(8,128)(2,1)}, u32[]{:S(2)}, u32[]{:S(2)}) collective-permute-start(bf16[2,256,2048]{2,1,0:T(8,128)(2,1)} %select_bitcast_fusion), channel_id=1, source_target_pairs={{0,1},{1,0},{2,3},{3,2},{4,5},{5,4},{6,7},{7,6},{8,9},{9,8},{10,11... | collective-permute-start | bytes 6291464 | tf_op jit(solution)/shard_map/ppermute | solution.py:402
  921.9 47.6 %collective-permute-start.17 = (bf16[512,2048]{1,0:T(8,128)(2,1)}, bf16[512,2048]{1,0:T(8,128)(2,1)}, u32[]{:S(2)}, u32[]{:S(2)}) collective-permute-start(bf16[512,2048]{1,0:T(8,128)(2,1)} %reduce-scatter.6.cloned.1.call-done), channel_id=1, source_target_pairs={{0,2},{1,3},{6,4},{7,5},{8,10},{9,11},{14,12},{15,13},{16,18},{17,... | collective-permute-start | bytes 6291464 | tf_op jit(solution)/shard_map/ppermute | solution.py:427
  927.7 4.8 collective-permute-start.12
  932.4 43.6 %copy-start.37 = (f32[2048]{0:T(1024)S(1)}, f32[2048]{0:T(1024)}, u32[]{:S(2)}) copy-start(f32[2048]{0:T(1024)} %param.14) | copy-start | bytes 24580
  932.4 105.1 %collective-permute-start.3 = (bf16[2,256,2048]{2,1,0:T(8,128)(2,1)}, bf16[2,256,2048]{2,1,0:T(8,128)(2,1)}, u32[]{:S(2)}, u32[]{:S(2)}) collective-permute-start(bf16[2,256,2048]{2,1,0:T(8,128)(2,1)} %select_bitcast_fusion.1), channel_id=1, source_target_pairs={{0,1},{1,0},{2,3},{3,2},{4,5},{5,4},{6,7},{7,6},{8,9},{9,8},{10,11... | collective-permute-start | bytes 6291464 | tf_op jit(solution)/shard_map/ppermute | solution.py:402
  932.4 49.1 %collective-permute-start.13 = (f32[24,2048]{1,0:T(8,128)S(1)}, f32[24,2048]{1,0:T(8,128)S(1)}, u32[]{:S(2)}, u32[]{:S(2)}) collective-permute-start(f32[24,2048]{1,0:T(8,128)S(1)} %add.199), channel_id=1, source_target_pairs={{0,2},{1,3},{2,0},{3,1},{4,6},{5,7},{6,4},{7,5},{8,10},{9,11},{10,... | collective-permute-start | bytes 589832 | tf_op jit(solution)/shard_map/ppermute | solution.py:436
  944.8 51.4 %collective-permute-start.21 = (bf16[512,1024]{1,0:T(8,128)(2,1)}, bf16[512,1024]{1,0:T(8,128)(2,1)S(1)}, u32[]{:S(2)}, u32[]{:S(2)}) collective-permute-start(bf16[512,1024]{1,0:T(8,128)(2,1)} %reduce-scatter.8.cloned.1.call-done), channel_id=1, source_target_pairs={{0,2},{1,3},{6,4},{7,5},{8,10},{9,11},{14,12},{15,13},{16,18},{17,... | collective-permute-start | bytes 3145736 | tf_op jit(solution)/shard_map/ppermute | solution.py:427
  974.0 355.9 %collective-permute-start.18 = (bf16[512,2048]{1,0:T(8,128)(2,1)}, bf16[512,2048]{1,0:T(8,128)(2,1)}, u32[]{:S(2)}, u32[]{:S(2)}) collective-permute-start(bf16[512,2048]{1,0:T(8,128)(2,1)} %add.204), channel_id=1, source_target_pairs={{2,4},{3,5},{4,2},{5,3},{10,12},{11,13},{12,10},{13,11},{18,20},{1... | collective-permute-start | bytes 6291464 | tf_op jit(solution)/shard_map/ppermute | solution.py:428
  981.4 349.1 %copy-start.2 = (bf16[2,256,2048]{2,1,0:T(8,128)(2,1)S(1)}, bf16[2,256,2048]{2,1,0:T(8,128)(2,1)}, u32[]{:S(2)}) copy-start(bf16[2,256,2048]{2,1,0:T(8,128)(2,1)} %copy-done) | copy-start | bytes 6291460
  981.4 16.8 collective-permute-start.7
  981.6 53.7 %collective-permute-start.14 = (f32[24,2048]{1,0:T(8,128)S(1)}, f32[24,2048]{1,0:T(8,128)S(1)}, u32[]{:S(2)}, u32[]{:S(2)}) collective-permute-start(f32[24,2048]{1,0:T(8,128)S(1)} %add.200), channel_id=1, source_target_pairs={{0,4},{1,5},{2,6},{3,7},{4,0},{5,1},{6,2},{7,3},{8,12},{9,13},{10,... | collective-permute-start | bytes 589832 | tf_op jit(solution)/shard_map/ppermute | solution.py:436
  996.6 331.9 %collective-permute-start.22 = (bf16[512,1024]{1,0:T(8,128)(2,1)S(1)}, bf16[512,1024]{1,0:T(8,128)(2,1)}, u32[]{:S(2)}, u32[]{:S(2)}) collective-permute-start(bf16[512,1024]{1,0:T(8,128)(2,1)S(1)} %add.207), channel_id=1, source_target_pairs={{2,4},{3,5},{4,2},{5,3},{10,12},{11,13},{12,10},{13,11},{18,20},{1... | collective-permute-start | bytes 3145736 | tf_op jit(solution)/shard_map/ppermute | solution.py:428
  998.3 38.6 %collective-permute-start.8 = (f32[2,2048]{1,0:T(2,128)S(1)}, f32[2,2048]{1,0:T(2,128)S(1)}, u32[]{:S(2)}, u32[]{:S(2)}) collective-permute-start(f32[2,2048]{1,0:T(2,128)S(1)} %fusion.51), channel_id=1, source_target_pairs={{0,2},{1,3},{2,0},{3,1},{4,6},{5,7},{6,4},{7,5},{8,10},{9,11},{10,... | collective-permute-start | bytes 49160 | tf_op jit(solution)/shard_map/ppermute | solution.py:436
  1035.3 42.5 %collective-permute-start.15 = (f32[24,2048]{1,0:T(8,128)S(1)}, f32[24,2048]{1,0:T(8,128)S(1)}, u32[]{:S(2)}, u32[]{:S(2)}) collective-permute-start(f32[24,2048]{1,0:T(8,128)S(1)} %add.201), channel_id=1, source_target_pairs={{0,8},{8,0},{16,24},{24,16},{1,9},{9,1},{17,25},{25,17},{2,10},{10... | collective-permute-start | bytes 589832 | tf_op jit(solution)/shard_map/ppermute | solution.py:436
  1037.5 164.6 %collective-permute-start.9 = (f32[2,2048]{1,0:T(2,128)}, f32[2,2048]{1,0:T(2,128)}, u32[]{:S(2)}, u32[]{:S(2)}) collective-permute-start(f32[2,2048]{1,0:T(2,128)} %fusion.91), channel_id=1, source_target_pairs={{0,4},{1,5},{2,6},{3,7},{4,0},{5,1},{6,2},{7,3},{8,12},{9,13},{10,... | collective-permute-start | bytes 49160 | tf_op jit(solution)/shard_map/ppermute | solution.py:436
  1073.3 317.5 %collective-permute-start.29 = (bf16[1536,1024]{1,0:T(8,128)(2,1)}, bf16[1536,1024]{1,0:T(8,128)(2,1)}, u32[]{:S(2)}, u32[]{:S(2)}) collective-permute-start(bf16[1536,1024]{1,0:T(8,128)(2,1)} %reduce-scatter.12.cloned.1.call-done), channel_id=1, source_target_pairs={{0,2},{1,3},{6,4},{7,5},{8,10},{9,11},{14,12},{15,13},{16,18},{17,... | collective-permute-start | bytes 9437192 | tf_op jit(solution)/shard_map/ppermute | solution.py:427
  1077.8 248.3 %copy-start.33 = (f32[24,2048]{1,0:T(8,128)}, f32[24,2048]{1,0:T(8,128)S(1)}, u32[]{:S(2)}) copy-start(f32[24,2048]{1,0:T(8,128)S(1)} %collective-permute-done.15) | copy-start | bytes 589828
  1197.0 198.4 %collective-permute-start.25 = (bf16[1536,1024]{1,0:T(8,128)(2,1)}, bf16[1536,1024]{1,0:T(8,128)(2,1)}, u32[]{:S(2)}, u32[]{:S(2)}) collective-permute-start(bf16[1536,1024]{1,0:T(8,128)(2,1)} %reduce-scatter.10.cloned.1.call-done), channel_id=1, source_target_pairs={{0,2},{1,3},{6,4},{7,5},{8,10},{9,11},{14,12},{15,13},{16,18},{17,... | collective-permute-start | bytes 9437192 | tf_op jit(solution)/shard_map/ppermute | solution.py:427
  1320.7 79.0 %collective-permute-start.33 = (bf16[512,3072]{1,0:T(8,128)(2,1)}, bf16[512,3072]{1,0:T(8,128)(2,1)}, u32[]{:S(2)}, u32[]{:S(2)}) collective-permute-start(bf16[512,3072]{1,0:T(8,128)(2,1)} %reduce-scatter.14.cloned.1.call-done), channel_id=1, source_target_pairs={{0,2},{1,3},{6,4},{7,5},{8,10},{9,11},{14,12},{15,13},{16,18},{17,... | collective-permute-start | bytes 9437192 | tf_op jit(solution)/shard_map/ppermute | solution.py:427
  1328.4 25.6 %collective-permute-start.16 = (f32[24,2048]{1,0:T(8,128)S(1)}, f32[24,2048]{1,0:T(8,128)S(1)}, u32[]{:S(2)}, u32[]{:S(2)}) collective-permute-start(f32[24,2048]{1,0:T(8,128)S(1)} %add.202), channel_id=1, source_target_pairs={{0,16},{8,24},{16,0},{24,8},{1,17},{9,25},{17,1},{25,9},{2,18},{10... | collective-permute-start | bytes 589832 | tf_op jit(solution)/shard_map/ppermute | solution.py:436
  1329.9 25.7 %collective-permute-start.10 = (f32[2,2048]{1,0:T(2,128)}, f32[2,2048]{1,0:T(2,128)}, u32[]{:S(2)}, u32[]{:S(2)}) collective-permute-start(f32[2,2048]{1,0:T(2,128)} %add.196), channel_id=1, source_target_pairs={{0,8},{8,0},{16,24},{24,16},{1,9},{9,1},{17,25},{25,17},{2,10},{10... | collective-permute-start | bytes 49160 | tf_op jit(solution)/shard_map/ppermute | solution.py:436
  1350.1 35.8 %slice-start = ((s8[8388608]{0:T(1024)(128)(4,1)}), s8[4194304]{0:T(1024)(128)(4,1)S(1)}, s32[]{:S(2)}) async-start(s8[8388608]{0:T(1024)(128)(4,1)} %bitcast.149), calls=%async_computation.22 | async-start | bytes 8388608
  1354.0 32.0 %slice-start.1 = ((s8[8388608]{0:T(1024)(128)(4,1)}), s8[4194304]{0:T(1024)(128)(4,1)S(1)}, s32[]{:S(2)}) async-start(s8[8388608]{0:T(1024)(128)(4,1)} %bitcast.149), calls=%async_computation.23 | async-start | bytes 8388608
  1354.1 28.2 %collective-permute-start.23 = (bf16[512,1024]{1,0:T(8,128)(2,1)S(1)}, bf16[512,1024]{1,0:T(8,128)(2,1)S(1)}, u32[]{:S(2)}, u32[]{:S(2)}) collective-permute-start(bf16[512,1024]{1,0:T(8,128)(2,1)S(1)} %add.208), channel_id=1, source_target_pairs={{2,0},{3,1},{4,6},{5,7},{10,8},{11,9},{12,14},{13,15},{18,16},{19,... | collective-permute-start | bytes 3145736 | tf_op jit(solution)/shard_map/ppermute | solution.py:429
  1355.6 69.5 %collective-permute-start.19 = (bf16[512,2048]{1,0:T(8,128)(2,1)S(1)}, bf16[512,2048]{1,0:T(8,128)(2,1)}, u32[]{:S(2)}, u32[]{:S(2)}) collective-permute-start(bf16[512,2048]{1,0:T(8,128)(2,1)S(1)} %add.205), channel_id=1, source_target_pairs={{2,0},{3,1},{4,6},{5,7},{10,8},{11,9},{12,14},{13,15},{18,16},{19,... | collective-permute-start | bytes 6291464 | tf_op jit(solution)/shard_map/ppermute | solution.py:429
  1382.2 3.7 collective-permute-start.11
  1386.0 41.1 %collective-permute-start.24 = (bf16[512,1024]{1,0:T(8,128)(2,1)S(1)}, bf16[512,1024]{1,0:T(8,128)(2,1)S(1)}, u32[]{:S(2)}, u32[]{:S(2)}) collective-permute-start(bf16[512,1024]{1,0:T(8,128)(2,1)S(1)} %broadcast_select_fusion.13), channel_id=1, source_target_pairs={{0,1},{1,0},{2,3},{3,2},{4,5},{5,4},{6,7},{7,6},{8,9},{9,8},{10,11... | collective-permute-start | bytes 3145736 | tf_op jit(solution)/shard_map/ppermute | solution.py:402
  1394.4 35.4 %collective-permute-start.30 = (bf16[1536,1024]{1,0:T(8,128)(2,1)S(1)}, bf16[1536,1024]{1,0:T(8,128)(2,1)S(1)}, u32[]{:S(2)}, u32[]{:S(2)}) collective-permute-start(bf16[1536,1024]{1,0:T(8,128)(2,1)S(1)} %add.211), channel_id=1, source_target_pairs={{2,4},{3,5},{4,2},{5,3},{10,12},{11,13},{12,10},{13,11},{18,20},{1... | collective-permute-start | bytes 9437192 | tf_op jit(solution)/shard_map/ppermute | solution.py:428
  1398.8 33.9 %collective-permute-start.26 = (bf16[1536,1024]{1,0:T(8,128)(2,1)S(1)}, bf16[1536,1024]{1,0:T(8,128)(2,1)S(1)}, u32[]{:S(2)}, u32[]{:S(2)}) collective-permute-start(bf16[1536,1024]{1,0:T(8,128)(2,1)S(1)} %add.209), channel_id=1, source_target_pairs={{2,4},{3,5},{4,2},{5,3},{10,12},{11,13},{12,10},{13,11},{18,20},{1... | collective-permute-start | bytes 9437192 | tf_op jit(solution)/shard_map/ppermute | solution.py:428
  1402.7 32.9 %collective-permute-start.34 = (bf16[512,3072]{1,0:T(8,128)(2,1)S(1)}, bf16[512,3072]{1,0:T(8,128)(2,1)S(1)}, u32[]{:S(2)}, u32[]{:S(2)}) collective-permute-start(bf16[512,3072]{1,0:T(8,128)(2,1)S(1)} %add.213), channel_id=1, source_target_pairs={{2,4},{3,5},{4,2},{5,3},{10,12},{11,13},{12,10},{13,11},{18,20},{1... | collective-permute-start | bytes 9437192 | tf_op jit(solution)/shard_map/ppermute | solution.py:428
  1427.0 11.2 collective-permute-start.20
  1431.4 252.7 %collective-permute-start.31 = (bf16[1536,1024]{1,0:T(8,128)(2,1)S(1)}, bf16[1536,1024]{1,0:T(8,128)(2,1)}, u32[]{:S(2)}, u32[]{:S(2)}) collective-permute-start(bf16[1536,1024]{1,0:T(8,128)(2,1)S(1)} %add.212), channel_id=1, source_target_pairs={{2,0},{3,1},{4,6},{5,7},{10,8},{11,9},{12,14},{13,15},{18,16},{19,... | collective-permute-start | bytes 9437192 | tf_op jit(solution)/shard_map/ppermute | solution.py:429
  1434.3 252.1 %collective-permute-start.27 = (bf16[1536,1024]{1,0:T(8,128)(2,1)S(1)}, bf16[1536,1024]{1,0:T(8,128)(2,1)}, u32[]{:S(2)}, u32[]{:S(2)}) collective-permute-start(bf16[1536,1024]{1,0:T(8,128)(2,1)S(1)} %add.210), channel_id=1, source_target_pairs={{2,0},{3,1},{4,6},{5,7},{10,8},{11,9},{12,14},{13,15},{18,16},{19,... | collective-permute-start | bytes 9437192 | tf_op jit(solution)/shard_map/ppermute | solution.py:429
  1436.8 235.5 %collective-permute-start.35 = (bf16[512,3072]{1,0:T(8,128)(2,1)S(1)}, bf16[512,3072]{1,0:T(8,128)(2,1)}, u32[]{:S(2)}, u32[]{:S(2)}) collective-permute-start(bf16[512,3072]{1,0:T(8,128)(2,1)S(1)} %add.214), channel_id=1, source_target_pairs={{2,0},{3,1},{4,6},{5,7},{10,8},{11,9},{12,14},{13,15},{18,16},{19,... | collective-permute-start | bytes 9437192 | tf_op jit(solution)/shard_map/ppermute | solution.py:429
  1674.6 14.7 collective-permute-start.36
  1686.4 8.2 collective-permute-start.32
  1688.8 8.1 collective-permute-start.28
  (52 other events, 503.6 us)
Sparse Core Ops, SparseCore 0:
  15.0 90.1 all-gather.5
  107.1 52.5 all-gather.7
  162.2 228.0 all-gather.9
  392.6 122.3 all-gather.11
  804.8 84.4 reduce-scatter.5
  892.1 52.5 reduce-scatter.7
  948.4 124.7 reduce-scatter.11
  1076.4 120.5 reduce-scatter.9
  1200.1 120.5 reduce-scatter.13

commit v2 on v1

--- a/solution.py
+++ b/solution.py
@@ -367,6 +367,89 @@
         out_shape=[jax.ShapeDtypeStruct((chips, size, lanes), BF), jax.ShapeDtypeStruct((size, HEAD), BF)],
         name="gate_back",
     )(grad, result, logits)
+
+
+def join_rows_kernel(count, which_ref, *refs):
+    out_ref = refs[2 * count]
+    size = refs[0].shape[1]
+    own_half = pl.program_id(0) == which_ref[0]
+
+    def put(parts):
+        for k in range(count):
+            out_ref[:, k * size : (k + 1) * size] = parts[k][...].astype(F32)
+
+    pl.when(own_half)(lambda: put(refs[:count]))
+    pl.when(jnp.logical_not(own_half))(lambda: put(refs[count : 2 * count]))
+
+
+def join_rows(mine, other, core, unit, block):
+    count = len(mine)
+    height, size = mine[0].shape
+    steps = height // block
+    blocks = unit // block
+
+    def source(side):
+        def index(h, i, which):
+            active = (h == which[0]) if side == 0 else (h != which[0])
+            return (jnp.where(active, i, jnp.where(h == 0, 0, steps - 1)), 0)
+
+        return pl.BlockSpec((block, size), index)
+
+    def target(h, i, which):
+        per = which[1]
+        return ((i // per) * 2 * per + h * per + i % per, 0)
+
+    return pl.pallas_call(
+        functools.partial(join_rows_kernel, count),
+        grid_spec=pltpu.PrefetchScalarGridSpec(
+            num_scalar_prefetch=1,
+            grid=(CORES, steps),
+            in_specs=[source(0)] * count + [source(1)] * count,
+            out_specs=pl.BlockSpec((block, count * size), target),
+        ),
+        out_shape=jax.ShapeDtypeStruct((CORES * height, count * size), F32),
+        name="join_rows",
+    )(jnp.stack([core, jnp.asarray(blocks, jnp.int32)]), *mine, *other)
+
+
+def join_cols_kernel(count, per, which_ref, *refs):
+    out_ref = refs[2 * count]
+    u = pl.program_id(0)
+    own_half = pl.program_id(1) == which_ref[0]
+
+    def put(ref):
+        out_ref[...] = ref[...].astype(F32)
+
+    for k in range(count):
+        here = u // per == k
+        pl.when(here & own_half)(functools.partial(put, refs[k]))
+        pl.when(here & jnp.logical_not(own_half))(functools.partial(put, refs[count + k]))
+
+
+def join_cols(mine, other, core, unit):
+    count = len(mine)
+    height, size = mine[0].shape
+    per = size // unit
+
+    def source(k):
+        return pl.BlockSpec((height, unit), lambda u, h, which: (0, jnp.clip(u - k * per, 0, per - 1)))
+
+    sources = [source(k) for k in range(count)]
+    return pl.pallas_call(
+        functools.partial(join_cols_kernel, count, per),
+        grid_spec=pltpu.PrefetchScalarGridSpec(
+            num_scalar_prefetch=1,
+            grid=(count * per, CORES),
+            in_specs=sources + sources,
+            out_specs=pl.BlockSpec((height, unit), lambda u, h, which: (0, u * CORES + h)),
+        ),
+        out_shape=jax.ShapeDtypeStruct((height, CORES * count * size), F32),
+        name="join_cols",
+    )(core[None], *mine, *other)
+
+
+def tie(value, work):
+    return lax.optimization_barrier((value, work))
 
 
 def shards(
@@ -429,8 +512,9 @@
         spread = lax.ppermute(full, "seq", outward)
         return jnp.where((chip == 1) | (chip == 2), full, spread)
 
-    def total_sum(x):
-        for name, size in (("seq", seq), ("dp", dp)):
+    def total_sum(x, names=("seq", "dp")):
+        for name in names:
+            size = lax.axis_size(name)
             step = 1
             while step < size:
                 x = x + lax.ppermute(x, name, [(s, s ^ step) for s in range(size)])
@@ -454,22 +538,14 @@
             axis=1,
         )
 
-    def join_rows(low, high, unit):
-        parts = []
-        for a in range(0, low.shape[0], unit):
-            parts += [low[a : a + unit], high[a : a + unit]]
-        return jnp.concatenate(parts, axis=0)
-
-    def join_cols(low, high, unit):
-        parts = []
-        for a in range(0, low.shape[1], unit):
-            parts += [low[:, a : a + unit], high[:, a : a + unit]]
-        return jnp.concatenate(parts, axis=1)
-
     ff_unit = w_gu.shape[0] // CORES
     qkv_half = jnp.where(q_shard, core_rows(w_qkv, GROUP * HEAD), core_rows(w_qkv, HEAD))
     qkv_full = gather(qkv_half)
-    gate_full = gather(w_gate)
+    gate_count = w_gate.shape[0]
+    gate_full = lax.dynamic_update_slice_in_dim(
+        jnp.zeros((QUERY_HEADS, width), BF), w_gate, lax.axis_index("dp") * gate_count, 0
+    )
+    gate_full = total_sum(gate_full, ("dp",))
     out_full = gather(core_cols(w_out, GROUP * HEAD))
     gu_full = gather(core_rows(w_gu, ff_unit))
     down_full = gather(core_cols(w_down, ff_unit))
@@ -498,6 +574,7 @@
     packed, results, logs, gated, partial = [], [], [], [], []
     for row in range(rows):
         packed.append(exchange(pack_heads(proj, cos, sin, q_gain, k_gain, row, chips, chip_tok)))
+    packed[0], logits = tie(packed[0], logits)
     for row in range(rows):
         head_out, log = attend(packed[row], start[row : row + 1], low[row])
         results.append(head_out)
@@ -517,24 +594,27 @@
     gate_act = jax.nn.sigmoid(gate_part)
     silu = gate_part * gate_act
     hidden = (silu * up_part).astype(BF)
-    shard_down = scatter(dot_tn(d_out, hidden, BF))
+    part_down = [dot_tn(d_out, hidden[:, a : a + ff_unit], BF) for a in range(0, FF // CORES, ff_unit)]
+    down_full, part_down = tie(down_full, part_down)
+    shard_down = [scatter(p) for p in part_down]
     d_hidden = dot_nn(d_out, down_full)
     d_gate = d_hidden * up_part * gate_act * (1.0 + gate_part * (1.0 - gate_act))
     d_up = d_hidden * silu
     d_gate_up = jnp.concatenate([d_gate.astype(BF), d_up.astype(BF)], axis=1)
-    d_normed = pair_sum(dot_nn(d_gate_up, gu_full, BF))
-    half_cols = width // 2
-    shard_gu = [scatter(dot_tn(d_gate_up, normed_f[:, a : a + half_cols], BF)) for a in (0, half_cols)]
-    out_part = dot_nt(hidden, down_full, BF).reshape(rows, CORES, tok, width)
-    out_other = swap(pick(out_part[:, 1], out_part[:, 0]))
-    output = (own(mid) + pick(out_part[:, 0], out_part[:, 1]).astype(F32) + out_other.astype(F32)).astype(BF)
+    d_norm_mine = dot_nn(d_gate_up, gu_full, BF)
+    d_norm_pair = swap(d_norm_mine)
+    piece = width // 4
+    part_gu = [dot_tn(d_gate_up, normed_f[:, a : a + piece], BF) for a in range(0, width, piece)]
+    d_norm_pair, part_gu[:2] = tie(d_norm_pair, part_gu[:2])
+    d_normed = d_norm_mine.astype(F32) + d_norm_pair.astype(F32)
+    out_part = dot_nt(hidden, down_full, BF)
 
     part_ffn = 0.5 * jnp.sum(d_normed * mid * factor_f, axis=0)
     weighted = d_normed * ffn_norm
     inner = jnp.mean(weighted * mid, axis=-1, keepdims=True)
     d_mid = d_out.astype(F32) + factor_f * weighted - mid * factor_f**3 * inner
     d_mid_low = d_mid.astype(BF)
-    shard_out = scatter(dot_tn(d_mid_low, gated, BF))
+    part_out = dot_tn(d_mid_low, gated, BF)
 
     d_proj, d_logit, d_heads = [], [], []
     q_sum = 0.0
@@ -544,17 +624,28 @@
         d_attn, dl = gate_back(d_gated, tok_results[row], logits, row)
         d_logit.append(dl)
         d_heads.append(exchange(d_attn))
+    d_heads[0], part_gu[2:] = tie(d_heads[0], part_gu[2:])
+    d_heads[-1], part_out = tie(d_heads[-1], part_out)
+    shard_gu = [scatter(p) for p in part_gu]
+    shard_out = [scatter(part_out)]
+    back = []
     for row in range(rows):
-        grads = exchange(
-            attend_back(packed[row], d_heads[row], results[row], logs[row], start[row : row + 1], low[row])
+        back.append(
+            exchange(attend_back(packed[row], d_heads[row], results[row], logs[row], start[row : row + 1], low[row]))
         )
-        dpr, qs, ks = unpack_heads(grads, proj, cos, sin, q_gain, k_gain, row, chips, chip_tok)
+    back[0], out_part = tie(back[0], out_part)
+    out_part = out_part.reshape(rows, CORES, tok, width)
+    out_other = swap(pick(out_part[:, 1], out_part[:, 0]))
+    output = (own(mid) + pick(out_part[:, 0], out_part[:, 1]).astype(F32) + out_other.astype(F32)).astype(BF)
+    for row in range(rows):
+        dpr, qs, ks = unpack_heads(back[row], proj, cos, sin, q_gain, k_gain, row, chips, chip_tok)
         d_proj.append(dpr)
         q_sum = q_sum + qs
         k_sum = k_sum + ks
     d_proj = jnp.concatenate(d_proj, axis=0)
     d_logit = jnp.concatenate(d_logit, axis=0)
-    shard_qkv = scatter(dot_tn(d_proj, normed_a, BF))
+    half = width // 2
+    shard_qkv = [scatter(dot_tn(d_proj, normed_a[:, a : a + half], BF)) for a in (0, half)]
     d_norm_part = (dot_nn(d_proj, qkv_full) + dot_nn(d_logit, gate_core)).astype(BF)
     d_norm_part = d_norm_part.reshape(rows, CORES, tok, width)
     d_norm_other = swap(pick(d_norm_part[:, 1], d_norm_part[:, 0]))
@@ -568,27 +659,22 @@
 
     part_gate = dot_tn(d_logit, normed_a)[:CORE_Q]
     zero = jnp.zeros_like(part_gate)
-    part_gate = join_rows(pick(part_gate, zero), pick(zero, part_gate), GROUP)
+    part_gate = jnp.stack([pick(part_gate, zero).reshape(-1, GROUP, width), pick(zero, part_gate).reshape(-1, GROUP, width)], 1)
+    part_gate = part_gate.reshape(QUERY_HEADS, width)
     heads = jnp.concatenate([jnp.sum(q_sum, axis=0), jnp.sum(k_sum, axis=0)])
     heads = jnp.pad(heads, (0, width - heads.shape[0]))
     early = total_sum(jnp.concatenate([part_gate, part_ffn[None], jnp.zeros((7, width), F32)], axis=0))
     late = total_sum(jnp.stack([part_attn, heads]))
-    gate_count = w_gate.shape[0]
     grad_w_gate = lax.dynamic_slice_in_dim(early, lax.axis_index("dp") * gate_count, gate_count, 0)
 
-    def halves(shard):
-        mine = chip_sum(shard)
-        other = swap(mine)
-        return pick(mine, other).astype(F32), pick(other, mine).astype(F32)
-
-    grad_down = join_cols(*halves(shard_down), ff_unit)
-    gu_low, gu_high = zip(*[halves(s) for s in shard_gu])
-    grad_gu = jnp.concatenate([jnp.concatenate(gu_low, axis=1), jnp.concatenate(gu_high, axis=1)], axis=0)
-    grad_out = join_cols(*halves(shard_out), GROUP * HEAD)
-    qkv_low, qkv_high = halves(shard_qkv)
-    grad_qkv = jnp.where(
-        q_shard, join_rows(qkv_low, qkv_high, GROUP * HEAD), join_rows(qkv_low, qkv_high, HEAD)
-    )
+    def halves(parts):
+        mine = [chip_sum(p) for p in parts]
+        return mine, [swap(p) for p in mine]
+
+    grad_down = join_cols(*halves(shard_down), core, ff_unit)
+    grad_gu = join_rows(*halves(shard_gu), core, ff_unit, 256)
+    grad_out = join_cols(*halves(shard_out), core, GROUP * HEAD)
+    grad_qkv = join_rows(*halves(shard_qkv), core, jnp.where(q_shard, GROUP * HEAD, HEAD), HEAD)
     return (
         output,
         grad_input,

time: 1770 us -> 1510 us (0.85)
  waiting for transfers between devices: 1040 us -> 755 us
  other arithmetic: 220 us -> 168 us
  starting transfers between devices: 83.8 us -> 122 us
  Pallas kernels: 102 us -> 136 us
    reduce_scatter x5 -> x9, waiting for transfers between devices: 286 us -> 41.8 us  [scatter(): return lax.psum_scatter(x, 'dp', scatter_dimension=0, tiled=True)]
    ppermute x5 -> x9, waiting for transfers between devices: 269 us -> 167 us  [chip_sum(): spread = lax.ppermute(full, 'seq', outward)]
    ppermute x5 -> x9, waiting for transfers between devices: 31.2 us -> 117 us  [chip_sum(): half = x + lax.ppermute(x, 'seq', inward)]
    concatenate x2 -> x1, other arithmetic: 56.4 us -> 0.08 us  [shards(): jnp.concatenate([part_gate, part_ffn[None], jnp.zeros((7, width), F32)],...]
    pallas_call x0 -> x4, Pallas kernels: none -> 38.8 us  [the longest x2 24.7 us: join_rows(): pl.pallas_call(functools.partial(join_rows_kernel, count), grid_spec=pltp...]
    ppermute x10 -> x12, waiting for transfers between devices: 35.9 us -> 63.7 us  [total_sum(): x = x + lax.ppermute(x, name, [(s, s ^ step) for s in range(size)])]
    all_gather x4, waiting for transfers between devices: 236 us -> 209 us  [gather(): return lax.all_gather(x, 'dp', axis=0, tiled=True)]
    all_to_all x8, waiting for transfers between devices: 176 us -> 154 us  [exchange(): return lax.all_to_all(x, 'seq', 0, 0, axis_index_groups=groups, tiled=True)]
  transfers between devices with their start and end apart: 54 -> 76, of which waited for: 24 -> 30; matrix products, arithmetic and copies ran while one was open for 18% -> 29% of each run, Pallas kernels for 5% -> 8%
where the time goes in v2:
time: 1510 us; the launch traced here: 1500 us
  waiting for transfers between devices  755 us (50%)
  matrix products  273 us (18%)
  other arithmetic  168 us (11%)
  Pallas kernels  136 us (9%)
  starting transfers between devices  122 us (8%)
  local copies, waits for them, and re-layouts  27.6 us (2%)
  between operations  15.5 us (1%)
    all_gather x4, waiting for transfers between devices, gather(): return lax.all_gather(x, 'dp', axis=0, tiled=True)  209 us
    ppermute x9, waiting for transfers between devices, chip_sum(): spread = lax.ppermute(full, 'seq', outward)  167 us
    all_to_all x8, waiting for transfers between devices, exchange(): return lax.all_to_all(x, 'seq', 0, 0, axis_index_groups=groups, tiled=True)  154 us
    ppermute x9, waiting for transfers between devices, chip_sum(): half = x + lax.ppermute(x, 'seq', inward)  117 us
    dot_general x10, matrix products, dot_tn(): lax.dot_general(left, right, (((0,), (0,)), ((), ())), preferred_element_...  104 us
    dot_general x6, matrix products, dot_nn(): lax.dot_general(left, right, (((1,), (0,)), ((), ())), preferred_element_...  88.4 us
    dot_general x6, matrix products, dot_nt(): lax.dot_general(left, right, (((1,), (1,)), ((), ())), preferred_element_...  80.5 us
    ppermute x12, waiting for transfers between devices, total_sum(): x = x + lax.ppermute(x, name, [(s, s ^ step) for s in range(size)])  63.7 us
  transfers between devices with their start and end apart: 76, of which 30 were waited for; matrix products, arithmetic and copies ran while one was open for 29% of the time, Pallas kernels for 8%

profile of v2, /device:TPU:0, one launch (start us, length us, event | category | flops | bytes accessed | tf_op | source)
XLA Modules:
  0.0 1496.5 jit_solution(12974325261521526173)
XLA Ops:
  16.9 8.0 slice_select_fusion
  37.3 67.0 %all-gather.5.cloned.1.call-done = bf16[2048,2048]{1,0:T(8,128)(2,1)} async-done(((bf16[512,2048]{1,0:T(8,128)(2,1)}), bf16[2048,2048]{1,0:T(8,128)(2,1)}) %all-gather.5.cloned.1.call-update) | async-done | bytes 8388624 | tf_op jit(solution)/shard_map/all_gather | solution.py:528
  104.4 14.6 fusion.62.proj_ref
  118.9 6.2 pack_heads.3
  125.1 4.8 all-to-all-start.2
  129.9 6.2 pack_heads.2
  136.1 42.0 %all-to-all-done.2.q_ref.k_ref.v_ref = bf16[4,512,512]{2,1,0:T(8,128)(2,1)} async-done(((bf16[4,512,512]{2,1,0:T(8,128)(2,1)}), bf16[4,512,512]{2,1,0:T(8,128)(2,1)}, u32[]{:S(2)}, u32[]{:S(2)}) %all-to-all-start.2) | async-done | bytes 2097184 | tf_op jit(solution)/shard_map/all_to_all | solution.py:502
  184.0 10.9 attend.3
  194.9 35.7 %all-to-all-done.q_ref.k_ref.v_ref = bf16[4,512,512]{2,1,0:T(8,128)(2,1)} async-done(((bf16[4,512,512]{2,1,0:T(8,128)(2,1)}), bf16[4,512,512]{2,1,0:T(8,128)(2,1)}, u32[]{:S(2)}, u32[]{:S(2)}) %all-to-all-start) | async-done | bytes 2097184 | tf_op jit(solution)/shard_map/all_to_all | solution.py:502
  250.3 8.8 attend.2
  260.3 4.7 all-to-all-start.1
  273.4 6.2 convolution_convert_fusion.12
  280.1 9.0 all-to-all-done.1.res_ref
  292.7 5.0 convolution_convert_fusion.13
  313.9 76.3 %all-gather.11.cloned.1.call-done = bf16[6144,2048]{1,0:T(8,128)(2,1)} async-done(((bf16[1536,2048]{1,0:T(8,128)(2,1)}), bf16[6144,2048]{1,0:T(8,128)(2,1)}) %all-gather.11.cloned.1.call-update) | async-done | bytes 25165840 | tf_op jit(solution)/shard_map/all_gather | solution.py:528
  390.3 30.7 %convolution_convert_fusion = bf16[1024,6144]{1,0:T(8,128)(2,1)S(1)} fusion(bf16[1024,2048]{1,0:T(8,128)(2,1)} %multiply_convert_fusion.1, bf16[6144,2048]{1,0:T(8,128)(2,1)} %all-gather.11.cloned.1.call-done), kind=kOutput, calls=%fused_computation.15 | convolution fusion | flops 25776095232 | bytes 41943040 | tf_op jit(solution)/shard_map/dot_general | solution.py:29
  429.3 9.1 convolution_convert_fusion.5
  438.4 11.5 convolution_convert_fusion.6
  449.8 65.1 %all-gather.9.cloned.1.call-done = bf16[2048,3072]{1,0:T(8,128)(2,1)} async-done(((bf16[512,3072]{1,0:T(8,128)(2,1)}), bf16[2048,3072]{1,0:T(8,128)(2,1)}) %all-gather.9.cloned.1.call-update) | async-done | bytes 12582928 | tf_op jit(solution)/shard_map/all_gather | solution.py:528
  515.0 26.8 %fusion.3 = (bf16[1024,3072]{1,0:T(8,128)(2,1)}, bf16[1024,3072]{1,0:T(8,128)(2,1)}) fusion(bf16[1024,6144]{1,0:T(8,128)(2,1)} %copy-done.18, bf16[1024,2048]{1,0:T(8,128)(2,1)} %bitcast.160, bf16[2048,3072]{1,0:T(8,128)(2,1)} %all-gather.9.cloned.1.call-done), kind=kOutput, calls=%fused_computation.8 | convolution fusion | flops 12932087808 | bytes 41943040 | tf_op jit(solution)/shard_map/dot_general | solution.py:33
  541.8 34.8 %convolution_convert_fusion.8 = bf16[1024,2048]{1,0:T(8,128)(2,1)} fusion(bf16[6144,2048]{1,0:T(8,128)(2,1)} %all-gather.11.cloned.1.call-done, bf16[1024,3072]{1,0:T(8,128)(2,1)} %get-tuple-element.77, bf16[1024,3072]{1,0:T(8,128)(2,1)} %get-tuple-element.76), kind=kOutput, calls=%fused_computation.65 | convolution fusion | flops 25797066752 | bytes 41943040 | tf_op jit(solution)/shard_map/dot_general | solution.py:33
  576.8 14.4 convolution_convert_fusion.4
  591.1 14.6 convolution_convert_fusion.3
  605.8 9.1 multiply_reduce_fusion
  614.8 15.3 %fusion.60 = (bf16[1024,2048]{1,0:T(8,128)(2,1)}, f32[1024,2048]{1,0:T(8,128)}, f32[1024,2048]{1,0:T(8,128)}) fusion(f32[1024]{0:T(1024)S(1)} %broadcast_multiply_fusion.1, f32[1024]{0:T(1024)S(1)} %copy-done.69, f32[512,2048]{1,0:T(8,128)} %copy-done.6, f32[512,2048]{1,0:T(8,128)} %copy-done.7, bf16[2,256,2048]{2,1,0:T(8,128)(2,1)} %copy-done.3, ...), kind=kLoop, calls=%fused_computation.188 | loop fusion | flops 35651584 | bytes 46157824 | tf_op jit(solution)/shard_map/convert_element_type | solution.py:616
  630.1 6.6 fusion.30.grad_ref
  645.5 8.3 convolution_convert_fusion.11
  653.8 18.4 %all-to-all-done.6.grad_ref = bf16[4,512,256]{2,1,0:T(8,128)(2,1)S(1)} async-done(((bf16[4,512,256]{2,1,0:T(8,128)(2,1)}), bf16[4,512,256]{2,1,0:T(8,128)(2,1)S(1)}, u32[]{:S(2)}, u32[]{:S(2)}) %all-to-all-start.6) | async-done | bytes 1048608 | tf_op jit(solution)/shard_map/all_to_all | solution.py:502
  673.9 6.5 fusion.32.grad_ref
  688.2 14.7 convolution_convert_fusion.2
  702.9 14.7 convolution_convert_fusion.1
  718.6 16.4 %attend_back.2 = bf16[4,512,512]{2,1,0:T(8,128)(2,1)} custom-call(s32[4]{0:T(128)} %get-tuple-element.112.low_ref, bf16[4,512,512]{2,1,0:T(8,128)(2,1)} %all-to-all-done.q_ref.k_ref.v_ref, bf16[4,512,512]{2,1,0:T(8,128)(2,1)} %all-to-all-done.q_ref.k_ref.v_ref, bf16[4,512,512]{2,1,0:T(8,128)(2,1)} %all-to-all-done.q_ref.k_ref.v_ref, ...), custom_call_target="tpu_custom_call" | custom-call | tf_op jit(solution)/shard_map/attend_back/pallas_call | solution.py:281
  735.0 5.0 all-to-all-start.5
  740.0 19.9 %attend_back.3 = bf16[4,512,512]{2,1,0:T(8,128)(2,1)} custom-call(s32[4]{0:T(128)} %get-tuple-element.113.low_ref, bf16[4,512,512]{2,1,0:T(8,128)(2,1)} %all-to-all-done.2.q_ref.k_ref.v_ref, bf16[4,512,512]{2,1,0:T(8,128)(2,1)} %all-to-all-done.2.q_ref.k_ref.v_ref, bf16[4,512,512]{2,1,0:T(8,128)(2,1)} %all-to-all-done.2.q_ref.k_ref.v_ref, ...), custom_call_target="tpu_custom_call" | custom-call | tf_op jit(solution)/shard_map/attend_back/pallas_call | solution.py:281
  759.9 27.8 %all-to-all-done.5.grad_ref = bf16[4,512,512]{2,1,0:T(8,128)(2,1)S(1)} async-done(((bf16[4,512,512]{2,1,0:T(8,128)(2,1)}), bf16[4,512,512]{2,1,0:T(8,128)(2,1)S(1)}, u32[]{:S(2)}, u32[]{:S(2)}) %all-to-all-start.5) | async-done | bytes 2097184 | tf_op jit(solution)/shard_map/all_to_all | solution.py:502
  792.3 19.7 %convolution_convert_fusion.7 = bf16[1024,2048]{1,0:T(8,128)(2,1)} fusion(bf16[1024,3072]{1,0:T(8,128)(2,1)} %copy-done.23, bf16[2048,3072]{1,0:T(8,128)(2,1)} %all-gather.9.cloned.1.call-done), kind=kOutput, calls=%fused_computation.64 | convolution fusion | flops 12886999040 | bytes 23068672 | tf_op jit(solution)/shard_map/dot_general | solution.py:29
  812.0 7.5 unpack_heads.2
  819.5 20.6 %all-to-all-done.7.grad_ref = bf16[4,512,512]{2,1,0:T(8,128)(2,1)} async-done(((bf16[4,512,512]{2,1,0:T(8,128)(2,1)}), bf16[4,512,512]{2,1,0:T(8,128)(2,1)}, u32[]{:S(2)}, u32[]{:S(2)}) %all-to-all-start.7) | async-done | bytes 2097184 | tf_op jit(solution)/shard_map/all_to_all | solution.py:502
  840.1 7.5 unpack_heads.3
  852.8 6.3 convolution_convert_fusion.9
  862.1 9.5 convolution_convert_fusion.10
  871.7 12.5 fusion.63
  897.8 29.4 %collective-permute-done.50 = bf16[512,1536]{1,0:T(8,128)(2,1)} collective-permute-done((bf16[512,1536]{1,0:T(8,128)(2,1)}, bf16[512,1536]{1,0:T(8,128)(2,1)}, u32[]{:S(2)}, u32[]{:S(2)}) %collective-permute-start.50) | collective-permute-done | bytes 1572896 | tf_op jit(solution)/shard_map/ppermute | solution.py:510
  932.5 27.7 %collective-permute-done.47 = bf16[512,1536]{1,0:T(8,128)(2,1)} collective-permute-done((bf16[512,1536]{1,0:T(8,128)(2,1)}, bf16[512,1536]{1,0:T(8,128)(2,1)}, u32[]{:S(2)}, u32[]{:S(2)}) %collective-permute-start.47) | collective-permute-done | bytes 1572896 | tf_op jit(solution)/shard_map/ppermute | solution.py:510
  965.4 5.9 fusion.17
  980.9 26.6 %collective-permute-done.16 = f32[24,2048]{1,0:T(8,128)S(1)} collective-permute-done((f32[24,2048]{1,0:T(8,128)S(1)}, f32[24,2048]{1,0:T(8,128)S(1)}, u32[]{:S(2)}, u32[]{:S(2)}) %collective-permute-start.16) | collective-permute-done | bytes 196640 | tf_op jit(solution)/shard_map/ppermute | solution.py:520
  1012.7 24.8 %collective-permute-done.10 = f32[2,2048]{1,0:T(2,128)S(1)} collective-permute-done((f32[2,2048]{1,0:T(2,128)S(1)}, f32[2,2048]{1,0:T(2,128)S(1)}, u32[]{:S(2)}, u32[]{:S(2)}) %collective-permute-start.10) | collective-permute-done | bytes 16416 | tf_op jit(solution)/shard_map/ppermute | solution.py:520
  1044.8 5.7 collective-permute-start.18
  1054.3 4.9 collective-permute-start.31
  1076.3 12.4 collective-permute-start.37
  1088.6 41.7 %reduce-scatter.10.cloned.1.call-done = bf16[512,1024]{1,0:T(8,128)(2,1)} async-done(((bf16[2048,1024]{1,0:T(8,128)(2,1)}), bf16[512,1024]{1,0:T(8,128)(2,1)}) %reduce-scatter.10.cloned.1.call-update) | async-done | bytes 1048592 | tf_op jit(solution)/shard_map/reduce_scatter | solution.py:525
  1142.0 60.2 %collective-permute-done.19 = bf16[512,1024]{1,0:T(8,128)(2,1)S(1)} collective-permute-done((bf16[512,1024]{1,0:T(8,128)(2,1)}, bf16[512,1024]{1,0:T(8,128)(2,1)S(1)}, u32[]{:S(2)}, u32[]{:S(2)}) %collective-permute-start.19) | collective-permute-done | bytes 1048608 | tf_op jit(solution)/shard_map/ppermute | solution.py:510
  1224.9 11.9 add.223
  1247.5 12.4 collective-permute-done.29
  1273.1 14.7 collective-permute-done.24
  1294.6 26.9 %collective-permute-done.36 = bf16[1536,512]{1,0:T(8,128)(2,1)S(1)} collective-permute-done((bf16[1536,512]{1,0:T(8,128)(2,1)S(1)}, bf16[1536,512]{1,0:T(8,128)(2,1)S(1)}, u32[]{:S(2)}, u32[]{:S(2)}) %collective-permute-start.36) | collective-permute-done | bytes 1572896 | tf_op jit(solution)/shard_map/ppermute | solution.py:512
  1324.2 31.0 %collective-permute-done.33 = bf16[1536,512]{1,0:T(8,128)(2,1)S(1)} collective-permute-done((bf16[1536,512]{1,0:T(8,128)(2,1)S(1)}, bf16[1536,512]{1,0:T(8,128)(2,1)S(1)}, u32[]{:S(2)}, u32[]{:S(2)}) %collective-permute-start.33) | collective-permute-done | bytes 1572896 | tf_op jit(solution)/shard_map/ppermute | solution.py:512
  1357.2 31.8 %collective-permute-done.42 = bf16[1536,512]{1,0:T(8,128)(2,1)S(1)} collective-permute-done((bf16[1536,512]{1,0:T(8,128)(2,1)S(1)}, bf16[1536,512]{1,0:T(8,128)(2,1)S(1)}, u32[]{:S(2)}, u32[]{:S(2)}) %collective-permute-start.42) | collective-permute-done | bytes 1572896 | tf_op jit(solution)/shard_map/ppermute | solution.py:512
  1391.9 30.8 %collective-permute-done.39 = bf16[1536,512]{1,0:T(8,128)(2,1)S(1)} collective-permute-done((bf16[1536,512]{1,0:T(8,128)(2,1)S(1)}, bf16[1536,512]{1,0:T(8,128)(2,1)S(1)}, u32[]{:S(2)}, u32[]{:S(2)}) %collective-permute-start.39) | collective-permute-done | bytes 1572896 | tf_op jit(solution)/shard_map/ppermute | solution.py:512
  1425.2 15.0 %collective-permute-done.21 = bf16[512,1024]{1,0:T(8,128)(2,1)S(1)} collective-permute-done((bf16[512,1024]{1,0:T(8,128)(2,1)S(1)}, bf16[512,1024]{1,0:T(8,128)(2,1)S(1)}, u32[]{:S(2)}, u32[]{:S(2)}) %collective-permute-start.21) | collective-permute-done | bytes 1048608 | tf_op jit(solution)/shard_map/ppermute | solution.py:512
  1449.9 6.4 join_cols.2
  1456.3 7.7 join_cols.3
  1465.0 8.4 join_rows.2
  1473.4 16.3 %join_rows.3 = f32[3072,2048]{1,0:T(8,128)} custom-call(s32[2]{0:T(128)} %get-tuple-element.115.which_ref, bf16[1536,512]{1,0:T(8,128)(2,1)} %broadcast_select_fusion.10.refs_0_, bf16[1536,512]{1,0:T(8,128)(2,1)} %broadcast_select_fusion.9.refs_1_, bf16[1536,512]{1,0:T(8,128)(2,1)} %broadcast_select_fusion.8.refs_2_, ...), custom_call_target="tpu_custom_call" | custom-call | tf_op jit(solution)/shard_map/join_rows/pallas_call | solution.py:402
  (416 shorter events, 269.7 us)
Async XLA Ops:
  7.2 97.2 %all-gather.5.cloned.1.call-start = ((), (), s32[]{:S(2)}) async-start(), calls=%async_computation.17 | async-start | bytes 10485760 | tf_op jit(solution)/shard_map/all_gather | solution.py:528
  14.0 259.4 %all-gather.7.cloned.1.call-start = ((), (), s32[]{:S(2)}) async-start(), calls=%async_computation.18 | async-start | bytes 5242880 | tf_op jit(solution)/shard_map/all_gather | solution.py:528
  16.9 373.4 %all-gather.11.cloned.1.call-start = ((), (), s32[]{:S(2)}) async-start(), calls=%async_computation.20 | async-start | bytes 31457280 | tf_op jit(solution)/shard_map/all_gather | solution.py:528
  125.1 53.1 %all-to-all-start.2 = ((bf16[4,512,512]{2,1,0:T(8,128)(2,1)}), bf16[4,512,512]{2,1,0:T(8,128)(2,1)}, u32[]{:S(2)}, u32[]{:S(2)}) async-start(bf16[4,512,512]{2,1,0:T(8,128)(2,1)} %pack_heads.3), calls=%async_computation.2 | async-start | bytes 4194304 | tf_op jit(solution)/shard_map/all_to_all | solution.py:502
  178.1 52.4 %all-to-all-start = ((bf16[4,512,512]{2,1,0:T(8,128)(2,1)}), bf16[4,512,512]{2,1,0:T(8,128)(2,1)}, u32[]{:S(2)}, u32[]{:S(2)}) async-start(bf16[4,512,512]{2,1,0:T(8,128)(2,1)} %pack_heads.2), calls=%async_computation | async-start | bytes 4194304 | tf_op jit(solution)/shard_map/all_to_all | solution.py:502
  230.6 28.8 %all-to-all-start.3 = ((bf16[4,512,256]{2,1,0:T(8,128)(2,1)}), bf16[4,512,256]{2,1,0:T(8,128)(2,1)S(1)}, u32[]{:S(2)}, u32[]{:S(2)}) async-start(bf16[4,512,256]{2,1,0:T(8,128)(2,1)} %get-tuple-element.43.res_ref), calls=%async_computation.3 | async-start | bytes 2097152 | tf_op jit(solution)/shard_map/all_to_all | solution.py:502
  260.3 28.8 %all-to-all-start.1 = ((bf16[4,512,256]{2,1,0:T(8,128)(2,1)}), bf16[4,512,256]{2,1,0:T(8,128)(2,1)S(1)}, u32[]{:S(2)}, u32[]{:S(2)}) async-start(bf16[4,512,256]{2,1,0:T(8,128)(2,1)} %get-tuple-element.41.res_ref), calls=%async_computation.1 | async-start | bytes 2097152 | tf_op jit(solution)/shard_map/all_to_all | solution.py:502
  265.0 249.9 %all-gather.9.cloned.1.call-start = ((), (), s32[]{:S(2)}) async-start(), calls=%async_computation.19 | async-start | bytes 15728640 | tf_op jit(solution)/shard_map/all_gather | solution.py:528
  270.2 620.6 %reduce-scatter.26.cloned.1.call-start = ((), (), s32[]{:S(2)}) async-start(), calls=%async_computation.29 | async-start | bytes 7864320 | tf_op jit(solution)/shard_map/reduce_scatter | solution.py:525
  270.7 27.1 %collective-permute-start.5 = (bf16[2,256,2048]{2,1,0:T(8,128)(2,1)}, bf16[2,256,2048]{2,1,0:T(8,128)(2,1)}, u32[]{:S(2)}, u32[]{:S(2)}) collective-permute-start(bf16[2,256,2048]{2,1,0:T(8,128)(2,1)} %param.23), channel_id=1, source_target_pairs={{0,1},{1,0},{2,3},{3,2},{4,5},{5,4},{6,7},{7,6},{8,9},{9,8},{10,11... | collective-permute-start | bytes 6291464 | tf_op jit(solution)/shard_map/ppermute | solution.py:485
  279.7 22.8 %collective-permute-start.4 = (bf16[512,2048]{1,0:T(8,128)(2,1)}, bf16[512,2048]{1,0:T(8,128)(2,1)}, u32[]{:S(2)}, u32[]{:S(2)}) collective-permute-start(bf16[512,2048]{1,0:T(8,128)(2,1)} %convolution_convert_fusion.12), channel_id=1, source_target_pairs={{0,1},{1,0},{2,3},{3,2},{4,5},{5,4},{6,7},{7,6},{8,9},{9,8},{10,11... | collective-permute-start | bytes 6291464 | tf_op jit(solution)/shard_map/ppermute | solution.py:485
  515.0 378.4 %reduce-scatter.24.cloned.1.call-start = ((), (), s32[]{:S(2)}) async-start(), calls=%async_computation.28 | async-start | bytes 7864320 | tf_op jit(solution)/shard_map/reduce_scatter | solution.py:525
  576.7 29.1 %collective-permute-start.6 = (bf16[1024,2048]{1,0:T(8,128)(2,1)}, bf16[1024,2048]{1,0:T(8,128)(2,1)}, u32[]{:S(2)}, u32[]{:S(2)}) collective-permute-start(bf16[1024,2048]{1,0:T(8,128)(2,1)} %convolution_convert_fusion.8), channel_id=1, source_target_pairs={{0,1},{1,0},{2,3},{3,2},{4,5},{5,4},{6,7},{7,6},{8,9},{9,8},{10,11... | collective-permute-start | bytes 12582920 | tf_op jit(solution)/shard_map/ppermute | solution.py:485
  640.9 31.3 %all-to-all-start.6 = ((bf16[4,512,256]{2,1,0:T(8,128)(2,1)}), bf16[4,512,256]{2,1,0:T(8,128)(2,1)S(1)}, u32[]{:S(2)}, u32[]{:S(2)}) async-start(bf16[4,512,256]{2,1,0:T(8,128)(2,1)} %get-tuple-element.52), calls=%async_computation.6 | async-start | bytes 2097152 | tf_op jit(solution)/shard_map/all_to_all | solution.py:502
  645.5 330.6 %reduce-scatter.14.cloned.1.call-start = ((), (), s32[]{:S(2)}) async-start(), calls=%async_computation.23 | async-start | bytes 5242880 | tf_op jit(solution)/shard_map/reduce_scatter | solution.py:525
  672.3 305.2 %reduce-scatter.18.cloned.1.call-start = ((), (), s32[]{:S(2)}) async-start(), calls=%async_computation.25 | async-start | bytes 7864320 | tf_op jit(solution)/shard_map/reduce_scatter | solution.py:525
  673.2 381.1 %reduce-scatter.16.cloned.1.call-start = ((), (), s32[]{:S(2)}) async-start(), calls=%async_computation.24 | async-start | bytes 7864320 | tf_op jit(solution)/shard_map/reduce_scatter | solution.py:525
  684.4 33.2 %all-to-all-start.4 = ((bf16[4,512,256]{2,1,0:T(8,128)(2,1)}), bf16[4,512,256]{2,1,0:T(8,128)(2,1)S(1)}, u32[]{:S(2)}, u32[]{:S(2)}) async-start(bf16[4,512,256]{2,1,0:T(8,128)(2,1)} %get-tuple-element.46), calls=%async_computation.4 | async-start | bytes 2097152 | tf_op jit(solution)/shard_map/all_to_all | solution.py:502
  735.0 52.8 %all-to-all-start.5 = ((bf16[4,512,512]{2,1,0:T(8,128)(2,1)}), bf16[4,512,512]{2,1,0:T(8,128)(2,1)S(1)}, u32[]{:S(2)}, u32[]{:S(2)}) async-start(bf16[4,512,512]{2,1,0:T(8,128)(2,1)} %attend_back.2), calls=%async_computation.5 | async-start | bytes 4194304 | tf_op jit(solution)/shard_map/all_to_all | solution.py:502
  787.8 52.3 %all-to-all-start.7 = ((bf16[4,512,512]{2,1,0:T(8,128)(2,1)}), bf16[4,512,512]{2,1,0:T(8,128)(2,1)}, u32[]{:S(2)}, u32[]{:S(2)}) async-start(bf16[4,512,512]{2,1,0:T(8,128)(2,1)} %attend_back.3), calls=%async_computation.7 | async-start | bytes 4194304 | tf_op jit(solution)/shard_map/all_to_all | solution.py:502
  792.2 268.6 %reduce-scatter.12.cloned.1.call-start = ((), (), s32[]{:S(2)}) async-start(), calls=%async_computation.22 | async-start | bytes 5242880 | tf_op jit(solution)/shard_map/reduce_scatter | solution.py:525
  859.1 204.6 %reduce-scatter.22.cloned.1.call-start = ((), (), s32[]{:S(2)}) async-start(), calls=%async_computation.27 | async-start | bytes 7864320 | tf_op jit(solution)/shard_map/reduce_scatter | solution.py:525
  859.9 216.3 %reduce-scatter.20.cloned.1.call-start = ((), (), s32[]{:S(2)}) async-start(), calls=%async_computation.26 | async-start | bytes 7864320 | tf_op jit(solution)/shard_map/reduce_scatter | solution.py:525
  860.5 269.9 %reduce-scatter.10.cloned.1.call-start = ((), (), s32[]{:S(2)}) async-start(), calls=%async_computation.21 | async-start | bytes 5242880 | tf_op jit(solution)/shard_map/reduce_scatter | solution.py:525
  887.0 78.4 %collective-permute-start.8 = (bf16[2,256,2048]{2,1,0:T(8,128)(2,1)}, bf16[2,256,2048]{2,1,0:T(8,128)(2,1)}, u32[]{:S(2)}, u32[]{:S(2)}) collective-permute-start(bf16[2,256,2048]{2,1,0:T(8,128)(2,1)} %select_bitcast_fusion), channel_id=1, source_target_pairs={{0,1},{1,0},{2,3},{3,2},{4,5},{5,4},{6,7},{7,6},{8,9},{9,8},{10,11... | collective-permute-start | bytes 6291464 | tf_op jit(solution)/shard_map/ppermute | solution.py:485
  890.8 36.4 %collective-permute-start.50 = (bf16[512,1536]{1,0:T(8,128)(2,1)}, bf16[512,1536]{1,0:T(8,128)(2,1)}, u32[]{:S(2)}, u32[]{:S(2)}) collective-permute-start(bf16[512,1536]{1,0:T(8,128)(2,1)} %reduce-scatter.26.cloned.1.call-done), channel_id=1, source_target_pairs={{0,2},{1,3},{6,4},{7,5},{8,10},{9,11},{14,12},{15,13},{16,18},{17,... | collective-permute-start | bytes 4718600 | tf_op jit(solution)/shard_map/ppermute | solution.py:510
  893.4 66.8 %collective-permute-start.47 = (bf16[512,1536]{1,0:T(8,128)(2,1)}, bf16[512,1536]{1,0:T(8,128)(2,1)}, u32[]{:S(2)}, u32[]{:S(2)}) collective-permute-start(bf16[512,1536]{1,0:T(8,128)(2,1)} %reduce-scatter.24.cloned.1.call-done), channel_id=1, source_target_pairs={{0,2},{1,3},{6,4},{7,5},{8,10},{9,11},{14,12},{15,13},{16,18},{17,... | collective-permute-start | bytes 4718600 | tf_op jit(solution)/shard_map/ppermute | solution.py:510
  897.7 74.2 %collective-permute-start.15 = (f32[24,2048]{1,0:T(8,128)S(1)}, f32[24,2048]{1,0:T(8,128)S(1)}, u32[]{:S(2)}, u32[]{:S(2)}) collective-permute-start(f32[24,2048]{1,0:T(8,128)S(1)} %fusion.55), channel_id=1, source_target_pairs={{0,2},{1,3},{2,0},{3,1},{4,6},{5,7},{6,4},{7,5},{8,10},{9,11},{10,... | collective-permute-start | bytes 589832 | tf_op jit(solution)/shard_map/ppermute | solution.py:520
  930.6 77.0 %collective-permute-start.51 = (bf16[512,1536]{1,0:T(8,128)(2,1)}, bf16[512,1536]{1,0:T(8,128)(2,1)}, u32[]{:S(2)}, u32[]{:S(2)}) collective-permute-start(bf16[512,1536]{1,0:T(8,128)(2,1)} %add.267), channel_id=1, source_target_pairs={{2,4},{3,5},{4,2},{5,3},{10,12},{11,13},{12,10},{13,11},{18,20},{1... | collective-permute-start | bytes 4718600 | tf_op jit(solution)/shard_map/ppermute | solution.py:511
  963.1 97.7 %collective-permute-start.48 = (bf16[512,1536]{1,0:T(8,128)(2,1)}, bf16[512,1536]{1,0:T(8,128)(2,1)}, u32[]{:S(2)}, u32[]{:S(2)}) collective-permute-start(bf16[512,1536]{1,0:T(8,128)(2,1)} %add.265), channel_id=1, source_target_pairs={{2,4},{3,5},{4,2},{5,3},{10,12},{11,13},{12,10},{13,11},{18,20},{1... | collective-permute-start | bytes 4718600 | tf_op jit(solution)/shard_map/ppermute | solution.py:511
  972.0 35.6 %collective-permute-start.16 = (f32[24,2048]{1,0:T(8,128)S(1)}, f32[24,2048]{1,0:T(8,128)S(1)}, u32[]{:S(2)}, u32[]{:S(2)}) collective-permute-start(f32[24,2048]{1,0:T(8,128)S(1)} %add.246), channel_id=1, source_target_pairs={{0,4},{1,5},{2,6},{3,7},{4,0},{5,1},{6,2},{7,3},{8,12},{9,13},{10,... | collective-permute-start | bytes 589832 | tf_op jit(solution)/shard_map/ppermute | solution.py:520
  976.1 74.4 %collective-permute-start.27 = (bf16[512,1024]{1,0:T(8,128)(2,1)}, bf16[512,1024]{1,0:T(8,128)(2,1)S(1)}, u32[]{:S(2)}, u32[]{:S(2)}) collective-permute-start(bf16[512,1024]{1,0:T(8,128)(2,1)} %reduce-scatter.14.cloned.1.call-done), channel_id=1, source_target_pairs={{0,2},{1,3},{6,4},{7,5},{8,10},{9,11},{14,12},{15,13},{16,18},{17,... | collective-permute-start | bytes 3145736 | tf_op jit(solution)/shard_map/ppermute | solution.py:510
  977.5 86.2 %collective-permute-start.34 = (bf16[1536,512]{1,0:T(8,128)(2,1)}, bf16[1536,512]{1,0:T(8,128)(2,1)}, u32[]{:S(2)}, u32[]{:S(2)}) collective-permute-start(bf16[1536,512]{1,0:T(8,128)(2,1)} %reduce-scatter.18.cloned.1.call-done), channel_id=1, source_target_pairs={{0,2},{1,3},{6,4},{7,5},{8,10},{9,11},{14,12},{15,13},{16,18},{17,... | collective-permute-start | bytes 4718600 | tf_op jit(solution)/shard_map/ppermute | solution.py:510
  1007.6 29.9 %collective-permute-start.10 = (f32[2,2048]{1,0:T(2,128)S(1)}, f32[2,2048]{1,0:T(2,128)S(1)}, u32[]{:S(2)}, u32[]{:S(2)}) collective-permute-start(f32[2,2048]{1,0:T(2,128)S(1)} %fusion.54), channel_id=1, source_target_pairs={{0,2},{1,3},{2,0},{3,1},{4,6},{5,7},{6,4},{7,5},{8,10},{9,11},{10,... | collective-permute-start | bytes 49160 | tf_op jit(solution)/shard_map/ppermute | solution.py:520
  1007.6 31.9 %collective-permute-start.17 = (f32[24,2048]{1,0:T(8,128)S(1)}, f32[24,2048]{1,0:T(8,128)S(1)}, u32[]{:S(2)}, u32[]{:S(2)}) collective-permute-start(f32[24,2048]{1,0:T(8,128)S(1)} %add.247), channel_id=1, source_target_pairs={{0,8},{8,0},{16,24},{24,16},{1,9},{9,1},{17,25},{25,17},{2,10},{10... | collective-permute-start | bytes 589832 | tf_op jit(solution)/shard_map/ppermute | solution.py:520
  1037.5 38.7 %collective-permute-start.52 = (bf16[512,1536]{1,0:T(8,128)(2,1)}, bf16[512,1536]{1,0:T(8,128)(2,1)}, u32[]{:S(2)}, u32[]{:S(2)}) collective-permute-start(bf16[512,1536]{1,0:T(8,128)(2,1)} %add.268), channel_id=1, source_target_pairs={{2,0},{3,1},{4,6},{5,7},{10,8},{11,9},{12,14},{13,15},{18,16},{19,... | collective-permute-start | bytes 4718600 | tf_op jit(solution)/shard_map/ppermute | solution.py:512
  1054.3 82.6 %collective-permute-start.31 = (bf16[1536,512]{1,0:T(8,128)(2,1)}, bf16[1536,512]{1,0:T(8,128)(2,1)}, u32[]{:S(2)}, u32[]{:S(2)}) collective-permute-start(bf16[1536,512]{1,0:T(8,128)(2,1)} %reduce-scatter.16.cloned.1.call-done), channel_id=1, source_target_pairs={{0,2},{1,3},{6,4},{7,5},{8,10},{9,11},{14,12},{15,13},{16,18},{17,... | collective-permute-start | bytes 4718600 | tf_op jit(solution)/shard_map/ppermute | solution.py:510
  1060.9 69.5 %collective-permute-start.22 = (bf16[512,1024]{1,0:T(8,128)(2,1)}, bf16[512,1024]{1,0:T(8,128)(2,1)}, u32[]{:S(2)}, u32[]{:S(2)}) collective-permute-start(bf16[512,1024]{1,0:T(8,128)(2,1)} %reduce-scatter.12.cloned.1.call-done), channel_id=1, source_target_pairs={{0,2},{1,3},{6,4},{7,5},{8,10},{9,11},{14,12},{15,13},{16,18},{17,... | collective-permute-start | bytes 3145736 | tf_op jit(solution)/shard_map/ppermute | solution.py:510
  1063.7 142.8 %collective-permute-start.40 = (bf16[1536,512]{1,0:T(8,128)(2,1)}, bf16[1536,512]{1,0:T(8,128)(2,1)}, u32[]{:S(2)}, u32[]{:S(2)}) collective-permute-start(bf16[1536,512]{1,0:T(8,128)(2,1)} %reduce-scatter.22.cloned.1.call-done), channel_id=1, source_target_pairs={{0,2},{1,3},{6,4},{7,5},{8,10},{9,11},{14,12},{15,13},{16,18},{17,... | collective-permute-start | bytes 4718600 | tf_op jit(solution)/shard_map/ppermute | solution.py:510
  1069.8 147.1 %collective-permute-start.35 = (bf16[1536,512]{1,0:T(8,128)(2,1)}, bf16[1536,512]{1,0:T(8,128)(2,1)}, u32[]{:S(2)}, u32[]{:S(2)}) collective-permute-start(bf16[1536,512]{1,0:T(8,128)(2,1)} %add.259), channel_id=1, source_target_pairs={{2,4},{3,5},{4,2},{5,3},{10,12},{11,13},{12,10},{13,11},{18,20},{1... | collective-permute-start | bytes 4718600 | tf_op jit(solution)/shard_map/ppermute | solution.py:511
  1076.3 142.3 %collective-permute-start.37 = (bf16[1536,512]{1,0:T(8,128)(2,1)}, bf16[1536,512]{1,0:T(8,128)(2,1)}, u32[]{:S(2)}, u32[]{:S(2)}) collective-permute-start(bf16[1536,512]{1,0:T(8,128)(2,1)} %reduce-scatter.20.cloned.1.call-done), channel_id=1, source_target_pairs={{0,2},{1,3},{6,4},{7,5},{8,10},{9,11},{14,12},{15,13},{16,18},{17,... | collective-permute-start | bytes 4718600 | tf_op jit(solution)/shard_map/ppermute | solution.py:510
  1130.4 71.8 %collective-permute-start.19 = (bf16[512,1024]{1,0:T(8,128)(2,1)}, bf16[512,1024]{1,0:T(8,128)(2,1)S(1)}, u32[]{:S(2)}, u32[]{:S(2)}) collective-permute-start(bf16[512,1024]{1,0:T(8,128)(2,1)} %reduce-scatter.10.cloned.1.call-done), channel_id=1, source_target_pairs={{0,2},{1,3},{6,4},{7,5},{8,10},{9,11},{14,12},{15,13},{16,18},{17,... | collective-permute-start | bytes 3145736 | tf_op jit(solution)/shard_map/ppermute | solution.py:510
  1137.0 78.6 %collective-permute-start.23 = (bf16[512,1024]{1,0:T(8,128)(2,1)}, bf16[512,1024]{1,0:T(8,128)(2,1)}, u32[]{:S(2)}, u32[]{:S(2)}) collective-permute-start(bf16[512,1024]{1,0:T(8,128)(2,1)} %add.252), channel_id=1, source_target_pairs={{2,4},{3,5},{4,2},{5,3},{10,12},{11,13},{12,10},{13,11},{18,20},{1... | collective-permute-start | bytes 3145736 | tf_op jit(solution)/shard_map/ppermute | solution.py:511
  1202.2 45.3 %collective-permute-start.49 = (bf16[512,1536]{1,0:T(8,128)(2,1)}, bf16[512,1536]{1,0:T(8,128)(2,1)}, u32[]{:S(2)}, u32[]{:S(2)}) collective-permute-start(bf16[512,1536]{1,0:T(8,128)(2,1)} %add.266), channel_id=1, source_target_pairs={{2,0},{3,1},{4,6},{5,7},{10,8},{11,9},{12,14},{13,15},{18,16},{19,... | collective-permute-start | bytes 4718600 | tf_op jit(solution)/shard_map/ppermute | solution.py:512
  1206.5 56.0 %collective-permute-start.32 = (bf16[1536,512]{1,0:T(8,128)(2,1)}, bf16[1536,512]{1,0:T(8,128)(2,1)}, u32[]{:S(2)}, u32[]{:S(2)}) collective-permute-start(bf16[1536,512]{1,0:T(8,128)(2,1)} %add.257), channel_id=1, source_target_pairs={{2,4},{3,5},{4,2},{5,3},{10,12},{11,13},{12,10},{13,11},{18,20},{1... | collective-permute-start | bytes 4718600 | tf_op jit(solution)/shard_map/ppermute | solution.py:511
  1215.5 44.4 %collective-permute-start.29 = (bf16[512,1024]{1,0:T(8,128)(2,1)}, bf16[512,1024]{1,0:T(8,128)(2,1)}, u32[]{:S(2)}, u32[]{:S(2)}) collective-permute-start(bf16[512,1024]{1,0:T(8,128)(2,1)} %add.256), channel_id=1, source_target_pairs={{2,0},{3,1},{4,6},{5,7},{10,8},{11,9},{12,14},{13,15},{18,16},{19,... | collective-permute-start | bytes 3145736 | tf_op jit(solution)/shard_map/ppermute | solution.py:512
  1216.8 44.4 %collective-permute-start.20 = (bf16[512,1024]{1,0:T(8,128)(2,1)S(1)}, bf16[512,1024]{1,0:T(8,128)(2,1)}, u32[]{:S(2)}, u32[]{:S(2)}) collective-permute-start(bf16[512,1024]{1,0:T(8,128)(2,1)S(1)} %add.250), channel_id=1, source_target_pairs={{2,4},{3,5},{4,2},{5,3},{10,12},{11,13},{12,10},{13,11},{18,20},{1... | collective-permute-start | bytes 3145736 | tf_op jit(solution)/shard_map/ppermute | solution.py:511
  1218.6 49.2 %collective-permute-start.41 = (bf16[1536,512]{1,0:T(8,128)(2,1)S(1)}, bf16[1536,512]{1,0:T(8,128)(2,1)}, u32[]{:S(2)}, u32[]{:S(2)}) collective-permute-start(bf16[1536,512]{1,0:T(8,128)(2,1)S(1)} %add.263), channel_id=1, source_target_pairs={{2,4},{3,5},{4,2},{5,3},{10,12},{11,13},{12,10},{13,11},{18,20},{1... | collective-permute-start | bytes 4718600 | tf_op jit(solution)/shard_map/ppermute | solution.py:511
  1247.4 76.8 %collective-permute-start.7 = (bf16[2,256,2048]{2,1,0:T(8,128)(2,1)S(1)}, bf16[2,256,2048]{2,1,0:T(8,128)(2,1)S(1)}, u32[]{:S(2)}, u32[]{:S(2)}) collective-permute-start(bf16[2,256,2048]{2,1,0:T(8,128)(2,1)S(1)} %select_bitcast_fusion.1), channel_id=1, source_target_pairs={{0,1},{1,0},{2,3},{3,2},{4,5},{5,4},{6,7},{7,6},{8,9},{9,8},{10,11... | collective-permute-start | bytes 6291464 | tf_op jit(solution)/shard_map/ppermute | solution.py:485
  1259.9 27.9 %collective-permute-start.24 = (bf16[512,1024]{1,0:T(8,128)(2,1)S(1)}, bf16[512,1024]{1,0:T(8,128)(2,1)S(1)}, u32[]{:S(2)}, u32[]{:S(2)}) collective-permute-start(bf16[512,1024]{1,0:T(8,128)(2,1)S(1)} %add.253), channel_id=1, source_target_pairs={{2,0},{3,1},{4,6},{5,7},{10,8},{11,9},{12,14},{13,15},{18,16},{19,... | collective-permute-start | bytes 3145736 | tf_op jit(solution)/shard_map/ppermute | solution.py:512
  1261.2 60.3 %collective-permute-start.36 = (bf16[1536,512]{1,0:T(8,128)(2,1)S(1)}, bf16[1536,512]{1,0:T(8,128)(2,1)S(1)}, u32[]{:S(2)}, u32[]{:S(2)}) collective-permute-start(bf16[1536,512]{1,0:T(8,128)(2,1)S(1)} %add.260), channel_id=1, source_target_pairs={{2,0},{3,1},{4,6},{5,7},{10,8},{11,9},{12,14},{13,15},{18,16},{19,... | collective-permute-start | bytes 4718600 | tf_op jit(solution)/shard_map/ppermute | solution.py:512
  1262.5 30.1 %collective-permute-start.38 = (bf16[1536,512]{1,0:T(8,128)(2,1)S(1)}, bf16[1536,512]{1,0:T(8,128)(2,1)S(1)}, u32[]{:S(2)}, u32[]{:S(2)}) collective-permute-start(bf16[1536,512]{1,0:T(8,128)(2,1)S(1)} %add.261), channel_id=1, source_target_pairs={{2,4},{3,5},{4,2},{5,3},{10,12},{11,13},{12,10},{13,11},{18,20},{1... | collective-permute-start | bytes 4718600 | tf_op jit(solution)/shard_map/ppermute | solution.py:511
  1267.8 87.4 %collective-permute-start.33 = (bf16[1536,512]{1,0:T(8,128)(2,1)S(1)}, bf16[1536,512]{1,0:T(8,128)(2,1)S(1)}, u32[]{:S(2)}, u32[]{:S(2)}) collective-permute-start(bf16[1536,512]{1,0:T(8,128)(2,1)S(1)} %add.258), channel_id=1, source_target_pairs={{2,0},{3,1},{4,6},{5,7},{10,8},{11,9},{12,14},{13,15},{18,16},{19,... | collective-permute-start | bytes 4718600 | tf_op jit(solution)/shard_map/ppermute | solution.py:512
  1287.8 101.1 %collective-permute-start.42 = (bf16[1536,512]{1,0:T(8,128)(2,1)S(1)}, bf16[1536,512]{1,0:T(8,128)(2,1)S(1)}, u32[]{:S(2)}, u32[]{:S(2)}) collective-permute-start(bf16[1536,512]{1,0:T(8,128)(2,1)S(1)} %add.264), channel_id=1, source_target_pairs={{2,0},{3,1},{4,6},{5,7},{10,8},{11,9},{12,14},{13,15},{18,16},{19,... | collective-permute-start | bytes 4718600 | tf_op jit(solution)/shard_map/ppermute | solution.py:512
  1292.6 64.0 %collective-permute-start.13 = (f32[2,2048]{1,0:T(2,128)S(1)}, f32[2,2048]{1,0:T(2,128)S(1)}, u32[]{:S(2)}, u32[]{:S(2)}) collective-permute-start(f32[2,2048]{1,0:T(2,128)S(1)} %add.243), channel_id=1, source_target_pairs={{0,16},{8,24},{16,0},{24,8},{1,17},{9,25},{17,1},{25,9},{2,18},{10... | collective-permute-start | bytes 49160 | tf_op jit(solution)/shard_map/ppermute | solution.py:520
  1321.6 101.1 %collective-permute-start.39 = (bf16[1536,512]{1,0:T(8,128)(2,1)S(1)}, bf16[1536,512]{1,0:T(8,128)(2,1)S(1)}, u32[]{:S(2)}, u32[]{:S(2)}) collective-permute-start(bf16[1536,512]{1,0:T(8,128)(2,1)S(1)} %add.262), channel_id=1, source_target_pairs={{2,0},{3,1},{4,6},{5,7},{10,8},{11,9},{12,14},{13,15},{18,16},{19,... | collective-permute-start | bytes 4718600 | tf_op jit(solution)/shard_map/ppermute | solution.py:512
  1324.2 100.4 %collective-permute-start.54 = (bf16[512,1536]{1,0:T(8,128)(2,1)S(1)}, bf16[512,1536]{1,0:T(8,128)(2,1)S(1)}, u32[]{:S(2)}, u32[]{:S(2)}) collective-permute-start(bf16[512,1536]{1,0:T(8,128)(2,1)S(1)} %broadcast_select_fusion.5.refs_1_), channel_id=1, source_target_pairs={{0,1},{1,0},{2,3},{3,2},{4,5},{5,4},{6,7},{7,6},{8,9},{9,8},{10,11... | collective-permute-start | bytes 4718600 | tf_op jit(solution)/shard_map/ppermute | solution.py:485
  1355.3 69.5 %collective-permute-start.53 = (bf16[512,1536]{1,0:T(8,128)(2,1)S(1)}, bf16[512,1536]{1,0:T(8,128)(2,1)S(1)}, u32[]{:S(2)}, u32[]{:S(2)}) collective-permute-start(bf16[512,1536]{1,0:T(8,128)(2,1)S(1)} %broadcast_select_fusion.6.refs_0_), channel_id=1, source_target_pairs={{0,1},{1,0},{2,3},{3,2},{4,5},{5,4},{6,7},{7,6},{8,9},{9,8},{10,11... | collective-permute-start | bytes 4718600 | tf_op jit(solution)/shard_map/ppermute | solution.py:485
  1356.6 67.4 %collective-permute-start.30 = (bf16[512,1024]{1,0:T(8,128)(2,1)S(1)}, bf16[512,1024]{1,0:T(8,128)(2,1)S(1)}, u32[]{:S(2)}, u32[]{:S(2)}) collective-permute-start(bf16[512,1024]{1,0:T(8,128)(2,1)S(1)} %broadcast_select_fusion.11.refs_0_), channel_id=1, source_target_pairs={{0,1},{1,0},{2,3},{3,2},{4,5},{5,4},{6,7},{7,6},{8,9},{9,8},{10,11... | collective-permute-start | bytes 3145736 | tf_op jit(solution)/shard_map/ppermute | solution.py:485
  1389.0 51.2 %collective-permute-start.21 = (bf16[512,1024]{1,0:T(8,128)(2,1)S(1)}, bf16[512,1024]{1,0:T(8,128)(2,1)S(1)}, u32[]{:S(2)}, u32[]{:S(2)}) collective-permute-start(bf16[512,1024]{1,0:T(8,128)(2,1)S(1)} %add.251), channel_id=1, source_target_pairs={{2,0},{3,1},{4,6},{5,7},{10,8},{11,9},{12,14},{13,15},{18,16},{19,... | collective-permute-start | bytes 3145736 | tf_op jit(solution)/shard_map/ppermute | solution.py:512
  1424.1 49.3 %collective-permute-start.44 = (bf16[1536,512]{1,0:T(8,128)(2,1)}, bf16[1536,512]{1,0:T(8,128)(2,1)}, u32[]{:S(2)}, u32[]{:S(2)}) collective-permute-start(bf16[1536,512]{1,0:T(8,128)(2,1)} %broadcast_select_fusion.9.refs_1_), channel_id=1, source_target_pairs={{0,1},{1,0},{2,3},{3,2},{4,5},{5,4},{6,7},{7,6},{8,9},{9,8},{10,11... | collective-permute-start | bytes 4718600 | tf_op jit(solution)/shard_map/ppermute | solution.py:485
  1424.6 48.8 %collective-permute-start.43 = (bf16[1536,512]{1,0:T(8,128)(2,1)}, bf16[1536,512]{1,0:T(8,128)(2,1)}, u32[]{:S(2)}, u32[]{:S(2)}) collective-permute-start(bf16[1536,512]{1,0:T(8,128)(2,1)} %broadcast_select_fusion.10.refs_0_), channel_id=1, source_target_pairs={{0,1},{1,0},{2,3},{3,2},{4,5},{5,4},{6,7},{7,6},{8,9},{9,8},{10,11... | collective-permute-start | bytes 4718600 | tf_op jit(solution)/shard_map/ppermute | solution.py:485
  1424.7 48.7 %collective-permute-start.46 = (bf16[1536,512]{1,0:T(8,128)(2,1)}, bf16[1536,512]{1,0:T(8,128)(2,1)}, u32[]{:S(2)}, u32[]{:S(2)}) collective-permute-start(bf16[1536,512]{1,0:T(8,128)(2,1)} %broadcast_select_fusion.7.refs_3_), channel_id=1, source_target_pairs={{0,1},{1,0},{2,3},{3,2},{4,5},{5,4},{6,7},{7,6},{8,9},{9,8},{10,11... | collective-permute-start | bytes 4718600 | tf_op jit(solution)/shard_map/ppermute | solution.py:485
  1440.1 33.3 %collective-permute-start.45 = (bf16[1536,512]{1,0:T(8,128)(2,1)}, bf16[1536,512]{1,0:T(8,128)(2,1)}, u32[]{:S(2)}, u32[]{:S(2)}) collective-permute-start(bf16[1536,512]{1,0:T(8,128)(2,1)} %broadcast_select_fusion.8.refs_2_), channel_id=1, source_target_pairs={{0,1},{1,0},{2,3},{3,2},{4,5},{5,4},{6,7},{7,6},{8,9},{9,8},{10,11... | collective-permute-start | bytes 4718600 | tf_op jit(solution)/shard_map/ppermute | solution.py:485
  (93 other events, 2165.4 us)
Sparse Core Ops, SparseCore 0:
  14.1 90.1 all-gather.4
  106.2 52.5 all-gather.6
  161.3 228.9 all-gather.10
  392.5 122.3 all-gather.8
  517.8 70.0 reduce-scatter.25
  590.7 70.0 reduce-scatter.23
  672.4 50.6 reduce-scatter.13
  726.1 70.0 reduce-scatter.17
  799.2 70.0 reduce-scatter.15
  872.0 52.5 reduce-scatter.11
  927.6 70.0 reduce-scatter.21
  1000.5 74.2 reduce-scatter.19
  1077.7 52.5 reduce-scatter.9

commit v3 on v2

--- a/solution.py
+++ b/solution.py
@@ -382,11 +382,10 @@
     pl.when(jnp.logical_not(own_half))(lambda: put(refs[count : 2 * count]))
 
 
-def join_rows(mine, other, core, unit, block):
+def join_rows(mine, other, core, blocks, block):
     count = len(mine)
     height, size = mine[0].shape
     steps = height // block
-    blocks = unit // block
 
     def source(side):
         def index(h, i, which):
@@ -409,7 +408,7 @@
         ),
         out_shape=jax.ShapeDtypeStruct((CORES * height, count * size), F32),
         name="join_rows",
-    )(jnp.stack([core, jnp.asarray(blocks, jnp.int32)]), *mine, *other)
+    )(jnp.stack([core, blocks.astype(jnp.int32)]), *mine, *other)
 
 
 def join_cols_kernel(count, per, which_ref, *refs):
@@ -448,8 +447,109 @@
     )(core[None], *mine, *other)
 
 
+def join_units_kernel(which_ref, keep_ref, keep_other_ref, sent_ref, sent_other_ref, out_ref):
+    kept = pl.program_id(0) == which_ref[1]
+    mine = pl.program_id(1) == which_ref[0]
+    for side, pair in ((True, (keep_ref, keep_other_ref)), (False, (sent_ref, sent_other_ref))):
+        for here, ref in ((True, pair[0]), (False, pair[1])):
+
+            @pl.when((kept == side) & (mine == here))
+            def _(ref=ref):
+                out_ref[...] = ref[...].astype(F32)
+
+
+def join_units(mine, other, core, upper):
+    height, width = mine[0].shape
+    block = 256
+    steps = height // block
+    sources = []
+    for side in (0, 1):
+        for half in (0, 1):
+
+            def index(p, h, i, which, side=side, half=half):
+                at_side = (p == which[1]) if side == 0 else (p != which[1])
+                at_half = (h == which[0]) if half == 0 else (h != which[0])
+                side_p = which[1] if side == 0 else 1 - which[1]
+                side_h = which[0] if half == 0 else 1 - which[0]
+                before = (p * 2 + h) < (side_p * 2 + side_h)
+                return (jnp.where(at_side & at_half, i, jnp.where(before, 0, steps - 1)), 0)
+
+            sources.append(pl.BlockSpec((block, width), index))
+    return pl.pallas_call(
+        join_units_kernel,
+        grid_spec=pltpu.PrefetchScalarGridSpec(
+            num_scalar_prefetch=1,
+            grid=(2, CORES, steps),
+            in_specs=sources,
+            out_specs=pl.BlockSpec((block, width), lambda p, h, i, which: ((p * CORES + h) * steps + i, 0)),
+        ),
+        out_shape=jax.ShapeDtypeStruct((2 * CORES * height, width), F32),
+        name="join_units",
+    )(jnp.stack([core, upper]), mine[0], other[0], mine[1], other[1])
+
+
+def join_blocks_kernel(which_ref, mine_ref, other_ref, out_ref):
+    own_half = pl.program_id(0) == which_ref[0]
+    for here, ref in ((True, mine_ref), (False, other_ref)):
+
+        @pl.when(own_half == here)
+        def _(ref=ref):
+            out_ref[...] = ref[0].astype(F32)
+
+
+def join_blocks(mine, other, core, order):
+    count, height, size = mine.shape
+    source = pl.BlockSpec((1, height, size), lambda h, b, which, where: (where[b], 0, 0))
+    inverse = [order.index(b) for b in range(count)]
+    return pl.pallas_call(
+        lambda which_ref, where_ref, *refs: join_blocks_kernel(which_ref, *refs),
+        grid_spec=pltpu.PrefetchScalarGridSpec(
+            num_scalar_prefetch=2,
+            grid=(CORES, count),
+            in_specs=[source, source],
+            out_specs=pl.BlockSpec((height, size), lambda h, b, which, where: (h, b)),
+        ),
+        out_shape=jax.ShapeDtypeStruct((CORES * height, count * size), F32),
+        name="join_blocks",
+    )(core[None], jnp.asarray(inverse, jnp.int32), mine, other)
+
+
+class Line:
+    def __init__(self, chips, chip):
+        self.chips = chips
+        self.inner = (chip == 1) | (chip == 2)
+        ends = lambda pairs: [(a * CORES + c, b * CORES + c) for a, b in pairs for c in range(CORES)]
+        self.stages = [ends([(0, 1), (3, 2)]), ends([(1, 2), (2, 1)]), ends([(1, 0), (2, 3)])]
+        self.groups = [[z * CORES + c for z in range(chips)] for c in range(CORES)]
+
+    def send(self, x, stage):
+        if self.chips != 4:
+            return (x, lax.psum(x, "seq", axis_index_groups=self.groups) if stage == 0 else x)
+        return (x, lax.ppermute(x, "seq", self.stages[stage]))
+
+    def begin(self, x):
+        return (0,) + self.send(x, 0)
+
+    def next(self, state):
+        stage, x, moved = state
+        if self.chips != 4:
+            return (stage + 1, moved, moved)
+        return (stage + 1,) + self.send(x + moved, stage + 1)
+
+    def end(self, state):
+        stage, x, moved = state
+        return moved if self.chips != 4 else jnp.where(self.inner, x, moved)
+
+    def run(self, x):
+        return self.end(self.next(self.next(self.begin(x))))
+
+
 def tie(value, work):
-    return lax.optimization_barrier((value, work))
+    leaves, tree = jax.tree.flatten(work)
+    moving = [x for x in leaves if not isinstance(x, int)]
+    value, *moving = lax.optimization_barrier((value, *moving))
+    moving = iter(moving)
+    return value, jax.tree.unflatten(tree, [x if isinstance(x, int) else next(moving) for x in leaves])
 
 
 def shards(
@@ -491,26 +591,8 @@
         other = swap(x)
         return jnp.concatenate([pick(x, other), pick(other, x)], axis=1).reshape(tokens, width)
 
-    def own(x):
-        x = x.reshape(rows, CORES, tok, width)
-        return pick(x[:, 0], x[:, 1])
-
-    def pair_sum(x):
-        return x.astype(F32) + swap(x).astype(F32)
-
     def exchange(x):
         return lax.all_to_all(x, "seq", 0, 0, axis_index_groups=groups, tiled=True)
-
-    def chip_sum(x):
-        if chips != 4:
-            return lax.psum(x, "seq", axis_index_groups=groups)
-        inward = [(c, 2 + c) for c in range(CORES)] + [(6 + c, 4 + c) for c in range(CORES)]
-        middle = [(2 + c, 4 + c) for c in range(CORES)] + [(4 + c, 2 + c) for c in range(CORES)]
-        outward = [(2 + c, c) for c in range(CORES)] + [(4 + c, 6 + c) for c in range(CORES)]
-        half = x + lax.ppermute(x, "seq", inward)
-        full = half + lax.ppermute(half, "seq", middle)
-        spread = lax.ppermute(full, "seq", outward)
-        return jnp.where((chip == 1) | (chip == 2), full, spread)
 
     def total_sum(x, names=("seq", "dp")):
         for name in names:
@@ -538,18 +620,35 @@
             axis=1,
         )
 
-    ff_unit = w_gu.shape[0] // CORES
+    half_dp = dp // 2
+    me = lax.axis_index("dp")
+    upper = me >= half_dp
+    trade = [(d, d ^ half_dp) for d in range(dp)]
+    units = w_gu.shape[0] // 2
+    owned = rows * tok
+
     qkv_half = jnp.where(q_shard, core_rows(w_qkv, GROUP * HEAD), core_rows(w_qkv, HEAD))
     qkv_full = gather(qkv_half)
+    out_full = gather(core_cols(w_out, GROUP * HEAD))
+    ctg = cotangent.reshape(owned, width)
+    ctg_all = gather(ctg)
     gate_count = w_gate.shape[0]
-    gate_full = lax.dynamic_update_slice_in_dim(
-        jnp.zeros((QUERY_HEADS, width), BF), w_gate, lax.axis_index("dp") * gate_count, 0
+    gate_full = lax.dynamic_update_slice_in_dim(jnp.zeros((QUERY_HEADS, width), BF), w_gate, me * gate_count, 0)
+    gate_full = total_sum(gate_full, ("dp",))
+    gate_core = jnp.pad(core_rows(gate_full, GROUP), ((0, HEAD - CORE_Q), (0, 0)))
+
+    gu_keep = jnp.where(upper, w_gu[units:], w_gu[:units])
+    quarter = units // 2
+    gu_send = jnp.where(
+        upper, pick(w_gu[:quarter], w_gu[quarter:units]), pick(w_gu[units : units + quarter], w_gu[units + quarter :])
     )
-    gate_full = total_sum(gate_full, ("dp",))
-    out_full = gather(core_cols(w_out, GROUP * HEAD))
-    gu_full = gather(core_rows(w_gu, ff_unit))
-    down_full = gather(core_cols(w_down, ff_unit))
-    gate_core = jnp.pad(core_rows(gate_full, GROUP), ((0, HEAD - CORE_Q), (0, 0)))
+    out_rows = w_down.shape[0] // 2
+    down_core = pick(w_down[:out_rows], w_down[out_rows:])
+    unit_block = [(d % half_dp) * 2 + d // half_dp for d in range(dp)]
+    down_send = jnp.stack([down_core[:, b * units : (b + 1) * units] for b in unit_block])
+    (qkv_full, gu_send, down_send) = lax.optimization_barrier((qkv_full, gu_send, down_send))
+    gu_half = lax.ppermute(gu_send, "dp", trade)
+    down_half = lax.all_to_all(down_send, "dp", 0, 0, tiled=True)
 
     start, position = doc_positions(doc_lengths, length)
     low = start.reshape(rows, chips, chip_tok)[:, :, 0] // chip_tok
@@ -561,9 +660,7 @@
     cos = jnp.concatenate([cos, cos], axis=1)
     sin = jnp.concatenate([-sin, sin], axis=1)
 
-    inputs_low = both(layer_input)
-    d_out = both(cotangent)
-    inputs = inputs_low.astype(F32)
+    inputs = both(layer_input).astype(F32)
     factor_a = lax.rsqrt(jnp.mean(inputs * inputs, axis=-1, keepdims=True) + epsilon)
     normed_a = (inputs * factor_a * attn_norm).astype(BF)
     logits = dot_nt(normed_a, gate_core)
@@ -571,7 +668,7 @@
     q_gain = q_norm[None, :]
     k_gain = k_norm[None, :]
 
-    packed, results, logs, gated, partial = [], [], [], [], []
+    packed, results, logs, gated, mid = [], [], [], [], []
     for row in range(rows):
         packed.append(exchange(pack_heads(proj, cos, sin, q_gain, k_gain, row, chips, chip_tok)))
     packed[0], logits = tie(packed[0], logits)
@@ -580,42 +677,69 @@
         results.append(head_out)
         logs.append(log)
     tok_results = [exchange(r) for r in results]
+    tok_results[0], (gu_half, down_half) = tie(tok_results[0], (gu_half, down_half))
+    gu_other = swap(gu_half)
+    down_other = swap(down_half)
     for row in range(rows):
         gated.append(gate_rows(tok_results[row], logits, row))
-        partial.append(pair_sum(dot_nt(gated[row], out_full, BF)))
-    mid = inputs + jnp.concatenate(partial, axis=0)
+        part = dot_nt(gated[row], out_full, BF).reshape(CORES, tok, width)
+        other = swap(pick(part[1], part[0]))
+        mid.append(layer_input[row].astype(F32) + pick(part[0], part[1]).astype(F32) + other.astype(F32))
+    mid = jnp.concatenate(mid, axis=0)
     gated = jnp.concatenate(gated, axis=0)
 
     factor_f = lax.rsqrt(jnp.mean(mid * mid, axis=-1, keepdims=True) + epsilon)
     normed_f = (mid * factor_f * ffn_norm).astype(BF)
-    gate_up = dot_nt(normed_f, gu_full, BF)
-    gate_part = gate_up[:, : FF // CORES].astype(F32)
-    up_part = gate_up[:, FF // CORES :].astype(F32)
+    normed_all = gather(normed_f)
+    gu_recv = jnp.concatenate([pick(gu_half, gu_other), pick(gu_other, gu_half)], axis=0)
+    down_full = jnp.concatenate([pick(down_half, down_other), pick(down_other, down_half)], axis=1)
+    down_full = down_full.reshape(width, units)
+    d_hidden = dot_nn(ctg_all, down_full, BF)
+    normed_all, (d_hidden, gu_recv) = tie(normed_all, (d_hidden, gu_recv))
+    keep_part = dot_nt(normed_all, gu_keep, BF)
+    recv_part = dot_nt(normed_all, gu_recv, BF)
+    gate_part = jnp.where(upper, recv_part, keep_part).astype(F32)
+    up_part = jnp.where(upper, keep_part, recv_part).astype(F32)
+    d_hid = d_hidden.astype(F32)
     gate_act = jax.nn.sigmoid(gate_part)
     silu = gate_part * gate_act
     hidden = (silu * up_part).astype(BF)
-    part_down = [dot_tn(d_out, hidden[:, a : a + ff_unit], BF) for a in range(0, FF // CORES, ff_unit)]
-    down_full, part_down = tie(down_full, part_down)
-    shard_down = [scatter(p) for p in part_down]
-    d_hidden = dot_nn(d_out, down_full)
-    d_gate = d_hidden * up_part * gate_act * (1.0 + gate_part * (1.0 - gate_act))
-    d_up = d_hidden * silu
-    d_gate_up = jnp.concatenate([d_gate.astype(BF), d_up.astype(BF)], axis=1)
-    d_norm_mine = dot_nn(d_gate_up, gu_full, BF)
-    d_norm_pair = swap(d_norm_mine)
-    piece = width // 4
-    part_gu = [dot_tn(d_gate_up, normed_f[:, a : a + piece], BF) for a in range(0, width, piece)]
-    d_norm_pair, part_gu[:2] = tie(d_norm_pair, part_gu[:2])
-    d_normed = d_norm_mine.astype(F32) + d_norm_pair.astype(F32)
+    d_gate = d_hid * up_part * gate_act * (1.0 + gate_part * (1.0 - gate_act))
+    d_up = d_hid * silu
+    d_keep = jnp.where(upper, d_up, d_gate).astype(BF)
+    d_recv = jnp.where(upper, d_gate, d_up).astype(BF)
+    d_normed = scatter((dot_nn(d_keep, gu_keep) + dot_nn(d_recv, gu_recv)).astype(BF))
+
+    part_keep = dot_tn(d_keep, normed_all, BF)
+    part_recv = dot_tn(d_recv, normed_all, BF)
+    part_down = dot_tn(ctg_all, hidden, BF).reshape(dp, CORES, out_rows, units)
     out_part = dot_nt(hidden, down_full, BF)
-
-    part_ffn = 0.5 * jnp.sum(d_normed * mid * factor_f, axis=0)
+    keep_swap = swap(pick(part_keep[quarter:], part_keep[:quarter]))
+    recv_swap = swap(pick(part_recv[quarter:], part_recv[:quarter]))
+    down_swap = swap(pick(part_down[:, 1], part_down[:, 0]))
+    d_normed, (part_keep, part_recv, part_down, out_part) = tie(
+        d_normed, (part_keep, part_recv, part_down, out_part)
+    )
+    output = (mid + scatter(out_part).astype(F32)).astype(BF).reshape(rows, tok, width)
+
+    d_normed = d_normed.astype(F32)
+    part_ffn = jnp.sum(d_normed * mid * factor_f, axis=0)
     weighted = d_normed * ffn_norm
     inner = jnp.mean(weighted * mid, axis=-1, keepdims=True)
-    d_mid = d_out.astype(F32) + factor_f * weighted - mid * factor_f**3 * inner
-    d_mid_low = d_mid.astype(BF)
+    d_mid = ctg.astype(F32) + factor_f * weighted - mid * factor_f**3 * inner
+    low_mine = d_mid.astype(BF).reshape(rows, tok, width)
+    low_other = swap(low_mine)
+    low_other, (keep_swap, recv_swap, down_swap) = tie(low_other, (keep_swap, recv_swap, down_swap))
+    keep_sum = pick(part_keep[:quarter], part_keep[quarter:]) + keep_swap
+    recv_sum = pick(part_recv[:quarter], part_recv[quarter:]) + recv_swap
+    down_sum = pick(part_down[:, 0], part_down[:, 1]) + down_swap
+    sent_sum = lax.ppermute(recv_sum, "dp", trade)
+    down_sum = lax.all_to_all(down_sum, "dp", 0, 0, tiled=True)
+    line = Line(chips, chip)
+    keep_line = line.begin(keep_sum)
+
+    d_mid_low = jnp.concatenate([pick(low_mine, low_other), pick(low_other, low_mine)], axis=1).reshape(tokens, width)
     part_out = dot_tn(d_mid_low, gated, BF)
-
     d_proj, d_logit, d_heads = [], [], []
     q_sum = 0.0
     k_sum = 0.0
@@ -624,21 +748,32 @@
         d_attn, dl = gate_back(d_gated, tok_results[row], logits, row)
         d_logit.append(dl)
         d_heads.append(exchange(d_attn))
-    d_heads[0], part_gu[2:] = tie(d_heads[0], part_gu[2:])
-    d_heads[-1], part_out = tie(d_heads[-1], part_out)
-    shard_gu = [scatter(p) for p in part_gu]
-    shard_out = [scatter(part_out)]
+    d_heads[0], (keep_line, sent_sum, down_sum, part_out) = tie(d_heads[0], (keep_line, sent_sum, down_sum, part_out))
+    shard_out = scatter(part_out)
+    keep_line = line.next(keep_line)
+    down_line = line.begin(down_sum)
     back = []
     for row in range(rows):
-        back.append(
-            exchange(attend_back(packed[row], d_heads[row], results[row], logs[row], start[row : row + 1], low[row]))
-        )
-    back[0], out_part = tie(back[0], out_part)
-    out_part = out_part.reshape(rows, CORES, tok, width)
-    out_other = swap(pick(out_part[:, 1], out_part[:, 0]))
-    output = (own(mid) + pick(out_part[:, 0], out_part[:, 1]).astype(F32) + out_other.astype(F32)).astype(BF)
+        grad = d_heads[row]
+        if row:
+            grad, (keep_line, down_line) = tie(grad, (keep_line, down_line))
+            keep_line = line.next(keep_line)
+            down_line = line.next(down_line)
+            sent_line = line.begin(sent_sum)
+        back.append(exchange(attend_back(packed[row], grad, results[row], logs[row], start[row : row + 1], low[row])))
+    back[0], (keep_line, down_line, sent_line) = tie(back[0], (keep_line, down_line, sent_line))
+    keep_done = line.end(keep_line)
+    down_line = line.next(down_line)
+    sent_line = line.next(sent_line)
+    keep_other = swap(keep_done)
     for row in range(rows):
-        dpr, qs, ks = unpack_heads(back[row], proj, cos, sin, q_gain, k_gain, row, chips, chip_tok)
+        grads = back[row]
+        if row:
+            grads, (down_line, sent_line) = tie(grads, (down_line, sent_line))
+            down_done = line.end(down_line)
+            sent_line = line.next(sent_line)
+            down_other = swap(down_done)
+        dpr, qs, ks = unpack_heads(grads, proj, cos, sin, q_gain, k_gain, row, chips, chip_tok)
         d_proj.append(dpr)
         q_sum = q_sum + qs
         k_sum = k_sum + ks
@@ -649,32 +784,38 @@
     d_norm_part = (dot_nn(d_proj, qkv_full) + dot_nn(d_logit, gate_core)).astype(BF)
     d_norm_part = d_norm_part.reshape(rows, CORES, tok, width)
     d_norm_other = swap(pick(d_norm_part[:, 1], d_norm_part[:, 0]))
+    sent_done = line.end(sent_line)
+    sent_other = swap(sent_done)
     d_normed_a = pick(d_norm_part[:, 0], d_norm_part[:, 1]).astype(F32) + d_norm_other.astype(F32)
     own_in = layer_input.astype(F32)
     own_factor = lax.rsqrt(jnp.mean(own_in * own_in, axis=-1, keepdims=True) + epsilon)
     part_attn = jnp.sum(d_normed_a * own_in * own_factor, axis=(0, 1))
     weighted_a = d_normed_a * attn_norm
     inner_a = jnp.mean(weighted_a * own_in, axis=-1, keepdims=True)
-    grad_input = (own(d_mid) + own_factor * weighted_a - own_in * own_factor**3 * inner_a).astype(BF)
+    grad_input = (
+        d_mid.reshape(rows, tok, width) + own_factor * weighted_a - own_in * own_factor**3 * inner_a
+    ).astype(BF)
 
     part_gate = dot_tn(d_logit, normed_a)[:CORE_Q]
     zero = jnp.zeros_like(part_gate)
-    part_gate = jnp.stack([pick(part_gate, zero).reshape(-1, GROUP, width), pick(zero, part_gate).reshape(-1, GROUP, width)], 1)
+    part_gate = jnp.stack(
+        [pick(part_gate, zero).reshape(-1, GROUP, width), pick(zero, part_gate).reshape(-1, GROUP, width)], 1
+    )
     part_gate = part_gate.reshape(QUERY_HEADS, width)
     heads = jnp.concatenate([jnp.sum(q_sum, axis=0), jnp.sum(k_sum, axis=0)])
     heads = jnp.pad(heads, (0, width - heads.shape[0]))
     early = total_sum(jnp.concatenate([part_gate, part_ffn[None], jnp.zeros((7, width), F32)], axis=0))
     late = total_sum(jnp.stack([part_attn, heads]))
-    grad_w_gate = lax.dynamic_slice_in_dim(early, lax.axis_index("dp") * gate_count, gate_count, 0)
-
-    def halves(parts):
-        mine = [chip_sum(p) for p in parts]
-        return mine, [swap(p) for p in mine]
-
-    grad_down = join_cols(*halves(shard_down), core, ff_unit)
-    grad_gu = join_rows(*halves(shard_gu), core, ff_unit, 256)
-    grad_out = join_cols(*halves(shard_out), core, GROUP * HEAD)
-    grad_qkv = join_rows(*halves(shard_qkv), core, jnp.where(q_shard, GROUP * HEAD, HEAD), HEAD)
+    grad_w_gate = lax.dynamic_slice_in_dim(early, me * gate_count, gate_count, 0)
+
+    grad_gu = join_units([keep_done, sent_done], [keep_other, sent_other], core, upper.astype(jnp.int32))
+    grad_down = join_blocks(down_done, down_other, core, unit_block)
+    out_sum = line.run(shard_out)
+    grad_out = join_cols([out_sum], [swap(out_sum)], core, GROUP * HEAD)
+    qkv_sum = [line.run(p) for p in shard_qkv]
+    grad_qkv = join_rows(
+        qkv_sum, [swap(p) for p in qkv_sum], core, jnp.where(q_shard, GROUP * HEAD // HEAD, 1), HEAD
+    )
     return (
         output,
         grad_input,

time: 1510 us -> 1470 us (0.974)
  waiting for transfers between devices: 755 us -> 725 us
    ppermute x27 -> x20, waiting for transfers between devices: 285 us -> 172 us  [the longest x18 124 us: send(): return (x, lax.ppermute(x, 'seq', self.stages[stage]))]
    all_gather x4, waiting for transfers between devices: 209 us -> 111 us  [gather(): return lax.all_gather(x, 'dp', axis=0, tiled=True)]
    all_to_all x0 -> x2, waiting for transfers between devices: none -> 74.3 us  [the longest x1 50.5 us: shards(): down_sum = lax.all_to_all(down_sum, 'dp', 0, 0, tiled=True)]
    all_to_all x8, waiting for transfers between devices: 154 us -> 219 us  [exchange(): return lax.all_to_all(x, 'seq', 0, 0, axis_index_groups=groups, tiled=True)]
    reduce_scatter x9 -> x5, waiting for transfers between devices: 41.8 us -> 84.8 us  [scatter(): return lax.psum_scatter(x, 'dp', scatter_dimension=0, tiled=True)]
    pallas_call x0 -> x2, Pallas kernels: none -> 28.4 us  [the longest x1 16.4 us: join_units(): pl.pallas_call(join_units_kernel, grid_spec=pltpu.PrefetchScalarGridSpec(...]
    dot_general x6 -> x7, matrix products: 80.5 us -> 99.3 us  [dot_nt(): lax.dot_general(left, right, (((1,), (1,)), ((), ())), preferred_element_...]
    dot_general x10 -> x7, matrix products: 104 us -> 85.5 us  [dot_tn(): lax.dot_general(left, right, (((0,), (0,)), ((), ())), preferred_element_...]
  transfers between devices with their start and end apart: 76 -> 67, of which waited for: 30 -> 32; matrix products, arithmetic and copies ran while one was open for 29% -> 23% of each run, Pallas kernels for 8% -> 9%
where the time goes in v3:
time: 1470 us
  waiting for transfers between devices  725 us (49%)
  matrix products  267 us (18%)
  other arithmetic  165 us (11%)
  Pallas kernels  145 us (10%)
  starting transfers between devices  115 us (8%)
  local copies, waits for them, and re-layouts  35.6 us (2%)
  between operations  15.6 us (1%)
    all_to_all x8, waiting for transfers between devices, exchange(): return lax.all_to_all(x, 'seq', 0, 0, axis_index_groups=groups, tiled=True)  219 us
    ppermute x18, waiting for transfers between devices, send(): return (x, lax.ppermute(x, 'seq', self.stages[stage]))  124 us
    all_gather x4, waiting for transfers between devices, gather(): return lax.all_gather(x, 'dp', axis=0, tiled=True)  111 us
    dot_general x7, matrix products, dot_nt(): lax.dot_general(left, right, (((1,), (1,)), ((), ())), preferred_element_...  99.3 us
    dot_general x7, matrix products, dot_tn(): lax.dot_general(left, right, (((0,), (0,)), ((), ())), preferred_element_...  85.5 us
    reduce_scatter x5, waiting for transfers between devices, scatter(): return lax.psum_scatter(x, 'dp', scatter_dimension=0, tiled=True)  84.8 us
    dot_general x7, matrix products, dot_nn(): lax.dot_general(left, right, (((1,), (0,)), ((), ())), preferred_element_...  81.9 us
    ppermute x12, waiting for transfers between devices, total_sum(): x = x + lax.ppermute(x, name, [(s, s ^ step) for s in range(size)])  50.8 us
  transfers between devices with their start and end apart: 67, of which 32 were waited for; matrix products, arithmetic and copies ran while one was open for 23% of the time, Pallas kernels for 9%

profile of v3, /device:TPU:0, one launch (start us, length us, event | category | flops | bytes accessed | tf_op | source)
XLA Modules:
  0.0 1468.2 jit_solution(6596359086604736679)
XLA Ops:
  28.9 7.1 select_select_fusion
  46.4 59.7 %all-gather.5.cloned.1.call-done = bf16[2048,2048]{1,0:T(8,128)(2,1)} async-done(((bf16[512,2048]{1,0:T(8,128)(2,1)}), bf16[2048,2048]{1,0:T(8,128)(2,1)}) %all-gather.5.cloned.1.call-update) | async-done | bytes 8388624 | tf_op jit(solution)/shard_map/all_gather | solution.py:610
  116.3 11.1 fusion.71.proj_ref
  127.4 6.2 pack_heads.2
  133.5 23.8 %all-to-all-done.2 = bf16[4,256,1536]{2,1,0:T(8,128)(2,1)S(1)} async-done(((bf16[4,256,1536]{2,1,0:T(8,128)(2,1)}), bf16[4,256,1536]{2,1,0:T(8,128)(2,1)S(1)}, u32[]{:S(2)}, u32[]{:S(2)}) %all-to-all-start.2) | async-done | bytes 3145760 | tf_op jit(solution)/shard_map/all_to_all | solution.py:651
  164.3 6.2 pack_heads.3
  170.5 40.5 %all-to-all-done.q_ref.k_ref.v_ref = bf16[4,512,512]{2,1,0:T(8,128)(2,1)S(1)} async-done(((bf16[4,512,512]{2,1,0:T(8,128)(2,1)}), bf16[4,512,512]{2,1,0:T(8,128)(2,1)S(1)}, u32[]{:S(2)}, u32[]{:S(2)}) %all-to-all-start) | async-done | bytes 2097184 | tf_op jit(solution)/shard_map/all_to_all | solution.py:595
  231.5 11.0 attend.2
  242.5 20.9 %all-to-all-done.3.q_ref.k_ref.v_ref = bf16[4,512,512]{2,1,0:T(8,128)(2,1)} async-done(((bf16[4,512,512]{2,1,0:T(8,128)(2,1)}), bf16[4,512,512]{2,1,0:T(8,128)(2,1)}, u32[]{:S(2)}, u32[]{:S(2)}) %all-to-all-start.3) | async-done | bytes 2097184 | tf_op jit(solution)/shard_map/all_to_all | solution.py:595
  267.1 10.8 attend.3
  277.9 14.5 all-to-all-done.1.res_ref
  295.9 48.7 %collective-permute-done.3 = bf16[768,2048]{1,0:T(8,128)(2,1)} collective-permute-done((bf16[768,2048]{1,0:T(8,128)(2,1)}, bf16[768,2048]{1,0:T(8,128)(2,1)}, u32[]{:S(2)}, u32[]{:S(2)}) %collective-permute-start.3) | collective-permute-done | bytes 3145760 | tf_op jit(solution)/shard_map/ppermute | solution.py:650
  357.1 5.0 convolution_convert_fusion.11
  372.0 5.1 collective-permute-done.6
  387.9 19.0 %fusion.9 = bf16[2048,1536]{0,1:T(8,128)(2,1)} fusion(bf16[2048,1536]{1,0:T(8,128)(2,1)} %bitcast.153, bf16[2048,2048]{1,0:T(8,128)(2,1)} %all-gather.11.cloned.1.call-done), kind=kOutput, calls=%fused_computation.32 | convolution fusion | flops 12888047616 | bytes 20971520 | tf_op jit(solution)/shard_map/dot_general | solution.py:33
  406.9 51.2 %all-gather.9.cloned.1.call-done = bf16[2048,2048]{1,0:T(8,128)(2,1)} async-done(((bf16[512,2048]{1,0:T(8,128)(2,1)}), bf16[2048,2048]{1,0:T(8,128)(2,1)}) %all-gather.9.cloned.1.call-update) | async-done | bytes 8388624 | tf_op jit(solution)/shard_map/all_gather | solution.py:610
  458.1 19.6 %convolution_convert_fusion.4 = bf16[2048,1536]{0,1:T(8,128)(2,1)} fusion(bf16[2048,2048]{1,0:T(8,128)(2,1)} %all-gather.9.cloned.1.call-done, bf16[3072,2048]{1,0:T(8,128)(2,1)} %param.22, pred[]{:T(512)S(6)} %ge.19), kind=kOutput, calls=%fused_computation.25 | convolution fusion | flops 12891193344 | bytes 27262976 | tf_op jit(solution)/shard_map/dot_general | solution.py:29
  477.7 30.8 %select_convert_fusion = (bf16[2048,1536]{0,1:T(8,128)(2,1)}, bf16[2048,1536]{0,1:T(8,128)(2,1)}, bf16[2048,1536]{0,1:T(8,128)(2,1)}) fusion(bf16[2048,1536]{0,1:T(8,128)(2,1)} %fusion.9, pred[]{:T(512)S(6)} %ge.19, bf16[2048,1536]{0,1:T(8,128)(2,1)} %convolution_convert_fusion.4, bf16[2048,2048]{1,0:T(8,128)(2,1)} %all-gather.9.cloned.1.call-done, ...), kind=kOutput, calls=%fused_computation.14 | convolution fusion | flops 12950962176 | bytes 46137344 | tf_op jit(solution)/shard_map/dot_general | solution.py:29
  508.5 22.0 %fusion.49 = f32[2048,2048]{1,0:T(8,128)} fusion(bf16[2048,1536]{0,1:T(8,128)(2,1)} %get-tuple-element.133, bf16[3072,2048]{1,0:T(8,128)(2,1)} %param.22, pred[]{:T(512)S(6)} %ge.19), kind=kOutput, calls=%fused_computation.130 | convolution fusion | flops 12888047616 | bytes 35651584 | tf_op jit(solution)/shard_map/dot_general | solution.py:33
  530.5 19.5 %add_convert_fusion = bf16[2048,2048]{1,0:T(8,128)(2,1)} fusion(f32[2048,2048]{1,0:T(8,128)} %fusion.49, bf16[2048,1536]{0,1:T(8,128)(2,1)S(1)} %copy-done.68, bf16[1536,2048]{1,0:T(8,128)(2,1)} %pad_maximum_fusion.1), kind=kOutput, calls=%fused_computation.3 | convolution fusion | flops 12893290496 | bytes 37748736 | tf_op jit(solution)/shard_map/dot_general | solution.py:33
  550.1 21.7 %fusion.10 = bf16[2048,1536]{0,1:T(8,128)(2,1)} fusion(bf16[2048,2048]{1,0:T(8,128)(2,1)} %all-gather.11.cloned.1.call-done, bf16[2048,1536]{0,1:T(8,128)(2,1)} %convolution_convert_fusion.4, bf16[2048,1536]{0,1:T(8,128)(2,1)} %get-tuple-element.178, pred[]{:T(512)S(6)} %ge.19), kind=kOutput, calls=%fused_computation.33 | convolution fusion | flops 12919504896 | bytes 27262976 | tf_op jit(solution)/shard_map/dot_general | solution.py:37
  571.8 8.8 copy.44
  580.6 19.2 %convolution_convert_fusion.2 = bf16[1536,2048]{1,0:T(8,128)(2,1)} fusion(bf16[2048,1536]{0,1:T(8,128)(2,1)} %get-tuple-element.132, bf16[2048,2048]{1,0:T(8,128)(2,1)} %all-gather.9.cloned.1.call-done), kind=kOutput, calls=%fused_computation.23 | convolution fusion | flops 12888047616 | bytes 20971520 | tf_op jit(solution)/shard_map/dot_general | solution.py:37
  599.9 17.3 %convolution_convert_fusion.3 = bf16[1536,2048]{1,0:T(8,128)(2,1)} fusion(bf16[2048,1536]{0,1:T(8,128)(2,1)S(1)} %bitcast.178, bf16[2048,2048]{1,0:T(8,128)(2,1)} %all-gather.9.cloned.1.call-done), kind=kOutput, calls=%fused_computation.24 | convolution fusion | flops 12888047616 | bytes 20971520 | tf_op jit(solution)/shard_map/dot_general | solution.py:37
  617.2 23.6 %convolution_convert_fusion = bf16[2048,2048]{1,0:T(8,128)(2,1)} fusion(bf16[2048,1536]{1,0:T(8,128)(2,1)} %bitcast.154, bf16[2048,1536]{0,1:T(8,128)(2,1)} %convolution_convert_fusion.4, bf16[2048,1536]{0,1:T(8,128)(2,1)} %get-tuple-element.178, pred[]{:T(512)S(6)} %ge.19), kind=kOutput, calls=%fused_computation.21 | convolution fusion | flops 12920553472 | bytes 27262976 | tf_op jit(solution)/shard_map/dot_general | solution.py:29
  645.9 5.6 slice_select_fusion.2
  657.0 70.4 %reduce-scatter.8.cloned.1.call-done = bf16[512,2048]{1,0:T(8,128)(2,1)} async-done(((bf16[2048,2048]{1,0:T(8,128)(2,1)}), bf16[512,2048]{1,0:T(8,128)(2,1)}) %reduce-scatter.8.cloned.1.call-update) | async-done | bytes 2097168 | tf_op jit(solution)/shard_map/reduce_scatter | solution.py:607
  727.4 6.5 fusion.68
  738.4 5.5 select_add_fusion
  757.9 6.0 select_add_fusion.1
  763.9 5.6 collective-permute-start.12
  773.3 10.3 all-to-all-done.5.grad_ref
  791.3 6.2 convolution_convert_fusion.9
  797.5 50.5 %all-to-all-done.6 = bf16[4,256,1536]{2,1,0:T(8,128)(2,1)S(1)} async-done(((bf16[4,256,1536]{2,1,0:T(8,128)(2,1)}), bf16[4,256,1536]{2,1,0:T(8,128)(2,1)S(1)}, u32[]{:S(2)}, u32[]{:S(2)}) %all-to-all-start.6) | async-done | bytes 3145760 | tf_op jit(solution)/shard_map/all_to_all | solution.py:737
  848.0 6.2 add.216
  856.6 6.2 collective-permute-start.15
  875.5 5.6 collective-permute-start.18
  881.1 20.1 %attend_back.2 = bf16[4,512,512]{2,1,0:T(8,128)(2,1)} custom-call(s32[4]{0:T(128)} %get-tuple-element.176.low_ref, bf16[4,512,512]{2,1,0:T(8,128)(2,1)} %copy-done, bf16[4,512,512]{2,1,0:T(8,128)(2,1)} %copy-done, bf16[4,512,512]{2,1,0:T(8,128)(2,1)} %copy-done, bf16[4,512,256]{2,1,0:T(8,128)(2,1)} %copy-done.29, ...), custom_call_target="tpu_custom_call" | custom-call | tf_op jit(solution)/shard_map/attend_back/pallas_call | solution.py:281
  901.2 48.0 %all-to-all-done.8.grad_ref = bf16[4,512,256]{2,1,0:T(8,128)(2,1)} async-done(((bf16[4,512,256]{2,1,0:T(8,128)(2,1)}), bf16[4,512,256]{2,1,0:T(8,128)(2,1)}, u32[]{:S(2)}, u32[]{:S(2)}) %all-to-all-start.8) | async-done | bytes 1048608 | tf_op jit(solution)/shard_map/all_to_all | solution.py:595
  965.9 19.8 %attend_back.3 = bf16[4,512,512]{2,1,0:T(8,128)(2,1)} custom-call(s32[4]{0:T(128)} %get-tuple-element.177.low_ref, bf16[4,512,512]{2,1,0:T(8,128)(2,1)} %all-to-all-done.3.q_ref.k_ref.v_ref, bf16[4,512,512]{2,1,0:T(8,128)(2,1)} %all-to-all-done.3.q_ref.k_ref.v_ref, bf16[4,512,512]{2,1,0:T(8,128)(2,1)} %all-to-all-done.3.q_ref.k_ref.v_ref, ...), custom_call_target="tpu_custom_call" | custom-call | tf_op jit(solution)/shard_map/attend_back/pallas_call | solution.py:281
  985.7 60.1 %all-to-all-done.7.grad_ref = bf16[4,512,512]{2,1,0:T(8,128)(2,1)} async-done(((bf16[4,512,512]{2,1,0:T(8,128)(2,1)}), bf16[4,512,512]{2,1,0:T(8,128)(2,1)}, u32[]{:S(2)}, u32[]{:S(2)}) %all-to-all-start.7) | async-done | bytes 2097184 | tf_op jit(solution)/shard_map/all_to_all | solution.py:595
  1050.5 16.7 %collective-permute-done.16 = bf16[768,2048]{1,0:T(8,128)(2,1)} collective-permute-done((bf16[768,2048]{1,0:T(8,128)(2,1)S(1)}, bf16[768,2048]{1,0:T(8,128)(2,1)}, u32[]{:S(2)}, u32[]{:S(2)}) %collective-permute-start.16) | collective-permute-done | bytes 3145760 | tf_op jit(solution)/shard_map/ppermute | solution.py:528
  1067.2 6.0 add.220
  1080.7 7.5 unpack_heads.2
  1091.4 24.4 %all-to-all-done.9.grad_ref = bf16[4,512,512]{2,1,0:T(8,128)(2,1)} async-done(((bf16[4,512,512]{2,1,0:T(8,128)(2,1)}), bf16[4,512,512]{2,1,0:T(8,128)(2,1)}, u32[]{:S(2)}, u32[]{:S(2)}) %all-to-all-start.9) | async-done | bytes 2097184 | tf_op jit(solution)/shard_map/all_to_all | solution.py:595
  1115.8 62.1 %collective-permute-done.19 = bf16[4,256,1536]{2,1,0:T(8,128)(2,1)} collective-permute-done((bf16[4,256,1536]{2,1,0:T(8,128)(2,1)S(1)}, bf16[4,256,1536]{2,1,0:T(8,128)(2,1)}, u32[]{:S(2)}, u32[]{:S(2)}) %collective-permute-start.19) | collective-permute-done | bytes 3145760 | tf_op jit(solution)/shard_map/ppermute | solution.py:528
  1177.9 7.5 unpack_heads.3
  1188.7 8.5 convolution_convert_fusion.7
  1197.5 9.5 convolution_convert_fusion.8
  1211.4 12.7 fusion.72
  1236.2 5.2 collective-permute-done.28
  1243.7 9.4 collective-permute-done.29
  1262.0 6.1 add.243
  1269.5 5.9 fusion.24
  1275.5 7.1 collective-permute-start.35
  1290.8 14.3 reduce-scatter.10.cloned.1.call-done
  1318.8 20.1 %collective-permute-done.23 = f32[2,2048]{1,0:T(2,128)} collective-permute-done((f32[2,2048]{1,0:T(2,128)}, f32[2,2048]{1,0:T(2,128)}, u32[]{:S(2)}, u32[]{:S(2)}) %collective-permute-start.23) | collective-permute-done | bytes 16416 | tf_op jit(solution)/shard_map/ppermute | solution.py:602
  1351.2 15.8 %collective-permute-done.42 = bf16[512,1024]{1,0:T(8,128)(2,1)S(1)} collective-permute-done((bf16[512,1024]{1,0:T(8,128)(2,1)S(1)}, bf16[512,1024]{1,0:T(8,128)(2,1)S(1)}, u32[]{:S(2)}, u32[]{:S(2)}) %collective-permute-start.42) | collective-permute-done | bytes 1048608 | tf_op jit(solution)/shard_map/ppermute | solution.py:528
  1373.7 15.7 %collective-permute-done.37 = bf16[512,1024]{1,0:T(8,128)(2,1)S(1)} collective-permute-done((bf16[512,1024]{1,0:T(8,128)(2,1)S(1)}, bf16[512,1024]{1,0:T(8,128)(2,1)S(1)}, u32[]{:S(2)}, u32[]{:S(2)}) %collective-permute-start.37) | collective-permute-done | bytes 1048608 | tf_op jit(solution)/shard_map/ppermute | solution.py:528
  1395.4 13.2 collective-permute-done.34
  1417.9 6.4 join_cols.1
  1424.4 11.9 join_blocks.1
  1436.3 16.4 %join_units.1 = f32[3072,2048]{1,0:T(8,128)} custom-call(s32[2]{0:T(128)} %get-tuple-element.180.which_ref, bf16[768,2048]{1,0:T(8,128)(2,1)} %broadcast_select_fusion.4.keep_ref, bf16[768,2048]{1,0:T(8,128)(2,1)} %collective-permute-done.44.keep_other_ref, bf16[768,2048]{1,0:T(8,128)(2,1)} %broadcast_select_fusion.3.sent_ref, ...), custom_call_target="tpu_custom_call" | custom-call | tf_op jit(solution)/shard_map/join_units/pallas_call | solution.py:478
  1452.8 8.4 join_rows.1
  (386 shorter events, 285.6 us)
Async XLA Ops:
  7.2 98.9 %all-gather.5.cloned.1.call-start = ((), (), s32[]{:S(2)}) async-start(), calls=%async_computation.15 | async-start | bytes 10485760 | tf_op jit(solution)/shard_map/all_gather | solution.py:610
  15.7 332.6 %all-gather.7.cloned.1.call-start = ((), (), s32[]{:S(2)}) async-start(), calls=%async_computation.16 | async-start | bytes 5242880 | tf_op jit(solution)/shard_map/all_gather | solution.py:610
  15.8 23.4 %collective-permute-start = (bf16[2,256,2048]{2,1,0:T(8,128)(2,1)S(1)}, bf16[2,256,2048]{2,1,0:T(8,128)(2,1)}, u32[]{:S(2)}, u32[]{:S(2)}) collective-permute-start(bf16[2,256,2048]{2,1,0:T(8,128)(2,1)S(1)} %copy-done.1), channel_id=1, source_target_pairs={{0,1},{1,0},{2,3},{3,2},{4,5},{5,4},{6,7},{7,6},{8,9},{9,8},{10,11... | collective-permute-start | bytes 6291464 | tf_op jit(solution)/shard_map/ppermute | solution.py:585
  106.1 51.3 %all-to-all-start.2 = ((bf16[4,256,1536]{2,1,0:T(8,128)(2,1)}), bf16[4,256,1536]{2,1,0:T(8,128)(2,1)S(1)}, u32[]{:S(2)}, u32[]{:S(2)}) async-start(bf16[4,256,1536]{2,1,0:T(8,128)(2,1)} %pad_maximum_fusion.4), calls=%async_computation.2 | async-start | bytes 6291456 | tf_op jit(solution)/shard_map/all_to_all | solution.py:651
  159.0 52.1 %all-to-all-start = ((bf16[4,512,512]{2,1,0:T(8,128)(2,1)}), bf16[4,512,512]{2,1,0:T(8,128)(2,1)S(1)}, u32[]{:S(2)}, u32[]{:S(2)}) async-start(bf16[4,512,512]{2,1,0:T(8,128)(2,1)} %pack_heads.2), calls=%async_computation | async-start | bytes 4194304 | tf_op jit(solution)/shard_map/all_to_all | solution.py:595
  163.6 224.2 %all-gather.11.cloned.1.call-start = ((), (), s32[]{:S(2)}) async-start(), calls=%async_computation.18 | async-start | bytes 10485760 | tf_op jit(solution)/shard_map/all_gather | solution.py:610
  211.1 52.3 %all-to-all-start.3 = ((bf16[4,512,512]{2,1,0:T(8,128)(2,1)}), bf16[4,512,512]{2,1,0:T(8,128)(2,1)}, u32[]{:S(2)}, u32[]{:S(2)}) async-start(bf16[4,512,512]{2,1,0:T(8,128)(2,1)} %pack_heads.3), calls=%async_computation.3 | async-start | bytes 4194304 | tf_op jit(solution)/shard_map/all_to_all | solution.py:595
  215.6 5.9 collective-permute-start.1
  221.5 4.3 collective-permute-start.2
  230.2 114.4 %collective-permute-start.3 = (bf16[768,2048]{1,0:T(8,128)(2,1)}, bf16[768,2048]{1,0:T(8,128)(2,1)}, u32[]{:S(2)}, u32[]{:S(2)}) collective-permute-start(bf16[768,2048]{1,0:T(8,128)(2,1)} %select_select_fusion), channel_id=1, source_target_pairs={{0,16},{8,24},{16,0},{24,8},{1,17},{9,25},{17,1},{25,9},{2,18},{10... | collective-permute-start | bytes 9437192 | tf_op jit(solution)/shard_map/ppermute | solution.py:650
  263.4 29.0 %all-to-all-start.1 = ((bf16[4,512,256]{2,1,0:T(8,128)(2,1)}), bf16[4,512,256]{2,1,0:T(8,128)(2,1)S(1)}, u32[]{:S(2)}, u32[]{:S(2)}) async-start(bf16[4,512,256]{2,1,0:T(8,128)(2,1)} %get-tuple-element.70.res_ref), calls=%async_computation.1 | async-start | bytes 2097152 | tf_op jit(solution)/shard_map/all_to_all | solution.py:595
  292.3 52.3 %all-to-all-start.4 = ((bf16[4,512,256]{2,1,0:T(8,128)(2,1)}), bf16[4,512,256]{2,1,0:T(8,128)(2,1)S(1)}, u32[]{:S(2)}, u32[]{:S(2)}) async-start(bf16[4,512,256]{2,1,0:T(8,128)(2,1)} %get-tuple-element.75.res_ref), calls=%async_computation.4 | async-start | bytes 2097152 | tf_op jit(solution)/shard_map/all_to_all | solution.py:595
  295.9 162.2 %all-gather.9.cloned.1.call-start = ((), (), s32[]{:S(2)}) async-start(), calls=%async_computation.17 | async-start | bytes 10485760 | tf_op jit(solution)/shard_map/all_gather | solution.py:610
  354.5 8.3 collective-permute-start.5
  370.6 270.3 %reduce-scatter.6.cloned.1.call-start = ((), (), s32[]{:S(2)}) async-start(), calls=%async_computation.19 | async-start | bytes 10485760 | tf_op jit(solution)/shard_map/reduce_scatter | solution.py:607
  371.5 5.7 collective-permute-start.6
  371.8 9.8 collective-permute-start.7
  550.1 177.3 %reduce-scatter.8.cloned.1.call-start = ((), (), s32[]{:S(2)}) async-start(), calls=%async_computation.20 | async-start | bytes 10485760 | tf_op jit(solution)/shard_map/reduce_scatter | solution.py:607
  645.9 88.1 %collective-permute-start.11 = (bf16[4,256,1536]{2,1,0:T(8,128)(2,1)}, bf16[4,256,1536]{2,1,0:T(8,128)(2,1)}, u32[]{:S(2)}, u32[]{:S(2)}) collective-permute-start(bf16[4,256,1536]{2,1,0:T(8,128)(2,1)} %fusion.29), channel_id=1, source_target_pairs={{0,1},{1,0},{2,3},{3,2},{4,5},{5,4},{6,7},{7,6},{8,9},{9,8},{10,11... | collective-permute-start | bytes 9437192 | tf_op jit(solution)/shard_map/ppermute | solution.py:585
  651.5 82.4 %collective-permute-start.10 = (bf16[768,2048]{1,0:T(8,128)(2,1)}, bf16[768,2048]{1,0:T(8,128)(2,1)}, u32[]{:S(2)}, u32[]{:S(2)}) collective-permute-start(bf16[768,2048]{1,0:T(8,128)(2,1)} %slice_select_fusion.2), channel_id=1, source_target_pairs={{0,1},{1,0},{2,3},{3,2},{4,5},{5,4},{6,7},{7,6},{8,9},{9,8},{10,11... | collective-permute-start | bytes 9437192 | tf_op jit(solution)/shard_map/ppermute | solution.py:585
  654.0 80.0 %collective-permute-start.9 = (bf16[768,2048]{1,0:T(8,128)(2,1)}, bf16[768,2048]{1,0:T(8,128)(2,1)}, u32[]{:S(2)}, u32[]{:S(2)}) collective-permute-start(bf16[768,2048]{1,0:T(8,128)(2,1)} %slice_select_fusion.3), channel_id=1, source_target_pairs={{0,1},{1,0},{2,3},{3,2},{4,5},{5,4},{6,7},{7,6},{8,9},{9,8},{10,11... | collective-permute-start | bytes 9437192 | tf_op jit(solution)/shard_map/ppermute | solution.py:585
  733.9 4.2 collective-permute-start.8
  744.0 104.1 %collective-permute-start.13 = (bf16[768,2048]{1,0:T(8,128)(2,1)}, bf16[768,2048]{1,0:T(8,128)(2,1)}, u32[]{:S(2)}, u32[]{:S(2)}) collective-permute-start(bf16[768,2048]{1,0:T(8,128)(2,1)} %select_add_fusion), channel_id=1, source_target_pairs={{0,16},{8,24},{16,0},{24,8},{1,17},{9,25},{17,1},{25,9},{2,18},{10... | collective-permute-start | bytes 9437192 | tf_op jit(solution)/shard_map/ppermute | solution.py:736
  753.1 30.5 %all-to-all-start.5 = ((bf16[4,512,256]{2,1,0:T(8,128)(2,1)}), bf16[4,512,256]{2,1,0:T(8,128)(2,1)S(1)}, u32[]{:S(2)}, u32[]{:S(2)}) async-start(bf16[4,512,256]{2,1,0:T(8,128)(2,1)} %get-tuple-element.84), calls=%async_computation.7 | async-start | bytes 2097152 | tf_op jit(solution)/shard_map/all_to_all | solution.py:595
  763.9 84.2 %collective-permute-start.12 = (bf16[768,2048]{1,0:T(8,128)(2,1)}, bf16[768,2048]{1,0:T(8,128)(2,1)}, u32[]{:S(2)}, u32[]{:S(2)}) collective-permute-start(bf16[768,2048]{1,0:T(8,128)(2,1)} %select_add_fusion.1), channel_id=1, source_target_pairs={{0,2},{1,3},{6,4},{7,5},{8,10},{9,11},{14,12},{15,13},{16,18},{17,... | collective-permute-start | bytes 9437192 | tf_op jit(solution)/shard_map/ppermute | solution.py:528
  784.6 63.4 %all-to-all-start.6 = ((bf16[4,256,1536]{2,1,0:T(8,128)(2,1)}), bf16[4,256,1536]{2,1,0:T(8,128)(2,1)S(1)}, u32[]{:S(2)}, u32[]{:S(2)}) async-start(bf16[4,256,1536]{2,1,0:T(8,128)(2,1)} %fusion.27), calls=%async_computation.8 | async-start | bytes 6291456 | tf_op jit(solution)/shard_map/all_to_all | solution.py:737
  854.3 99.4 %collective-permute-start.14 = (bf16[768,2048]{1,0:T(8,128)(2,1)}, bf16[768,2048]{1,0:T(8,128)(2,1)}, u32[]{:S(2)}, u32[]{:S(2)}) collective-permute-start(bf16[768,2048]{1,0:T(8,128)(2,1)} %add.216), channel_id=1, source_target_pairs={{2,4},{3,5},{4,2},{5,3},{10,12},{11,13},{12,10},{13,11},{18,20},{1... | collective-permute-start | bytes 9437192 | tf_op jit(solution)/shard_map/ppermute | solution.py:528
  856.6 97.1 %collective-permute-start.15 = (bf16[4,256,1536]{2,1,0:T(8,128)(2,1)S(1)}, bf16[4,256,1536]{2,1,0:T(8,128)(2,1)}, u32[]{:S(2)}, u32[]{:S(2)}) collective-permute-start(bf16[4,256,1536]{2,1,0:T(8,128)(2,1)S(1)} %all-to-all-done.6), channel_id=1, source_target_pairs={{0,2},{1,3},{6,4},{7,5},{8,10},{9,11},{14,12},{15,13},{16,18},{17,... | collective-permute-start | bytes 9437192 | tf_op jit(solution)/shard_map/ppermute | solution.py:528
  870.5 78.7 %all-to-all-start.8 = ((bf16[4,512,256]{2,1,0:T(8,128)(2,1)}), bf16[4,512,256]{2,1,0:T(8,128)(2,1)}, u32[]{:S(2)}, u32[]{:S(2)}) async-start(bf16[4,512,256]{2,1,0:T(8,128)(2,1)} %get-tuple-element.93), calls=%async_computation.10 | async-start | bytes 2097152 | tf_op jit(solution)/shard_map/all_to_all | solution.py:595
  874.8 384.4 %reduce-scatter.14.cloned.1.call-start = ((), (), s32[]{:S(2)}) async-start(), calls=%async_computation.23 | async-start | bytes 5242880 | tf_op jit(solution)/shard_map/reduce_scatter | solution.py:607
  875.5 174.9 %collective-permute-start.18 = (bf16[768,2048]{1,0:T(8,128)(2,1)}, bf16[768,2048]{1,0:T(8,128)(2,1)}, u32[]{:S(2)}, u32[]{:S(2)}) collective-permute-start(bf16[768,2048]{1,0:T(8,128)(2,1)} %collective-permute-done.13), channel_id=1, source_target_pairs={{0,2},{1,3},{6,4},{7,5},{8,10},{9,11},{14,12},{15,13},{16,18},{17,... | collective-permute-start | bytes 9437192 | tf_op jit(solution)/shard_map/ppermute | solution.py:528
  949.2 96.6 %all-to-all-start.7 = ((bf16[4,512,512]{2,1,0:T(8,128)(2,1)}), bf16[4,512,512]{2,1,0:T(8,128)(2,1)}, u32[]{:S(2)}, u32[]{:S(2)}) async-start(bf16[4,512,512]{2,1,0:T(8,128)(2,1)} %attend_back.2), calls=%async_computation.9 | async-start | bytes 4194304 | tf_op jit(solution)/shard_map/all_to_all | solution.py:595
  958.1 92.4 %collective-permute-start.17 = (bf16[4,256,1536]{2,1,0:T(8,128)(2,1)}, bf16[4,256,1536]{2,1,0:T(8,128)(2,1)}, u32[]{:S(2)}, u32[]{:S(2)}) collective-permute-start(bf16[4,256,1536]{2,1,0:T(8,128)(2,1)} %add.218), channel_id=1, source_target_pairs={{2,4},{3,5},{4,2},{5,3},{10,12},{11,13},{12,10},{13,11},{18,20},{1... | collective-permute-start | bytes 9437192 | tf_op jit(solution)/shard_map/ppermute | solution.py:528
  964.6 102.6 %collective-permute-start.16 = (bf16[768,2048]{1,0:T(8,128)(2,1)S(1)}, bf16[768,2048]{1,0:T(8,128)(2,1)}, u32[]{:S(2)}, u32[]{:S(2)}) collective-permute-start(bf16[768,2048]{1,0:T(8,128)(2,1)S(1)} %add.217), channel_id=1, source_target_pairs={{2,0},{3,1},{4,6},{5,7},{10,8},{11,9},{12,14},{13,15},{18,16},{19,... | collective-permute-start | bytes 9437192 | tf_op jit(solution)/shard_map/ppermute | solution.py:528
  1045.8 70.0 %all-to-all-start.9 = ((bf16[4,512,512]{2,1,0:T(8,128)(2,1)}), bf16[4,512,512]{2,1,0:T(8,128)(2,1)}, u32[]{:S(2)}, u32[]{:S(2)}) async-start(bf16[4,512,512]{2,1,0:T(8,128)(2,1)} %attend_back.3), calls=%async_computation.11 | async-start | bytes 4194304 | tf_op jit(solution)/shard_map/all_to_all | solution.py:595
  1050.5 225.0 %reduce-scatter.12.cloned.1.call-start = ((), (), s32[]{:S(2)}) async-start(), calls=%async_computation.22 | async-start | bytes 5242880 | tf_op jit(solution)/shard_map/reduce_scatter | solution.py:607
  1073.2 42.6 %collective-permute-start.20 = (bf16[768,2048]{1,0:T(8,128)(2,1)}, bf16[768,2048]{1,0:T(8,128)(2,1)}, u32[]{:S(2)}, u32[]{:S(2)}) collective-permute-start(bf16[768,2048]{1,0:T(8,128)(2,1)} %add.220), channel_id=1, source_target_pairs={{2,4},{3,5},{4,2},{5,3},{10,12},{11,13},{12,10},{13,11},{18,20},{1... | collective-permute-start | bytes 9437192 | tf_op jit(solution)/shard_map/ppermute | solution.py:528
  1079.4 98.5 %collective-permute-start.19 = (bf16[4,256,1536]{2,1,0:T(8,128)(2,1)S(1)}, bf16[4,256,1536]{2,1,0:T(8,128)(2,1)}, u32[]{:S(2)}, u32[]{:S(2)}) collective-permute-start(bf16[4,256,1536]{2,1,0:T(8,128)(2,1)S(1)} %add.219), channel_id=1, source_target_pairs={{2,0},{3,1},{4,6},{5,7},{10,8},{11,9},{12,14},{13,15},{18,16},{19,... | collective-permute-start | bytes 9437192 | tf_op jit(solution)/shard_map/ppermute | solution.py:528
  1197.2 107.9 %reduce-scatter.10.cloned.1.call-start = ((), (), s32[]{:S(2)}) async-start(), calls=%async_computation.21 | async-start | bytes 5242880 | tf_op jit(solution)/shard_map/reduce_scatter | solution.py:607
  1229.1 40.4 %collective-permute-start.21 = (bf16[2,256,2048]{2,1,0:T(8,128)(2,1)}, bf16[2,256,2048]{2,1,0:T(8,128)(2,1)}, u32[]{:S(2)}, u32[]{:S(2)}) collective-permute-start(bf16[2,256,2048]{2,1,0:T(8,128)(2,1)} %select_bitcast_fusion), channel_id=1, source_target_pairs={{0,1},{1,0},{2,3},{3,2},{4,5},{5,4},{6,7},{7,6},{8,9},{9,8},{10,11... | collective-permute-start | bytes 6291464 | tf_op jit(solution)/shard_map/ppermute | solution.py:585
  1229.2 4.6 collective-permute-start.27
  1233.8 7.6 collective-permute-start.28
  1241.4 11.7 collective-permute-start.29
  1253.1 6.0 collective-permute-start.30
  1259.2 27.4 %collective-permute-start.40 = (bf16[512,1024]{1,0:T(8,128)(2,1)}, bf16[512,1024]{1,0:T(8,128)(2,1)}, u32[]{:S(2)}, u32[]{:S(2)}) collective-permute-start(bf16[512,1024]{1,0:T(8,128)(2,1)} %reduce-scatter.14.cloned.1.call-done), channel_id=1, source_target_pairs={{0,2},{1,3},{6,4},{7,5},{8,10},{9,11},{14,12},{15,13},{16,18},{17,... | collective-permute-start | bytes 3145736 | tf_op jit(solution)/shard_map/ppermute | solution.py:528
  1268.1 77.9 %collective-permute-start.45 = (bf16[768,2048]{1,0:T(8,128)(2,1)}, bf16[768,2048]{1,0:T(8,128)(2,1)}, u32[]{:S(2)}, u32[]{:S(2)}) collective-permute-start(bf16[768,2048]{1,0:T(8,128)(2,1)} %add.243), channel_id=1, source_target_pairs={{2,0},{3,1},{4,6},{5,7},{10,8},{11,9},{12,14},{13,15},{18,16},{19,... | collective-permute-start | bytes 9437192 | tf_op jit(solution)/shard_map/ppermute | solution.py:528
  1275.4 14.8 %collective-permute-start.22 = (f32[2,2048]{1,0:T(2,128)S(1)}, f32[2,2048]{1,0:T(2,128)S(1)}, u32[]{:S(2)}, u32[]{:S(2)}) collective-permute-start(f32[2,2048]{1,0:T(2,128)S(1)} %pad_maximum_fusion.9), channel_id=1, source_target_pairs={{0,1},{1,0},{2,3},{3,2},{4,5},{5,4},{6,7},{7,6},{8,9},{9,8},{10,11... | collective-permute-start | bytes 49160 | tf_op jit(solution)/shard_map/ppermute | solution.py:602
  1275.5 33.3 %collective-permute-start.35 = (bf16[512,1024]{1,0:T(8,128)(2,1)}, bf16[512,1024]{1,0:T(8,128)(2,1)}, u32[]{:S(2)}, u32[]{:S(2)}) collective-permute-start(bf16[512,1024]{1,0:T(8,128)(2,1)} %reduce-scatter.12.cloned.1.call-done), channel_id=1, source_target_pairs={{0,2},{1,3},{6,4},{7,5},{8,10},{9,11},{14,12},{15,13},{16,18},{17,... | collective-permute-start | bytes 3145736 | tf_op jit(solution)/shard_map/ppermute | solution.py:528
  1288.5 27.2 %collective-permute-start.41 = (bf16[512,1024]{1,0:T(8,128)(2,1)S(1)}, bf16[512,1024]{1,0:T(8,128)(2,1)}, u32[]{:S(2)}, u32[]{:S(2)}) collective-permute-start(bf16[512,1024]{1,0:T(8,128)(2,1)S(1)} %add.241), channel_id=1, source_target_pairs={{2,4},{3,5},{4,2},{5,3},{10,12},{11,13},{12,10},{13,11},{18,20},{1... | collective-permute-start | bytes 3145736 | tf_op jit(solution)/shard_map/ppermute | solution.py:528
  1290.8 48.1 %collective-permute-start.23 = (f32[2,2048]{1,0:T(2,128)}, f32[2,2048]{1,0:T(2,128)}, u32[]{:S(2)}, u32[]{:S(2)}) collective-permute-start(f32[2,2048]{1,0:T(2,128)} %fusion.61), channel_id=1, source_target_pairs={{0,2},{1,3},{2,0},{3,1},{4,6},{5,7},{6,4},{7,5},{8,10},{9,11},{10,... | collective-permute-start | bytes 49160 | tf_op jit(solution)/shard_map/ppermute | solution.py:602
  1305.2 35.8 %collective-permute-start.32 = (bf16[512,1024]{1,0:T(8,128)(2,1)}, bf16[512,1024]{1,0:T(8,128)(2,1)S(1)}, u32[]{:S(2)}, u32[]{:S(2)}) collective-permute-start(bf16[512,1024]{1,0:T(8,128)(2,1)} %reduce-scatter.10.cloned.1.call-done), channel_id=1, source_target_pairs={{0,2},{1,3},{6,4},{7,5},{8,10},{9,11},{14,12},{15,13},{16,18},{17,... | collective-permute-start | bytes 3145736 | tf_op jit(solution)/shard_map/ppermute | solution.py:528
  1310.8 34.0 %collective-permute-start.36 = (bf16[512,1024]{1,0:T(8,128)(2,1)S(1)}, bf16[512,1024]{1,0:T(8,128)(2,1)S(1)}, u32[]{:S(2)}, u32[]{:S(2)}) collective-permute-start(bf16[512,1024]{1,0:T(8,128)(2,1)S(1)} %add.238), channel_id=1, source_target_pairs={{2,4},{3,5},{4,2},{5,3},{10,12},{11,13},{12,10},{13,11},{18,20},{1... | collective-permute-start | bytes 3145736 | tf_op jit(solution)/shard_map/ppermute | solution.py:528
  1315.7 35.5 %collective-permute-start.31 = (f32[24,2048]{1,0:T(8,128)S(1)}, f32[24,2048]{1,0:T(8,128)S(1)}, u32[]{:S(2)}, u32[]{:S(2)}) collective-permute-start(f32[24,2048]{1,0:T(8,128)S(1)} %add.234), channel_id=1, source_target_pairs={{0,16},{8,24},{16,0},{24,8},{1,17},{9,25},{17,1},{25,9},{2,18},{10... | collective-permute-start | bytes 589832 | tf_op jit(solution)/shard_map/ppermute | solution.py:602
  1338.9 28.1 %collective-permute-start.42 = (bf16[512,1024]{1,0:T(8,128)(2,1)S(1)}, bf16[512,1024]{1,0:T(8,128)(2,1)S(1)}, u32[]{:S(2)}, u32[]{:S(2)}) collective-permute-start(bf16[512,1024]{1,0:T(8,128)(2,1)S(1)} %add.242), channel_id=1, source_target_pairs={{2,0},{3,1},{4,6},{5,7},{10,8},{11,9},{12,14},{13,15},{18,16},{19,... | collective-permute-start | bytes 3145736 | tf_op jit(solution)/shard_map/ppermute | solution.py:528
  1341.0 26.0 %collective-permute-start.24 = (f32[2,2048]{1,0:T(2,128)S(1)}, f32[2,2048]{1,0:T(2,128)S(1)}, u32[]{:S(2)}, u32[]{:S(2)}) collective-permute-start(f32[2,2048]{1,0:T(2,128)S(1)} %fusion.103), channel_id=1, source_target_pairs={{0,4},{1,5},{2,6},{3,7},{4,0},{5,1},{6,2},{7,3},{8,12},{9,13},{10,... | collective-permute-start | bytes 49160 | tf_op jit(solution)/shard_map/ppermute | solution.py:602
  1344.9 22.7 %collective-permute-start.33 = (bf16[512,1024]{1,0:T(8,128)(2,1)S(1)}, bf16[512,1024]{1,0:T(8,128)(2,1)S(1)}, u32[]{:S(2)}, u32[]{:S(2)}) collective-permute-start(bf16[512,1024]{1,0:T(8,128)(2,1)S(1)} %add.236), channel_id=1, source_target_pairs={{2,4},{3,5},{4,2},{5,3},{10,12},{11,13},{12,10},{13,11},{18,20},{1... | collective-permute-start | bytes 3145736 | tf_op jit(solution)/shard_map/ppermute | solution.py:528
  1346.0 43.4 %collective-permute-start.37 = (bf16[512,1024]{1,0:T(8,128)(2,1)S(1)}, bf16[512,1024]{1,0:T(8,128)(2,1)S(1)}, u32[]{:S(2)}, u32[]{:S(2)}) collective-permute-start(bf16[512,1024]{1,0:T(8,128)(2,1)S(1)} %add.239), channel_id=1, source_target_pairs={{2,0},{3,1},{4,6},{5,7},{10,8},{11,9},{12,14},{13,15},{18,16},{19,... | collective-permute-start | bytes 3145736 | tf_op jit(solution)/shard_map/ppermute | solution.py:528
  1351.2 73.1 %collective-permute-start.47 = (bf16[4,256,1536]{2,1,0:T(8,128)(2,1)}, bf16[4,256,1536]{2,1,0:T(8,128)(2,1)}, u32[]{:S(2)}, u32[]{:S(2)}) collective-permute-start(bf16[4,256,1536]{2,1,0:T(8,128)(2,1)} %broadcast_select_fusion.2.refs_0_), channel_id=1, source_target_pairs={{0,1},{1,0},{2,3},{3,2},{4,5},{5,4},{6,7},{7,6},{8,9},{9,8},{10,11... | collective-permute-start | bytes 9437192 | tf_op jit(solution)/shard_map/ppermute | solution.py:585
  1367.0 69.3 %collective-permute-start.44 = (bf16[768,2048]{1,0:T(8,128)(2,1)}, bf16[768,2048]{1,0:T(8,128)(2,1)}, u32[]{:S(2)}, u32[]{:S(2)}) collective-permute-start(bf16[768,2048]{1,0:T(8,128)(2,1)} %broadcast_select_fusion.4.keep_ref), channel_id=1, source_target_pairs={{0,1},{1,0},{2,3},{3,2},{4,5},{5,4},{6,7},{7,6},{8,9},{9,8},{10,11... | collective-permute-start | bytes 9437192 | tf_op jit(solution)/shard_map/ppermute | solution.py:585
  1367.0 69.3 %collective-permute-start.46 = (bf16[768,2048]{1,0:T(8,128)(2,1)}, bf16[768,2048]{1,0:T(8,128)(2,1)}, u32[]{:S(2)}, u32[]{:S(2)}) collective-permute-start(bf16[768,2048]{1,0:T(8,128)(2,1)} %broadcast_select_fusion.3.sent_ref), channel_id=1, source_target_pairs={{0,1},{1,0},{2,3},{3,2},{4,5},{5,4},{6,7},{7,6},{8,9},{9,8},{10,11... | collective-permute-start | bytes 9437192 | tf_op jit(solution)/shard_map/ppermute | solution.py:585
  1371.3 37.3 %collective-permute-start.34 = (bf16[512,1024]{1,0:T(8,128)(2,1)}, bf16[512,1024]{1,0:T(8,128)(2,1)}, u32[]{:S(2)}, u32[]{:S(2)}) collective-permute-start(bf16[512,1024]{1,0:T(8,128)(2,1)} %add.237), channel_id=1, source_target_pairs={{2,0},{3,1},{4,6},{5,7},{10,8},{11,9},{12,14},{13,15},{18,16},{19,... | collective-permute-start | bytes 3145736 | tf_op jit(solution)/shard_map/ppermute | solution.py:528
  1390.4 22.0 %collective-permute-start.43 = (bf16[512,1024]{1,0:T(8,128)(2,1)}, bf16[512,1024]{1,0:T(8,128)(2,1)}, u32[]{:S(2)}, u32[]{:S(2)}) collective-permute-start(bf16[512,1024]{1,0:T(8,128)(2,1)} %broadcast_select_fusion.14.refs_0_), channel_id=1, source_target_pairs={{0,1},{1,0},{2,3},{3,2},{4,5},{5,4},{6,7},{7,6},{8,9},{9,8},{10,11... | collective-permute-start | bytes 3145736 | tf_op jit(solution)/shard_map/ppermute | solution.py:585
  1412.4 40.4 %collective-permute-start.39 = (bf16[512,1024]{1,0:T(8,128)(2,1)}, bf16[512,1024]{1,0:T(8,128)(2,1)}, u32[]{:S(2)}, u32[]{:S(2)}) collective-permute-start(bf16[512,1024]{1,0:T(8,128)(2,1)} %broadcast_select_fusion.15.refs_1_), channel_id=1, source_target_pairs={{0,1},{1,0},{2,3},{3,2},{4,5},{5,4},{6,7},{7,6},{8,9},{9,8},{10,11... | collective-permute-start | bytes 3145736 | tf_op jit(solution)/shard_map/ppermute | solution.py:585
  1412.4 40.4 %collective-permute-start.38 = (bf16[512,1024]{1,0:T(8,128)(2,1)S(1)}, bf16[512,1024]{1,0:T(8,128)(2,1)}, u32[]{:S(2)}, u32[]{:S(2)}) collective-permute-start(bf16[512,1024]{1,0:T(8,128)(2,1)S(1)} %broadcast_select_fusion.16.refs_0_), channel_id=1, source_target_pairs={{0,1},{1,0},{2,3},{3,2},{4,5},{5,4},{6,7},{7,6},{8,9},{9,8},{10,11... | collective-permute-start | bytes 3145736 | tf_op jit(solution)/shard_map/ppermute | solution.py:585
  (80 other events, 1025.6 us)
Sparse Core Ops, SparseCore 0:
  15.8 90.1 all-gather.4
  107.9 79.5 all-gather.6
  189.4 133.0 all-gather.10
  370.7 87.3 all-gather.8
  550.2 86.3 reduce-scatter.5
  641.0 86.3 reduce-scatter.7
  878.6 53.0 reduce-scatter.13
  1197.3 51.5 reduce-scatter.11
  1252.5 52.5 reduce-scatter.9

commit v4 on v3

--- a/solution.py
+++ b/solution.py
@@ -500,7 +500,6 @@
 def join_blocks(mine, other, core, order):
     count, height, size = mine.shape
     source = pl.BlockSpec((1, height, size), lambda h, b, which, where: (where[b], 0, 0))
-    inverse = [order.index(b) for b in range(count)]
     return pl.pallas_call(
         lambda which_ref, where_ref, *refs: join_blocks_kernel(which_ref, *refs),
         grid_spec=pltpu.PrefetchScalarGridSpec(
@@ -511,7 +510,7 @@
         ),
         out_shape=jax.ShapeDtypeStruct((CORES * height, count * size), F32),
         name="join_blocks",
-    )(core[None], jnp.asarray(inverse, jnp.int32), mine, other)
+    )(core[None], jnp.stack(order).astype(jnp.int32), mine, other)
 
 
 class Line:
@@ -620,6 +619,14 @@
             axis=1,
         )
 
+    def trade_blocks(x):
+        mine = lax.axis_index("dp")
+        found = [(mine, lax.dynamic_index_in_dim(x, mine, 0, keepdims=False))]
+        for k in range(1, dp):
+            out = lax.dynamic_index_in_dim(x, mine ^ k, 0, keepdims=False)
+            found.append((mine ^ k, lax.ppermute(out, "dp", [(d, d ^ k) for d in range(dp)])))
+        return found
+
     half_dp = dp // 2
     me = lax.axis_index("dp")
     upper = me >= half_dp
@@ -631,7 +638,6 @@
     qkv_full = gather(qkv_half)
     out_full = gather(core_cols(w_out, GROUP * HEAD))
     ctg = cotangent.reshape(owned, width)
-    ctg_all = gather(ctg)
     gate_count = w_gate.shape[0]
     gate_full = lax.dynamic_update_slice_in_dim(jnp.zeros((QUERY_HEADS, width), BF), w_gate, me * gate_count, 0)
     gate_full = total_sum(gate_full, ("dp",))
@@ -648,7 +654,9 @@
     down_send = jnp.stack([down_core[:, b * units : (b + 1) * units] for b in unit_block])
     (qkv_full, gu_send, down_send) = lax.optimization_barrier((qkv_full, gu_send, down_send))
     gu_half = lax.ppermute(gu_send, "dp", trade)
-    down_half = lax.all_to_all(down_send, "dp", 0, 0, tiled=True)
+    down_half = jnp.zeros_like(down_send)
+    for other, moved in trade_blocks(down_send):
+        down_half = lax.dynamic_update_index_in_dim(down_half, moved, other, 0)
 
     start, position = doc_positions(doc_lengths, length)
     low = start.reshape(rows, chips, chip_tok)[:, :, 0] // chip_tok
@@ -670,8 +678,12 @@
 
     packed, results, logs, gated, mid = [], [], [], [], []
     for row in range(rows):
-        packed.append(exchange(pack_heads(proj, cos, sin, q_gain, k_gain, row, chips, chip_tok)))
-    packed[0], logits = tie(packed[0], logits)
+        cos_row = cos
+        if row:
+            cos_row, logits = tie(cos, logits)
+        packed.append(exchange(pack_heads(proj, cos_row, sin, q_gain, k_gain, row, chips, chip_tok)))
+    packed[-1], ctg_late = tie(packed[-1], ctg)
+    ctg_all = gather(ctg_late)
     for row in range(rows):
         head_out, log = attend(packed[row], start[row : row + 1], low[row])
         results.append(head_out)
@@ -713,14 +725,17 @@
     part_keep = dot_tn(d_keep, normed_all, BF)
     part_recv = dot_tn(d_recv, normed_all, BF)
     part_down = dot_tn(ctg_all, hidden, BF).reshape(dp, CORES, out_rows, units)
-    out_part = dot_nt(hidden, down_full, BF)
     keep_swap = swap(pick(part_keep[quarter:], part_keep[:quarter]))
     recv_swap = swap(pick(part_recv[quarter:], part_recv[:quarter]))
     down_swap = swap(pick(part_down[:, 1], part_down[:, 0]))
-    d_normed, (part_keep, part_recv, part_down, out_part) = tie(
-        d_normed, (part_keep, part_recv, part_down, out_part)
+    d_normed, (part_keep, part_recv, part_down, keep_swap, recv_swap) = tie(
+        d_normed, (part_keep, part_recv, part_down, keep_swap, recv_swap)
     )
-    output = (mid + scatter(out_part).astype(F32)).astype(BF).reshape(rows, tok, width)
+    keep_sum = pick(part_keep[:quarter], part_keep[quarter:]) + keep_swap
+    recv_sum = pick(part_recv[:quarter], part_recv[quarter:]) + recv_swap
+    line = Line(chips, chip)
+    keep_line = line.begin(keep_sum)
+    sent_sum = lax.ppermute(recv_sum, "dp", trade)
 
     d_normed = d_normed.astype(F32)
     part_ffn = jnp.sum(d_normed * mid * factor_f, axis=0)
@@ -729,63 +744,67 @@
     d_mid = ctg.astype(F32) + factor_f * weighted - mid * factor_f**3 * inner
     low_mine = d_mid.astype(BF).reshape(rows, tok, width)
     low_other = swap(low_mine)
-    low_other, (keep_swap, recv_swap, down_swap) = tie(low_other, (keep_swap, recv_swap, down_swap))
-    keep_sum = pick(part_keep[:quarter], part_keep[quarter:]) + keep_swap
-    recv_sum = pick(part_recv[:quarter], part_recv[quarter:]) + recv_swap
+    low_other, down_swap = tie(low_other, down_swap)
     down_sum = pick(part_down[:, 0], part_down[:, 1]) + down_swap
-    sent_sum = lax.ppermute(recv_sum, "dp", trade)
-    down_sum = lax.all_to_all(down_sum, "dp", 0, 0, tiled=True)
-    line = Line(chips, chip)
-    keep_line = line.begin(keep_sum)
+    down_sum = jnp.stack([moved for _, moved in trade_blocks(down_sum)])
 
     d_mid_low = jnp.concatenate([pick(low_mine, low_other), pick(low_other, low_mine)], axis=1).reshape(tokens, width)
     part_out = dot_tn(d_mid_low, gated, BF)
+    out_part = dot_nt(hidden, down_full, BF)
     d_proj, d_logit, d_heads = [], [], []
     q_sum = 0.0
     k_sum = 0.0
     for row in range(rows):
-        d_gated = dot_nn(d_mid_low[row * chip_tok : (row + 1) * chip_tok], out_full)
+        low_row = d_mid_low[row * chip_tok : (row + 1) * chip_tok]
+        if row == 1:
+            low_row, (part_out, out_part) = tie(low_row, (part_out, out_part))
+        d_gated = dot_nn(low_row, out_full)
         d_attn, dl = gate_back(d_gated, tok_results[row], logits, row)
         d_logit.append(dl)
         d_heads.append(exchange(d_attn))
-    d_heads[0], (keep_line, sent_sum, down_sum, part_out) = tie(d_heads[0], (keep_line, sent_sum, down_sum, part_out))
     shard_out = scatter(part_out)
+    out_sum = scatter(out_part)
+    d_heads[0], (keep_line, sent_sum) = tie(d_heads[0], (keep_line, sent_sum))
     keep_line = line.next(keep_line)
-    down_line = line.begin(down_sum)
+    sent_line = line.begin(sent_sum)
     back = []
     for row in range(rows):
-        grad = d_heads[row]
-        if row:
-            grad, (keep_line, down_line) = tie(grad, (keep_line, down_line))
-            keep_line = line.next(keep_line)
-            down_line = line.next(down_line)
-            sent_line = line.begin(sent_sum)
-        back.append(exchange(attend_back(packed[row], grad, results[row], logs[row], start[row : row + 1], low[row])))
-    back[0], (keep_line, down_line, sent_line) = tie(back[0], (keep_line, down_line, sent_line))
-    keep_done = line.end(keep_line)
-    down_line = line.next(down_line)
+        back.append(
+            exchange(attend_back(packed[row], d_heads[row], results[row], logs[row], start[row : row + 1], low[row]))
+        )
+    back[0], (keep_line, sent_line, down_sum) = tie(back[0], (keep_line, sent_line, down_sum))
+    keep_line = line.next(keep_line)
     sent_line = line.next(sent_line)
-    keep_other = swap(keep_done)
+    down_line = line.begin(down_sum)
+    back[1], (out_sum, shard_out) = tie(back[1], (out_sum, shard_out))
+    output = (mid + out_sum.astype(F32)).astype(BF).reshape(rows, tok, width)
+    out_line = line.begin(shard_out)
     for row in range(rows):
-        grads = back[row]
-        if row:
-            grads, (down_line, sent_line) = tie(grads, (down_line, sent_line))
-            down_done = line.end(down_line)
-            sent_line = line.next(sent_line)
-            down_other = swap(down_done)
-        dpr, qs, ks = unpack_heads(grads, proj, cos, sin, q_gain, k_gain, row, chips, chip_tok)
+        dpr, qs, ks = unpack_heads(back[row], proj, cos, sin, q_gain, k_gain, row, chips, chip_tok)
         d_proj.append(dpr)
         q_sum = q_sum + qs
         k_sum = k_sum + ks
     d_proj = jnp.concatenate(d_proj, axis=0)
     d_logit = jnp.concatenate(d_logit, axis=0)
     half = width // 2
-    shard_qkv = [scatter(dot_tn(d_proj, normed_a[:, a : a + half], BF)) for a in (0, half)]
+    part_qkv = [dot_tn(d_proj, normed_a[:, a : a + half], BF) for a in (0, half)]
+    part_qkv[1], (keep_line, sent_line, down_line, out_line) = tie(
+        part_qkv[1], (keep_line, sent_line, down_line, out_line)
+    )
+    shard_qkv = [scatter(p) for p in part_qkv]
+    keep_done = line.end(keep_line)
+    keep_other = swap(keep_done)
+    sent_line = line.next(sent_line)
+    down_line = line.next(down_line)
+    out_line = line.next(out_line)
     d_norm_part = (dot_nn(d_proj, qkv_full) + dot_nn(d_logit, gate_core)).astype(BF)
     d_norm_part = d_norm_part.reshape(rows, CORES, tok, width)
     d_norm_other = swap(pick(d_norm_part[:, 1], d_norm_part[:, 0]))
+    d_norm_other, (sent_line, down_line, out_line) = tie(d_norm_other, (sent_line, down_line, out_line))
     sent_done = line.end(sent_line)
     sent_other = swap(sent_done)
+    down_line = line.next(down_line)
+    out_line = line.next(out_line)
     d_normed_a = pick(d_norm_part[:, 0], d_norm_part[:, 1]).astype(F32) + d_norm_other.astype(F32)
     own_in = layer_input.astype(F32)
     own_factor = lax.rsqrt(jnp.mean(own_in * own_in, axis=-1, keepdims=True) + epsilon)
@@ -808,14 +827,16 @@
     late = total_sum(jnp.stack([part_attn, heads]))
     grad_w_gate = lax.dynamic_slice_in_dim(early, me * gate_count, gate_count, 0)
 
+    shard_qkv[0], down_line, out_line = lax.optimization_barrier((shard_qkv[0], down_line[1:], out_line[1:]))
+    qkv_line = line.begin(shard_qkv[0])
+    down_done = line.end((2, *down_line))
+    out_done = line.end((2, *out_line))
     grad_gu = join_units([keep_done, sent_done], [keep_other, sent_other], core, upper.astype(jnp.int32))
-    grad_down = join_blocks(down_done, down_other, core, unit_block)
-    out_sum = line.run(shard_out)
-    grad_out = join_cols([out_sum], [swap(out_sum)], core, GROUP * HEAD)
-    qkv_sum = [line.run(p) for p in shard_qkv]
-    grad_qkv = join_rows(
-        qkv_sum, [swap(p) for p in qkv_sum], core, jnp.where(q_shard, GROUP * HEAD // HEAD, 1), HEAD
-    )
+    grad_down = join_blocks(down_done, swap(down_done), core, [unit_block.index(b) ^ me for b in range(dp)])
+    grad_out = join_cols([out_done], [swap(out_done)], core, GROUP * HEAD)
+    shard_qkv[1], (grad_gu, grad_down, grad_out) = tie(shard_qkv[1], (grad_gu, grad_down, grad_out))
+    qkv_sum = [line.end(line.next(line.next(qkv_line))), line.run(shard_qkv[1])]
+    grad_qkv = join_rows(qkv_sum, [swap(p) for p in qkv_sum], core, jnp.where(q_shard, GROUP, 1), HEAD)
     return (
         output,
         grad_input,

time: 1470 us -> 1590 us (1.082)
  waiting for transfers between devices: 725 us -> 779 us
  blocking collectives: 0 us -> 53 us
  starting transfers between devices: 115 us -> 135 us
    ppermute x0 -> x6, waiting for transfers between devices: none -> 166 us  [trade_blocks(): lax.ppermute(out, 'dp', [(d, d ^ k) for d in range(dp)])]
    ppermute x18, waiting for transfers between devices: 124 us -> 247 us  [send(): return (x, lax.ppermute(x, 'seq', self.stages[stage]))]
    all_to_all x2 -> x0, waiting for transfers between devices: 74.3 us -> none  [the longest x1 50.5 us: shards(): down_sum = lax.all_to_all(down_sum, 'dp', 0, 0, tiled=True)]
    reduce_scatter x5, waiting for transfers between devices: 84.8 us -> 23.2 us  [scatter(): return lax.psum_scatter(x, 'dp', scatter_dimension=0, tiled=True)]
    all_to_all x0 -> x1, blocking collectives: none -> 53 us  [exchange(): return lax.all_to_all(x, 'seq', 0, 0, axis_index_groups=groups, tiled=True)]
    all_to_all x8 -> x7, waiting for transfers between devices: 219 us -> 167 us  [exchange(): return lax.all_to_all(x, 'seq', 0, 0, axis_index_groups=groups, tiled=True)]
    ppermute x1, waiting for transfers between devices: 48.7 us -> 0.01 us  [shards(): gu_half = lax.ppermute(gu_send, 'dp', trade)]
    ppermute x12, starting transfers between devices: 16.7 us -> 43.1 us  [total_sum(): x = x + lax.ppermute(x, name, [(s, s ^ step) for s in range(size)])]
  transfers between devices with their start and end apart: 67 -> 70, of which waited for: 32 -> 29; matrix products, arithmetic and copies ran while one was open for 23% -> 20% of each run, Pallas kernels for 9% -> 8%
where the time goes in v4:
time: 1590 us; the launch traced here: 1580 us
  waiting for transfers between devices  779 us (49%)
  matrix products  260 us (16%)
  other arithmetic  159 us (10%)
  Pallas kernels  140 us (9%)
  starting transfers between devices  135 us (8%)
  blocking collectives  53 us (3%)
  local copies, waits for them, and re-layouts  38.9 us (2%)
    ppermute x18, waiting for transfers between devices, send(): return (x, lax.ppermute(x, 'seq', self.stages[stage]))  247 us
    all_to_all x7, waiting for transfers between devices, exchange(): return lax.all_to_all(x, 'seq', 0, 0, axis_index_groups=groups, tiled=True)  167 us
    ppermute x6, waiting for transfers between devices, trade_blocks(): lax.ppermute(out, 'dp', [(d, d ^ k) for d in range(dp)])  166 us
    all_gather x4, waiting for transfers between devices, gather(): return lax.all_gather(x, 'dp', axis=0, tiled=True)  107 us
    dot_general x7, matrix products, dot_nt(): lax.dot_general(left, right, (((1,), (1,)), ((), ())), preferred_element_...  99.8 us
    dot_general x7, matrix products, dot_nn(): lax.dot_general(left, right, (((1,), (0,)), ((), ())), preferred_element_...  83.9 us
    dot_general x7, matrix products, dot_tn(): lax.dot_general(left, right, (((0,), (0,)), ((), ())), preferred_element_...  76.3 us
    all_to_all x1, blocking collectives, exchange(): return lax.all_to_all(x, 'seq', 0, 0, axis_index_groups=groups, tiled=True)  53 us
  transfers between devices with their start and end apart: 70, of which 29 were waited for; matrix products, arithmetic and copies ran while one was open for 20% of the time, Pallas kernels for 8%

profile of v4, /device:TPU:0, one launch (start us, length us, event | category | flops | bytes accessed | tf_op | source)
XLA Modules:
  0.0 1580.5 jit_solution(7051828671906846960)
XLA Ops:
  30.3 6.6 select_select_fusion
  52.1 55.4 %all-gather.5.cloned.1.call-done = bf16[2048,2048]{1,0:T(8,128)(2,1)} async-done(((bf16[512,2048]{1,0:T(8,128)(2,1)}), bf16[2048,2048]{1,0:T(8,128)(2,1)}) %all-gather.5.cloned.1.call-update) | async-done | bytes 8388624 | tf_op jit(solution)/shard_map/all_gather | solution.py:609
  107.5 14.5 fusion.67.proj_ref
  122.0 6.2 pack_heads.3
  128.2 53.0 %all_to_all.40.q_ref.k_ref.v_ref = bf16[4,512,512]{2,1,0:T(8,128)(2,1)} all-to-all(bf16[4,512,512]{2,1,0:T(8,128)(2,1)} %pack_heads.3), channel_id=1, replica_groups={{0,2,4,6},{1,3,5,7},{8,10,12,14},{9,11,13,15},{16,18,20,22},{17,19,21,2..., dimensions={0} | all-to-all | bytes 4194304 | tf_op jit(solution)/shard_map/all_to_all | solution.py:594
  181.2 6.2 pack_heads.2
  198.3 10.8 attend.3
  209.1 29.3 %all-to-all-done.q_ref.k_ref.v_ref = bf16[4,512,512]{2,1,0:T(8,128)(2,1)S(1)} async-done(((bf16[4,512,512]{2,1,0:T(8,128)(2,1)}), bf16[4,512,512]{2,1,0:T(8,128)(2,1)S(1)}, u32[]{:S(2)}, u32[]{:S(2)}) %all-to-all-start) | async-done | bytes 2097184 | tf_op jit(solution)/shard_map/all_to_all | solution.py:594
  247.5 134.7 %collective-permute-done.3 = bf16[256,1536]{1,0:T(8,128)(2,1)S(1)} collective-permute-done((bf16[256,1536]{1,0:T(8,128)(2,1)}, bf16[256,1536]{1,0:T(8,128)(2,1)S(1)}, u32[]{:S(2)}, u32[]{:S(2)}) %collective-permute-start.3) | collective-permute-done | bytes 786464 | tf_op jit(solution)/shard_map/ppermute | solution.py:627
  383.1 8.8 attend.2
  401.2 4.9 convolution_convert_fusion.10
  407.2 14.7 all-to-all-done.1.res_ref
  425.4 4.9 convolution_convert_fusion.11
  441.2 5.1 collective-permute-done.9
  457.2 18.9 %convolution_convert_fusion.3 = bf16[2048,1536]{1,0:T(8,128)(2,1)} fusion(bf16[2048,2048]{1,0:T(8,128)(2,1)} %all-gather.11.cloned.1.call-done, bf16[2048,1536]{1,0:T(8,128)(2,1)} %bitcast.170), kind=kOutput, calls=%fused_computation.24 | convolution fusion | flops 12888047616 | bytes 20971520 | tf_op jit(solution)/shard_map/dot_general | solution.py:33
  476.2 51.4 %all-gather.9.cloned.1.call-done = bf16[2048,2048]{1,0:T(8,128)(2,1)} async-done(((bf16[512,2048]{1,0:T(8,128)(2,1)}), bf16[2048,2048]{1,0:T(8,128)(2,1)}) %all-gather.9.cloned.1.call-update) | async-done | bytes 8388624 | tf_op jit(solution)/shard_map/all_gather | solution.py:609
  527.6 19.8 %convolution_convert_fusion.1 = bf16[2048,1536]{1,0:T(8,128)(2,1)} fusion(bf16[2048,2048]{1,0:T(8,128)(2,1)} %all-gather.9.cloned.1.call-done, bf16[3072,2048]{1,0:T(8,128)(2,1)} %param.21, pred[]{:T(512)S(6)} %ge.19), kind=kOutput, calls=%fused_computation.22 | convolution fusion | flops 12891193344 | bytes 27262976 | tf_op jit(solution)/shard_map/dot_general | solution.py:29
  547.4 31.7 %select_convert_fusion = (bf16[2048,1536]{1,0:T(8,128)(2,1)}, bf16[2048,1536]{1,0:T(8,128)(2,1)}, bf16[2048,1536]{1,0:T(8,128)(2,1)}) fusion(bf16[2048,1536]{1,0:T(8,128)(2,1)} %convolution_convert_fusion.3, pred[]{:T(512)S(6)} %ge.19, bf16[2048,1536]{1,0:T(8,128)(2,1)} %convolution_convert_fusion.1, bf16[2048,2048]{1,0:T(8,128)(2,1)} %all-gather.9.cloned.1.call-done, ...), kind=kOutput, calls=%fused_computation.14 | convolution fusion | flops 12950962176 | bytes 46137344 | tf_op jit(solution)/shard_map/dot_general | solution.py:29
  579.1 21.8 %fusion.45 = f32[2048,2048]{1,0:T(8,128)} fusion(bf16[2048,1536]{1,0:T(8,128)(2,1)} %get-tuple-element.171, bf16[3072,2048]{1,0:T(8,128)(2,1)} %param.21, pred[]{:T(512)S(6)} %ge.19), kind=kOutput, calls=%fused_computation.128 | convolution fusion | flops 12888047616 | bytes 35651584 | tf_op jit(solution)/shard_map/dot_general | solution.py:33
  600.9 19.1 %add_convert_fusion = bf16[2048,2048]{1,0:T(8,128)(2,1)} fusion(f32[2048,2048]{1,0:T(8,128)} %fusion.45, bf16[2048,1536]{1,0:T(8,128)(2,1)S(1)} %copy-done.85, bf16[1536,2048]{1,0:T(8,128)(2,1)} %pad_maximum_fusion.1), kind=kOutput, calls=%fused_computation.3 | convolution fusion | flops 12893290496 | bytes 37748736 | tf_op jit(solution)/shard_map/dot_general | solution.py:33
  620.1 17.8 %convolution_convert_fusion.5 = bf16[1536,2048]{1,0:T(8,128)(2,1)S(1)} fusion(bf16[2048,1536]{1,0:T(8,128)(2,1)} %get-tuple-element.170, bf16[2048,2048]{1,0:T(8,128)(2,1)} %all-gather.9.cloned.1.call-done), kind=kOutput, calls=%fused_computation.26 | convolution fusion | flops 12888047616 | bytes 20971520 | tf_op jit(solution)/shard_map/dot_general | solution.py:37
  641.2 18.7 %convolution_convert_fusion.6 = bf16[1536,2048]{1,0:T(8,128)(2,1)S(1)} fusion(bf16[2048,1536]{1,0:T(8,128)(2,1)} %get-tuple-element.171, bf16[2048,2048]{1,0:T(8,128)(2,1)} %all-gather.9.cloned.1.call-done), kind=kOutput, calls=%fused_computation.27 | convolution fusion | flops 12888047616 | bytes 20971520 | tf_op jit(solution)/shard_map/dot_general | solution.py:37
  662.9 16.2 %convolution_convert_fusion.4 = bf16[2048,1536]{1,0:T(8,128)(2,1)S(1)} fusion(bf16[2048,2048]{1,0:T(8,128)(2,1)S(1)} %bitcast.198, bf16[2048,1536]{1,0:T(8,128)(2,1)S(1)} %bitcast.200, bf16[2048,1536]{1,0:T(8,128)(2,1)} %get-tuple-element.223, pred[]{:T(512)S(6)} %ge.19), kind=kOutput, calls=%fused_computation.25 | convolution fusion | flops 12919504896 | bytes 27262976 | tf_op jit(solution)/shard_map/dot_general | solution.py:37
  683.3 23.2 %reduce-scatter.6.cloned.1.call-done = bf16[512,2048]{1,0:T(8,128)(2,1)} async-done(((bf16[2048,2048]{1,0:T(8,128)(2,1)}), bf16[512,2048]{1,0:T(8,128)(2,1)}) %reduce-scatter.6.cloned.1.call-update) | async-done | bytes 2097168 | tf_op jit(solution)/shard_map/reduce_scatter | solution.py:606
  714.7 21.9 %convolution_convert_fusion = bf16[2048,2048]{1,0:T(8,128)(2,1)} fusion(bf16[2048,1536]{1,0:T(8,128)(2,1)} %bitcast.171, bf16[2048,1536]{1,0:T(8,128)(2,1)} %convolution_convert_fusion.1, bf16[2048,1536]{1,0:T(8,128)(2,1)} %get-tuple-element.223, pred[]{:T(512)S(6)} %ge.19), kind=kOutput, calls=%fused_computation.21 | convolution fusion | flops 12920553472 | bytes 27262976 | tf_op jit(solution)/shard_map/dot_general | solution.py:29
  742.0 6.2 convolution_convert_fusion.9
  748.9 6.0 select_add_fusion
  761.2 5.0 collective-permute-start.15
  777.7 5.8 fusion.68.grad_ref
  787.5 61.9 %all-to-all-done.6.grad_ref = bf16[4,512,256]{2,1,0:T(8,128)(2,1)S(1)} async-done(((bf16[4,512,256]{2,1,0:T(8,128)(2,1)}), bf16[4,512,256]{2,1,0:T(8,128)(2,1)S(1)}, u32[]{:S(2)}, u32[]{:S(2)}) %all-to-all-start.6) | async-done | bytes 1048608 | tf_op jit(solution)/shard_map/all_to_all | solution.py:594
  854.0 16.5 %collective-permute-done.16 = bf16[768,2048]{1,0:T(8,128)(2,1)} collective-permute-done((bf16[768,2048]{1,0:T(8,128)(2,1)}, bf16[768,2048]{1,0:T(8,128)(2,1)}, u32[]{:S(2)}, u32[]{:S(2)}) %collective-permute-start.16) | collective-permute-done | bytes 3145760 | tf_op jit(solution)/shard_map/ppermute | solution.py:738
  870.5 16.3 %attend_back.3 = bf16[4,512,512]{2,1,0:T(8,128)(2,1)} custom-call(s32[4]{0:T(128)} %get-tuple-element.221.low_ref, bf16[4,512,512]{2,1,0:T(8,128)(2,1)} %copy-done, bf16[4,512,512]{2,1,0:T(8,128)(2,1)} %copy-done, bf16[4,512,512]{2,1,0:T(8,128)(2,1)} %copy-done, bf16[4,512,256]{2,1,0:T(8,128)(2,1)} %copy-done.43, ...), custom_call_target="tpu_custom_call" | custom-call | tf_op jit(solution)/shard_map/attend_back/pallas_call | solution.py:281
  891.4 6.3 add.241
  900.1 7.0 collective-permute-start.18
  907.1 19.8 %attend_back.2 = bf16[4,512,512]{2,1,0:T(8,128)(2,1)} custom-call(s32[4]{0:T(128)} %get-tuple-element.222.low_ref, bf16[4,512,512]{2,1,0:T(8,128)(2,1)} %all_to_all.40.q_ref.k_ref.v_ref, bf16[4,512,512]{2,1,0:T(8,128)(2,1)} %all_to_all.40.q_ref.k_ref.v_ref, bf16[4,512,512]{2,1,0:T(8,128)(2,1)} %all_to_all.40.q_ref.k_ref.v_ref, ...), custom_call_target="tpu_custom_call" | custom-call | tf_op jit(solution)/shard_map/attend_back/pallas_call | solution.py:281
  926.9 13.5 all-to-all-done.7.grad_ref
  951.1 4.9 collective-permute-start.20
  956.0 15.0 collective-permute-done.21
  971.0 15.6 collective-permute-done.20
  988.1 5.9 collective-permute-done.18
  994.0 7.5 unpack_heads.2
  1004.6 47.3 %all-to-all-done.5.grad_ref = bf16[4,512,512]{2,1,0:T(8,128)(2,1)} async-done(((bf16[4,512,512]{2,1,0:T(8,128)(2,1)}), bf16[4,512,512]{2,1,0:T(8,128)(2,1)}, u32[]{:S(2)}, u32[]{:S(2)}) %all-to-all-start.5) | async-done | bytes 2097184 | tf_op jit(solution)/shard_map/all_to_all | solution.py:594
  1051.9 7.5 unpack_heads.3
  1062.7 8.3 convolution_convert_fusion.7
  1071.2 6.0 add.245
  1079.7 6.2 add.244
  1087.2 7.9 collective-permute-start.25
  1097.8 13.3 fusion.69
  1111.1 6.4 convolution_convert_fusion.8
  1117.5 40.3 %collective-permute-done.23 = bf16[768,2048]{1,0:T(8,128)(2,1)} collective-permute-done((bf16[768,2048]{1,0:T(8,128)(2,1)}, bf16[768,2048]{1,0:T(8,128)(2,1)}, u32[]{:S(2)}, u32[]{:S(2)}) %collective-permute-start.23) | collective-permute-done | bytes 3145760 | tf_op jit(solution)/shard_map/ppermute | solution.py:527
  1162.0 21.0 %collective-permute-done.26 = bf16[512,1024]{1,0:T(8,128)(2,1)} collective-permute-done((bf16[512,1024]{1,0:T(8,128)(2,1)}, bf16[512,1024]{1,0:T(8,128)(2,1)}, u32[]{:S(2)}, u32[]{:S(2)}) %collective-permute-start.26) | collective-permute-done | bytes 1048608 | tf_op jit(solution)/shard_map/ppermute | solution.py:527
  1206.2 58.7 %collective-permute-done.27 = bf16[768,2048]{1,0:T(8,128)(2,1)} collective-permute-done((bf16[768,2048]{1,0:T(8,128)(2,1)S(1)}, bf16[768,2048]{1,0:T(8,128)(2,1)}, u32[]{:S(2)}, u32[]{:S(2)}) %collective-permute-start.27) | collective-permute-done | bytes 3145760 | tf_op jit(solution)/shard_map/ppermute | solution.py:527
  1264.8 5.5 add.263
  1276.0 5.0 broadcast_select_fusion.3.sent_ref
  1281.0 98.9 %collective-permute-done.41 = bf16[512,1024]{1,0:T(8,128)(2,1)S(1)} collective-permute-done((bf16[512,1024]{1,0:T(8,128)(2,1)S(1)}, bf16[512,1024]{1,0:T(8,128)(2,1)S(1)}, u32[]{:S(2)}, u32[]{:S(2)}) %collective-permute-start.41) | collective-permute-done | bytes 1048608 | tf_op jit(solution)/shard_map/ppermute | solution.py:527
  1392.2 16.6 %join_units.1 = f32[3072,2048]{1,0:T(8,128)} custom-call(s32[2]{0:T(128)} %pad_add_fusion.1.which_ref, bf16[768,2048]{1,0:T(8,128)(2,1)} %copy-done.26, bf16[768,2048]{1,0:T(8,128)(2,1)} %collective-permute-done.45.keep_other_ref, bf16[768,2048]{1,0:T(8,128)(2,1)} %broadcast_select_fusion.3.sent_ref, bf16[768,2048]{1,0:T(8,128)(2,1)} %collective-permute-done.46.sent_other_ref), custom_call_target="tpu_custom_call" | custom-call | tf_op jit(solution)/shard_map/join_units/pallas_call | solution.py:478
  1411.2 6.4 join_cols.1
  1417.7 12.1 join_blocks.1
  1433.2 26.9 %collective-permute-done.36 = f32[24,2048]{1,0:T(8,128)} collective-permute-done((f32[24,2048]{1,0:T(8,128)S(1)}, f32[24,2048]{1,0:T(8,128)}, u32[]{:S(2)}, u32[]{:S(2)}) %collective-permute-start.36) | collective-permute-done | bytes 196640 | tf_op jit(solution)/shard_map/ppermute | solution.py:601
  1464.2 8.6 collective-permute-done.37
  1491.1 5.9 fusion.22
  1511.1 26.2 %collective-permute-start.32 = (f32[2,2048]{1,0:T(2,128)S(1)}, f32[2,2048]{1,0:T(2,128)S(1)}, u32[]{:S(2)}, u32[]{:S(2)}) collective-permute-start(f32[2,2048]{1,0:T(2,128)S(1)} %fusion.101), channel_id=1, source_target_pairs={{0,4},{1,5},{2,6},{3,7},{4,0},{5,1},{6,2},{7,3},{8,12},{9,13},{10,... | collective-permute-start | bytes 49160 | tf_op jit(solution)/shard_map/ppermute | solution.py:601
  1540.2 17.8 %collective-permute-done.51 = bf16[512,1024]{1,0:T(8,128)(2,1)S(1)} collective-permute-done((bf16[512,1024]{1,0:T(8,128)(2,1)S(1)}, bf16[512,1024]{1,0:T(8,128)(2,1)S(1)}, u32[]{:S(2)}, u32[]{:S(2)}) %collective-permute-start.51) | collective-permute-done | bytes 1048608 | tf_op jit(solution)/shard_map/ppermute | solution.py:527
  1565.3 8.4 join_rows.1
  (437 shorter events, 275.3 us)
Async XLA Ops:
  7.2 100.3 %all-gather.5.cloned.1.call-start = ((), (), s32[]{:S(2)}) async-start(), calls=%async_computation.13 | async-start | bytes 10485760 | tf_op jit(solution)/shard_map/all_gather | solution.py:609
  15.7 385.5 %all-gather.7.cloned.1.call-start = ((), (), s32[]{:S(2)}) async-start(), calls=%async_computation.14 | async-start | bytes 5242880 | tf_op jit(solution)/shard_map/all_gather | solution.py:609
  15.8 23.0 %collective-permute-start.5 = (bf16[16,2048]{1,0:T(8,128)(2,1)S(1)}, bf16[16,2048]{1,0:T(8,128)(2,1)S(1)}, u32[]{:S(2)}, u32[]{:S(2)}) collective-permute-start(bf16[16,2048]{1,0:T(8,128)(2,1)S(1)} %constant_dynamic-update-slice_fusion.4), channel_id=1, source_target_pairs={{0,8},{8,0},{16,24},{24,16},{1,9},{9,1},{17,25},{25,17},{2,10},{10... | collective-permute-start | bytes 196616 | tf_op jit(solution)/shard_map/ppermute | solution.py:601
  18.9 26.5 %collective-permute-start = (bf16[2,256,2048]{2,1,0:T(8,128)(2,1)S(1)}, bf16[2,256,2048]{2,1,0:T(8,128)(2,1)}, u32[]{:S(2)}, u32[]{:S(2)}) collective-permute-start(bf16[2,256,2048]{2,1,0:T(8,128)(2,1)S(1)} %copy-done.7), channel_id=1, source_target_pairs={{0,1},{1,0},{2,3},{3,2},{4,5},{5,4},{6,7},{7,6},{8,9},{9,8},{10,11... | collective-permute-start | bytes 6291464 | tf_op jit(solution)/shard_map/ppermute | solution.py:584
  21.6 435.6 %all-gather.11.cloned.1.call-start = ((), (), s32[]{:S(2)}) async-start(), calls=%async_computation.16 | async-start | bytes 10485760 | tf_op jit(solution)/shard_map/all_gather | solution.py:609
  38.8 6.3 collective-permute-start.6
  187.4 50.9 %all-to-all-start = ((bf16[4,512,512]{2,1,0:T(8,128)(2,1)}), bf16[4,512,512]{2,1,0:T(8,128)(2,1)S(1)}, u32[]{:S(2)}, u32[]{:S(2)}) async-start(bf16[4,512,512]{2,1,0:T(8,128)(2,1)} %pack_heads.2), calls=%async_computation | async-start | bytes 4194304 | tf_op jit(solution)/shard_map/all_to_all | solution.py:594
  196.2 49.2 %collective-permute-start.2 = (bf16[256,1536]{1,0:T(8,128)(2,1)}, bf16[256,1536]{1,0:T(8,128)(2,1)}, u32[]{:S(2)}, u32[]{:S(2)}) collective-permute-start(bf16[256,1536]{1,0:T(8,128)(2,1)} %get-tuple-element.192), channel_id=1, source_target_pairs={{0,8},{8,0},{16,24},{24,16},{1,9},{9,1},{17,25},{25,17},{2,10},{10... | collective-permute-start | bytes 2359304 | tf_op jit(solution)/shard_map/ppermute | solution.py:627
  238.3 153.5 %all-to-all-start.3 = ((bf16[4,512,256]{2,1,0:T(8,128)(2,1)}), bf16[4,512,256]{2,1,0:T(8,128)(2,1)S(1)}, u32[]{:S(2)}, u32[]{:S(2)}) async-start(bf16[4,512,256]{2,1,0:T(8,128)(2,1)} %get-tuple-element.95.res_ref), calls=%async_computation.3 | async-start | bytes 2097152 | tf_op jit(solution)/shard_map/all_to_all | solution.py:594
  241.9 165.3 %collective-permute-start.1 = (bf16[768,2048]{1,0:T(8,128)(2,1)}, bf16[768,2048]{1,0:T(8,128)(2,1)}, u32[]{:S(2)}, u32[]{:S(2)}) collective-permute-start(bf16[768,2048]{1,0:T(8,128)(2,1)} %select_select_fusion), channel_id=1, source_target_pairs={{0,16},{8,24},{16,0},{24,8},{1,17},{9,25},{17,1},{25,9},{2,18},{10... | collective-permute-start | bytes 9437192 | tf_op jit(solution)/shard_map/ppermute | solution.py:656
  243.4 138.8 %collective-permute-start.3 = (bf16[256,1536]{1,0:T(8,128)(2,1)}, bf16[256,1536]{1,0:T(8,128)(2,1)S(1)}, u32[]{:S(2)}, u32[]{:S(2)}) collective-permute-start(bf16[256,1536]{1,0:T(8,128)(2,1)} %get-tuple-element.191), channel_id=1, source_target_pairs={{0,16},{8,24},{16,0},{24,8},{1,17},{9,25},{17,1},{25,9},{2,18},{10... | collective-permute-start | bytes 2359304 | tf_op jit(solution)/shard_map/ppermute | solution.py:627
  244.0 152.5 %collective-permute-start.4 = (bf16[256,1536]{1,0:T(8,128)(2,1)}, bf16[256,1536]{1,0:T(8,128)(2,1)}, u32[]{:S(2)}, u32[]{:S(2)}) collective-permute-start(bf16[256,1536]{1,0:T(8,128)(2,1)} %get-tuple-element.190), channel_id=1, source_target_pairs={{0,24},{8,16},{16,8},{24,0},{1,25},{9,17},{17,9},{25,1},{2,26},{10... | collective-permute-start | bytes 2359304 | tf_op jit(solution)/shard_map/ppermute | solution.py:627
  391.9 29.9 %all-to-all-start.1 = ((bf16[4,512,256]{2,1,0:T(8,128)(2,1)}), bf16[4,512,256]{2,1,0:T(8,128)(2,1)S(1)}, u32[]{:S(2)}, u32[]{:S(2)}) async-start(bf16[4,512,256]{2,1,0:T(8,128)(2,1)} %get-tuple-element.88.res_ref), calls=%async_computation.1 | async-start | bytes 2097152 | tf_op jit(solution)/shard_map/all_to_all | solution.py:594
  396.5 131.1 %all-gather.9.cloned.1.call-start = ((), (), s32[]{:S(2)}) async-start(), calls=%async_computation.15 | async-start | bytes 10485760 | tf_op jit(solution)/shard_map/all_gather | solution.py:609
  407.2 23.3 %collective-permute-start.8 = (bf16[256,2048]{1,0:T(8,128)(2,1)}, bf16[256,2048]{1,0:T(8,128)(2,1)}, u32[]{:S(2)}, u32[]{:S(2)}) collective-permute-start(bf16[256,2048]{1,0:T(8,128)(2,1)} %broadcast_select_fusion.17), channel_id=1, source_target_pairs={{0,1},{1,0},{2,3},{3,2},{4,5},{5,4},{6,7},{7,6},{8,9},{9,8},{10,11... | collective-permute-start | bytes 3145736 | tf_op jit(solution)/shard_map/ppermute | solution.py:584
  439.8 266.7 %reduce-scatter.6.cloned.1.call-start = ((), (), s32[]{:S(2)}) async-start(), calls=%async_computation.17 | async-start | bytes 10485760 | tf_op jit(solution)/shard_map/reduce_scatter | solution.py:606
  440.8 10.0 collective-permute-start.10
  620.0 431.8 %reduce-scatter.10.cloned.1.call-start = ((), (), s32[]{:S(2)}) async-start(), calls=%async_computation.19 | async-start | bytes 5242880 | tf_op jit(solution)/shard_map/reduce_scatter | solution.py:606
  641.2 42.1 %collective-permute-start.12 = (bf16[768,2048]{1,0:T(8,128)(2,1)S(1)}, bf16[768,2048]{1,0:T(8,128)(2,1)}, u32[]{:S(2)}, u32[]{:S(2)}) collective-permute-start(bf16[768,2048]{1,0:T(8,128)(2,1)S(1)} %slice_select_fusion.2), channel_id=1, source_target_pairs={{0,1},{1,0},{2,3},{3,2},{4,5},{5,4},{6,7},{7,6},{8,9},{9,8},{10,11... | collective-permute-start | bytes 9437192 | tf_op jit(solution)/shard_map/ppermute | solution.py:584
  662.6 20.8 %collective-permute-start.11 = (bf16[768,2048]{1,0:T(8,128)(2,1)S(1)}, bf16[768,2048]{1,0:T(8,128)(2,1)}, u32[]{:S(2)}, u32[]{:S(2)}) collective-permute-start(bf16[768,2048]{1,0:T(8,128)(2,1)S(1)} %slice_select_fusion.3), channel_id=1, source_target_pairs={{0,1},{1,0},{2,3},{3,2},{4,5},{5,4},{6,7},{7,6},{8,9},{9,8},{10,11... | collective-permute-start | bytes 9437192 | tf_op jit(solution)/shard_map/ppermute | solution.py:584
  683.0 53.6 %collective-permute-start.14 = (bf16[4,256,1536]{2,1,0:T(8,128)(2,1)}, bf16[4,256,1536]{2,1,0:T(8,128)(2,1)}, u32[]{:S(2)}, u32[]{:S(2)}) collective-permute-start(bf16[4,256,1536]{2,1,0:T(8,128)(2,1)} %fusion.27), channel_id=1, source_target_pairs={{0,1},{1,0},{2,3},{3,2},{4,5},{5,4},{6,7},{7,6},{8,9},{9,8},{10,11... | collective-permute-start | bytes 9437192 | tf_op jit(solution)/shard_map/ppermute | solution.py:584
  714.7 21.9 %collective-permute-start.13 = (bf16[2,256,2048]{2,1,0:T(8,128)(2,1)}, bf16[2,256,2048]{2,1,0:T(8,128)(2,1)S(1)}, u32[]{:S(2)}, u32[]{:S(2)}) collective-permute-start(bf16[2,256,2048]{2,1,0:T(8,128)(2,1)} %bitcast.21), channel_id=1, source_target_pairs={{0,1},{1,0},{2,3},{3,2},{4,5},{5,4},{6,7},{7,6},{8,9},{9,8},{10,11... | collective-permute-start | bytes 6291464 | tf_op jit(solution)/shard_map/ppermute | solution.py:584
  748.2 303.7 %reduce-scatter.8.cloned.1.call-start = ((), (), s32[]{:S(2)}) async-start(), calls=%async_computation.18 | async-start | bytes 10485760 | tf_op jit(solution)/shard_map/reduce_scatter | solution.py:606
  755.0 115.5 %collective-permute-start.16 = (bf16[768,2048]{1,0:T(8,128)(2,1)}, bf16[768,2048]{1,0:T(8,128)(2,1)}, u32[]{:S(2)}, u32[]{:S(2)}) collective-permute-start(bf16[768,2048]{1,0:T(8,128)(2,1)} %select_add_fusion), channel_id=1, source_target_pairs={{0,16},{8,24},{16,0},{24,8},{1,17},{9,25},{17,1},{25,9},{2,18},{10... | collective-permute-start | bytes 9437192 | tf_op jit(solution)/shard_map/ppermute | solution.py:738
  761.2 109.3 %collective-permute-start.15 = (bf16[768,2048]{1,0:T(8,128)(2,1)}, bf16[768,2048]{1,0:T(8,128)(2,1)}, u32[]{:S(2)}, u32[]{:S(2)}) collective-permute-start(bf16[768,2048]{1,0:T(8,128)(2,1)} %select_add_fusion.1), channel_id=1, source_target_pairs={{0,2},{1,3},{6,4},{7,5},{8,10},{9,11},{14,12},{15,13},{16,18},{17,... | collective-permute-start | bytes 9437192 | tf_op jit(solution)/shard_map/ppermute | solution.py:527
  774.0 75.4 %all-to-all-start.6 = ((bf16[4,512,256]{2,1,0:T(8,128)(2,1)}), bf16[4,512,256]{2,1,0:T(8,128)(2,1)S(1)}, u32[]{:S(2)}, u32[]{:S(2)}) async-start(bf16[4,512,256]{2,1,0:T(8,128)(2,1)} %get-tuple-element.110), calls=%async_computation.9 | async-start | bytes 2097152 | tf_op jit(solution)/shard_map/all_to_all | solution.py:594
  849.4 37.4 %all-to-all-start.4 = ((bf16[4,512,256]{2,1,0:T(8,128)(2,1)}), bf16[4,512,256]{2,1,0:T(8,128)(2,1)S(1)}, u32[]{:S(2)}, u32[]{:S(2)}) async-start(bf16[4,512,256]{2,1,0:T(8,128)(2,1)} %get-tuple-element.105), calls=%async_computation.5 | async-start | bytes 2097152 | tf_op jit(solution)/shard_map/all_to_all | solution.py:594
  886.8 53.6 %all-to-all-start.7 = ((bf16[4,512,512]{2,1,0:T(8,128)(2,1)}), bf16[4,512,512]{2,1,0:T(8,128)(2,1)S(1)}, u32[]{:S(2)}, u32[]{:S(2)}) async-start(bf16[4,512,512]{2,1,0:T(8,128)(2,1)} %attend_back.3), calls=%async_computation.10 | async-start | bytes 4194304 | tf_op jit(solution)/shard_map/all_to_all | solution.py:594
  897.8 90.3 %collective-permute-start.17 = (bf16[768,2048]{1,0:T(8,128)(2,1)}, bf16[768,2048]{1,0:T(8,128)(2,1)}, u32[]{:S(2)}, u32[]{:S(2)}) collective-permute-start(bf16[768,2048]{1,0:T(8,128)(2,1)} %add.241), channel_id=1, source_target_pairs={{2,4},{3,5},{4,2},{5,3},{10,12},{11,13},{12,10},{13,11},{18,20},{1... | collective-permute-start | bytes 9437192 | tf_op jit(solution)/shard_map/ppermute | solution.py:527
  900.1 93.9 %collective-permute-start.18 = (bf16[768,2048]{1,0:T(8,128)(2,1)}, bf16[768,2048]{1,0:T(8,128)(2,1)}, u32[]{:S(2)}, u32[]{:S(2)}) collective-permute-start(bf16[768,2048]{1,0:T(8,128)(2,1)} %collective-permute-done.16), channel_id=1, source_target_pairs={{0,2},{1,3},{6,4},{7,5},{8,10},{9,11},{14,12},{15,13},{16,18},{17,... | collective-permute-start | bytes 9437192 | tf_op jit(solution)/shard_map/ppermute | solution.py:527
  940.4 111.5 %all-to-all-start.5 = ((bf16[4,512,512]{2,1,0:T(8,128)(2,1)}), bf16[4,512,512]{2,1,0:T(8,128)(2,1)}, u32[]{:S(2)}, u32[]{:S(2)}) async-start(bf16[4,512,512]{2,1,0:T(8,128)(2,1)} %attend_back.2), calls=%async_computation.6 | async-start | bytes 4194304 | tf_op jit(solution)/shard_map/all_to_all | solution.py:594
  944.9 436.0 %reduce-scatter.12.cloned.1.call-start = ((), (), s32[]{:S(2)}) async-start(), calls=%async_computation.20 | async-start | bytes 5242880 | tf_op jit(solution)/shard_map/reduce_scatter | solution.py:606
  949.5 21.4 %collective-permute-start.21 = (bf16[256,1536]{1,0:T(8,128)(2,1)S(1)}, bf16[256,1536]{1,0:T(8,128)(2,1)S(1)}, u32[]{:S(2)}, u32[]{:S(2)}) collective-permute-start(bf16[256,1536]{1,0:T(8,128)(2,1)S(1)} %get-tuple-element.187), channel_id=1, source_target_pairs={{0,24},{8,16},{16,8},{24,0},{1,25},{9,17},{17,9},{25,1},{2,26},{10... | collective-permute-start | bytes 2359304 | tf_op jit(solution)/shard_map/ppermute | solution.py:627
  951.1 35.5 %collective-permute-start.20 = (bf16[256,1536]{1,0:T(8,128)(2,1)S(1)}, bf16[256,1536]{1,0:T(8,128)(2,1)S(1)}, u32[]{:S(2)}, u32[]{:S(2)}) collective-permute-start(bf16[256,1536]{1,0:T(8,128)(2,1)S(1)} %get-tuple-element.188), channel_id=1, source_target_pairs={{0,16},{8,24},{16,0},{24,8},{1,17},{9,25},{17,1},{25,9},{2,18},{10... | collective-permute-start | bytes 2359304 | tf_op jit(solution)/shard_map/ppermute | solution.py:627
  956.0 31.6 %collective-permute-start.19 = (bf16[256,1536]{1,0:T(8,128)(2,1)S(1)}, bf16[256,1536]{1,0:T(8,128)(2,1)S(1)}, u32[]{:S(2)}, u32[]{:S(2)}) collective-permute-start(bf16[256,1536]{1,0:T(8,128)(2,1)S(1)} %get-tuple-element.189), channel_id=1, source_target_pairs={{0,8},{8,0},{16,24},{24,16},{1,9},{9,1},{17,25},{25,17},{2,10},{10... | collective-permute-start | bytes 2359304 | tf_op jit(solution)/shard_map/ppermute | solution.py:627
  1071.0 358.8 %reduce-scatter.14.cloned.1.call-start = ((), (), s32[]{:S(2)}) async-start(), calls=%async_computation.21 | async-start | bytes 5242880 | tf_op jit(solution)/shard_map/reduce_scatter | solution.py:606
  1077.3 40.2 %collective-permute-start.24 = (bf16[768,2048]{1,0:T(8,128)(2,1)}, bf16[768,2048]{1,0:T(8,128)(2,1)}, u32[]{:S(2)}, u32[]{:S(2)}) collective-permute-start(bf16[768,2048]{1,0:T(8,128)(2,1)} %add.245), channel_id=1, source_target_pairs={{2,4},{3,5},{4,2},{5,3},{10,12},{11,13},{12,10},{13,11},{18,20},{1... | collective-permute-start | bytes 9437192 | tf_op jit(solution)/shard_map/ppermute | solution.py:527
  1085.9 71.9 %collective-permute-start.23 = (bf16[768,2048]{1,0:T(8,128)(2,1)}, bf16[768,2048]{1,0:T(8,128)(2,1)}, u32[]{:S(2)}, u32[]{:S(2)}) collective-permute-start(bf16[768,2048]{1,0:T(8,128)(2,1)} %add.244), channel_id=1, source_target_pairs={{2,0},{3,1},{4,6},{5,7},{10,8},{11,9},{12,14},{13,15},{18,16},{19,... | collective-permute-start | bytes 9437192 | tf_op jit(solution)/shard_map/ppermute | solution.py:527
  1087.2 74.8 %collective-permute-start.25 = (bf16[4,256,1536]{2,1,0:T(8,128)(2,1)S(1)}, bf16[4,256,1536]{2,1,0:T(8,128)(2,1)}, u32[]{:S(2)}, u32[]{:S(2)}) collective-permute-start(bf16[4,256,1536]{2,1,0:T(8,128)(2,1)S(1)} %pad_maximum_fusion.5), channel_id=1, source_target_pairs={{0,2},{1,3},{6,4},{7,5},{8,10},{9,11},{14,12},{15,13},{16,18},{17,... | collective-permute-start | bytes 9437192 | tf_op jit(solution)/shard_map/ppermute | solution.py:527
  1095.2 87.8 %collective-permute-start.26 = (bf16[512,1024]{1,0:T(8,128)(2,1)}, bf16[512,1024]{1,0:T(8,128)(2,1)}, u32[]{:S(2)}, u32[]{:S(2)}) collective-permute-start(bf16[512,1024]{1,0:T(8,128)(2,1)} %reduce-scatter.10.cloned.1.call-done), channel_id=1, source_target_pairs={{0,2},{1,3},{6,4},{7,5},{8,10},{9,11},{14,12},{15,13},{16,18},{17,... | collective-permute-start | bytes 3145736 | tf_op jit(solution)/shard_map/ppermute | solution.py:527
  1187.6 17.6 %collective-permute-start.28 = (bf16[4,256,1536]{2,1,0:T(8,128)(2,1)}, bf16[4,256,1536]{2,1,0:T(8,128)(2,1)}, u32[]{:S(2)}, u32[]{:S(2)}) collective-permute-start(bf16[4,256,1536]{2,1,0:T(8,128)(2,1)} %add.247), channel_id=1, source_target_pairs={{2,4},{3,5},{4,2},{5,3},{10,12},{11,13},{12,10},{13,11},{18,20},{1... | collective-permute-start | bytes 9437192 | tf_op jit(solution)/shard_map/ppermute | solution.py:527
  1194.3 70.5 %collective-permute-start.27 = (bf16[768,2048]{1,0:T(8,128)(2,1)S(1)}, bf16[768,2048]{1,0:T(8,128)(2,1)}, u32[]{:S(2)}, u32[]{:S(2)}) collective-permute-start(bf16[768,2048]{1,0:T(8,128)(2,1)S(1)} %add.246), channel_id=1, source_target_pairs={{2,0},{3,1},{4,6},{5,7},{10,8},{11,9},{12,14},{13,15},{18,16},{19,... | collective-permute-start | bytes 9437192 | tf_op jit(solution)/shard_map/ppermute | solution.py:527
  1270.4 110.4 %collective-permute-start.40 = (bf16[4,256,1536]{2,1,0:T(8,128)(2,1)}, bf16[4,256,1536]{2,1,0:T(8,128)(2,1)}, u32[]{:S(2)}, u32[]{:S(2)}) collective-permute-start(bf16[4,256,1536]{2,1,0:T(8,128)(2,1)} %add.263), channel_id=1, source_target_pairs={{2,0},{3,1},{4,6},{5,7},{10,8},{11,9},{12,14},{13,15},{18,16},{19,... | collective-permute-start | bytes 9437192 | tf_op jit(solution)/shard_map/ppermute | solution.py:527
  1272.1 107.7 %collective-permute-start.41 = (bf16[512,1024]{1,0:T(8,128)(2,1)S(1)}, bf16[512,1024]{1,0:T(8,128)(2,1)S(1)}, u32[]{:S(2)}, u32[]{:S(2)}) collective-permute-start(bf16[512,1024]{1,0:T(8,128)(2,1)S(1)} %add.264), channel_id=1, source_target_pairs={{2,0},{3,1},{4,6},{5,7},{10,8},{11,9},{12,14},{13,15},{18,16},{19,... | collective-permute-start | bytes 3145736 | tf_op jit(solution)/shard_map/ppermute | solution.py:527
  1275.9 116.3 %collective-permute-start.45 = (bf16[768,2048]{1,0:T(8,128)(2,1)S(1)}, bf16[768,2048]{1,0:T(8,128)(2,1)}, u32[]{:S(2)}, u32[]{:S(2)}) collective-permute-start(bf16[768,2048]{1,0:T(8,128)(2,1)S(1)} %broadcast_select_fusion.4.keep_ref), channel_id=1, source_target_pairs={{0,1},{1,0},{2,3},{3,2},{4,5},{5,4},{6,7},{7,6},{8,9},{9,8},{10,11... | collective-permute-start | bytes 9437192 | tf_op jit(solution)/shard_map/ppermute | solution.py:584
  1281.0 111.2 %collective-permute-start.46 = (bf16[768,2048]{1,0:T(8,128)(2,1)}, bf16[768,2048]{1,0:T(8,128)(2,1)}, u32[]{:S(2)}, u32[]{:S(2)}) collective-permute-start(bf16[768,2048]{1,0:T(8,128)(2,1)} %broadcast_select_fusion.3.sent_ref), channel_id=1, source_target_pairs={{0,1},{1,0},{2,3},{3,2},{4,5},{5,4},{6,7},{7,6},{8,9},{9,8},{10,11... | collective-permute-start | bytes 9437192 | tf_op jit(solution)/shard_map/ppermute | solution.py:584
  1384.7 33.0 %collective-permute-start.47 = (bf16[4,256,1536]{2,1,0:T(8,128)(2,1)}, bf16[4,256,1536]{2,1,0:T(8,128)(2,1)}, u32[]{:S(2)}, u32[]{:S(2)}) collective-permute-start(bf16[4,256,1536]{2,1,0:T(8,128)(2,1)} %broadcast_select_fusion.2.refs_0_), channel_id=1, source_target_pairs={{0,1},{1,0},{2,3},{3,2},{4,5},{5,4},{6,7},{7,6},{8,9},{9,8},{10,11... | collective-permute-start | bytes 9437192 | tf_op jit(solution)/shard_map/ppermute | solution.py:584
  1387.1 24.1 %collective-permute-start.48 = (bf16[512,1024]{1,0:T(8,128)(2,1)}, bf16[512,1024]{1,0:T(8,128)(2,1)}, u32[]{:S(2)}, u32[]{:S(2)}) collective-permute-start(bf16[512,1024]{1,0:T(8,128)(2,1)} %broadcast_select_fusion.15.refs_0_), channel_id=1, source_target_pairs={{0,1},{1,0},{2,3},{3,2},{4,5},{5,4},{6,7},{7,6},{8,9},{9,8},{10,11... | collective-permute-start | bytes 3145736 | tf_op jit(solution)/shard_map/ppermute | solution.py:584
  1390.9 41.2 %collective-permute-start.35 = (f32[24,2048]{1,0:T(8,128)S(1)}, f32[24,2048]{1,0:T(8,128)}, u32[]{:S(2)}, u32[]{:S(2)}) collective-permute-start(f32[24,2048]{1,0:T(8,128)S(1)} %maximum_maximum_fusion), channel_id=1, source_target_pairs={{0,1},{1,0},{2,3},{3,2},{4,5},{5,4},{6,7},{7,6},{8,9},{9,8},{10,11... | collective-permute-start | bytes 589832 | tf_op jit(solution)/shard_map/ppermute | solution.py:601
  1408.8 74.7 %collective-permute-start.42 = (bf16[512,1024]{1,0:T(8,128)(2,1)S(1)}, bf16[512,1024]{1,0:T(8,128)(2,1)}, u32[]{:S(2)}, u32[]{:S(2)}) collective-permute-start(bf16[512,1024]{1,0:T(8,128)(2,1)S(1)} %copy-done.46), channel_id=1, source_target_pairs={{0,2},{1,3},{6,4},{7,5},{8,10},{9,11},{14,12},{15,13},{16,18},{17,... | collective-permute-start | bytes 3145736 | tf_op jit(solution)/shard_map/ppermute | solution.py:527
  1429.8 58.0 %collective-permute-start.49 = (bf16[512,1024]{1,0:T(8,128)(2,1)}, bf16[512,1024]{1,0:T(8,128)(2,1)}, u32[]{:S(2)}, u32[]{:S(2)}) collective-permute-start(bf16[512,1024]{1,0:T(8,128)(2,1)} %reduce-scatter.14.cloned.1.call-done), channel_id=1, source_target_pairs={{0,2},{1,3},{6,4},{7,5},{8,10},{9,11},{14,12},{15,13},{16,18},{17,... | collective-permute-start | bytes 3145736 | tf_op jit(solution)/shard_map/ppermute | solution.py:527
  1433.1 27.0 %collective-permute-start.36 = (f32[24,2048]{1,0:T(8,128)S(1)}, f32[24,2048]{1,0:T(8,128)}, u32[]{:S(2)}, u32[]{:S(2)}) collective-permute-start(f32[24,2048]{1,0:T(8,128)S(1)} %fusion.58), channel_id=1, source_target_pairs={{0,2},{1,3},{2,0},{3,1},{4,6},{5,7},{6,4},{7,5},{8,10},{9,11},{10,... | collective-permute-start | bytes 589832 | tf_op jit(solution)/shard_map/ppermute | solution.py:601
  1461.1 11.7 collective-permute-start.37
  1472.8 7.6 collective-permute-start.38
  1480.5 17.8 %collective-permute-start.39 = (f32[24,2048]{1,0:T(8,128)S(1)}, f32[24,2048]{1,0:T(8,128)S(1)}, u32[]{:S(2)}, u32[]{:S(2)}) collective-permute-start(f32[24,2048]{1,0:T(8,128)S(1)} %add.261), channel_id=1, source_target_pairs={{0,16},{8,24},{16,0},{24,8},{1,17},{9,25},{17,1},{25,9},{2,18},{10... | collective-permute-start | bytes 589832 | tf_op jit(solution)/shard_map/ppermute | solution.py:601
  1486.1 16.5 %collective-permute-start.43 = (bf16[512,1024]{1,0:T(8,128)(2,1)}, bf16[512,1024]{1,0:T(8,128)(2,1)}, u32[]{:S(2)}, u32[]{:S(2)}) collective-permute-start(bf16[512,1024]{1,0:T(8,128)(2,1)} %add.265), channel_id=1, source_target_pairs={{2,4},{3,5},{4,2},{5,3},{10,12},{11,13},{12,10},{13,11},{18,20},{1... | collective-permute-start | bytes 3145736 | tf_op jit(solution)/shard_map/ppermute | solution.py:527
  1489.4 17.9 %collective-permute-start.50 = (bf16[512,1024]{1,0:T(8,128)(2,1)S(1)}, bf16[512,1024]{1,0:T(8,128)(2,1)}, u32[]{:S(2)}, u32[]{:S(2)}) collective-permute-start(bf16[512,1024]{1,0:T(8,128)(2,1)S(1)} %add.267), channel_id=1, source_target_pairs={{2,4},{3,5},{4,2},{5,3},{10,12},{11,13},{12,10},{13,11},{18,20},{1... | collective-permute-start | bytes 3145736 | tf_op jit(solution)/shard_map/ppermute | solution.py:527
  1500.2 10.1 collective-permute-start.31
  1504.6 35.4 %collective-permute-start.44 = (bf16[512,1024]{1,0:T(8,128)(2,1)S(1)}, bf16[512,1024]{1,0:T(8,128)(2,1)S(1)}, u32[]{:S(2)}, u32[]{:S(2)}) collective-permute-start(bf16[512,1024]{1,0:T(8,128)(2,1)S(1)} %add.266), channel_id=1, source_target_pairs={{2,0},{3,1},{4,6},{5,7},{10,8},{11,9},{12,14},{13,15},{18,16},{19,... | collective-permute-start | bytes 3145736 | tf_op jit(solution)/shard_map/ppermute | solution.py:527
  1509.0 49.0 %collective-permute-start.51 = (bf16[512,1024]{1,0:T(8,128)(2,1)S(1)}, bf16[512,1024]{1,0:T(8,128)(2,1)S(1)}, u32[]{:S(2)}, u32[]{:S(2)}) collective-permute-start(bf16[512,1024]{1,0:T(8,128)(2,1)S(1)} %add.268), channel_id=1, source_target_pairs={{2,0},{3,1},{4,6},{5,7},{10,8},{11,9},{12,14},{13,15},{18,16},{19,... | collective-permute-start | bytes 3145736 | tf_op jit(solution)/shard_map/ppermute | solution.py:527
  1511.1 28.3 %collective-permute-start.32 = (f32[2,2048]{1,0:T(2,128)S(1)}, f32[2,2048]{1,0:T(2,128)S(1)}, u32[]{:S(2)}, u32[]{:S(2)}) collective-permute-start(f32[2,2048]{1,0:T(2,128)S(1)} %fusion.101), channel_id=1, source_target_pairs={{0,4},{1,5},{2,6},{3,7},{4,0},{5,1},{6,2},{7,3},{8,12},{9,13},{10,... | collective-permute-start | bytes 49160 | tf_op jit(solution)/shard_map/ppermute | solution.py:601
  1539.3 18.9 %collective-permute-start.33 = (f32[2,2048]{1,0:T(2,128)S(1)}, f32[2,2048]{1,0:T(2,128)S(1)}, u32[]{:S(2)}, u32[]{:S(2)}) collective-permute-start(f32[2,2048]{1,0:T(2,128)S(1)} %add.255), channel_id=1, source_target_pairs={{0,8},{8,0},{16,24},{24,16},{1,9},{9,1},{17,25},{25,17},{2,10},{10... | collective-permute-start | bytes 49160 | tf_op jit(solution)/shard_map/ppermute | solution.py:601
  1540.1 24.3 %collective-permute-start.52 = (bf16[512,1024]{1,0:T(8,128)(2,1)S(1)}, bf16[512,1024]{1,0:T(8,128)(2,1)S(1)}, u32[]{:S(2)}, u32[]{:S(2)}) collective-permute-start(bf16[512,1024]{1,0:T(8,128)(2,1)S(1)} %broadcast_select_fusion.16.refs_0_), channel_id=1, source_target_pairs={{0,1},{1,0},{2,3},{3,2},{4,5},{5,4},{6,7},{7,6},{8,9},{9,8},{10,11... | collective-permute-start | bytes 3145736 | tf_op jit(solution)/shard_map/ppermute | solution.py:584
  1558.1 6.2 collective-permute-start.53
  (100 other events, 1360.0 us)
Sparse Core Ops, SparseCore 0:
  15.8 91.5 all-gather.4
  109.9 52.5 all-gather.6
  181.3 153.6 all-gather.10
  439.9 87.6 all-gather.8
  620.2 86.3 reduce-scatter.5
  748.3 85.4 reduce-scatter.9
  837.4 98.4 reduce-scatter.7
  1071.1 54.1 reduce-scatter.11
  1200.9 57.6 reduce-scatter.13

commit v5 on v4

--- a/solution.py
+++ b/solution.py
@@ -539,8 +539,31 @@
         stage, x, moved = state
         return moved if self.chips != 4 else jnp.where(self.inner, x, moved)
 
-    def run(self, x):
-        return self.end(self.next(self.next(self.begin(x))))
+    def pipeline(self, parts):
+        if self.chips != 4:
+            return lax.psum(parts, "seq", axis_index_groups=self.groups)
+        count = len(parts)
+        states = [None] * count
+        for step in range(count + 2):
+            for k in range(count):
+                if k == step:
+                    states[k] = self.begin(parts[k])
+                elif k < step <= k + 2:
+                    states[k] = self.next(states[k])
+            live = [k for k in range(count) if states[k] is not None]
+            later = [k for k in range(step + 1, min(step + 2, count))]
+            moved = lax.optimization_barrier([states[k][1:] for k in live] + [parts[k] for k in later])
+            for k, value in zip(live + later, moved):
+                if k in later:
+                    parts[k] = value
+                else:
+                    states[k] = (states[k][0], *value)
+        return [self.end(state) for state in states]
+
+
+def tie_all(values, work):
+    *values, work = lax.optimization_barrier((*values, work))
+    return values, work
 
 
 def tie(value, work):
@@ -627,6 +650,21 @@
             found.append((mine ^ k, lax.ppermute(out, "dp", [(d, d ^ k) for d in range(dp)])))
         return found
 
+    def halving(x, flip):
+        bits = dp.bit_length() - 1
+        mine = lax.axis_index("dp")
+        x = x.reshape((2,) * bits + (x.shape[0] // dp, x.shape[1]))
+        order = list(range(bits))
+        gone = []
+        for bit in reversed(order) if flip else order:
+            axis = sum(1 for b in order if b > bit and b not in gone)
+            low, high = lax.index_in_dim(x, 0, axis, False), lax.index_in_dim(x, 1, axis, False)
+            mark = (mine >> bit) % 2 == 1
+            sent = lax.ppermute(jnp.where(mark, low, high), "dp", [(d, d ^ (1 << bit)) for d in range(dp)])
+            x = jnp.where(mark, high, low) + sent
+            gone.append(bit)
+        return x
+
     half_dp = dp // 2
     me = lax.axis_index("dp")
     upper = me >= half_dp
@@ -653,7 +691,8 @@
     unit_block = [(d % half_dp) * 2 + d // half_dp for d in range(dp)]
     down_send = jnp.stack([down_core[:, b * units : (b + 1) * units] for b in unit_block])
     (qkv_full, gu_send, down_send) = lax.optimization_barrier((qkv_full, gu_send, down_send))
-    gu_half = lax.ppermute(gu_send, "dp", trade)
+    gu_pair = lax.all_gather(gu_send, "dp", axis_index_groups=[[d, d + half_dp] for d in range(half_dp)])
+    gu_half = jnp.where(upper, gu_pair[0], gu_pair[1])
     down_half = jnp.zeros_like(down_send)
     for other, moved in trade_blocks(down_send):
         down_half = lax.dynamic_update_index_in_dim(down_half, moved, other, 0)
@@ -682,6 +721,7 @@
         if row:
             cos_row, logits = tie(cos, logits)
         packed.append(exchange(pack_heads(proj, cos_row, sin, q_gain, k_gain, row, chips, chip_tok)))
+    packed[0], down_half = tie(packed[0], down_half)
     packed[-1], ctg_late = tie(packed[-1], ctg)
     ctg_all = gather(ctg_late)
     for row in range(rows):
@@ -689,7 +729,6 @@
         results.append(head_out)
         logs.append(log)
     tok_results = [exchange(r) for r in results]
-    tok_results[0], (gu_half, down_half) = tie(tok_results[0], (gu_half, down_half))
     gu_other = swap(gu_half)
     down_other = swap(down_half)
     for row in range(rows):
@@ -733,9 +772,8 @@
     )
     keep_sum = pick(part_keep[:quarter], part_keep[quarter:]) + keep_swap
     recv_sum = pick(part_recv[:quarter], part_recv[quarter:]) + recv_swap
-    line = Line(chips, chip)
-    keep_line = line.begin(keep_sum)
-    sent_sum = lax.ppermute(recv_sum, "dp", trade)
+    d_normed, gu_sum = tie(d_normed, jnp.concatenate([keep_sum, recv_sum], axis=0))
+    gu_sum = lax.psum(gu_sum, "seq", axis_index_groups=groups)
 
     d_normed = d_normed.astype(F32)
     part_ffn = jnp.sum(d_normed * mid * factor_f, axis=0)
@@ -763,22 +801,15 @@
         d_logit.append(dl)
         d_heads.append(exchange(d_attn))
     shard_out = scatter(part_out)
-    out_sum = scatter(out_part)
-    d_heads[0], (keep_line, sent_sum) = tie(d_heads[0], (keep_line, sent_sum))
-    keep_line = line.next(keep_line)
-    sent_line = line.begin(sent_sum)
     back = []
     for row in range(rows):
         back.append(
             exchange(attend_back(packed[row], d_heads[row], results[row], logs[row], start[row : row + 1], low[row]))
         )
-    back[0], (keep_line, sent_line, down_sum) = tie(back[0], (keep_line, sent_line, down_sum))
-    keep_line = line.next(keep_line)
-    sent_line = line.next(sent_line)
-    down_line = line.begin(down_sum)
-    back[1], (out_sum, shard_out) = tie(back[1], (out_sum, shard_out))
+    back[1], (out_part, down_sum) = tie(back[1], (out_part, down_sum))
+    cut = width // 2
+    out_sum = jnp.concatenate([halving(out_part[:, :cut], False), halving(out_part[:, cut:], True)], axis=1)
     output = (mid + out_sum.astype(F32)).astype(BF).reshape(rows, tok, width)
-    out_line = line.begin(shard_out)
     for row in range(rows):
         dpr, qs, ks = unpack_heads(back[row], proj, cos, sin, q_gain, k_gain, row, chips, chip_tok)
         d_proj.append(dpr)
@@ -788,23 +819,11 @@
     d_logit = jnp.concatenate(d_logit, axis=0)
     half = width // 2
     part_qkv = [dot_tn(d_proj, normed_a[:, a : a + half], BF) for a in (0, half)]
-    part_qkv[1], (keep_line, sent_line, down_line, out_line) = tie(
-        part_qkv[1], (keep_line, sent_line, down_line, out_line)
-    )
+    part_qkv, gu_sum = tie_all(part_qkv, gu_sum)
     shard_qkv = [scatter(p) for p in part_qkv]
-    keep_done = line.end(keep_line)
-    keep_other = swap(keep_done)
-    sent_line = line.next(sent_line)
-    down_line = line.next(down_line)
-    out_line = line.next(out_line)
     d_norm_part = (dot_nn(d_proj, qkv_full) + dot_nn(d_logit, gate_core)).astype(BF)
     d_norm_part = d_norm_part.reshape(rows, CORES, tok, width)
     d_norm_other = swap(pick(d_norm_part[:, 1], d_norm_part[:, 0]))
-    d_norm_other, (sent_line, down_line, out_line) = tie(d_norm_other, (sent_line, down_line, out_line))
-    sent_done = line.end(sent_line)
-    sent_other = swap(sent_done)
-    down_line = line.next(down_line)
-    out_line = line.next(out_line)
     d_normed_a = pick(d_norm_part[:, 0], d_norm_part[:, 1]).astype(F32) + d_norm_other.astype(F32)
     own_in = layer_input.astype(F32)
     own_factor = lax.rsqrt(jnp.mean(own_in * own_in, axis=-1, keepdims=True) + epsilon)
@@ -827,16 +846,18 @@
     late = total_sum(jnp.stack([part_attn, heads]))
     grad_w_gate = lax.dynamic_slice_in_dim(early, me * gate_count, gate_count, 0)
 
-    shard_qkv[0], down_line, out_line = lax.optimization_barrier((shard_qkv[0], down_line[1:], out_line[1:]))
-    qkv_line = line.begin(shard_qkv[0])
-    down_done = line.end((2, *down_line))
-    out_done = line.end((2, *out_line))
-    grad_gu = join_units([keep_done, sent_done], [keep_other, sent_other], core, upper.astype(jnp.int32))
+    mid_cut = down_sum.shape[1] // 2
+    line = Line(chips, chip)
+    down_a, down_b, out_done, qkv_a, qkv_b = line.pipeline(
+        [down_sum[:, :mid_cut], down_sum[:, mid_cut:], shard_out, *shard_qkv]
+    )
+    sent = lax.ppermute(gu_sum[quarter:], "dp", trade)
+    keep = gu_sum[:quarter]
+    down_done = jnp.concatenate([down_a, down_b], axis=1)
+    grad_gu = join_units([keep, sent], [swap(keep), swap(sent)], core, upper.astype(jnp.int32))
     grad_down = join_blocks(down_done, swap(down_done), core, [unit_block.index(b) ^ me for b in range(dp)])
     grad_out = join_cols([out_done], [swap(out_done)], core, GROUP * HEAD)
-    shard_qkv[1], (grad_gu, grad_down, grad_out) = tie(shard_qkv[1], (grad_gu, grad_down, grad_out))
-    qkv_sum = [line.end(line.next(line.next(qkv_line))), line.run(shard_qkv[1])]
-    grad_qkv = join_rows(qkv_sum, [swap(p) for p in qkv_sum], core, jnp.where(q_shard, GROUP, 1), HEAD)
+    grad_qkv = join_rows([qkv_a, qkv_b], [swap(qkv_a), swap(qkv_b)], core, jnp.where(q_shard, GROUP, 1), HEAD)
     return (
         output,
         grad_input,

time: 1590 us -> 1430 us (0.90)
  waiting for transfers between devices: 779 us -> 640 us
  other arithmetic: 159 us -> 139 us
  starting transfers between devices: 135 us -> 119 us
    ppermute x18 -> x15, waiting for transfers between devices: 247 us -> 91.5 us  [send(): return (x, lax.ppermute(x, 'seq', self.stages[stage]))]
    ppermute x6, waiting for transfers between devices: 166 us -> 43.9 us  [trade_blocks(): lax.ppermute(out, 'dp', [(d, d ^ k) for d in range(dp)])]
    all_to_all x7, waiting for transfers between devices: 167 us -> 225 us  [exchange(): return lax.all_to_all(x, 'seq', 0, 0, axis_index_groups=groups, tiled=True)]
    all_gather x4, waiting for transfers between devices: 107 us -> 146 us  [gather(): return lax.all_gather(x, 'dp', axis=0, tiled=True)]
    ppermute x12, waiting for transfers between devices: 43.1 us -> 76.3 us  [total_sum(): x = x + lax.ppermute(x, name, [(s, s ^ step) for s in range(size)])]
    add x12 -> x10, other arithmetic: 42.9 us -> 14.6 us  [next(): return (stage + 1,) + self.send(x + moved, stage + 1)]
    ppermute x18 -> x15, starting transfers between devices: 47 us -> 36.7 us  [send(): return (x, lax.ppermute(x, 'seq', self.stages[stage]))]
  transfers between devices with their start and end apart: 70 -> 71, of which waited for: 29 -> 34; matrix products, arithmetic and copies ran while one was open for 20% -> 23% of each run, Pallas kernels for 8% -> 9%
where the time goes in v5:
time: 1430 us; the launch traced here: 1420 us
  waiting for transfers between devices  640 us (45%)
  matrix products  260 us (18%)
  Pallas kernels  145 us (10%)
  other arithmetic  139 us (10%)
  starting transfers between devices  119 us (8%)
  blocking collectives  52.5 us (4%)
  local copies, waits for them, and re-layouts  52 us (4%)
  between operations  16 us (1%)
    all_to_all x7, waiting for transfers between devices, exchange(): return lax.all_to_all(x, 'seq', 0, 0, axis_index_groups=groups, tiled=True)  225 us
    all_gather x4, waiting for transfers between devices, gather(): return lax.all_gather(x, 'dp', axis=0, tiled=True)  146 us
    dot_general x7, matrix products, dot_nt(): lax.dot_general(left, right, (((1,), (1,)), ((), ())), preferred_element_...  97.1 us
    ppermute x15, waiting for transfers between devices, send(): return (x, lax.ppermute(x, 'seq', self.stages[stage]))  91.5 us
    dot_general x7, matrix products, dot_nn(): lax.dot_general(left, right, (((1,), (0,)), ((), ())), preferred_element_...  86.9 us
    ppermute x12, waiting for transfers between devices, total_sum(): x = x + lax.ppermute(x, name, [(s, s ^ step) for s in range(size)])  76.3 us
    dot_general x7, matrix products, dot_tn(): lax.dot_general(left, right, (((0,), (0,)), ((), ())), preferred_element_...  75.8 us
    all_to_all x1, blocking collectives, exchange(): return lax.all_to_all(x, 'seq', 0, 0, axis_index_groups=groups, tiled=True)  52.5 us
  transfers between devices with their start and end apart: 71, of which 34 were waited for; matrix products, arithmetic and copies ran while one was open for 23% of the time, Pallas kernels for 9%

profile of v5, /device:TPU:0, one launch (start us, length us, event | category | flops | bytes accessed | tf_op | source)
XLA Modules:
  0.0 1423.5 jit_solution(13039468906096343247)
XLA Ops:
  30.5 6.6 select_select_fusion
  53.1 54.4 %all-gather.7.cloned.1.call-done = bf16[2048,2048]{1,0:T(8,128)(2,1)} async-done(((bf16[512,2048]{1,0:T(8,128)(2,1)}), bf16[2048,2048]{1,0:T(8,128)(2,1)}) %all-gather.7.cloned.1.call-update) | async-done | bytes 8388624 | tf_op jit(solution)/shard_map/all_gather | solution.py:632
  117.2 11.1 fusion.72.proj_ref
  128.3 6.2 pack_heads.3
  134.5 52.5 %all_to_all.40.q_ref.k_ref.v_ref = bf16[4,512,512]{2,1,0:T(8,128)(2,1)} all-to-all(bf16[4,512,512]{2,1,0:T(8,128)(2,1)} %pack_heads.3), channel_id=1, replica_groups={{0,2,4,6},{1,3,5,7},{8,10,12,14},{9,11,13,15},{16,18,20,22},{17,19,21,2..., dimensions={0} | all-to-all | bytes 4194304 | tf_op jit(solution)/shard_map/all_to_all | solution.py:617
  187.0 6.2 pack_heads.2
  205.2 10.8 attend.3
  216.0 28.0 %all-to-all-done.q_ref.k_ref.v_ref = bf16[4,512,512]{2,1,0:T(8,128)(2,1)S(1)} async-done(((bf16[4,512,512]{2,1,0:T(8,128)(2,1)}), bf16[4,512,512]{2,1,0:T(8,128)(2,1)S(1)}, u32[]{:S(2)}, u32[]{:S(2)}) %all-to-all-start) | async-done | bytes 2097184 | tf_op jit(solution)/shard_map/all_to_all | solution.py:617
  253.5 14.1 collective-permute-done.3
  268.5 10.7 attend.2
  286.7 5.8 convolution_convert_fusion.10
  293.6 14.4 %all-to-all-done.1.res_ref = bf16[4,512,256]{2,1,0:T(8,128)(2,1)S(1)} async-done(((bf16[4,512,256]{2,1,0:T(8,128)(2,1)}), bf16[4,512,256]{2,1,0:T(8,128)(2,1)S(1)}, u32[]{:S(2)}, u32[]{:S(2)}) %all-to-all-start.1) | async-done | bytes 1048608 | tf_op jit(solution)/shard_map/all_to_all | solution.py:617
  336.6 5.1 pad_maximum_fusion
  347.6 20.3 %all-gather.13.cloned.1.call-done = bf16[2048,2048]{1,0:T(8,128)(2,1)} async-done(((bf16[512,2048]{1,0:T(8,128)(2,1)}), bf16[2048,2048]{1,0:T(8,128)(2,1)}) %all-gather.13.cloned.1.call-update) | async-done | bytes 8388624 | tf_op jit(solution)/shard_map/all_gather | solution.py:632
  367.9 18.6 %convolution_convert_fusion.3 = bf16[2048,1536]{1,0:T(8,128)(2,1)} fusion(bf16[2048,2048]{1,0:T(8,128)(2,1)} %all-gather.13.cloned.1.call-done, bf16[2048,1536]{1,0:T(8,128)(2,1)} %bitcast.205), kind=kOutput, calls=%fused_computation.24 | convolution fusion | flops 12888047616 | bytes 20971520 | tf_op jit(solution)/shard_map/dot_general | solution.py:33
  386.5 71.2 %all-gather.11.cloned.1.call-done = bf16[2048,2048]{1,0:T(8,128)(2,1)} async-done(((bf16[512,2048]{1,0:T(8,128)(2,1)}), bf16[2048,2048]{1,0:T(8,128)(2,1)}) %all-gather.11.cloned.1.call-update) | async-done | bytes 8388624 | tf_op jit(solution)/shard_map/all_gather | solution.py:632
  457.7 19.8 %convolution_convert_fusion.1 = bf16[2048,1536]{1,0:T(8,128)(2,1)} fusion(bf16[2048,2048]{1,0:T(8,128)(2,1)} %all-gather.11.cloned.1.call-done, bf16[3072,2048]{1,0:T(8,128)(2,1)} %param.21, pred[]{:T(512)S(6)} %ge.19), kind=kOutput, calls=%fused_computation.22 | convolution fusion | flops 12891193344 | bytes 27262976 | tf_op jit(solution)/shard_map/dot_general | solution.py:29
  477.5 31.6 %select_convert_fusion = (bf16[2048,1536]{1,0:T(8,128)(2,1)}, bf16[2048,1536]{1,0:T(8,128)(2,1)}, bf16[2048,1536]{1,0:T(8,128)(2,1)}) fusion(bf16[2048,1536]{1,0:T(8,128)(2,1)} %convolution_convert_fusion.3, pred[]{:T(512)S(6)} %ge.19, bf16[2048,1536]{1,0:T(8,128)(2,1)} %convolution_convert_fusion.1, bf16[2048,2048]{1,0:T(8,128)(2,1)} %all-gather.11.cloned.1.call-done, ...), kind=kOutput, calls=%fused_computation.14 | convolution fusion | flops 12950962176 | bytes 46137344 | tf_op jit(solution)/shard_map/dot_general | solution.py:29
  509.1 21.8 %fusion.48 = f32[2048,2048]{1,0:T(8,128)} fusion(bf16[2048,1536]{1,0:T(8,128)(2,1)} %get-tuple-element.217, bf16[3072,2048]{1,0:T(8,128)(2,1)} %param.21, pred[]{:T(512)S(6)} %ge.19), kind=kOutput, calls=%fused_computation.141 | convolution fusion | flops 12888047616 | bytes 35651584 | tf_op jit(solution)/shard_map/dot_general | solution.py:33
  531.0 19.1 %add_convert_fusion = bf16[2048,2048]{1,0:T(8,128)(2,1)} fusion(f32[2048,2048]{1,0:T(8,128)} %fusion.48, bf16[2048,1536]{1,0:T(8,128)(2,1)S(1)} %copy-done.76, bf16[1536,2048]{1,0:T(8,128)(2,1)} %pad_maximum_fusion.1), kind=kOutput, calls=%fused_computation.3 | convolution fusion | flops 12893290496 | bytes 37748736 | tf_op jit(solution)/shard_map/dot_general | solution.py:33
  550.1 17.8 %convolution_convert_fusion.5 = bf16[1536,2048]{1,0:T(8,128)(2,1)S(1)} fusion(bf16[2048,1536]{1,0:T(8,128)(2,1)} %get-tuple-element.216, bf16[2048,2048]{1,0:T(8,128)(2,1)} %all-gather.11.cloned.1.call-done), kind=kOutput, calls=%fused_computation.26 | convolution fusion | flops 12888047616 | bytes 20971520 | tf_op jit(solution)/shard_map/dot_general | solution.py:37
  571.2 18.2 %convolution_convert_fusion.6 = bf16[1536,2048]{1,0:T(8,128)(2,1)S(1)} fusion(bf16[2048,1536]{1,0:T(8,128)(2,1)} %get-tuple-element.217, bf16[2048,2048]{1,0:T(8,128)(2,1)} %all-gather.11.cloned.1.call-done), kind=kOutput, calls=%fused_computation.27 | convolution fusion | flops 12888047616 | bytes 20971520 | tf_op jit(solution)/shard_map/dot_general | solution.py:37
  592.7 16.9 %convolution_convert_fusion.4 = bf16[2048,1536]{1,0:T(8,128)(2,1)S(1)} fusion(bf16[2048,2048]{1,0:T(8,128)(2,1)S(1)} %bitcast.235, bf16[2048,1536]{1,0:T(8,128)(2,1)} %convolution_convert_fusion.1, bf16[2048,1536]{1,0:T(8,128)(2,1)} %get-tuple-element.276, pred[]{:T(512)S(6)} %ge.19), kind=kOutput, calls=%fused_computation.25 | convolution fusion | flops 12919504896 | bytes 27262976 | tf_op jit(solution)/shard_map/dot_general | solution.py:37
  613.3 23.2 %reduce-scatter.5.cloned.1.call-done = bf16[512,2048]{1,0:T(8,128)(2,1)} async-done(((bf16[2048,2048]{1,0:T(8,128)(2,1)}), bf16[512,2048]{1,0:T(8,128)(2,1)}) %reduce-scatter.5.cloned.1.call-update) | async-done | bytes 2097168 | tf_op jit(solution)/shard_map/reduce_scatter | solution.py:629
  636.6 6.1 select_add_fusion
  650.7 5.1 fusion.67
  655.8 21.9 %convolution_convert_fusion = bf16[2048,2048]{1,0:T(8,128)(2,1)} fusion(bf16[2048,1536]{1,0:T(8,128)(2,1)} %bitcast.206, bf16[2048,1536]{1,0:T(8,128)(2,1)} %convolution_convert_fusion.1, bf16[2048,1536]{1,0:T(8,128)(2,1)} %get-tuple-element.276, pred[]{:T(512)S(6)} %ge.19), kind=kOutput, calls=%fused_computation.21 | convolution fusion | flops 12920553472 | bytes 27262976 | tf_op jit(solution)/shard_map/dot_general | solution.py:29
  683.4 6.4 convolution_convert_fusion.9
  689.9 6.5 fusion.73.grad_ref
  704.8 6.2 fusion.33.grad_ref
  715.0 45.0 %all-to-all-done.4.grad_ref = bf16[4,512,256]{2,1,0:T(8,128)(2,1)S(1)} async-done(((bf16[4,512,256]{2,1,0:T(8,128)(2,1)}), bf16[4,512,256]{2,1,0:T(8,128)(2,1)S(1)}, u32[]{:S(2)}, u32[]{:S(2)}) %all-to-all-start.4) | async-done | bytes 1048608 | tf_op jit(solution)/shard_map/all_to_all | solution.py:617
  764.5 19.8 %attend_back.2 = bf16[4,512,512]{2,1,0:T(8,128)(2,1)} custom-call(s32[4]{0:T(128)} %get-tuple-element.275.low_ref, bf16[4,512,512]{2,1,0:T(8,128)(2,1)} %all_to_all.40.q_ref.k_ref.v_ref, bf16[4,512,512]{2,1,0:T(8,128)(2,1)} %all_to_all.40.q_ref.k_ref.v_ref, bf16[4,512,512]{2,1,0:T(8,128)(2,1)} %all_to_all.40.q_ref.k_ref.v_ref, ...), custom_call_target="tpu_custom_call" | custom-call | tf_op jit(solution)/shard_map/attend_back/pallas_call | solution.py:281
  784.3 34.9 %all-to-all-done.6.grad_ref = bf16[4,512,256]{2,1,0:T(8,128)(2,1)S(1)} async-done(((bf16[4,512,256]{2,1,0:T(8,128)(2,1)}), bf16[4,512,256]{2,1,0:T(8,128)(2,1)S(1)}, u32[]{:S(2)}, u32[]{:S(2)}) %all-to-all-start.6) | async-done | bytes 1048608 | tf_op jit(solution)/shard_map/all_to_all | solution.py:617
  823.6 20.2 %attend_back.3 = bf16[4,512,512]{2,1,0:T(8,128)(2,1)} custom-call(s32[4]{0:T(128)} %get-tuple-element.274.low_ref, bf16[4,512,512]{2,1,0:T(8,128)(2,1)} %copy-done, bf16[4,512,512]{2,1,0:T(8,128)(2,1)} %copy-done, bf16[4,512,512]{2,1,0:T(8,128)(2,1)} %copy-done, bf16[4,512,256]{2,1,0:T(8,128)(2,1)} %copy-done.37, ...), custom_call_target="tpu_custom_call" | custom-call | tf_op jit(solution)/shard_map/attend_back/pallas_call | solution.py:281
  843.9 46.5 %all-to-all-done.5.grad_ref = bf16[4,512,512]{2,1,0:T(8,128)(2,1)S(1)} async-done(((bf16[4,512,512]{2,1,0:T(8,128)(2,1)}), bf16[4,512,512]{2,1,0:T(8,128)(2,1)S(1)}, u32[]{:S(2)}, u32[]{:S(2)}) %all-to-all-start.5) | async-done | bytes 2097184 | tf_op jit(solution)/shard_map/all_to_all | solution.py:617
  890.4 7.7 all-to-all-start.7
  906.4 17.8 %collective-permute-done.16 = bf16[256,1536]{1,0:T(8,128)(2,1)S(1)} collective-permute-done((bf16[256,1536]{1,0:T(8,128)(2,1)S(1)}, bf16[256,1536]{1,0:T(8,128)(2,1)S(1)}, u32[]{:S(2)}, u32[]{:S(2)}) %collective-permute-start.16) | collective-permute-done | bytes 786464 | tf_op jit(solution)/shard_map/ppermute | solution.py:650
  924.2 11.9 collective-permute-done.15
  936.6 7.5 unpack_heads.3
  944.1 56.1 %all-to-all-done.7.grad_ref = bf16[4,512,512]{2,1,0:T(8,128)(2,1)} async-done(((bf16[4,512,512]{2,1,0:T(8,128)(2,1)}), bf16[4,512,512]{2,1,0:T(8,128)(2,1)}, u32[]{:S(2)}, u32[]{:S(2)}) %all-to-all-start.7) | async-done | bytes 2097184 | tf_op jit(solution)/shard_map/all_to_all | solution.py:617
  1000.2 7.5 unpack_heads.2
  1012.1 6.5 convolution_convert_fusion.7
  1018.5 9.4 convolution_convert_fusion.8
  1034.3 30.8 %collective-permute-done.32 = bf16[4,128,1536]{2,1,0:T(8,128)(2,1)} collective-permute-done((bf16[4,128,1536]{2,1,0:T(8,128)(2,1)}, bf16[4,128,1536]{2,1,0:T(8,128)(2,1)}, u32[]{:S(2)}, u32[]{:S(2)}) %collective-permute-start.32) | collective-permute-done | bytes 1572896 | tf_op jit(solution)/shard_map/ppermute | solution.py:527
  1068.1 7.1 collective-permute-start.34
  1077.0 33.1 %collective-permute-done.28 = f32[24,2048]{1,0:T(8,128)S(1)} collective-permute-done((f32[24,2048]{1,0:T(8,128)S(1)}, f32[24,2048]{1,0:T(8,128)S(1)}, u32[]{:S(2)}, u32[]{:S(2)}) %collective-permute-start.28) | collective-permute-done | bytes 196640 | tf_op jit(solution)/shard_map/ppermute | solution.py:624
  1114.7 5.7 collective-permute-done.29
  1122.0 9.6 collective-permute-done.30
  1141.5 11.5 fusion.74
  1158.5 17.4 %collective-permute-done.35 = bf16[4,128,1536]{2,1,0:T(8,128)(2,1)} collective-permute-done((bf16[4,128,1536]{2,1,0:T(8,128)(2,1)S(1)}, bf16[4,128,1536]{2,1,0:T(8,128)(2,1)}, u32[]{:S(2)}, u32[]{:S(2)}) %collective-permute-start.35) | collective-permute-done | bytes 1572896 | tf_op jit(solution)/shard_map/ppermute | solution.py:527
  1184.8 6.9 collective-permute-start.40
  1198.9 6.6 fusion.69
  1205.8 8.4 collective-permute-done.40
  1220.1 7.1 collective-permute-start.43
  1231.2 16.3 %collective-permute-done.41 = bf16[512,1024]{1,0:T(8,128)(2,1)S(1)} collective-permute-done((bf16[512,1024]{1,0:T(8,128)(2,1)S(1)}, bf16[512,1024]{1,0:T(8,128)(2,1)S(1)}, u32[]{:S(2)}, u32[]{:S(2)}) %collective-permute-start.41) | collective-permute-done | bytes 1048608 | tf_op jit(solution)/shard_map/ppermute | solution.py:527
  1258.0 19.0 %collective-permute-start.23 = (f32[2,2048]{1,0:T(2,128)S(1)}, f32[2,2048]{1,0:T(2,128)S(1)}, u32[]{:S(2)}, u32[]{:S(2)}) collective-permute-start(f32[2,2048]{1,0:T(2,128)S(1)} %fusion.60), channel_id=1, source_target_pairs={{0,2},{1,3},{2,0},{3,1},{4,6},{5,7},{6,4},{7,5},{8,10},{9,11},{10,... | collective-permute-start | bytes 49160 | tf_op jit(solution)/shard_map/ppermute | solution.py:624
  1286.9 16.2 %collective-permute-done.46 = bf16[512,1024]{1,0:T(8,128)(2,1)S(1)} collective-permute-done((bf16[512,1024]{1,0:T(8,128)(2,1)S(1)}, bf16[512,1024]{1,0:T(8,128)(2,1)S(1)}, u32[]{:S(2)}, u32[]{:S(2)}) %collective-permute-start.46) | collective-permute-done | bytes 1048608 | tf_op jit(solution)/shard_map/ppermute | solution.py:527
  1309.4 11.5 collective-permute-done.19
  1324.2 21.5 %collective-permute-done.26 = f32[2,2048]{1,0:T(2,128)S(1)} collective-permute-done((f32[2,2048]{1,0:T(2,128)S(1)}, f32[2,2048]{1,0:T(2,128)S(1)}, u32[]{:S(2)}, u32[]{:S(2)}) %collective-permute-start.26) | collective-permute-done | bytes 16416 | tf_op jit(solution)/shard_map/ppermute | solution.py:624
  1351.2 18.1 %collective-permute-done.20 = bf16[512,1024]{1,0:T(8,128)(2,1)S(1)} collective-permute-done((bf16[512,1024]{1,0:T(8,128)(2,1)S(1)}, bf16[512,1024]{1,0:T(8,128)(2,1)S(1)}, u32[]{:S(2)}, u32[]{:S(2)}) %collective-permute-start.20) | collective-permute-done | bytes 1048608 | tf_op jit(solution)/shard_map/ppermute | solution.py:663
  1373.1 16.4 %join_units.1 = f32[3072,2048]{1,0:T(8,128)} custom-call(s32[2]{0:T(128)} %get-tuple-element.278.which_ref, bf16[768,2048]{1,0:T(8,128)(2,1)} %get-tuple-element.221.keep_ref, bf16[768,2048]{1,0:T(8,128)(2,1)} %copy-done.39, bf16[768,2048]{1,0:T(8,128)(2,1)} %collective-permute-done.51.sent_ref, bf16[768,2048]{1,0:T(8,128)(2,1)} %collective-permute-done.52.sent_other_ref), custom_call_target="tpu_custom_call" | custom-call | tf_op jit(solution)/shard_map/join_units/pallas_call | solution.py:478
  1389.6 6.5 join_cols.1
  1396.0 8.4 join_rows.1
  1404.4 11.9 join_blocks.1
  (422 shorter events, 270.0 us)
Async XLA Ops:
  7.2 100.3 %all-gather.7.cloned.1.call-start = ((), (), s32[]{:S(2)}) async-start(), calls=%async_computation.12 | async-start | bytes 10485760 | tf_op jit(solution)/shard_map/all_gather | solution.py:632
  15.7 271.0 %all-gather.9.cloned.1.call-start = ((), (), s32[]{:S(2)}) async-start(), calls=%async_computation.13 | async-start | bytes 5242880 | tf_op jit(solution)/shard_map/all_gather | solution.py:632
  15.8 23.6 %collective-permute-start.4 = (bf16[16,2048]{1,0:T(8,128)(2,1)S(1)}, bf16[16,2048]{1,0:T(8,128)(2,1)S(1)}, u32[]{:S(2)}, u32[]{:S(2)}) collective-permute-start(bf16[16,2048]{1,0:T(8,128)(2,1)S(1)} %constant_dynamic-update-slice_fusion.4), channel_id=1, source_target_pairs={{0,8},{8,0},{16,24},{24,16},{1,9},{9,1},{17,25},{25,17},{2,10},{10... | collective-permute-start | bytes 196616 | tf_op jit(solution)/shard_map/ppermute | solution.py:624
  18.8 27.1 %collective-permute-start = (bf16[2,256,2048]{2,1,0:T(8,128)(2,1)S(1)}, bf16[2,256,2048]{2,1,0:T(8,128)(2,1)}, u32[]{:S(2)}, u32[]{:S(2)}) collective-permute-start(bf16[2,256,2048]{2,1,0:T(8,128)(2,1)S(1)} %copy-done.1), channel_id=1, source_target_pairs={{0,1},{1,0},{2,3},{3,2},{4,5},{5,4},{6,7},{7,6},{8,9},{9,8},{10,11... | collective-permute-start | bytes 6291464 | tf_op jit(solution)/shard_map/ppermute | solution.py:607
  21.6 305.3 %all-gather.15.cloned.1.call-start = ((), (), s32[]{:S(2)}) async-start(), calls=%async_computation.21 | async-start | bytes 9437184 | tf_op jit(solution)/shard_map/all_gather | solution.py:694
  107.5 260.4 %all-gather.13.cloned.1.call-start = ((), (), s32[]{:S(2)}) async-start(), calls=%async_computation.15 | async-start | bytes 10485760 | tf_op jit(solution)/shard_map/all_gather | solution.py:632
  193.2 50.8 %all-to-all-start = ((bf16[4,512,512]{2,1,0:T(8,128)(2,1)}), bf16[4,512,512]{2,1,0:T(8,128)(2,1)S(1)}, u32[]{:S(2)}, u32[]{:S(2)}) async-start(bf16[4,512,512]{2,1,0:T(8,128)(2,1)} %pack_heads.2), calls=%async_computation | async-start | bytes 4194304 | tf_op jit(solution)/shard_map/all_to_all | solution.py:617
  202.0 47.3 %collective-permute-start.1 = (bf16[256,1536]{1,0:T(8,128)(2,1)}, bf16[256,1536]{1,0:T(8,128)(2,1)}, u32[]{:S(2)}, u32[]{:S(2)}) collective-permute-start(bf16[256,1536]{1,0:T(8,128)(2,1)} %get-tuple-element.245), channel_id=1, source_target_pairs={{0,8},{8,0},{16,24},{24,16},{1,9},{9,1},{17,25},{25,17},{2,10},{10... | collective-permute-start | bytes 2359304 | tf_op jit(solution)/shard_map/ppermute | solution.py:650
  204.1 47.3 %collective-permute-start.2 = (bf16[256,1536]{1,0:T(8,128)(2,1)}, bf16[256,1536]{1,0:T(8,128)(2,1)}, u32[]{:S(2)}, u32[]{:S(2)}) collective-permute-start(bf16[256,1536]{1,0:T(8,128)(2,1)} %get-tuple-element.244), channel_id=1, source_target_pairs={{0,16},{8,24},{16,0},{24,8},{1,17},{9,25},{17,1},{25,9},{2,18},{10... | collective-permute-start | bytes 2359304 | tf_op jit(solution)/shard_map/ppermute | solution.py:650
  244.0 35.3 %all-to-all-start.3 = ((bf16[4,512,256]{2,1,0:T(8,128)(2,1)}), bf16[4,512,256]{2,1,0:T(8,128)(2,1)S(1)}, u32[]{:S(2)}, u32[]{:S(2)}) async-start(bf16[4,512,256]{2,1,0:T(8,128)(2,1)} %get-tuple-element.117.res_ref), calls=%async_computation.3 | async-start | bytes 2097152 | tf_op jit(solution)/shard_map/all_to_all | solution.py:617
  247.8 19.8 %collective-permute-start.3 = (bf16[256,1536]{1,0:T(8,128)(2,1)}, bf16[256,1536]{1,0:T(8,128)(2,1)S(1)}, u32[]{:S(2)}, u32[]{:S(2)}) collective-permute-start(bf16[256,1536]{1,0:T(8,128)(2,1)} %get-tuple-element.243), channel_id=1, source_target_pairs={{0,24},{8,16},{16,8},{24,0},{1,25},{9,17},{17,9},{25,1},{2,26},{10... | collective-permute-start | bytes 2359304 | tf_op jit(solution)/shard_map/ppermute | solution.py:650
  279.3 28.7 %all-to-all-start.1 = ((bf16[4,512,256]{2,1,0:T(8,128)(2,1)}), bf16[4,512,256]{2,1,0:T(8,128)(2,1)S(1)}, u32[]{:S(2)}, u32[]{:S(2)}) async-start(bf16[4,512,256]{2,1,0:T(8,128)(2,1)} %get-tuple-element.113.res_ref), calls=%async_computation.1 | async-start | bytes 2097152 | tf_op jit(solution)/shard_map/all_to_all | solution.py:617
  284.1 173.6 %all-gather.11.cloned.1.call-start = ((), (), s32[]{:S(2)}) async-start(), calls=%async_computation.14 | async-start | bytes 10485760 | tf_op jit(solution)/shard_map/all_gather | solution.py:632
  293.6 23.1 %collective-permute-start.7 = (bf16[256,2048]{1,0:T(8,128)(2,1)}, bf16[256,2048]{1,0:T(8,128)(2,1)}, u32[]{:S(2)}, u32[]{:S(2)}) collective-permute-start(bf16[256,2048]{1,0:T(8,128)(2,1)} %broadcast_select_fusion.18), channel_id=1, source_target_pairs={{0,1},{1,0},{2,3},{3,2},{4,5},{5,4},{6,7},{7,6},{8,9},{9,8},{10,11... | collective-permute-start | bytes 3145736 | tf_op jit(solution)/shard_map/ppermute | solution.py:607
  325.9 310.6 %reduce-scatter.5.cloned.1.call-start = ((), (), s32[]{:S(2)}) async-start(), calls=%async_computation.16 | async-start | bytes 10485760 | tf_op jit(solution)/shard_map/reduce_scatter | solution.py:629
  550.1 477.9 %all-reduce.4.cloned.1.call-start = ((), (), s32[]{:S(2)}) async-start(), calls=%async_computation.18 | async-start | bytes 12582912 | tf_op jit(solution)/shard_map/psum | solution.py:776
  571.2 42.1 %collective-permute-start.11 = (bf16[768,2048]{1,0:T(8,128)(2,1)S(1)}, bf16[768,2048]{1,0:T(8,128)(2,1)S(1)}, u32[]{:S(2)}, u32[]{:S(2)}) collective-permute-start(bf16[768,2048]{1,0:T(8,128)(2,1)S(1)} %slice_select_fusion.2), channel_id=1, source_target_pairs={{0,1},{1,0},{2,3},{3,2},{4,5},{5,4},{6,7},{7,6},{8,9},{9,8},{10,11... | collective-permute-start | bytes 9437192 | tf_op jit(solution)/shard_map/ppermute | solution.py:607
  592.0 21.4 %collective-permute-start.10 = (bf16[768,2048]{1,0:T(8,128)(2,1)S(1)}, bf16[768,2048]{1,0:T(8,128)(2,1)}, u32[]{:S(2)}, u32[]{:S(2)}) collective-permute-start(bf16[768,2048]{1,0:T(8,128)(2,1)S(1)} %slice_select_fusion.3), channel_id=1, source_target_pairs={{0,1},{1,0},{2,3},{3,2},{4,5},{5,4},{6,7},{7,6},{8,9},{9,8},{10,11... | collective-permute-start | bytes 9437192 | tf_op jit(solution)/shard_map/ppermute | solution.py:607
  613.3 64.4 %collective-permute-start.13 = (bf16[4,256,1536]{2,1,0:T(8,128)(2,1)}, bf16[4,256,1536]{2,1,0:T(8,128)(2,1)}, u32[]{:S(2)}, u32[]{:S(2)}) collective-permute-start(bf16[4,256,1536]{2,1,0:T(8,128)(2,1)} %fusion.27), channel_id=1, source_target_pairs={{0,1},{1,0},{2,3},{3,2},{4,5},{5,4},{6,7},{7,6},{8,9},{9,8},{10,11... | collective-permute-start | bytes 9437192 | tf_op jit(solution)/shard_map/ppermute | solution.py:607
  655.8 21.9 %collective-permute-start.12 = (bf16[2,256,2048]{2,1,0:T(8,128)(2,1)}, bf16[2,256,2048]{2,1,0:T(8,128)(2,1)}, u32[]{:S(2)}, u32[]{:S(2)}) collective-permute-start(bf16[2,256,2048]{2,1,0:T(8,128)(2,1)} %bitcast.22), channel_id=1, source_target_pairs={{0,1},{1,0},{2,3},{3,2},{4,5},{5,4},{6,7},{7,6},{8,9},{9,8},{10,11... | collective-permute-start | bytes 6291464 | tf_op jit(solution)/shard_map/ppermute | solution.py:607
  700.4 59.6 %all-to-all-start.4 = ((bf16[4,512,256]{2,1,0:T(8,128)(2,1)}), bf16[4,512,256]{2,1,0:T(8,128)(2,1)S(1)}, u32[]{:S(2)}, u32[]{:S(2)}) async-start(bf16[4,512,256]{2,1,0:T(8,128)(2,1)} %get-tuple-element.132), calls=%async_computation.5 | async-start | bytes 2097152 | tf_op jit(solution)/shard_map/all_to_all | solution.py:617
  761.0 58.2 %all-to-all-start.6 = ((bf16[4,512,256]{2,1,0:T(8,128)(2,1)}), bf16[4,512,256]{2,1,0:T(8,128)(2,1)S(1)}, u32[]{:S(2)}, u32[]{:S(2)}) async-start(bf16[4,512,256]{2,1,0:T(8,128)(2,1)} %get-tuple-element.138), calls=%async_computation.7 | async-start | bytes 2097152 | tf_op jit(solution)/shard_map/all_to_all | solution.py:617
  819.2 71.2 %all-to-all-start.5 = ((bf16[4,512,512]{2,1,0:T(8,128)(2,1)}), bf16[4,512,512]{2,1,0:T(8,128)(2,1)S(1)}, u32[]{:S(2)}, u32[]{:S(2)}) async-start(bf16[4,512,512]{2,1,0:T(8,128)(2,1)} %attend_back.2), calls=%async_computation.6 | async-start | bytes 4194304 | tf_op jit(solution)/shard_map/all_to_all | solution.py:617
  822.8 311.5 %reduce-scatter.7.cloned.1.call-start = ((), (), s32[]{:S(2)}) async-start(), calls=%async_computation.17 | async-start | bytes 5242880 | tf_op jit(solution)/shard_map/reduce_scatter | solution.py:629
  890.4 109.8 %all-to-all-start.7 = ((bf16[4,512,512]{2,1,0:T(8,128)(2,1)}), bf16[4,512,512]{2,1,0:T(8,128)(2,1)}, u32[]{:S(2)}, u32[]{:S(2)}) async-start(bf16[4,512,512]{2,1,0:T(8,128)(2,1)} %attend_back.3), calls=%async_computation.8 | async-start | bytes 4194304 | tf_op jit(solution)/shard_map/all_to_all | solution.py:617
  898.1 277.7 %reduce-scatter.9.cloned.1.call-start = ((), (), s32[]{:S(2)}) async-start(), calls=%async_computation.19 | async-start | bytes 5242880 | tf_op jit(solution)/shard_map/reduce_scatter | solution.py:629
  902.8 21.4 %collective-permute-start.16 = (bf16[256,1536]{1,0:T(8,128)(2,1)S(1)}, bf16[256,1536]{1,0:T(8,128)(2,1)S(1)}, u32[]{:S(2)}, u32[]{:S(2)}) collective-permute-start(bf16[256,1536]{1,0:T(8,128)(2,1)S(1)} %get-tuple-element.240), channel_id=1, source_target_pairs={{0,24},{8,16},{16,8},{24,0},{1,25},{9,17},{17,9},{25,1},{2,26},{10... | collective-permute-start | bytes 2359304 | tf_op jit(solution)/shard_map/ppermute | solution.py:650
  905.3 30.8 %collective-permute-start.15 = (bf16[256,1536]{1,0:T(8,128)(2,1)S(1)}, bf16[256,1536]{1,0:T(8,128)(2,1)S(1)}, u32[]{:S(2)}, u32[]{:S(2)}) collective-permute-start(bf16[256,1536]{1,0:T(8,128)(2,1)S(1)} %get-tuple-element.241), channel_id=1, source_target_pairs={{0,16},{8,24},{16,0},{24,8},{1,17},{9,25},{17,1},{25,9},{2,18},{10... | collective-permute-start | bytes 2359304 | tf_op jit(solution)/shard_map/ppermute | solution.py:650
  906.0 30.1 %collective-permute-start.14 = (bf16[256,1536]{1,0:T(8,128)(2,1)S(1)}, bf16[256,1536]{1,0:T(8,128)(2,1)S(1)}, u32[]{:S(2)}, u32[]{:S(2)}) collective-permute-start(bf16[256,1536]{1,0:T(8,128)(2,1)S(1)} %get-tuple-element.242), channel_id=1, source_target_pairs={{0,8},{8,0},{16,24},{24,16},{1,9},{9,1},{17,25},{25,17},{2,10},{10... | collective-permute-start | bytes 2359304 | tf_op jit(solution)/shard_map/ppermute | solution.py:650
  1028.0 177.8 %reduce-scatter.11.cloned.1.call-start = ((), (), s32[]{:S(2)}) async-start(), calls=%async_computation.20 | async-start | bytes 5242880 | tf_op jit(solution)/shard_map/reduce_scatter | solution.py:629
  1030.6 34.5 %collective-permute-start.32 = (bf16[4,128,1536]{2,1,0:T(8,128)(2,1)}, bf16[4,128,1536]{2,1,0:T(8,128)(2,1)}, u32[]{:S(2)}, u32[]{:S(2)}) collective-permute-start(bf16[4,128,1536]{2,1,0:T(8,128)(2,1)} %get-tuple-element.150), channel_id=1, source_target_pairs={{0,2},{1,3},{6,4},{7,5},{8,10},{9,11},{14,12},{15,13},{16,18},{17,... | collective-permute-start | bytes 4718600 | tf_op jit(solution)/shard_map/ppermute | solution.py:527
  1067.4 65.8 %collective-permute-start.33 = (bf16[4,128,1536]{2,1,0:T(8,128)(2,1)S(1)}, bf16[4,128,1536]{2,1,0:T(8,128)(2,1)S(1)}, u32[]{:S(2)}, u32[]{:S(2)}) collective-permute-start(bf16[4,128,1536]{2,1,0:T(8,128)(2,1)S(1)} %add.278), channel_id=1, source_target_pairs={{2,4},{3,5},{4,2},{5,3},{10,12},{11,13},{12,10},{13,11},{18,20},{1... | collective-permute-start | bytes 4718600 | tf_op jit(solution)/shard_map/ppermute | solution.py:527
  1068.1 66.2 %collective-permute-start.34 = (bf16[4,128,1536]{2,1,0:T(8,128)(2,1)S(1)}, bf16[4,128,1536]{2,1,0:T(8,128)(2,1)}, u32[]{:S(2)}, u32[]{:S(2)}) collective-permute-start(bf16[4,128,1536]{2,1,0:T(8,128)(2,1)S(1)} %copy-done.33), channel_id=1, source_target_pairs={{0,2},{1,3},{6,4},{7,5},{8,10},{9,11},{14,12},{15,13},{16,18},{17,... | collective-permute-start | bytes 4718600 | tf_op jit(solution)/shard_map/ppermute | solution.py:527
  1076.9 33.1 %collective-permute-start.28 = (f32[24,2048]{1,0:T(8,128)S(1)}, f32[24,2048]{1,0:T(8,128)S(1)}, u32[]{:S(2)}, u32[]{:S(2)}) collective-permute-start(f32[24,2048]{1,0:T(8,128)S(1)} %fusion.61), channel_id=1, source_target_pairs={{0,2},{1,3},{2,0},{3,1},{4,6},{5,7},{6,4},{7,5},{8,10},{9,11},{10,... | collective-permute-start | bytes 589832 | tf_op jit(solution)/shard_map/ppermute | solution.py:624
  1110.1 10.3 collective-permute-start.29
  1120.4 11.2 collective-permute-start.30
  1131.6 61.4 %collective-permute-start.31 = (f32[24,2048]{1,0:T(8,128)S(1)}, f32[24,2048]{1,0:T(8,128)S(1)}, u32[]{:S(2)}, u32[]{:S(2)}) collective-permute-start(f32[24,2048]{1,0:T(8,128)S(1)} %add.276), channel_id=1, source_target_pairs={{0,16},{8,24},{16,0},{24,8},{1,17},{9,25},{17,1},{25,9},{2,18},{10... | collective-permute-start | bytes 589832 | tf_op jit(solution)/shard_map/ppermute | solution.py:624
  1134.3 22.0 %collective-permute-start.37 = (bf16[512,1024]{1,0:T(8,128)(2,1)}, bf16[512,1024]{1,0:T(8,128)(2,1)S(1)}, u32[]{:S(2)}, u32[]{:S(2)}) collective-permute-start(bf16[512,1024]{1,0:T(8,128)(2,1)} %reduce-scatter.7.cloned.1.call-done), channel_id=1, source_target_pairs={{0,2},{1,3},{6,4},{7,5},{8,10},{9,11},{14,12},{15,13},{16,18},{17,... | collective-permute-start | bytes 3145736 | tf_op jit(solution)/shard_map/ppermute | solution.py:527
  1138.8 17.5 %collective-permute-start.36 = (bf16[4,128,1536]{2,1,0:T(8,128)(2,1)S(1)}, bf16[4,128,1536]{2,1,0:T(8,128)(2,1)S(1)}, u32[]{:S(2)}, u32[]{:S(2)}) collective-permute-start(bf16[4,128,1536]{2,1,0:T(8,128)(2,1)S(1)} %add.280), channel_id=1, source_target_pairs={{2,4},{3,5},{4,2},{5,3},{10,12},{11,13},{12,10},{13,11},{18,20},{1... | collective-permute-start | bytes 4718600 | tf_op jit(solution)/shard_map/ppermute | solution.py:527
  1140.1 35.8 %collective-permute-start.35 = (bf16[4,128,1536]{2,1,0:T(8,128)(2,1)S(1)}, bf16[4,128,1536]{2,1,0:T(8,128)(2,1)}, u32[]{:S(2)}, u32[]{:S(2)}) collective-permute-start(bf16[4,128,1536]{2,1,0:T(8,128)(2,1)S(1)} %add.279), channel_id=1, source_target_pairs={{2,0},{3,1},{4,6},{5,7},{10,8},{11,9},{12,14},{13,15},{18,16},{19,... | collective-permute-start | bytes 4718600 | tf_op jit(solution)/shard_map/ppermute | solution.py:527
  1179.8 34.8 %collective-permute-start.38 = (bf16[4,128,1536]{2,1,0:T(8,128)(2,1)}, bf16[4,128,1536]{2,1,0:T(8,128)(2,1)}, u32[]{:S(2)}, u32[]{:S(2)}) collective-permute-start(bf16[4,128,1536]{2,1,0:T(8,128)(2,1)} %add.281), channel_id=1, source_target_pairs={{2,0},{3,1},{4,6},{5,7},{10,8},{11,9},{12,14},{13,15},{18,16},{19,... | collective-permute-start | bytes 4718600 | tf_op jit(solution)/shard_map/ppermute | solution.py:527
  1182.7 68.9 %collective-permute-start.21 = (bf16[2,256,2048]{2,1,0:T(8,128)(2,1)}, bf16[2,256,2048]{2,1,0:T(8,128)(2,1)}, u32[]{:S(2)}, u32[]{:S(2)}) collective-permute-start(bf16[2,256,2048]{2,1,0:T(8,128)(2,1)} %select_bitcast_fusion), channel_id=1, source_target_pairs={{0,1},{1,0},{2,3},{3,2},{4,5},{5,4},{6,7},{7,6},{8,9},{9,8},{10,11... | collective-permute-start | bytes 6291464 | tf_op jit(solution)/shard_map/ppermute | solution.py:607
  1183.1 22.7 %collective-permute-start.39 = (bf16[512,1024]{1,0:T(8,128)(2,1)S(1)}, bf16[512,1024]{1,0:T(8,128)(2,1)}, u32[]{:S(2)}, u32[]{:S(2)}) collective-permute-start(bf16[512,1024]{1,0:T(8,128)(2,1)S(1)} %add.282), channel_id=1, source_target_pairs={{2,4},{3,5},{4,2},{5,3},{10,12},{11,13},{12,10},{13,11},{18,20},{1... | collective-permute-start | bytes 3145736 | tf_op jit(solution)/shard_map/ppermute | solution.py:527
  1184.8 29.4 %collective-permute-start.40 = (bf16[512,1024]{1,0:T(8,128)(2,1)}, bf16[512,1024]{1,0:T(8,128)(2,1)}, u32[]{:S(2)}, u32[]{:S(2)}) collective-permute-start(bf16[512,1024]{1,0:T(8,128)(2,1)} %reduce-scatter.9.cloned.1.call-done), channel_id=1, source_target_pairs={{0,2},{1,3},{6,4},{7,5},{8,10},{9,11},{14,12},{15,13},{16,18},{17,... | collective-permute-start | bytes 3145736 | tf_op jit(solution)/shard_map/ppermute | solution.py:527
  1205.5 77.9 %collective-permute-start.51 = (bf16[768,2048]{1,0:T(8,128)(2,1)}, bf16[768,2048]{1,0:T(8,128)(2,1)}, u32[]{:S(2)}, u32[]{:S(2)}) collective-permute-start(bf16[768,2048]{1,0:T(8,128)(2,1)} %get-tuple-element.220), channel_id=1, source_target_pairs={{0,16},{8,24},{16,0},{24,8},{1,17},{9,25},{17,1},{25,9},{2,18},{10... | collective-permute-start | bytes 9437192 | tf_op jit(solution)/shard_map/ppermute | solution.py:854
  1216.5 13.6 collective-permute-start.42
  1218.8 28.7 %collective-permute-start.41 = (bf16[512,1024]{1,0:T(8,128)(2,1)S(1)}, bf16[512,1024]{1,0:T(8,128)(2,1)S(1)}, u32[]{:S(2)}, u32[]{:S(2)}) collective-permute-start(bf16[512,1024]{1,0:T(8,128)(2,1)S(1)} %add.283), channel_id=1, source_target_pairs={{2,0},{3,1},{4,6},{5,7},{10,8},{11,9},{12,14},{13,15},{18,16},{19,... | collective-permute-start | bytes 3145736 | tf_op jit(solution)/shard_map/ppermute | solution.py:527
  1220.1 28.7 %collective-permute-start.43 = (bf16[512,1024]{1,0:T(8,128)(2,1)S(1)}, bf16[512,1024]{1,0:T(8,128)(2,1)S(1)}, u32[]{:S(2)}, u32[]{:S(2)}) collective-permute-start(bf16[512,1024]{1,0:T(8,128)(2,1)S(1)} %copy-done.44), channel_id=1, source_target_pairs={{0,2},{1,3},{6,4},{7,5},{8,10},{9,11},{14,12},{15,13},{16,18},{17,... | collective-permute-start | bytes 3145736 | tf_op jit(solution)/shard_map/ppermute | solution.py:527
  1230.1 76.4 %collective-permute-start.17 = (bf16[2,512,1024]{2,1,0:T(8,128)(2,1)S(1)}, bf16[2,512,1024]{2,1,0:T(8,128)(2,1)S(1)}, u32[]{:S(2)}, u32[]{:S(2)}) collective-permute-start(bf16[2,512,1024]{2,1,0:T(8,128)(2,1)S(1)} %fusion.28), channel_id=1, source_target_pairs={{0,8},{8,0},{16,24},{24,16},{1,9},{9,1},{17,25},{25,17},{2,10},{10... | collective-permute-start | bytes 6291464 | tf_op jit(solution)/shard_map/ppermute | solution.py:663
  1250.3 27.3 %collective-permute-start.44 = (bf16[512,1024]{1,0:T(8,128)(2,1)S(1)}, bf16[512,1024]{1,0:T(8,128)(2,1)S(1)}, u32[]{:S(2)}, u32[]{:S(2)}) collective-permute-start(bf16[512,1024]{1,0:T(8,128)(2,1)S(1)} %add.285), channel_id=1, source_target_pairs={{2,0},{3,1},{4,6},{5,7},{10,8},{11,9},{12,14},{13,15},{18,16},{19,... | collective-permute-start | bytes 3145736 | tf_op jit(solution)/shard_map/ppermute | solution.py:527
  1257.8 63.2 %collective-permute-start.19 = (bf16[2,512,1024]{2,1,0:T(8,128)(2,1)S(1)}, bf16[2,512,1024]{2,1,0:T(8,128)(2,1)S(1)}, u32[]{:S(2)}, u32[]{:S(2)}) collective-permute-start(bf16[2,512,1024]{2,1,0:T(8,128)(2,1)S(1)} %bitcast.210), channel_id=1, source_target_pairs={{0,16},{8,24},{16,0},{24,8},{1,17},{9,25},{17,1},{25,9},{2,18},{10... | collective-permute-start | bytes 6291464 | tf_op jit(solution)/shard_map/ppermute | solution.py:663
  1258.0 25.5 %collective-permute-start.23 = (f32[2,2048]{1,0:T(2,128)S(1)}, f32[2,2048]{1,0:T(2,128)S(1)}, u32[]{:S(2)}, u32[]{:S(2)}) collective-permute-start(f32[2,2048]{1,0:T(2,128)S(1)} %fusion.60), channel_id=1, source_target_pairs={{0,2},{1,3},{2,0},{3,1},{4,6},{5,7},{6,4},{7,5},{8,10},{9,11},{10,... | collective-permute-start | bytes 49160 | tf_op jit(solution)/shard_map/ppermute | solution.py:624
  1278.1 25.0 %collective-permute-start.46 = (bf16[512,1024]{1,0:T(8,128)(2,1)S(1)}, bf16[512,1024]{1,0:T(8,128)(2,1)S(1)}, u32[]{:S(2)}, u32[]{:S(2)}) collective-permute-start(bf16[512,1024]{1,0:T(8,128)(2,1)S(1)} %add.287), channel_id=1, source_target_pairs={{2,0},{3,1},{4,6},{5,7},{10,8},{11,9},{12,14},{13,15},{18,16},{19,... | collective-permute-start | bytes 3145736 | tf_op jit(solution)/shard_map/ppermute | solution.py:527
  1283.4 85.9 %collective-permute-start.50 = (bf16[768,2048]{1,0:T(8,128)(2,1)S(1)}, bf16[768,2048]{1,0:T(8,128)(2,1)S(1)}, u32[]{:S(2)}, u32[]{:S(2)}) collective-permute-start(bf16[768,2048]{1,0:T(8,128)(2,1)S(1)} %copy-done.22), channel_id=1, source_target_pairs={{0,1},{1,0},{2,3},{3,2},{4,5},{5,4},{6,7},{7,6},{8,9},{9,8},{10,11... | collective-permute-start | bytes 9437192 | tf_op jit(solution)/shard_map/ppermute | solution.py:607
  1283.5 24.7 %collective-permute-start.24 = (f32[2,2048]{1,0:T(2,128)S(1)}, f32[2,2048]{1,0:T(2,128)S(1)}, u32[]{:S(2)}, u32[]{:S(2)}) collective-permute-start(f32[2,2048]{1,0:T(2,128)S(1)} %fusion.106), channel_id=1, source_target_pairs={{0,4},{1,5},{2,6},{3,7},{4,0},{5,1},{6,2},{7,3},{8,12},{9,13},{10,... | collective-permute-start | bytes 49160 | tf_op jit(solution)/shard_map/ppermute | solution.py:624
  1303.1 70.0 %collective-permute-start.52 = (bf16[768,2048]{1,0:T(8,128)(2,1)}, bf16[768,2048]{1,0:T(8,128)(2,1)}, u32[]{:S(2)}, u32[]{:S(2)}) collective-permute-start(bf16[768,2048]{1,0:T(8,128)(2,1)} %collective-permute-done.51.sent_ref), channel_id=1, source_target_pairs={{0,1},{1,0},{2,3},{3,2},{4,5},{5,4},{6,7},{7,6},{8,9},{9,8},{10,11... | collective-permute-start | bytes 9437192 | tf_op jit(solution)/shard_map/ppermute | solution.py:607
  1306.5 97.9 %collective-permute-start.53 = (bf16[4,256,1536]{2,1,0:T(8,128)(2,1)S(1)}, bf16[4,256,1536]{2,1,0:T(8,128)(2,1)}, u32[]{:S(2)}, u32[]{:S(2)}) collective-permute-start(bf16[4,256,1536]{2,1,0:T(8,128)(2,1)S(1)} %pad_maximum_fusion.7.refs_0_), channel_id=1, source_target_pairs={{0,1},{1,0},{2,3},{3,2},{4,5},{5,4},{6,7},{7,6},{8,9},{9,8},{10,11... | collective-permute-start | bytes 9437192 | tf_op jit(solution)/shard_map/ppermute | solution.py:607
  1308.2 14.1 collective-permute-start.25
  1321.0 30.2 %collective-permute-start.18 = (bf16[512,1024]{1,0:T(8,128)(2,1)S(1)}, bf16[512,1024]{1,0:T(8,128)(2,1)S(1)}, u32[]{:S(2)}, u32[]{:S(2)}) collective-permute-start(bf16[512,1024]{1,0:T(8,128)(2,1)S(1)} %select_bitcast_fusion.2), channel_id=1, source_target_pairs={{0,16},{8,24},{16,0},{24,8},{1,17},{9,25},{17,1},{25,9},{2,18},{10... | collective-permute-start | bytes 3145736 | tf_op jit(solution)/shard_map/ppermute | solution.py:663
  1322.3 23.4 %collective-permute-start.26 = (f32[2,2048]{1,0:T(2,128)S(1)}, f32[2,2048]{1,0:T(2,128)S(1)}, u32[]{:S(2)}, u32[]{:S(2)}) collective-permute-start(f32[2,2048]{1,0:T(2,128)S(1)} %add.271), channel_id=1, source_target_pairs={{0,16},{8,24},{16,0},{24,8},{1,17},{9,25},{17,1},{25,9},{2,18},{10... | collective-permute-start | bytes 49160 | tf_op jit(solution)/shard_map/ppermute | solution.py:624
  1345.8 23.6 %collective-permute-start.20 = (bf16[512,1024]{1,0:T(8,128)(2,1)S(1)}, bf16[512,1024]{1,0:T(8,128)(2,1)S(1)}, u32[]{:S(2)}, u32[]{:S(2)}) collective-permute-start(bf16[512,1024]{1,0:T(8,128)(2,1)S(1)} %select_bitcast_fusion.1), channel_id=1, source_target_pairs={{0,8},{8,0},{16,24},{24,16},{1,9},{9,1},{17,25},{25,17},{2,10},{10... | collective-permute-start | bytes 3145736 | tf_op jit(solution)/shard_map/ppermute | solution.py:663
  1351.2 38.3 %collective-permute-start.49 = (bf16[512,1024]{1,0:T(8,128)(2,1)}, bf16[512,1024]{1,0:T(8,128)(2,1)}, u32[]{:S(2)}, u32[]{:S(2)}) collective-permute-start(bf16[512,1024]{1,0:T(8,128)(2,1)} %broadcast_select_fusion.15.refs_0_), channel_id=1, source_target_pairs={{0,1},{1,0},{2,3},{3,2},{4,5},{5,4},{6,7},{7,6},{8,9},{9,8},{10,11... | collective-permute-start | bytes 3145736 | tf_op jit(solution)/shard_map/ppermute | solution.py:607
  1369.3 26.7 %collective-permute-start.48 = (bf16[512,1024]{1,0:T(8,128)(2,1)}, bf16[512,1024]{1,0:T(8,128)(2,1)}, u32[]{:S(2)}, u32[]{:S(2)}) collective-permute-start(bf16[512,1024]{1,0:T(8,128)(2,1)} %broadcast_select_fusion.16.refs_1_), channel_id=1, source_target_pairs={{0,1},{1,0},{2,3},{3,2},{4,5},{5,4},{6,7},{7,6},{8,9},{9,8},{10,11... | collective-permute-start | bytes 3145736 | tf_op jit(solution)/shard_map/ppermute | solution.py:607
  1369.4 26.7 %collective-permute-start.47 = (bf16[512,1024]{1,0:T(8,128)(2,1)}, bf16[512,1024]{1,0:T(8,128)(2,1)}, u32[]{:S(2)}, u32[]{:S(2)}) collective-permute-start(bf16[512,1024]{1,0:T(8,128)(2,1)} %broadcast_select_fusion.17.refs_0_), channel_id=1, source_target_pairs={{0,1},{1,0},{2,3},{3,2},{4,5},{5,4},{6,7},{7,6},{8,9},{9,8},{10,11... | collective-permute-start | bytes 3145736 | tf_op jit(solution)/shard_map/ppermute | solution.py:607
  (88 other events, 1069.9 us)
Sparse Core Ops, SparseCore 0:
  15.8 91.5 all-gather.6
  109.9 52.5 all-gather.8
  164.6 114.0 all-gather.14
  280.4 87.4 all-gather.12
  370.2 87.4 all-gather.10
  550.2 86.3 reduce-scatter.4
  677.8 346.2 all-reduce.3
  1027.1 51.5 reduce-scatter.6
  1081.7 56.7 reduce-scatter.8
  1141.3 50.9 reduce-scatter.10

commit v6 on v5

--- a/solution.py
+++ b/solution.py
@@ -513,6 +513,29 @@
     )(core[None], jnp.stack(order).astype(jnp.int32), mine, other)
 
 
+class Halving:
+    def __init__(self, x, dp, flip):
+        self.dp = dp
+        self.mine = lax.axis_index("dp")
+        bits = dp.bit_length() - 1
+        self.left = list(range(bits))
+        self.order = self.left[::-1] if flip else self.left[:]
+        self.x = x.reshape((2,) * bits + (x.shape[0] // dp, x.shape[1]))
+
+    def send(self):
+        bit = self.order.pop(0)
+        axis = sum(1 for b in self.left if b > bit)
+        self.left.remove(bit)
+        low, high = lax.index_in_dim(self.x, 0, axis, False), lax.index_in_dim(self.x, 1, axis, False)
+        mark = (self.mine >> bit) % 2 == 1
+        pairs = [(d, d ^ (1 << bit)) for d in range(self.dp)]
+        self.keep = jnp.where(mark, high, low)
+        return lax.ppermute(jnp.where(mark, low, high), "dp", pairs)
+
+    def add(self, moved):
+        self.x = self.keep + moved
+
+
 class Line:
     def __init__(self, chips, chip):
         self.chips = chips
@@ -539,26 +562,34 @@
         stage, x, moved = state
         return moved if self.chips != 4 else jnp.where(self.inner, x, moved)
 
-    def pipeline(self, parts):
+    def pipeline(self, parts, fillers):
         if self.chips != 4:
-            return lax.psum(parts, "seq", axis_index_groups=self.groups)
+            done = lax.psum(parts, "seq", axis_index_groups=self.groups)
+            return done, [filler(done) for filler in fillers.values()]
         count = len(parts)
         states = [None] * count
+        made = []
         for step in range(count + 2):
             for k in range(count):
                 if k == step:
                     states[k] = self.begin(parts[k])
                 elif k < step <= k + 2:
                     states[k] = self.next(states[k])
+            done = [self.end(states[k]) if k + 3 <= step else None for k in range(count)]
+            extra = fillers[step](done) if step in fillers else []
             live = [k for k in range(count) if states[k] is not None]
             later = [k for k in range(step + 1, min(step + 2, count))]
-            moved = lax.optimization_barrier([states[k][1:] for k in live] + [parts[k] for k in later])
+            moved, extra = lax.optimization_barrier(
+                ([states[k][1:] for k in live] + [parts[k] for k in later], extra)
+            )
+            if step in fillers:
+                made.append(extra)
             for k, value in zip(live + later, moved):
                 if k in later:
                     parts[k] = value
                 else:
                     states[k] = (states[k][0], *value)
-        return [self.end(state) for state in states]
+        return [self.end(state) for state in states], made
 
 
 def tie_all(values, work):
@@ -650,21 +681,6 @@
             found.append((mine ^ k, lax.ppermute(out, "dp", [(d, d ^ k) for d in range(dp)])))
         return found
 
-    def halving(x, flip):
-        bits = dp.bit_length() - 1
-        mine = lax.axis_index("dp")
-        x = x.reshape((2,) * bits + (x.shape[0] // dp, x.shape[1]))
-        order = list(range(bits))
-        gone = []
-        for bit in reversed(order) if flip else order:
-            axis = sum(1 for b in order if b > bit and b not in gone)
-            low, high = lax.index_in_dim(x, 0, axis, False), lax.index_in_dim(x, 1, axis, False)
-            mark = (mine >> bit) % 2 == 1
-            sent = lax.ppermute(jnp.where(mark, low, high), "dp", [(d, d ^ (1 << bit)) for d in range(dp)])
-            x = jnp.where(mark, high, low) + sent
-            gone.append(bit)
-        return x
-
     half_dp = dp // 2
     me = lax.axis_index("dp")
     upper = me >= half_dp
@@ -772,8 +788,8 @@
     )
     keep_sum = pick(part_keep[:quarter], part_keep[quarter:]) + keep_swap
     recv_sum = pick(part_recv[:quarter], part_recv[quarter:]) + recv_swap
-    d_normed, gu_sum = tie(d_normed, jnp.concatenate([keep_sum, recv_sum], axis=0))
-    gu_sum = lax.psum(gu_sum, "seq", axis_index_groups=groups)
+    d_normed, (keep_sum, recv_sum) = tie(d_normed, (keep_sum, recv_sum))
+    keep = lax.psum(keep_sum, "seq", axis_index_groups=groups)
 
     d_normed = d_normed.astype(F32)
     part_ffn = jnp.sum(d_normed * mid * factor_f, axis=0)
@@ -787,6 +803,15 @@
     down_sum = jnp.stack([moved for _, moved in trade_blocks(down_sum)])
 
     d_mid_low = jnp.concatenate([pick(low_mine, low_other), pick(low_other, low_mine)], axis=1).reshape(tokens, width)
+    def early_sum(d_logit):
+        part_gate = dot_tn(d_logit, normed_a)[:CORE_Q]
+        zero = jnp.zeros_like(part_gate)
+        part_gate = jnp.stack(
+            [pick(part_gate, zero).reshape(-1, GROUP, width), pick(zero, part_gate).reshape(-1, GROUP, width)], 1
+        )
+        part_gate = part_gate.reshape(QUERY_HEADS, width)
+        return total_sum(jnp.concatenate([part_gate, part_ffn[None], jnp.zeros((7, width), F32)], axis=0))
+
     part_out = dot_tn(d_mid_low, gated, BF)
     out_part = dot_nt(hidden, down_full, BF)
     d_proj, d_logit, d_heads = [], [], []
@@ -800,15 +825,33 @@
         d_attn, dl = gate_back(d_gated, tok_results[row], logits, row)
         d_logit.append(dl)
         d_heads.append(exchange(d_attn))
-    shard_out = scatter(part_out)
     back = []
     for row in range(rows):
-        back.append(
-            exchange(attend_back(packed[row], d_heads[row], results[row], logs[row], start[row : row + 1], low[row]))
-        )
-    back[1], (out_part, down_sum) = tie(back[1], (out_part, down_sum))
+        grads = attend_back(packed[row], d_heads[row], results[row], logs[row], start[row : row + 1], low[row])
+        if row == 0:
+            grads, keep = tie(grads, keep)
+        back.append(exchange(grads))
     cut = width // 2
-    out_sum = jnp.concatenate([halving(out_part[:, :cut], False), halving(out_part[:, cut:], True)], axis=1)
+    half_out = part_out.shape[1] // 2
+    trading = [
+        Halving(out_part[:, :cut], dp, False),
+        Halving(out_part[:, cut:], dp, True),
+        Halving(part_out[:, :half_out], dp, False),
+        Halving(part_out[:, half_out:], dp, True),
+    ]
+    moved = [t.send() for t in trading]
+    back[0], (moved, recv_sum) = tie(back[0], (moved, recv_sum))
+    recv = lax.psum(recv_sum, "seq", axis_index_groups=groups)
+    while trading[0].order:
+        for t, m in zip(trading, moved):
+            t.add(m)
+        moved = [t.send() for t in trading]
+    early = early_sum(jnp.concatenate(d_logit, axis=0))
+    back[1], (moved, down_sum, early) = tie(back[1], (moved, down_sum, early))
+    for t, m in zip(trading, moved):
+        t.add(m)
+    out_sum = jnp.concatenate([trading[0].x, trading[1].x], axis=1)
+    shard_out = jnp.concatenate([trading[2].x, trading[3].x], axis=1)
     output = (mid + out_sum.astype(F32)).astype(BF).reshape(rows, tok, width)
     for row in range(rows):
         dpr, qs, ks = unpack_heads(back[row], proj, cos, sin, q_gain, k_gain, row, chips, chip_tok)
@@ -819,8 +862,16 @@
     d_logit = jnp.concatenate(d_logit, axis=0)
     half = width // 2
     part_qkv = [dot_tn(d_proj, normed_a[:, a : a + half], BF) for a in (0, half)]
-    part_qkv, gu_sum = tie_all(part_qkv, gu_sum)
-    shard_qkv = [scatter(p) for p in part_qkv]
+    trading = [Halving(p, dp, flip) for p, flip in zip(part_qkv, (False, True))]
+    moved = [t.send() for t in trading]
+    moved, recv = tie_all(moved, recv)
+    while trading[0].order:
+        for t, m in zip(trading, moved):
+            t.add(m)
+        moved = [t.send() for t in trading]
+    for t, m in zip(trading, moved):
+        t.add(m)
+    shard_qkv = [t.x for t in trading]
     d_norm_part = (dot_nn(d_proj, qkv_full) + dot_nn(d_logit, gate_core)).astype(BF)
     d_norm_part = d_norm_part.reshape(rows, CORES, tok, width)
     d_norm_other = swap(pick(d_norm_part[:, 1], d_norm_part[:, 0]))
@@ -834,30 +885,31 @@
         d_mid.reshape(rows, tok, width) + own_factor * weighted_a - own_in * own_factor**3 * inner_a
     ).astype(BF)
 
-    part_gate = dot_tn(d_logit, normed_a)[:CORE_Q]
-    zero = jnp.zeros_like(part_gate)
-    part_gate = jnp.stack(
-        [pick(part_gate, zero).reshape(-1, GROUP, width), pick(zero, part_gate).reshape(-1, GROUP, width)], 1
-    )
-    part_gate = part_gate.reshape(QUERY_HEADS, width)
     heads = jnp.concatenate([jnp.sum(q_sum, axis=0), jnp.sum(k_sum, axis=0)])
     heads = jnp.pad(heads, (0, width - heads.shape[0]))
-    early = total_sum(jnp.concatenate([part_gate, part_ffn[None], jnp.zeros((7, width), F32)], axis=0))
     late = total_sum(jnp.stack([part_attn, heads]))
     grad_w_gate = lax.dynamic_slice_in_dim(early, me * gate_count, gate_count, 0)
 
     mid_cut = down_sum.shape[1] // 2
     line = Line(chips, chip)
-    down_a, down_b, out_done, qkv_a, qkv_b = line.pipeline(
-        [down_sum[:, :mid_cut], down_sum[:, mid_cut:], shard_out, *shard_qkv]
+    sent = lax.ppermute(recv, "dp", trade)
+
+    def join_early(done):
+        down_done = jnp.concatenate(done[:2], axis=1)
+        places = [unit_block.index(b) ^ me for b in range(dp)]
+        return [
+            join_units([keep, sent], [swap(keep), swap(sent)], core, upper.astype(jnp.int32)),
+            join_blocks(down_done, swap(down_done), core, places),
+        ]
+
+    def join_late(done):
+        return [join_cols([done[2]], [swap(done[2])], core, GROUP * HEAD)]
+
+    sums, ((grad_gu, grad_down), (grad_out,)) = line.pipeline(
+        [down_sum[:, :mid_cut], down_sum[:, mid_cut:], shard_out, *shard_qkv], {5: join_early, 6: join_late}
     )
-    sent = lax.ppermute(gu_sum[quarter:], "dp", trade)
-    keep = gu_sum[:quarter]
-    down_done = jnp.concatenate([down_a, down_b], axis=1)
-    grad_gu = join_units([keep, sent], [swap(keep), swap(sent)], core, upper.astype(jnp.int32))
-    grad_down = join_blocks(down_done, swap(down_done), core, [unit_block.index(b) ^ me for b in range(dp)])
-    grad_out = join_cols([out_done], [swap(out_done)], core, GROUP * HEAD)
-    grad_qkv = join_rows([qkv_a, qkv_b], [swap(qkv_a), swap(qkv_b)], core, jnp.where(q_shard, GROUP, 1), HEAD)
+    qkv_sum = sums[3:]
+    grad_qkv = join_rows(qkv_sum, [swap(p) for p in qkv_sum], core, jnp.where(q_shard, GROUP, 1), HEAD)
     return (
         output,
         grad_input,

time: 1430 us -> 1410 us (0.986)
  waiting for transfers between devices: 640 us -> 579 us
  other arithmetic: 139 us -> 187 us
    all_to_all x7, waiting for transfers between devices: 225 us -> 79 us  [exchange(): return lax.all_to_all(x, 'seq', 0, 0, axis_index_groups=groups, tiled=True)]
    psum x1 -> x2, waiting for transfers between devices: 0.01 us -> 124 us  [the longest x1 66.3 us: shards(): recv = lax.psum(recv_sum, 'seq', axis_index_groups=groups)]
    ppermute x12, waiting for transfers between devices: 76.3 us -> 54.1 us  [total_sum(): x = x + lax.ppermute(x, name, [(s, s ^ step) for s in range(size)])]
    add x4 -> x12, other arithmetic: 1.56 us -> 23 us  [add(): self.x = self.keep + moved]
    ppermute x5 -> x13, waiting for transfers between devices: 29.7 us -> 10.3 us  [the longest x12 9.57 us: send(): return lax.ppermute(jnp.where(mark, low, high), 'dp', pairs)]
    ppermute x15, waiting for transfers between devices: 91.5 us -> 109 us  [send(): return (x, lax.ppermute(x, 'seq', self.stages[stage]))]
    ppermute x5 -> x13, starting transfers between devices: 2.92 us -> 17.7 us  [the longest x12 16.1 us: send(): return lax.ppermute(jnp.where(mark, low, high), 'dp', pairs)]
  transfers between devices with their start and end apart: 71 -> 77, of which waited for: 34 -> 28; matrix products, arithmetic and copies ran while one was open for 23% -> 26% of each run, Pallas kernels for 9% -> 10%
where the time goes in v6:
time: 1410 us
  waiting for transfers between devices  579 us (41%)
  matrix products  251 us (18%)
  other arithmetic  187 us (13%)
  Pallas kernels  145 us (10%)
  starting transfers between devices  128 us (9%)
  blocking collectives  52.5 us (4%)
  local copies, waits for them, and re-layouts  47.9 us (3%)
  between operations  16.4 us (1%)
    all_gather x4, waiting for transfers between devices, gather(): return lax.all_gather(x, 'dp', axis=0, tiled=True)  146 us
    ppermute x15, waiting for transfers between devices, send(): return (x, lax.ppermute(x, 'seq', self.stages[stage]))  109 us
    dot_general x7, matrix products, dot_nt(): lax.dot_general(left, right, (((1,), (1,)), ((), ())), preferred_element_...  97.1 us
    dot_general x7, matrix products, dot_nn(): lax.dot_general(left, right, (((1,), (0,)), ((), ())), preferred_element_...  79.6 us
    all_to_all x7, waiting for transfers between devices, exchange(): return lax.all_to_all(x, 'seq', 0, 0, axis_index_groups=groups, tiled=True)  79 us
    dot_general x7, matrix products, dot_tn(): lax.dot_general(left, right, (((0,), (0,)), ((), ())), preferred_element_...  74.5 us
    psum x1, waiting for transfers between devices, shards(): recv = lax.psum(recv_sum, 'seq', axis_index_groups=groups)  66.3 us
    psum x1, waiting for transfers between devices, shards(): keep = lax.psum(keep_sum, 'seq', axis_index_groups=groups)  58.1 us
  transfers between devices with their start and end apart: 77, of which 28 were waited for; matrix products, arithmetic and copies ran while one was open for 26% of the time, Pallas kernels for 10%

profile of v6, /device:TPU:0, one launch (start us, length us, event | category | flops | bytes accessed | tf_op | source)
XLA Modules:
  0.0 1407.1 jit_solution(7836911078274677071)
XLA Ops:
  30.5 6.6 select_select_fusion
  53.1 54.4 %all-gather.7.cloned.1.call-done = bf16[2048,2048]{1,0:T(8,128)(2,1)} async-done(((bf16[512,2048]{1,0:T(8,128)(2,1)}), bf16[2048,2048]{1,0:T(8,128)(2,1)}) %all-gather.7.cloned.1.call-update) | async-done | bytes 8388624 | tf_op jit(solution)/shard_map/all_gather | solution.py:663
  117.3 11.1 fusion.68.proj_ref
  128.4 6.2 pack_heads.3
  134.5 52.5 %all_to_all.40.q_ref.k_ref.v_ref = bf16[4,512,512]{2,1,0:T(8,128)(2,1)} all-to-all(bf16[4,512,512]{2,1,0:T(8,128)(2,1)} %pack_heads.3), channel_id=1, replica_groups={{0,2,4,6},{1,3,5,7},{8,10,12,14},{9,11,13,15},{16,18,20,22},{17,19,21,2..., dimensions={0} | all-to-all | bytes 4194304 | tf_op jit(solution)/shard_map/all_to_all | solution.py:648
  187.1 6.2 pack_heads.2
  205.3 10.8 attend.3
  216.0 28.0 %all-to-all-done.q_ref.k_ref.v_ref = bf16[4,512,512]{2,1,0:T(8,128)(2,1)S(1)} async-done(((bf16[4,512,512]{2,1,0:T(8,128)(2,1)}), bf16[4,512,512]{2,1,0:T(8,128)(2,1)S(1)}, u32[]{:S(2)}, u32[]{:S(2)}) %all-to-all-start) | async-done | bytes 2097184 | tf_op jit(solution)/shard_map/all_to_all | solution.py:648
  253.5 14.2 %collective-permute-done.3 = bf16[256,1536]{1,0:T(8,128)(2,1)S(1)} collective-permute-done((bf16[256,1536]{1,0:T(8,128)(2,1)}, bf16[256,1536]{1,0:T(8,128)(2,1)S(1)}, u32[]{:S(2)}, u32[]{:S(2)}) %collective-permute-start.3) | collective-permute-done | bytes 786464 | tf_op jit(solution)/shard_map/ppermute | solution.py:681
  268.6 10.8 attend.2
  279.4 4.8 all-to-all-start.1
  286.8 5.8 convolution_convert_fusion.10
  293.7 14.3 %all-to-all-done.1.res_ref = bf16[4,512,256]{2,1,0:T(8,128)(2,1)S(1)} async-done(((bf16[4,512,256]{2,1,0:T(8,128)(2,1)}), bf16[4,512,256]{2,1,0:T(8,128)(2,1)S(1)}, u32[]{:S(2)}, u32[]{:S(2)}) %all-to-all-start.1) | async-done | bytes 1048608 | tf_op jit(solution)/shard_map/all_to_all | solution.py:648
  311.6 4.9 convolution_convert_fusion.11
  327.1 4.8 slice_select_fusion.4
  336.7 5.1 pad_maximum_fusion
  347.7 20.2 %all-gather.13.cloned.1.call-done = bf16[2048,2048]{1,0:T(8,128)(2,1)} async-done(((bf16[512,2048]{1,0:T(8,128)(2,1)}), bf16[2048,2048]{1,0:T(8,128)(2,1)}) %all-gather.13.cloned.1.call-update) | async-done | bytes 8388624 | tf_op jit(solution)/shard_map/all_gather | solution.py:663
  367.9 18.6 %convolution_convert_fusion.3 = bf16[2048,1536]{1,0:T(8,128)(2,1)} fusion(bf16[2048,2048]{1,0:T(8,128)(2,1)} %all-gather.13.cloned.1.call-done, bf16[2048,1536]{1,0:T(8,128)(2,1)} %bitcast.262), kind=kOutput, calls=%fused_computation.24 | convolution fusion | flops 12888047616 | bytes 20971520 | tf_op jit(solution)/shard_map/dot_general | solution.py:33
  386.5 71.2 %all-gather.11.cloned.1.call-done = bf16[2048,2048]{1,0:T(8,128)(2,1)} async-done(((bf16[512,2048]{1,0:T(8,128)(2,1)}), bf16[2048,2048]{1,0:T(8,128)(2,1)}) %all-gather.11.cloned.1.call-update) | async-done | bytes 8388624 | tf_op jit(solution)/shard_map/all_gather | solution.py:663
  457.7 19.8 %convolution_convert_fusion.1 = bf16[2048,1536]{1,0:T(8,128)(2,1)} fusion(bf16[2048,2048]{1,0:T(8,128)(2,1)} %all-gather.11.cloned.1.call-done, bf16[3072,2048]{1,0:T(8,128)(2,1)} %param.21, pred[]{:T(512)S(6)} %ge.19), kind=kOutput, calls=%fused_computation.22 | convolution fusion | flops 12891193344 | bytes 27262976 | tf_op jit(solution)/shard_map/dot_general | solution.py:29
  477.5 31.7 %select_convert_fusion = (bf16[2048,1536]{1,0:T(8,128)(2,1)}, bf16[2048,1536]{1,0:T(8,128)(2,1)}, bf16[2048,1536]{1,0:T(8,128)(2,1)}) fusion(bf16[2048,1536]{1,0:T(8,128)(2,1)} %convolution_convert_fusion.3, pred[]{:T(512)S(6)} %ge.19, bf16[2048,1536]{1,0:T(8,128)(2,1)} %convolution_convert_fusion.1, bf16[2048,2048]{1,0:T(8,128)(2,1)} %all-gather.11.cloned.1.call-done, ...), kind=kOutput, calls=%fused_computation.14 | convolution fusion | flops 12950962176 | bytes 46137344 | tf_op jit(solution)/shard_map/dot_general | solution.py:29
  509.2 21.9 %fusion.45 = f32[2048,2048]{1,0:T(8,128)} fusion(bf16[2048,1536]{1,0:T(8,128)(2,1)} %get-tuple-element.229, bf16[3072,2048]{1,0:T(8,128)(2,1)} %param.21, pred[]{:T(512)S(6)} %ge.19), kind=kOutput, calls=%fused_computation.156 | convolution fusion | flops 12888047616 | bytes 35651584 | tf_op jit(solution)/shard_map/dot_general | solution.py:33
  531.0 19.1 %add_convert_fusion = bf16[2048,2048]{1,0:T(8,128)(2,1)} fusion(f32[2048,2048]{1,0:T(8,128)} %fusion.45, bf16[2048,1536]{1,0:T(8,128)(2,1)S(1)} %copy-done.87, bf16[1536,2048]{1,0:T(8,128)(2,1)} %pad_maximum_fusion.1), kind=kOutput, calls=%fused_computation.3 | convolution fusion | flops 12893290496 | bytes 37748736 | tf_op jit(solution)/shard_map/dot_general | solution.py:33
  550.2 17.8 %convolution_convert_fusion.5 = bf16[1536,2048]{1,0:T(8,128)(2,1)S(1)} fusion(bf16[2048,1536]{1,0:T(8,128)(2,1)} %get-tuple-element.228, bf16[2048,2048]{1,0:T(8,128)(2,1)} %all-gather.11.cloned.1.call-done), kind=kOutput, calls=%fused_computation.26 | convolution fusion | flops 12888047616 | bytes 20971520 | tf_op jit(solution)/shard_map/dot_general | solution.py:37
  571.3 18.2 %convolution_convert_fusion.6 = bf16[1536,2048]{1,0:T(8,128)(2,1)S(1)} fusion(bf16[2048,1536]{1,0:T(8,128)(2,1)} %get-tuple-element.229, bf16[2048,2048]{1,0:T(8,128)(2,1)} %all-gather.11.cloned.1.call-done), kind=kOutput, calls=%fused_computation.27 | convolution fusion | flops 12888047616 | bytes 20971520 | tf_op jit(solution)/shard_map/dot_general | solution.py:37
  592.9 17.0 %convolution_convert_fusion.4 = bf16[2048,1536]{1,0:T(8,128)(2,1)S(1)} fusion(bf16[2048,2048]{1,0:T(8,128)(2,1)S(1)} %bitcast.292, bf16[2048,1536]{1,0:T(8,128)(2,1)} %convolution_convert_fusion.1, bf16[2048,1536]{1,0:T(8,128)(2,1)} %get-tuple-element.290, pred[]{:T(512)S(6)} %ge.19), kind=kOutput, calls=%fused_computation.25 | convolution fusion | flops 12919504896 | bytes 27262976 | tf_op jit(solution)/shard_map/dot_general | solution.py:37
  615.3 21.3 %reduce-scatter.2.cloned.1.call-done = bf16[512,2048]{1,0:T(8,128)(2,1)} async-done(((bf16[2048,2048]{1,0:T(8,128)(2,1)}), bf16[512,2048]{1,0:T(8,128)(2,1)}) %reduce-scatter.2.cloned.1.call-update) | async-done | bytes 2097168 | tf_op jit(solution)/shard_map/reduce_scatter | solution.py:660
  636.6 9.6 select_add_fusion
  650.4 5.1 fusion.64
  655.5 21.9 %convolution_convert_fusion = bf16[2048,2048]{1,0:T(8,128)(2,1)} fusion(bf16[2048,1536]{1,0:T(8,128)(2,1)} %bitcast.263, bf16[2048,1536]{1,0:T(8,128)(2,1)} %convolution_convert_fusion.1, bf16[2048,1536]{1,0:T(8,128)(2,1)} %get-tuple-element.290, pred[]{:T(512)S(6)} %ge.19), kind=kOutput, calls=%fused_computation.21 | convolution fusion | flops 12920553472 | bytes 27262976 | tf_op jit(solution)/shard_map/dot_general | solution.py:29
  692.1 4.9 all-to-all-start.4
  700.2 6.3 convolution_convert_fusion.9
  714.1 36.6 %all-to-all-done.4.grad_ref = bf16[4,512,256]{2,1,0:T(8,128)(2,1)S(1)} async-done(((bf16[4,512,256]{2,1,0:T(8,128)(2,1)}), bf16[4,512,256]{2,1,0:T(8,128)(2,1)S(1)}, u32[]{:S(2)}, u32[]{:S(2)}) %all-to-all-start.4) | async-done | bytes 1048608 | tf_op jit(solution)/shard_map/all_to_all | solution.py:648
  754.9 19.9 %attend_back.2 = bf16[4,512,512]{2,1,0:T(8,128)(2,1)} custom-call(s32[4]{0:T(128)} %get-tuple-element.288.low_ref, bf16[4,512,512]{2,1,0:T(8,128)(2,1)} %copy-done, bf16[4,512,512]{2,1,0:T(8,128)(2,1)} %copy-done, bf16[4,512,512]{2,1,0:T(8,128)(2,1)} %copy-done, bf16[4,512,256]{2,1,0:T(8,128)(2,1)} %copy-done.46, ...), custom_call_target="tpu_custom_call" | custom-call | tf_op jit(solution)/shard_map/attend_back/pallas_call | solution.py:281
  774.8 58.1 %all-reduce.5.cloned.1.call-done.keep_ref = bf16[768,2048]{1,0:T(8,128)(2,1)} async-done(((bf16[768,2048]{1,0:T(8,128)(2,1)}), bf16[768,2048]{1,0:T(8,128)(2,1)}) %all-reduce.5.cloned.1.call-update) | async-done | bytes 3145744 | tf_op jit(solution)/shard_map/psum | solution.py:792
  833.0 4.9 all-to-all-start.5
  858.6 17.8 %collective-permute-done.26 = f32[24,2048]{1,0:T(8,128)S(1)} collective-permute-done((f32[24,2048]{1,0:T(8,128)S(1)}, f32[24,2048]{1,0:T(8,128)S(1)}, u32[]{:S(2)}, u32[]{:S(2)}) %collective-permute-start.26) | collective-permute-done | bytes 196640 | tf_op jit(solution)/shard_map/ppermute | solution.py:655
  877.0 4.6 collective-permute-start.27
  881.6 19.8 %attend_back.3 = bf16[4,512,512]{2,1,0:T(8,128)(2,1)} custom-call(s32[4]{0:T(128)} %get-tuple-element.289.low_ref, bf16[4,512,512]{2,1,0:T(8,128)(2,1)} %all_to_all.40.q_ref.k_ref.v_ref, bf16[4,512,512]{2,1,0:T(8,128)(2,1)} %all_to_all.40.q_ref.k_ref.v_ref, bf16[4,512,512]{2,1,0:T(8,128)(2,1)} %all_to_all.40.q_ref.k_ref.v_ref, ...), custom_call_target="tpu_custom_call" | custom-call | tf_op jit(solution)/shard_map/attend_back/pallas_call | solution.py:281
  913.4 9.3 collective-permute-done.28
  945.5 14.2 %collective-permute-done.23 = bf16[256,1536]{1,0:T(8,128)(2,1)S(1)} collective-permute-done((bf16[256,1536]{1,0:T(8,128)(2,1)S(1)}, bf16[256,1536]{1,0:T(8,128)(2,1)S(1)}, u32[]{:S(2)}, u32[]{:S(2)}) %collective-permute-start.23) | collective-permute-done | bytes 786464 | tf_op jit(solution)/shard_map/ppermute | solution.py:681
  963.1 23.3 %collective-permute-done.29 = f32[24,2048]{1,0:T(8,128)S(1)} collective-permute-done((f32[24,2048]{1,0:T(8,128)S(1)}, f32[24,2048]{1,0:T(8,128)S(1)}, u32[]{:S(2)}, u32[]{:S(2)}) %collective-permute-start.29) | collective-permute-done | bytes 196640 | tf_op jit(solution)/shard_map/ppermute | solution.py:655
  987.1 7.5 unpack_heads.2
  997.8 7.5 unpack_heads.3
  1008.6 7.2 convolution_convert_fusion.7
  1015.8 5.2 convolution_convert_fusion.8
  1032.0 50.6 %collective-permute-done.36 = bf16[4,128,1536]{2,1,0:T(8,128)(2,1)S(1)} collective-permute-done((bf16[4,128,1536]{2,1,0:T(8,128)(2,1)S(1)}, bf16[4,128,1536]{2,1,0:T(8,128)(2,1)S(1)}, u32[]{:S(2)}, u32[]{:S(2)}) %collective-permute-start.36) | collective-permute-done | bytes 1572896 | tf_op jit(solution)/shard_map/ppermute | solution.py:550
  1085.9 8.3 collective-permute-start.38
  1096.7 66.3 %all-reduce.7.cloned.1.call-done = bf16[768,2048]{1,0:T(8,128)(2,1)} async-done(((bf16[768,2048]{1,0:T(8,128)(2,1)}), bf16[768,2048]{1,0:T(8,128)(2,1)}) %all-reduce.7.cloned.1.call-update) | async-done | bytes 3145744 | tf_op jit(solution)/shard_map/psum | solution.py:844
  1178.9 9.2 collective-permute-start.41
  1193.1 9.5 collective-permute-done.44
  1209.1 7.0 collective-permute-done.39
  1225.0 11.5 fusion.70
  1236.9 6.0 collective-permute-done.47
  1243.0 17.7 %collective-permute-done.45 = bf16[4,128,1536]{2,1,0:T(8,128)(2,1)S(1)} collective-permute-done((bf16[4,128,1536]{2,1,0:T(8,128)(2,1)S(1)}, bf16[4,128,1536]{2,1,0:T(8,128)(2,1)S(1)}, u32[]{:S(2)}, u32[]{:S(2)}) %collective-permute-start.45) | collective-permute-done | bytes 1572896 | tf_op jit(solution)/shard_map/ppermute | solution.py:550
  1263.6 4.7 collective-permute-start.51
  1272.5 14.8 %collective-permute-done.49 = bf16[512,1024]{1,0:T(8,128)(2,1)S(1)} collective-permute-done((bf16[512,1024]{1,0:T(8,128)(2,1)S(1)}, bf16[512,1024]{1,0:T(8,128)(2,1)S(1)}, u32[]{:S(2)}, u32[]{:S(2)}) %collective-permute-start.49) | collective-permute-done | bytes 1048608 | tf_op jit(solution)/shard_map/ppermute | solution.py:550
  1294.5 6.0 fusion.22
  1315.2 5.0 collective-permute-start.32
  1320.2 16.7 %join_units.1 = f32[3072,2048]{1,0:T(8,128)} custom-call(s32[2]{0:T(128)} %pad_add_fusion.1.which_ref, bf16[768,2048]{1,0:T(8,128)(2,1)} %all-reduce.5.cloned.1.call-done.keep_ref, bf16[768,2048]{1,0:T(8,128)(2,1)} %collective-permute-done.54.keep_other_ref, bf16[768,2048]{1,0:T(8,128)(2,1)} %collective-permute-done.55.sent_ref, ...), custom_call_target="tpu_custom_call" | custom-call | tf_op jit(solution)/shard_map/join_units/pallas_call | solution.py:478
  1336.9 12.1 join_blocks.1
  1365.3 6.4 join_cols.1
  1371.8 8.7 collective-permute-done.58
  1391.3 8.4 join_rows.1
  (476 shorter events, 321.2 us)
Async XLA Ops:
  7.2 100.3 %all-gather.7.cloned.1.call-start = ((), (), s32[]{:S(2)}) async-start(), calls=%async_computation.9 | async-start | bytes 10485760 | tf_op jit(solution)/shard_map/all_gather | solution.py:663
  15.7 271.1 %all-gather.9.cloned.1.call-start = ((), (), s32[]{:S(2)}) async-start(), calls=%async_computation.10 | async-start | bytes 5242880 | tf_op jit(solution)/shard_map/all_gather | solution.py:663
  15.8 23.6 %collective-permute-start.4 = (bf16[16,2048]{1,0:T(8,128)(2,1)S(1)}, bf16[16,2048]{1,0:T(8,128)(2,1)S(1)}, u32[]{:S(2)}, u32[]{:S(2)}) collective-permute-start(bf16[16,2048]{1,0:T(8,128)(2,1)S(1)} %constant_dynamic-update-slice_fusion.4), channel_id=1, source_target_pairs={{0,8},{8,0},{16,24},{24,16},{1,9},{9,1},{17,25},{25,17},{2,10},{10... | collective-permute-start | bytes 196616 | tf_op jit(solution)/shard_map/ppermute | solution.py:655
  18.8 27.1 %collective-permute-start = (bf16[2,256,2048]{2,1,0:T(8,128)(2,1)S(1)}, bf16[2,256,2048]{2,1,0:T(8,128)(2,1)}, u32[]{:S(2)}, u32[]{:S(2)}) collective-permute-start(bf16[2,256,2048]{2,1,0:T(8,128)(2,1)S(1)} %copy-done.1), channel_id=1, source_target_pairs={{0,1},{1,0},{2,3},{3,2},{4,5},{5,4},{6,7},{7,6},{8,9},{9,8},{10,11... | collective-permute-start | bytes 6291464 | tf_op jit(solution)/shard_map/ppermute | solution.py:638
  21.6 305.4 %all-gather.15.cloned.1.call-start = ((), (), s32[]{:S(2)}) async-start(), calls=%async_computation.16 | async-start | bytes 9437184 | tf_op jit(solution)/shard_map/all_gather | solution.py:710
  107.5 260.4 %all-gather.13.cloned.1.call-start = ((), (), s32[]{:S(2)}) async-start(), calls=%async_computation.12 | async-start | bytes 10485760 | tf_op jit(solution)/shard_map/all_gather | solution.py:663
  193.3 50.8 %all-to-all-start = ((bf16[4,512,512]{2,1,0:T(8,128)(2,1)}), bf16[4,512,512]{2,1,0:T(8,128)(2,1)S(1)}, u32[]{:S(2)}, u32[]{:S(2)}) async-start(bf16[4,512,512]{2,1,0:T(8,128)(2,1)} %pack_heads.2), calls=%async_computation | async-start | bytes 4194304 | tf_op jit(solution)/shard_map/all_to_all | solution.py:648
  202.1 47.3 %collective-permute-start.1 = (bf16[256,1536]{1,0:T(8,128)(2,1)}, bf16[256,1536]{1,0:T(8,128)(2,1)}, u32[]{:S(2)}, u32[]{:S(2)}) collective-permute-start(bf16[256,1536]{1,0:T(8,128)(2,1)} %get-tuple-element.259), channel_id=1, source_target_pairs={{0,8},{8,0},{16,24},{24,16},{1,9},{9,1},{17,25},{25,17},{2,10},{10... | collective-permute-start | bytes 2359304 | tf_op jit(solution)/shard_map/ppermute | solution.py:681
  204.1 47.3 %collective-permute-start.2 = (bf16[256,1536]{1,0:T(8,128)(2,1)}, bf16[256,1536]{1,0:T(8,128)(2,1)}, u32[]{:S(2)}, u32[]{:S(2)}) collective-permute-start(bf16[256,1536]{1,0:T(8,128)(2,1)} %get-tuple-element.258), channel_id=1, source_target_pairs={{0,16},{8,24},{16,0},{24,8},{1,17},{9,25},{17,1},{25,9},{2,18},{10... | collective-permute-start | bytes 2359304 | tf_op jit(solution)/shard_map/ppermute | solution.py:681
  244.1 35.3 %all-to-all-start.3 = ((bf16[4,512,256]{2,1,0:T(8,128)(2,1)}), bf16[4,512,256]{2,1,0:T(8,128)(2,1)S(1)}, u32[]{:S(2)}, u32[]{:S(2)}) async-start(bf16[4,512,256]{2,1,0:T(8,128)(2,1)} %get-tuple-element.123.res_ref), calls=%async_computation.3 | async-start | bytes 2097152 | tf_op jit(solution)/shard_map/all_to_all | solution.py:648
  247.8 19.8 %collective-permute-start.3 = (bf16[256,1536]{1,0:T(8,128)(2,1)}, bf16[256,1536]{1,0:T(8,128)(2,1)S(1)}, u32[]{:S(2)}, u32[]{:S(2)}) collective-permute-start(bf16[256,1536]{1,0:T(8,128)(2,1)} %get-tuple-element.257), channel_id=1, source_target_pairs={{0,24},{8,16},{16,8},{24,0},{1,25},{9,17},{17,9},{25,1},{2,26},{10... | collective-permute-start | bytes 2359304 | tf_op jit(solution)/shard_map/ppermute | solution.py:681
  279.4 28.6 %all-to-all-start.1 = ((bf16[4,512,256]{2,1,0:T(8,128)(2,1)}), bf16[4,512,256]{2,1,0:T(8,128)(2,1)S(1)}, u32[]{:S(2)}, u32[]{:S(2)}) async-start(bf16[4,512,256]{2,1,0:T(8,128)(2,1)} %get-tuple-element.119.res_ref), calls=%async_computation.1 | async-start | bytes 2097152 | tf_op jit(solution)/shard_map/all_to_all | solution.py:648
  284.2 173.5 %all-gather.11.cloned.1.call-start = ((), (), s32[]{:S(2)}) async-start(), calls=%async_computation.11 | async-start | bytes 10485760 | tf_op jit(solution)/shard_map/all_gather | solution.py:663
  293.7 23.0 %collective-permute-start.7 = (bf16[256,2048]{1,0:T(8,128)(2,1)}, bf16[256,2048]{1,0:T(8,128)(2,1)}, u32[]{:S(2)}, u32[]{:S(2)}) collective-permute-start(bf16[256,2048]{1,0:T(8,128)(2,1)} %broadcast_select_fusion.22), channel_id=1, source_target_pairs={{0,1},{1,0},{2,3},{3,2},{4,5},{5,4},{6,7},{7,6},{8,9},{9,8},{10,11... | collective-permute-start | bytes 3145736 | tf_op jit(solution)/shard_map/ppermute | solution.py:638
  326.0 310.6 %reduce-scatter.2.cloned.1.call-start = ((), (), s32[]{:S(2)}) async-start(), calls=%async_computation.13 | async-start | bytes 10485760 | tf_op jit(solution)/shard_map/reduce_scatter | solution.py:660
  550.1 282.8 %all-reduce.5.cloned.1.call-start = ((), (), s32[]{:S(2)}) async-start(), calls=%async_computation.14 | async-start | bytes 6291456 | tf_op jit(solution)/shard_map/psum | solution.py:792
  571.3 42.4 %collective-permute-start.11 = (bf16[768,2048]{1,0:T(8,128)(2,1)S(1)}, bf16[768,2048]{1,0:T(8,128)(2,1)S(1)}, u32[]{:S(2)}, u32[]{:S(2)}) collective-permute-start(bf16[768,2048]{1,0:T(8,128)(2,1)S(1)} %slice_select_fusion.2), channel_id=1, source_target_pairs={{0,1},{1,0},{2,3},{3,2},{4,5},{5,4},{6,7},{7,6},{8,9},{9,8},{10,11... | collective-permute-start | bytes 9437192 | tf_op jit(solution)/shard_map/ppermute | solution.py:638
  592.1 23.2 %collective-permute-start.10 = (bf16[768,2048]{1,0:T(8,128)(2,1)S(1)}, bf16[768,2048]{1,0:T(8,128)(2,1)}, u32[]{:S(2)}, u32[]{:S(2)}) collective-permute-start(bf16[768,2048]{1,0:T(8,128)(2,1)S(1)} %slice_select_fusion.3), channel_id=1, source_target_pairs={{0,1},{1,0},{2,3},{3,2},{4,5},{5,4},{6,7},{7,6},{8,9},{9,8},{10,11... | collective-permute-start | bytes 9437192 | tf_op jit(solution)/shard_map/ppermute | solution.py:638
  613.5 63.8 %collective-permute-start.13 = (bf16[4,256,1536]{2,1,0:T(8,128)(2,1)}, bf16[4,256,1536]{2,1,0:T(8,128)(2,1)}, u32[]{:S(2)}, u32[]{:S(2)}) collective-permute-start(bf16[4,256,1536]{2,1,0:T(8,128)(2,1)} %fusion.27), channel_id=1, source_target_pairs={{0,1},{1,0},{2,3},{3,2},{4,5},{5,4},{6,7},{7,6},{8,9},{9,8},{10,11... | collective-permute-start | bytes 9437192 | tf_op jit(solution)/shard_map/ppermute | solution.py:638
  655.5 21.9 %collective-permute-start.12 = (bf16[2,256,2048]{2,1,0:T(8,128)(2,1)}, bf16[2,256,2048]{2,1,0:T(8,128)(2,1)}, u32[]{:S(2)}, u32[]{:S(2)}) collective-permute-start(bf16[2,256,2048]{2,1,0:T(8,128)(2,1)} %bitcast.22), channel_id=1, source_target_pairs={{0,1},{1,0},{2,3},{3,2},{4,5},{5,4},{6,7},{7,6},{8,9},{9,8},{10,11... | collective-permute-start | bytes 6291464 | tf_op jit(solution)/shard_map/ppermute | solution.py:638
  692.1 58.6 %all-to-all-start.4 = ((bf16[4,512,256]{2,1,0:T(8,128)(2,1)}), bf16[4,512,256]{2,1,0:T(8,128)(2,1)S(1)}, u32[]{:S(2)}, u32[]{:S(2)}) async-start(bf16[4,512,256]{2,1,0:T(8,128)(2,1)} %get-tuple-element.138), calls=%async_computation.5 | async-start | bytes 2097152 | tf_op jit(solution)/shard_map/all_to_all | solution.py:648
  750.8 82.2 %all-to-all-start.6 = ((bf16[4,512,256]{2,1,0:T(8,128)(2,1)}), bf16[4,512,256]{2,1,0:T(8,128)(2,1)S(1)}, u32[]{:S(2)}, u32[]{:S(2)}) async-start(bf16[4,512,256]{2,1,0:T(8,128)(2,1)} %get-tuple-element.146), calls=%async_computation.7 | async-start | bytes 2097152 | tf_op jit(solution)/shard_map/all_to_all | solution.py:648
  833.0 68.5 %all-to-all-start.5 = ((bf16[4,512,512]{2,1,0:T(8,128)(2,1)}), bf16[4,512,512]{2,1,0:T(8,128)(2,1)}, u32[]{:S(2)}, u32[]{:S(2)}) async-start(bf16[4,512,512]{2,1,0:T(8,128)(2,1)} %attend_back.2), calls=%async_computation.6 | async-start | bytes 4194304 | tf_op jit(solution)/shard_map/all_to_all | solution.py:648
  847.8 78.5 %collective-permute-start.14 = (bf16[2,512,1024]{2,1,0:T(8,128)(2,1)}, bf16[2,512,1024]{2,1,0:T(8,128)(2,1)}, u32[]{:S(2)}, u32[]{:S(2)}) collective-permute-start(bf16[2,512,1024]{2,1,0:T(8,128)(2,1)} %select_bitcast_fusion.2), channel_id=1, source_target_pairs={{0,8},{8,0},{16,24},{24,16},{1,9},{9,1},{17,25},{25,17},{2,10},{10... | collective-permute-start | bytes 6291464 | tf_op jit(solution)/shard_map/ppermute | solution.py:533
  851.5 74.8 %collective-permute-start.15 = (bf16[2,512,1024]{2,1,0:T(8,128)(2,1)}, bf16[2,512,1024]{2,1,0:T(8,128)(2,1)}, u32[]{:S(2)}, u32[]{:S(2)}) collective-permute-start(bf16[2,512,1024]{2,1,0:T(8,128)(2,1)} %bitcast.30), channel_id=1, source_target_pairs={{0,16},{8,24},{16,0},{24,8},{1,17},{9,25},{17,1},{25,9},{2,18},{10... | collective-permute-start | bytes 6291464 | tf_op jit(solution)/shard_map/ppermute | solution.py:533
  854.0 71.0 %collective-permute-start.16 = (bf16[2,512,512]{2,1,0:T(8,128)(2,1)}, bf16[2,512,512]{2,1,0:T(8,128)(2,1)}, u32[]{:S(2)}, u32[]{:S(2)}) collective-permute-start(bf16[2,512,512]{2,1,0:T(8,128)(2,1)} %select_bitcast_fusion.7), channel_id=1, source_target_pairs={{0,8},{8,0},{16,24},{24,16},{1,9},{9,1},{17,25},{25,17},{2,10},{10... | collective-permute-start | bytes 3145736 | tf_op jit(solution)/shard_map/ppermute | solution.py:533
  854.9 21.5 %collective-permute-start.26 = (f32[24,2048]{1,0:T(8,128)S(1)}, f32[24,2048]{1,0:T(8,128)S(1)}, u32[]{:S(2)}, u32[]{:S(2)}) collective-permute-start(f32[24,2048]{1,0:T(8,128)S(1)} %fusion.58), channel_id=1, source_target_pairs={{0,2},{1,3},{2,0},{3,1},{4,6},{5,7},{6,4},{7,5},{8,10},{9,11},{10,... | collective-permute-start | bytes 589832 | tf_op jit(solution)/shard_map/ppermute | solution.py:655
  858.0 67.7 %collective-permute-start.17 = (bf16[2,512,512]{2,1,0:T(8,128)(2,1)}, bf16[2,512,512]{2,1,0:T(8,128)(2,1)}, u32[]{:S(2)}, u32[]{:S(2)}) collective-permute-start(bf16[2,512,512]{2,1,0:T(8,128)(2,1)} %bitcast.33), channel_id=1, source_target_pairs={{0,16},{8,24},{16,0},{24,8},{1,17},{9,25},{17,1},{25,9},{2,18},{10... | collective-permute-start | bytes 3145736 | tf_op jit(solution)/shard_map/ppermute | solution.py:533
  877.0 33.4 %collective-permute-start.27 = (f32[24,2048]{1,0:T(8,128)}, f32[24,2048]{1,0:T(8,128)}, u32[]{:S(2)}, u32[]{:S(2)}) collective-permute-start(f32[24,2048]{1,0:T(8,128)} %add.289), channel_id=1, source_target_pairs={{0,4},{1,5},{2,6},{3,7},{4,0},{5,1},{6,2},{7,3},{8,12},{9,13},{10,... | collective-permute-start | bytes 589832 | tf_op jit(solution)/shard_map/ppermute | solution.py:655
  901.4 96.4 %all-to-all-start.7 = ((bf16[4,512,512]{2,1,0:T(8,128)(2,1)}), bf16[4,512,512]{2,1,0:T(8,128)(2,1)}, u32[]{:S(2)}, u32[]{:S(2)}) async-start(bf16[4,512,512]{2,1,0:T(8,128)(2,1)} %attend_back.3), calls=%async_computation.8 | async-start | bytes 4194304 | tf_op jit(solution)/shard_map/all_to_all | solution.py:648
  905.9 257.1 %all-reduce.7.cloned.1.call-start = ((), (), s32[]{:S(2)}) async-start(), calls=%async_computation.15 | async-start | bytes 6291456 | tf_op jit(solution)/shard_map/psum | solution.py:844
  922.7 21.4 %collective-permute-start.24 = (bf16[256,1536]{1,0:T(8,128)(2,1)S(1)}, bf16[256,1536]{1,0:T(8,128)(2,1)S(1)}, u32[]{:S(2)}, u32[]{:S(2)}) collective-permute-start(bf16[256,1536]{1,0:T(8,128)(2,1)S(1)} %get-tuple-element.254), channel_id=1, source_target_pairs={{0,24},{8,16},{16,8},{24,0},{1,25},{9,17},{17,9},{25,1},{2,26},{10... | collective-permute-start | bytes 2359304 | tf_op jit(solution)/shard_map/ppermute | solution.py:681
  925.1 34.7 %collective-permute-start.23 = (bf16[256,1536]{1,0:T(8,128)(2,1)S(1)}, bf16[256,1536]{1,0:T(8,128)(2,1)S(1)}, u32[]{:S(2)}, u32[]{:S(2)}) collective-permute-start(bf16[256,1536]{1,0:T(8,128)(2,1)S(1)} %get-tuple-element.255), channel_id=1, source_target_pairs={{0,16},{8,24},{16,0},{24,8},{1,17},{9,25},{17,1},{25,9},{2,18},{10... | collective-permute-start | bytes 2359304 | tf_op jit(solution)/shard_map/ppermute | solution.py:681
  925.7 35.5 %collective-permute-start.22 = (bf16[256,1536]{1,0:T(8,128)(2,1)S(1)}, bf16[256,1536]{1,0:T(8,128)(2,1)S(1)}, u32[]{:S(2)}, u32[]{:S(2)}) collective-permute-start(bf16[256,1536]{1,0:T(8,128)(2,1)S(1)} %get-tuple-element.256), channel_id=1, source_target_pairs={{0,8},{8,0},{16,24},{24,16},{1,9},{9,1},{17,25},{25,17},{2,10},{10... | collective-permute-start | bytes 2359304 | tf_op jit(solution)/shard_map/ppermute | solution.py:681
  929.5 68.3 %collective-permute-start.18 = (bf16[512,1024]{1,0:T(8,128)(2,1)}, bf16[512,1024]{1,0:T(8,128)(2,1)}, u32[]{:S(2)}, u32[]{:S(2)}) collective-permute-start(bf16[512,1024]{1,0:T(8,128)(2,1)} %select_bitcast_fusion.6), channel_id=1, source_target_pairs={{0,16},{8,24},{16,0},{24,8},{1,17},{9,25},{17,1},{25,9},{2,18},{10... | collective-permute-start | bytes 3145736 | tf_op jit(solution)/shard_map/ppermute | solution.py:533
  934.8 63.0 %collective-permute-start.19 = (bf16[512,1024]{1,0:T(8,128)(2,1)}, bf16[512,1024]{1,0:T(8,128)(2,1)}, u32[]{:S(2)}, u32[]{:S(2)}) collective-permute-start(bf16[512,1024]{1,0:T(8,128)(2,1)} %select_bitcast_fusion.5), channel_id=1, source_target_pairs={{0,8},{8,0},{16,24},{24,16},{1,9},{9,1},{17,25},{25,17},{2,10},{10... | collective-permute-start | bytes 3145736 | tf_op jit(solution)/shard_map/ppermute | solution.py:533
  944.0 42.4 %collective-permute-start.29 = (f32[24,2048]{1,0:T(8,128)S(1)}, f32[24,2048]{1,0:T(8,128)S(1)}, u32[]{:S(2)}, u32[]{:S(2)}) collective-permute-start(f32[24,2048]{1,0:T(8,128)S(1)} %add.291), channel_id=1, source_target_pairs={{0,16},{8,24},{16,0},{24,8},{1,17},{9,25},{17,1},{25,9},{2,18},{10... | collective-permute-start | bytes 589832 | tf_op jit(solution)/shard_map/ppermute | solution.py:655
  959.7 38.1 %collective-permute-start.21 = (bf16[512,512]{1,0:T(8,128)(2,1)}, bf16[512,512]{1,0:T(8,128)(2,1)}, u32[]{:S(2)}, u32[]{:S(2)}) collective-permute-start(bf16[512,512]{1,0:T(8,128)(2,1)} %select_bitcast_fusion.8), channel_id=1, source_target_pairs={{0,8},{8,0},{16,24},{24,16},{1,9},{9,1},{17,25},{25,17},{2,10},{10... | collective-permute-start | bytes 1572872 | tf_op jit(solution)/shard_map/ppermute | solution.py:533
  961.2 36.6 %collective-permute-start.20 = (bf16[512,512]{1,0:T(8,128)(2,1)}, bf16[512,512]{1,0:T(8,128)(2,1)}, u32[]{:S(2)}, u32[]{:S(2)}) collective-permute-start(bf16[512,512]{1,0:T(8,128)(2,1)} %select_bitcast_fusion.9), channel_id=1, source_target_pairs={{0,16},{8,24},{16,0},{24,8},{1,17},{9,25},{17,1},{25,9},{2,18},{10... | collective-permute-start | bytes 1572872 | tf_op jit(solution)/shard_map/ppermute | solution.py:533
  1022.5 60.0 %collective-permute-start.36 = (bf16[4,128,1536]{2,1,0:T(8,128)(2,1)S(1)}, bf16[4,128,1536]{2,1,0:T(8,128)(2,1)S(1)}, u32[]{:S(2)}, u32[]{:S(2)}) collective-permute-start(bf16[4,128,1536]{2,1,0:T(8,128)(2,1)S(1)} %get-tuple-element.167), channel_id=1, source_target_pairs={{0,2},{1,3},{6,4},{7,5},{8,10},{9,11},{14,12},{15,13},{16,18},{17,... | collective-permute-start | bytes 4718600 | tf_op jit(solution)/shard_map/ppermute | solution.py:550
  1026.8 136.2 %collective-permute-start.42 = (bf16[2,512,1024]{2,1,0:T(8,128)(2,1)S(1)}, bf16[2,512,1024]{2,1,0:T(8,128)(2,1)}, u32[]{:S(2)}, u32[]{:S(2)}) collective-permute-start(bf16[2,512,1024]{2,1,0:T(8,128)(2,1)S(1)} %select_bitcast_fusion), channel_id=1, source_target_pairs={{0,8},{8,0},{16,24},{24,16},{1,9},{9,1},{17,25},{25,17},{2,10},{10... | collective-permute-start | bytes 6291464 | tf_op jit(solution)/shard_map/ppermute | solution.py:533
  1030.6 132.4 %collective-permute-start.43 = (bf16[2,512,1024]{2,1,0:T(8,128)(2,1)}, bf16[2,512,1024]{2,1,0:T(8,128)(2,1)}, u32[]{:S(2)}, u32[]{:S(2)}) collective-permute-start(bf16[2,512,1024]{2,1,0:T(8,128)(2,1)} %bitcast.70), channel_id=1, source_target_pairs={{0,16},{8,24},{16,0},{24,8},{1,17},{9,25},{17,1},{25,9},{2,18},{10... | collective-permute-start | bytes 6291464 | tf_op jit(solution)/shard_map/ppermute | solution.py:533
  1084.2 82.0 %collective-permute-start.37 = (bf16[4,128,1536]{2,1,0:T(8,128)(2,1)}, bf16[4,128,1536]{2,1,0:T(8,128)(2,1)}, u32[]{:S(2)}, u32[]{:S(2)}) collective-permute-start(bf16[4,128,1536]{2,1,0:T(8,128)(2,1)} %add.308), channel_id=1, source_target_pairs={{2,4},{3,5},{4,2},{5,3},{10,12},{11,13},{12,10},{13,11},{18,20},{1... | collective-permute-start | bytes 4718600 | tf_op jit(solution)/shard_map/ppermute | solution.py:550
  1085.9 80.2 %collective-permute-start.38 = (bf16[4,128,1536]{2,1,0:T(8,128)(2,1)}, bf16[4,128,1536]{2,1,0:T(8,128)(2,1)}, u32[]{:S(2)}, u32[]{:S(2)}) collective-permute-start(bf16[4,128,1536]{2,1,0:T(8,128)(2,1)} %get-tuple-element.174), channel_id=1, source_target_pairs={{0,2},{1,3},{6,4},{7,5},{8,10},{9,11},{14,12},{15,13},{16,18},{17,... | collective-permute-start | bytes 4718600 | tf_op jit(solution)/shard_map/ppermute | solution.py:550
  1169.6 39.5 %collective-permute-start.40 = (bf16[4,128,1536]{2,1,0:T(8,128)(2,1)}, bf16[4,128,1536]{2,1,0:T(8,128)(2,1)}, u32[]{:S(2)}, u32[]{:S(2)}) collective-permute-start(bf16[4,128,1536]{2,1,0:T(8,128)(2,1)} %add.312), channel_id=1, source_target_pairs={{2,4},{3,5},{4,2},{5,3},{10,12},{11,13},{12,10},{13,11},{18,20},{1... | collective-permute-start | bytes 4718600 | tf_op jit(solution)/shard_map/ppermute | solution.py:550
  1174.8 41.2 %collective-permute-start.39 = (bf16[4,128,1536]{2,1,0:T(8,128)(2,1)}, bf16[4,128,1536]{2,1,0:T(8,128)(2,1)}, u32[]{:S(2)}, u32[]{:S(2)}) collective-permute-start(bf16[4,128,1536]{2,1,0:T(8,128)(2,1)} %add.311), channel_id=1, source_target_pairs={{2,0},{3,1},{4,6},{5,7},{10,8},{11,9},{12,14},{13,15},{18,16},{19,... | collective-permute-start | bytes 4718600 | tf_op jit(solution)/shard_map/ppermute | solution.py:550
  1177.2 25.4 %collective-permute-start.44 = (bf16[512,1024]{1,0:T(8,128)(2,1)}, bf16[512,1024]{1,0:T(8,128)(2,1)}, u32[]{:S(2)}, u32[]{:S(2)}) collective-permute-start(bf16[512,1024]{1,0:T(8,128)(2,1)} %select_bitcast_fusion.4), channel_id=1, source_target_pairs={{0,16},{8,24},{16,0},{24,8},{1,17},{9,25},{17,1},{25,9},{2,18},{10... | collective-permute-start | bytes 3145736 | tf_op jit(solution)/shard_map/ppermute | solution.py:533
  1178.9 30.2 %collective-permute-start.41 = (bf16[512,1024]{1,0:T(8,128)(2,1)S(1)}, bf16[512,1024]{1,0:T(8,128)(2,1)}, u32[]{:S(2)}, u32[]{:S(2)}) collective-permute-start(bf16[512,1024]{1,0:T(8,128)(2,1)S(1)} %pad_maximum_fusion.8), channel_id=1, source_target_pairs={{0,2},{1,3},{6,4},{7,5},{8,10},{9,11},{14,12},{15,13},{16,18},{17,... | collective-permute-start | bytes 3145736 | tf_op jit(solution)/shard_map/ppermute | solution.py:550
  1191.6 44.9 %collective-permute-start.48 = (bf16[512,1024]{1,0:T(8,128)(2,1)S(1)}, bf16[512,1024]{1,0:T(8,128)(2,1)S(1)}, u32[]{:S(2)}, u32[]{:S(2)}) collective-permute-start(bf16[512,1024]{1,0:T(8,128)(2,1)S(1)} %select_bitcast_fusion.3), channel_id=1, source_target_pairs={{0,8},{8,0},{16,24},{24,16},{1,9},{9,1},{17,25},{25,17},{2,10},{10... | collective-permute-start | bytes 3145736 | tf_op jit(solution)/shard_map/ppermute | solution.py:533
  1202.7 69.3 %collective-permute-start.55 = (bf16[768,2048]{1,0:T(8,128)(2,1)S(1)}, bf16[768,2048]{1,0:T(8,128)(2,1)}, u32[]{:S(2)}, u32[]{:S(2)}) collective-permute-start(bf16[768,2048]{1,0:T(8,128)(2,1)S(1)} %copy-done.86), channel_id=1, source_target_pairs={{0,16},{8,24},{16,0},{24,8},{1,17},{9,25},{17,1},{25,9},{2,18},{10... | collective-permute-start | bytes 9437192 | tf_op jit(solution)/shard_map/ppermute | solution.py:895
  1217.7 19.3 %collective-permute-start.46 = (bf16[512,1024]{1,0:T(8,128)(2,1)S(1)}, bf16[512,1024]{1,0:T(8,128)(2,1)S(1)}, u32[]{:S(2)}, u32[]{:S(2)}) collective-permute-start(bf16[512,1024]{1,0:T(8,128)(2,1)S(1)} %add.316), channel_id=1, source_target_pairs={{2,4},{3,5},{4,2},{5,3},{10,12},{11,13},{12,10},{13,11},{18,20},{1... | collective-permute-start | bytes 3145736 | tf_op jit(solution)/shard_map/ppermute | solution.py:550
  1218.4 24.6 %collective-permute-start.47 = (bf16[512,1024]{1,0:T(8,128)(2,1)S(1)}, bf16[512,1024]{1,0:T(8,128)(2,1)S(1)}, u32[]{:S(2)}, u32[]{:S(2)}) collective-permute-start(bf16[512,1024]{1,0:T(8,128)(2,1)S(1)} %bitcast_add_fusion.3), channel_id=1, source_target_pairs={{0,2},{1,3},{6,4},{7,5},{8,10},{9,11},{14,12},{15,13},{16,18},{17,... | collective-permute-start | bytes 3145736 | tf_op jit(solution)/shard_map/ppermute | solution.py:550
  1223.7 37.0 %collective-permute-start.45 = (bf16[4,128,1536]{2,1,0:T(8,128)(2,1)S(1)}, bf16[4,128,1536]{2,1,0:T(8,128)(2,1)S(1)}, u32[]{:S(2)}, u32[]{:S(2)}) collective-permute-start(bf16[4,128,1536]{2,1,0:T(8,128)(2,1)S(1)} %add.315), channel_id=1, source_target_pairs={{2,0},{3,1},{4,6},{5,7},{10,8},{11,9},{12,14},{13,15},{18,16},{19,... | collective-permute-start | bytes 4718600 | tf_op jit(solution)/shard_map/ppermute | solution.py:550
  1236.6 78.6 %collective-permute-start.54 = (bf16[768,2048]{1,0:T(8,128)(2,1)}, bf16[768,2048]{1,0:T(8,128)(2,1)}, u32[]{:S(2)}, u32[]{:S(2)}) collective-permute-start(bf16[768,2048]{1,0:T(8,128)(2,1)} %all-reduce.5.cloned.1.call-done.keep_ref), channel_id=1, source_target_pairs={{0,1},{1,0},{2,3},{3,2},{4,5},{5,4},{6,7},{7,6},{8,9},{9,8},{10,11... | collective-permute-start | bytes 9437192 | tf_op jit(solution)/shard_map/ppermute | solution.py:638
  1262.3 25.0 %collective-permute-start.49 = (bf16[512,1024]{1,0:T(8,128)(2,1)S(1)}, bf16[512,1024]{1,0:T(8,128)(2,1)S(1)}, u32[]{:S(2)}, u32[]{:S(2)}) collective-permute-start(bf16[512,1024]{1,0:T(8,128)(2,1)S(1)} %add.319), channel_id=1, source_target_pairs={{2,0},{3,1},{4,6},{5,7},{10,8},{11,9},{12,14},{13,15},{18,16},{19,... | collective-permute-start | bytes 3145736 | tf_op jit(solution)/shard_map/ppermute | solution.py:550
  1263.6 25.0 %collective-permute-start.51 = (bf16[512,1024]{1,0:T(8,128)(2,1)S(1)}, bf16[512,1024]{1,0:T(8,128)(2,1)S(1)}, u32[]{:S(2)}, u32[]{:S(2)}) collective-permute-start(bf16[512,1024]{1,0:T(8,128)(2,1)S(1)} %bitcast_add_fusion.2), channel_id=1, source_target_pairs={{0,2},{1,3},{6,4},{7,5},{8,10},{9,11},{14,12},{15,13},{16,18},{17,... | collective-permute-start | bytes 3145736 | tf_op jit(solution)/shard_map/ppermute | solution.py:550
  1272.0 22.5 %collective-permute-start.30 = (bf16[2,256,2048]{2,1,0:T(8,128)(2,1)}, bf16[2,256,2048]{2,1,0:T(8,128)(2,1)}, u32[]{:S(2)}, u32[]{:S(2)}) collective-permute-start(bf16[2,256,2048]{2,1,0:T(8,128)(2,1)} %select_bitcast_fusion.1), channel_id=1, source_target_pairs={{0,1},{1,0},{2,3},{3,2},{4,5},{5,4},{6,7},{7,6},{8,9},{9,8},{10,11... | collective-permute-start | bytes 6291464 | tf_op jit(solution)/shard_map/ppermute | solution.py:638
  1272.0 48.2 %collective-permute-start.56 = (bf16[768,2048]{1,0:T(8,128)(2,1)}, bf16[768,2048]{1,0:T(8,128)(2,1)}, u32[]{:S(2)}, u32[]{:S(2)}) collective-permute-start(bf16[768,2048]{1,0:T(8,128)(2,1)} %collective-permute-done.55.sent_ref), channel_id=1, source_target_pairs={{0,1},{1,0},{2,3},{3,2},{4,5},{5,4},{6,7},{7,6},{8,9},{9,8},{10,11... | collective-permute-start | bytes 9437192 | tf_op jit(solution)/shard_map/ppermute | solution.py:638
  1292.6 44.3 %collective-permute-start.57 = (bf16[4,256,1536]{2,1,0:T(8,128)(2,1)}, bf16[4,256,1536]{2,1,0:T(8,128)(2,1)}, u32[]{:S(2)}, u32[]{:S(2)}) collective-permute-start(bf16[4,256,1536]{2,1,0:T(8,128)(2,1)} %pad_maximum_fusion.6.refs_0_), channel_id=1, source_target_pairs={{0,1},{1,0},{2,3},{3,2},{4,5},{5,4},{6,7},{7,6},{8,9},{9,8},{10,11... | collective-permute-start | bytes 9437192 | tf_op jit(solution)/shard_map/ppermute | solution.py:638
  1304.4 44.6 %collective-permute-start.53 = (bf16[512,1024]{1,0:T(8,128)(2,1)}, bf16[512,1024]{1,0:T(8,128)(2,1)}, u32[]{:S(2)}, u32[]{:S(2)}) collective-permute-start(bf16[512,1024]{1,0:T(8,128)(2,1)} %add.322), channel_id=1, source_target_pairs={{2,4},{3,5},{4,2},{5,3},{10,12},{11,13},{12,10},{13,11},{18,20},{1... | collective-permute-start | bytes 3145736 | tf_op jit(solution)/shard_map/ppermute | solution.py:550
  1309.1 39.9 %collective-permute-start.52 = (bf16[512,1024]{1,0:T(8,128)(2,1)}, bf16[512,1024]{1,0:T(8,128)(2,1)}, u32[]{:S(2)}, u32[]{:S(2)}) collective-permute-start(bf16[512,1024]{1,0:T(8,128)(2,1)} %add.321), channel_id=1, source_target_pairs={{2,0},{3,1},{4,6},{5,7},{10,8},{11,9},{12,14},{13,15},{18,16},{19,... | collective-permute-start | bytes 3145736 | tf_op jit(solution)/shard_map/ppermute | solution.py:550
  1315.2 41.7 %collective-permute-start.32 = (f32[2,2048]{1,0:T(2,128)S(1)}, f32[2,2048]{1,0:T(2,128)S(1)}, u32[]{:S(2)}, u32[]{:S(2)}) collective-permute-start(f32[2,2048]{1,0:T(2,128)S(1)} %fusion.57), channel_id=1, source_target_pairs={{0,2},{1,3},{2,0},{3,1},{4,6},{5,7},{6,4},{7,5},{8,10},{9,11},{10,... | collective-permute-start | bytes 49160 | tf_op jit(solution)/shard_map/ppermute | solution.py:655
  1353.5 27.0 %collective-permute-start.58 = (bf16[512,1024]{1,0:T(8,128)(2,1)S(1)}, bf16[512,1024]{1,0:T(8,128)(2,1)}, u32[]{:S(2)}, u32[]{:S(2)}) collective-permute-start(bf16[512,1024]{1,0:T(8,128)(2,1)S(1)} %add.323), channel_id=1, source_target_pairs={{2,0},{3,1},{4,6},{5,7},{10,8},{11,9},{12,14},{13,15},{18,16},{19,... | collective-permute-start | bytes 3145736 | tf_op jit(solution)/shard_map/ppermute | solution.py:550
  1363.8 20.0 %collective-permute-start.34 = (f32[2,2048]{1,0:T(2,128)S(1)}, f32[2,2048]{1,0:T(2,128)S(1)}, u32[]{:S(2)}, u32[]{:S(2)}) collective-permute-start(f32[2,2048]{1,0:T(2,128)S(1)} %add.305), channel_id=1, source_target_pairs={{0,8},{8,0},{16,24},{24,16},{1,9},{9,1},{17,25},{25,17},{2,10},{10... | collective-permute-start | bytes 49160 | tf_op jit(solution)/shard_map/ppermute | solution.py:655
  (107 other events, 1466.7 us)
Sparse Core Ops, SparseCore 0:
  15.8 91.5 all-gather.6
  109.9 52.5 all-gather.8
  164.6 114.0 all-gather.14
  280.4 87.4 all-gather.12
  370.2 87.4 all-gather.10
  550.3 86.3 reduce-scatter.1
  677.5 155.4 all-reduce.4
  987.2 175.6 all-reduce.6

commit v7 on v6

--- a/solution.py
+++ b/solution.py
@@ -813,23 +813,26 @@
         return total_sum(jnp.concatenate([part_gate, part_ffn[None], jnp.zeros((7, width), F32)], axis=0))
 
     part_out = dot_tn(d_mid_low, gated, BF)
-    out_part = dot_nt(hidden, down_full, BF)
     d_proj, d_logit, d_heads = [], [], []
     q_sum = 0.0
     k_sum = 0.0
     for row in range(rows):
         low_row = d_mid_low[row * chip_tok : (row + 1) * chip_tok]
         if row == 1:
+            out_part = dot_nt(hidden, down_full, BF)
             low_row, (part_out, out_part) = tie(low_row, (part_out, out_part))
         d_gated = dot_nn(low_row, out_full)
         d_attn, dl = gate_back(d_gated, tok_results[row], logits, row)
+        if row == 0:
+            d_attn, hidden = tie(d_attn, hidden)
         d_logit.append(dl)
         d_heads.append(exchange(d_attn))
     back = []
     for row in range(rows):
         grads = attend_back(packed[row], d_heads[row], results[row], logs[row], start[row : row + 1], low[row])
         if row == 0:
-            grads, keep = tie(grads, keep)
+            grads, (keep, recv_sum) = tie(grads, (keep, recv_sum))
+            recv = lax.psum(recv_sum, "seq", axis_index_groups=groups)
         back.append(exchange(grads))
     cut = width // 2
     half_out = part_out.shape[1] // 2
@@ -840,8 +843,7 @@
         Halving(part_out[:, half_out:], dp, True),
     ]
     moved = [t.send() for t in trading]
-    back[0], (moved, recv_sum) = tie(back[0], (moved, recv_sum))
-    recv = lax.psum(recv_sum, "seq", axis_index_groups=groups)
+    back[0], moved = tie(back[0], moved)
     while trading[0].order:
         for t, m in zip(trading, moved):
             t.add(m)
@@ -859,12 +861,12 @@
         q_sum = q_sum + qs
         k_sum = k_sum + ks
     d_proj = jnp.concatenate(d_proj, axis=0)
+    d_proj, recv = tie(d_proj, recv)
     d_logit = jnp.concatenate(d_logit, axis=0)
     half = width // 2
     part_qkv = [dot_tn(d_proj, normed_a[:, a : a + half], BF) for a in (0, half)]
     trading = [Halving(p, dp, flip) for p, flip in zip(part_qkv, (False, True))]
     moved = [t.send() for t in trading]
-    moved, recv = tie_all(moved, recv)
     while trading[0].order:
         for t, m in zip(trading, moved):
             t.add(m)
@@ -887,7 +889,13 @@
 
     heads = jnp.concatenate([jnp.sum(q_sum, axis=0), jnp.sum(k_sum, axis=0)])
     heads = jnp.pad(heads, (0, width - heads.shape[0]))
-    late = total_sum(jnp.stack([part_attn, heads]))
+
+    def norm_done(done):
+        return [part_attn, grad_input]
+
+    def late_sum(done):
+        return [total_sum(jnp.stack([part_attn, heads]))]
+
     grad_w_gate = lax.dynamic_slice_in_dim(early, me * gate_count, gate_count, 0)
 
     mid_cut = down_sum.shape[1] // 2
@@ -905,8 +913,9 @@
     def join_late(done):
         return [join_cols([done[2]], [swap(done[2])], core, GROUP * HEAD)]
 
-    sums, ((grad_gu, grad_down), (grad_out,)) = line.pipeline(
-        [down_sum[:, :mid_cut], down_sum[:, mid_cut:], shard_out, *shard_qkv], {5: join_early, 6: join_late}
+    sums, ((_, grad_input), (late,), (grad_gu, grad_down), (grad_out,)) = line.pipeline(
+        [down_sum[:, :mid_cut], down_sum[:, mid_cut:], shard_out, *shard_qkv],
+        {1: norm_done, 3: late_sum, 5: join_early, 6: join_late},
     )
     qkv_sum = sums[3:]
     grad_qkv = join_rows(qkv_sum, [swap(p) for p in qkv_sum], core, jnp.where(q_shard, GROUP, 1), HEAD)

time: 1410 us -> 1440 us (1.021)
  waiting for transfers between devices: 579 us -> 640 us
    ppermute x12, waiting for transfers between devices: 54.1 us -> 165 us  [total_sum(): x = x + lax.ppermute(x, name, [(s, s ^ step) for s in range(size)])]
    psum x1, waiting for transfers between devices: 66.3 us -> 0.01 us  [shards(): recv = lax.psum(recv_sum, 'seq', axis_index_groups=groups)]
    ppermute x6, waiting for transfers between devices: 31.2 us -> 63.5 us  [trade_blocks(): lax.ppermute(out, 'dp', [(d, d ^ k) for d in range(dp)])]
    all_gather x4, waiting for transfers between devices: 146 us -> 127 us  [gather(): return lax.all_gather(x, 'dp', axis=0, tiled=True)]
    ppermute x15, waiting for transfers between devices: 109 us -> 92.4 us  [send(): return (x, lax.ppermute(x, 'seq', self.stages[stage]))]
  transfers between devices with their start and end apart: 77 -> 77, of which waited for: 28 -> 33; matrix products, arithmetic and copies ran while one was open for 26% -> 21% of each run, Pallas kernels for 10% -> 10%
where the time goes in v7:
time: 1440 us
  waiting for transfers between devices  640 us (44%)
  matrix products  243 us (17%)
  other arithmetic  173 us (12%)
  Pallas kernels  145 us (10%)
  starting transfers between devices  125 us (9%)
  blocking collectives  52.5 us (4%)
  local copies, waits for them, and re-layouts  41.2 us (3%)
  between operations  16.3 us (1%)
    ppermute x12, waiting for transfers between devices, total_sum(): x = x + lax.ppermute(x, name, [(s, s ^ step) for s in range(size)])  165 us
    all_gather x4, waiting for transfers between devices, gather(): return lax.all_gather(x, 'dp', axis=0, tiled=True)  127 us
    dot_general x7, matrix products, dot_nt(): lax.dot_general(left, right, (((1,), (1,)), ((), ())), preferred_element_...  94.2 us
    ppermute x15, waiting for transfers between devices, send(): return (x, lax.ppermute(x, 'seq', self.stages[stage]))  92.4 us
    all_to_all x7, waiting for transfers between devices, exchange(): return lax.all_to_all(x, 'seq', 0, 0, axis_index_groups=groups, tiled=True)  84.7 us
    dot_general x7, matrix products, dot_nn(): lax.dot_general(left, right, (((1,), (0,)), ((), ())), preferred_element_...  80.8 us
    dot_general x7, matrix products, dot_tn(): lax.dot_general(left, right, (((0,), (0,)), ((), ())), preferred_element_...  67.9 us
    ppermute x6, waiting for transfers between devices, trade_blocks(): lax.ppermute(out, 'dp', [(d, d ^ k) for d in range(dp)])  63.5 us
  transfers between devices with their start and end apart: 77, of which 33 were waited for; matrix products, arithmetic and copies ran while one was open for 21% of the time, Pallas kernels for 10%

profile of v7, /device:TPU:0, one launch (start us, length us, event | category | flops | bytes accessed | tf_op | source)
XLA Modules:
  0.0 1435.3 jit_solution(18191861084328328374)
XLA Ops:
  30.5 6.6 select_select_fusion
  53.0 54.4 %all-gather.7.cloned.1.call-done = bf16[2048,2048]{1,0:T(8,128)(2,1)} async-done(((bf16[512,2048]{1,0:T(8,128)(2,1)}), bf16[2048,2048]{1,0:T(8,128)(2,1)}) %all-gather.7.cloned.1.call-update) | async-done | bytes 8388624 | tf_op jit(solution)/shard_map/all_gather | solution.py:663
  117.2 11.1 fusion.66.proj_ref
  128.3 6.2 pack_heads.3
  134.4 52.5 %all_to_all.40.q_ref.k_ref.v_ref = bf16[4,512,512]{2,1,0:T(8,128)(2,1)} all-to-all(bf16[4,512,512]{2,1,0:T(8,128)(2,1)} %pack_heads.3), channel_id=1, replica_groups={{0,2,4,6},{1,3,5,7},{8,10,12,14},{9,11,13,15},{16,18,20,22},{17,19,21,2..., dimensions={0} | all-to-all | bytes 4194304 | tf_op jit(solution)/shard_map/all_to_all | solution.py:648
  187.0 6.2 pack_heads.2
  205.8 15.7 %collective-permute-done.1 = bf16[256,1536]{1,0:T(8,128)(2,1)S(1)} collective-permute-done((bf16[256,1536]{1,0:T(8,128)(2,1)S(1)}, bf16[256,1536]{1,0:T(8,128)(2,1)S(1)}, u32[]{:S(2)}, u32[]{:S(2)}) %collective-permute-start.1) | collective-permute-done | bytes 786464 | tf_op jit(solution)/shard_map/ppermute | solution.py:681
  222.4 34.0 %collective-permute-done.2 = bf16[256,1536]{1,0:T(8,128)(2,1)S(1)} collective-permute-done((bf16[256,1536]{1,0:T(8,128)(2,1)S(1)}, bf16[256,1536]{1,0:T(8,128)(2,1)S(1)}, u32[]{:S(2)}, u32[]{:S(2)}) %collective-permute-start.2) | collective-permute-done | bytes 786464 | tf_op jit(solution)/shard_map/ppermute | solution.py:681
  259.6 10.8 attend.2
  270.4 5.2 all-to-all-start.1
  275.6 10.8 attend.3
  286.3 12.5 all-to-all-done.1.res_ref
  305.1 4.9 convolution_convert_fusion.11
  311.0 16.5 %all-to-all-done.3.res_ref = bf16[4,512,256]{2,1,0:T(8,128)(2,1)S(1)} async-done(((bf16[4,512,256]{2,1,0:T(8,128)(2,1)}), bf16[4,512,256]{2,1,0:T(8,128)(2,1)S(1)}, u32[]{:S(2)}, u32[]{:S(2)}) %all-to-all-start.3) | async-done | bytes 1048608 | tf_op jit(solution)/shard_map/all_to_all | solution.py:648
  331.2 4.9 convolution_convert_fusion.10
  346.3 4.8 slice_select_fusion.4
  367.8 18.6 %convolution_convert_fusion.3 = bf16[2048,1536]{1,0:T(8,128)(2,1)} fusion(bf16[2048,2048]{1,0:T(8,128)(2,1)} %all-gather.13.cloned.1.call-done, bf16[2048,1536]{1,0:T(8,128)(2,1)} %bitcast.264), kind=kOutput, calls=%fused_computation.24 | convolution fusion | flops 12888047616 | bytes 20971520 | tf_op jit(solution)/shard_map/dot_general | solution.py:33
  386.5 71.1 %all-gather.11.cloned.1.call-done = bf16[2048,2048]{1,0:T(8,128)(2,1)} async-done(((bf16[512,2048]{1,0:T(8,128)(2,1)}), bf16[2048,2048]{1,0:T(8,128)(2,1)}) %all-gather.11.cloned.1.call-update) | async-done | bytes 8388624 | tf_op jit(solution)/shard_map/all_gather | solution.py:663
  457.6 19.7 %convolution_convert_fusion.1 = bf16[2048,1536]{1,0:T(8,128)(2,1)} fusion(bf16[2048,2048]{1,0:T(8,128)(2,1)} %all-gather.11.cloned.1.call-done, bf16[3072,2048]{1,0:T(8,128)(2,1)} %param.21, pred[]{:T(512)S(6)} %ge.19), kind=kOutput, calls=%fused_computation.22 | convolution fusion | flops 12891193344 | bytes 27262976 | tf_op jit(solution)/shard_map/dot_general | solution.py:29
  477.3 32.4 %select_convert_fusion = (bf16[2048,1536]{1,0:T(8,128)(2,1)}, bf16[2048,1536]{1,0:T(8,128)(2,1)}, bf16[2048,1536]{1,0:T(8,128)(2,1)}) fusion(bf16[2048,1536]{1,0:T(8,128)(2,1)} %convolution_convert_fusion.3, pred[]{:T(512)S(6)} %ge.19, bf16[2048,1536]{1,0:T(8,128)(2,1)} %convolution_convert_fusion.1, bf16[2048,2048]{1,0:T(8,128)(2,1)} %all-gather.11.cloned.1.call-done, ...), kind=kOutput, calls=%fused_computation.14 | convolution fusion | flops 12957253632 | bytes 46137344 | tf_op jit(solution)/shard_map/dot_general | solution.py:29
  509.7 21.8 %fusion.45 = f32[2048,2048]{1,0:T(8,128)} fusion(bf16[2048,1536]{1,0:T(8,128)(2,1)} %get-tuple-element.235, bf16[3072,2048]{1,0:T(8,128)(2,1)} %param.21, pred[]{:T(512)S(6)} %ge.19), kind=kOutput, calls=%fused_computation.157 | convolution fusion | flops 12888047616 | bytes 35651584 | tf_op jit(solution)/shard_map/dot_general | solution.py:33
  531.6 19.1 %add_convert_fusion = bf16[2048,2048]{1,0:T(8,128)(2,1)} fusion(f32[2048,2048]{1,0:T(8,128)} %fusion.45, bf16[2048,1536]{1,0:T(8,128)(2,1)S(1)} %copy-done.80, bf16[1536,2048]{1,0:T(8,128)(2,1)} %pad_maximum_fusion.1), kind=kOutput, calls=%fused_computation.3 | convolution fusion | flops 12893290496 | bytes 37748736 | tf_op jit(solution)/shard_map/dot_general | solution.py:33
  550.7 17.8 %convolution_convert_fusion.6 = bf16[1536,2048]{1,0:T(8,128)(2,1)S(1)} fusion(bf16[2048,1536]{1,0:T(8,128)(2,1)} %get-tuple-element.235, bf16[2048,2048]{1,0:T(8,128)(2,1)} %all-gather.11.cloned.1.call-done), kind=kOutput, calls=%fused_computation.27 | convolution fusion | flops 12888047616 | bytes 20971520 | tf_op jit(solution)/shard_map/dot_general | solution.py:37
  571.8 18.6 %convolution_convert_fusion.5 = bf16[1536,2048]{1,0:T(8,128)(2,1)S(1)} fusion(bf16[2048,1536]{1,0:T(8,128)(2,1)} %get-tuple-element.234, bf16[2048,2048]{1,0:T(8,128)(2,1)} %all-gather.11.cloned.1.call-done), kind=kOutput, calls=%fused_computation.26 | convolution fusion | flops 12888047616 | bytes 20971520 | tf_op jit(solution)/shard_map/dot_general | solution.py:37
  593.5 14.3 convolution_convert_fusion.4
  613.4 23.7 %reduce-scatter.2.cloned.1.call-done = bf16[512,2048]{1,0:T(8,128)(2,1)} async-done(((bf16[2048,2048]{1,0:T(8,128)(2,1)}), bf16[512,2048]{1,0:T(8,128)(2,1)}) %reduce-scatter.2.cloned.1.call-update) | async-done | bytes 2097168 | tf_op jit(solution)/shard_map/reduce_scatter | solution.py:660
  637.1 9.8 select_add_fusion
  651.1 5.1 fusion.62
  675.8 19.3 %convolution_convert_fusion = bf16[2048,2048]{1,0:T(8,128)(2,1)} fusion(bf16[2048,1536]{1,0:T(8,128)(2,1)} %get-tuple-element.141, bf16[2048,1536]{1,0:T(8,128)(2,1)} %bitcast.265), kind=kOutput, calls=%fused_computation.21 | convolution fusion | flops 12889096192 | bytes 20971520 | tf_op jit(solution)/shard_map/dot_general | solution.py:29
  703.1 6.3 convolution_convert_fusion.9
  717.0 21.2 %all-to-all-done.4.grad_ref = bf16[4,512,256]{2,1,0:T(8,128)(2,1)S(1)} async-done(((bf16[4,512,256]{2,1,0:T(8,128)(2,1)}), bf16[4,512,256]{2,1,0:T(8,128)(2,1)S(1)}, u32[]{:S(2)}, u32[]{:S(2)}) %all-to-all-start.4) | async-done | bytes 1048608 | tf_op jit(solution)/shard_map/all_to_all | solution.py:648
  742.8 19.9 %attend_back.2 = bf16[4,512,512]{2,1,0:T(8,128)(2,1)} custom-call(s32[4]{0:T(128)} %get-tuple-element.295.low_ref, bf16[4,512,512]{2,1,0:T(8,128)(2,1)} %copy-done, bf16[4,512,512]{2,1,0:T(8,128)(2,1)} %copy-done, bf16[4,512,512]{2,1,0:T(8,128)(2,1)} %copy-done, bf16[4,512,256]{2,1,0:T(8,128)(2,1)} %copy-done.38, ...), custom_call_target="tpu_custom_call" | custom-call | tf_op jit(solution)/shard_map/attend_back/pallas_call | solution.py:281
  762.7 54.6 %all-reduce.5.cloned.1.call-done.keep_ref = bf16[768,2048]{1,0:T(8,128)(2,1)} async-done(((bf16[768,2048]{1,0:T(8,128)(2,1)}), bf16[768,2048]{1,0:T(8,128)(2,1)}) %all-reduce.5.cloned.1.call-update) | async-done | bytes 3145744 | tf_op jit(solution)/shard_map/psum | solution.py:792
  843.9 19.8 %attend_back.3 = bf16[4,512,512]{2,1,0:T(8,128)(2,1)} custom-call(s32[4]{0:T(128)} %get-tuple-element.296.low_ref, bf16[4,512,512]{2,1,0:T(8,128)(2,1)} %all_to_all.40.q_ref.k_ref.v_ref, bf16[4,512,512]{2,1,0:T(8,128)(2,1)} %all_to_all.40.q_ref.k_ref.v_ref, bf16[4,512,512]{2,1,0:T(8,128)(2,1)} %all_to_all.40.q_ref.k_ref.v_ref, ...), custom_call_target="tpu_custom_call" | custom-call | tf_op jit(solution)/shard_map/attend_back/pallas_call | solution.py:281
  863.7 34.6 %all-to-all-done.5.grad_ref = bf16[4,512,512]{2,1,0:T(8,128)(2,1)} async-done(((bf16[4,512,512]{2,1,0:T(8,128)(2,1)}), bf16[4,512,512]{2,1,0:T(8,128)(2,1)}, u32[]{:S(2)}, u32[]{:S(2)}) %all-to-all-start.5) | async-done | bytes 2097184 | tf_op jit(solution)/shard_map/all_to_all | solution.py:648
  910.6 82.8 %collective-permute-done.27 = f32[24,2048]{1,0:T(8,128)S(1)} collective-permute-done((f32[24,2048]{1,0:T(8,128)S(1)}, f32[24,2048]{1,0:T(8,128)S(1)}, u32[]{:S(2)}, u32[]{:S(2)}) %collective-permute-start.27) | collective-permute-done | bytes 196640 | tf_op jit(solution)/shard_map/ppermute | solution.py:655
  1017.0 9.9 collective-permute-done.23
  1028.4 26.8 %collective-permute-done.28 = f32[24,2048]{1,0:T(8,128)S(1)} collective-permute-done((f32[24,2048]{1,0:T(8,128)S(1)}, f32[24,2048]{1,0:T(8,128)S(1)}, u32[]{:S(2)}, u32[]{:S(2)}) %collective-permute-start.28) | collective-permute-done | bytes 196640 | tf_op jit(solution)/shard_map/ppermute | solution.py:655
  1059.2 5.5 collective-permute-done.29
  1065.4 7.5 unpack_heads.2
  1072.9 7.5 unpack_heads.3
  1085.3 12.6 fusion.68
  1097.9 5.2 convolution_convert_fusion.8
  1110.5 4.9 convolution_convert_fusion.7
  1119.1 19.7 %collective-permute-done.30 = bf16[4,128,1536]{2,1,0:T(8,128)(2,1)} collective-permute-done((bf16[4,128,1536]{2,1,0:T(8,128)(2,1)S(1)}, bf16[4,128,1536]{2,1,0:T(8,128)(2,1)}, u32[]{:S(2)}, u32[]{:S(2)}) %collective-permute-start.30) | collective-permute-done | bytes 1572896 | tf_op jit(solution)/shard_map/ppermute | solution.py:550
  1141.4 5.8 collective-permute-start.32
  1150.5 6.6 collective-permute-done.37
  1161.7 18.7 %collective-permute-done.32 = bf16[4,128,1536]{2,1,0:T(8,128)(2,1)S(1)} collective-permute-done((bf16[4,128,1536]{2,1,0:T(8,128)(2,1)S(1)}, bf16[4,128,1536]{2,1,0:T(8,128)(2,1)S(1)}, u32[]{:S(2)}, u32[]{:S(2)}) %collective-permute-start.32) | collective-permute-done | bytes 1572896 | tf_op jit(solution)/shard_map/ppermute | solution.py:550
  1185.3 7.6 collective-permute-start.36
  1195.0 15.0 %collective-permute-done.38 = bf16[512,1024]{1,0:T(8,128)(2,1)S(1)} collective-permute-done((bf16[512,1024]{1,0:T(8,128)(2,1)S(1)}, bf16[512,1024]{1,0:T(8,128)(2,1)S(1)}, u32[]{:S(2)}, u32[]{:S(2)}) %collective-permute-start.38) | collective-permute-done | bytes 1048608 | tf_op jit(solution)/shard_map/ppermute | solution.py:533
  1210.0 5.6 collective-permute-start.45
  1221.6 5.3 collective-permute-start.46
  1229.4 14.0 collective-permute-done.47
  1245.7 29.8 %collective-permute-done.48 = f32[2,2048]{1,0:T(2,128)S(1)} collective-permute-done((f32[2,2048]{1,0:T(2,128)S(1)}, f32[2,2048]{1,0:T(2,128)S(1)}, u32[]{:S(2)}, u32[]{:S(2)}) %collective-permute-start.48) | collective-permute-done | bytes 16416 | tf_op jit(solution)/shard_map/ppermute | solution.py:655
  1275.5 6.9 collective-permute-start.41
  1283.5 18.6 %collective-permute-done.41 = bf16[512,1024]{1,0:T(8,128)(2,1)S(1)} collective-permute-done((bf16[512,1024]{1,0:T(8,128)(2,1)S(1)}, bf16[512,1024]{1,0:T(8,128)(2,1)S(1)}, u32[]{:S(2)}, u32[]{:S(2)}) %collective-permute-start.41) | collective-permute-done | bytes 1048608 | tf_op jit(solution)/shard_map/ppermute | solution.py:550
  1307.9 7.7 collective-permute-start.51
  1316.1 11.3 collective-permute-done.49
  1327.4 6.3 collective-permute-done.51
  1346.7 16.4 %join_units.1 = f32[3072,2048]{1,0:T(8,128)} custom-call(s32[2]{0:T(128)} %pad_add_fusion.1.which_ref, bf16[768,2048]{1,0:T(8,128)(2,1)} %all-reduce.5.cloned.1.call-done.keep_ref, bf16[768,2048]{1,0:T(8,128)(2,1)} %collective-permute-done.54.keep_other_ref, bf16[768,2048]{1,0:T(8,128)(2,1)} %collective-permute-done.55.sent_ref, ...), custom_call_target="tpu_custom_call" | custom-call | tf_op jit(solution)/shard_map/join_units/pallas_call | solution.py:478
  1363.2 12.0 join_blocks.1
  1387.7 6.4 join_cols.1
  1394.2 15.4 %collective-permute-done.58 = bf16[512,1024]{1,0:T(8,128)(2,1)} collective-permute-done((bf16[512,1024]{1,0:T(8,128)(2,1)S(1)}, bf16[512,1024]{1,0:T(8,128)(2,1)}, u32[]{:S(2)}, u32[]{:S(2)}) %collective-permute-start.58) | collective-permute-done | bytes 1048608 | tf_op jit(solution)/shard_map/ppermute | solution.py:550
  1419.6 8.4 join_rows.1
  (466 shorter events, 314.1 us)
Async XLA Ops:
  7.2 100.2 %all-gather.7.cloned.1.call-start = ((), (), s32[]{:S(2)}) async-start(), calls=%async_computation.9 | async-start | bytes 10485760 | tf_op jit(solution)/shard_map/all_gather | solution.py:663
  15.6 289.5 %all-gather.9.cloned.1.call-start = ((), (), s32[]{:S(2)}) async-start(), calls=%async_computation.10 | async-start | bytes 5242880 | tf_op jit(solution)/shard_map/all_gather | solution.py:663
  15.7 30.1 %collective-permute-start = (bf16[2,256,2048]{2,1,0:T(8,128)(2,1)S(1)}, bf16[2,256,2048]{2,1,0:T(8,128)(2,1)}, u32[]{:S(2)}, u32[]{:S(2)}) collective-permute-start(bf16[2,256,2048]{2,1,0:T(8,128)(2,1)S(1)} %copy-done.1), channel_id=1, source_target_pairs={{0,1},{1,0},{2,3},{3,2},{4,5},{5,4},{6,7},{7,6},{8,9},{9,8},{10,11... | collective-permute-start | bytes 6291464 | tf_op jit(solution)/shard_map/ppermute | solution.py:638
  16.3 23.2 %collective-permute-start.4 = (bf16[16,2048]{1,0:T(8,128)(2,1)S(1)}, bf16[16,2048]{1,0:T(8,128)(2,1)S(1)}, u32[]{:S(2)}, u32[]{:S(2)}) collective-permute-start(bf16[16,2048]{1,0:T(8,128)(2,1)S(1)} %constant_dynamic-update-slice_fusion.2), channel_id=1, source_target_pairs={{0,8},{8,0},{16,24},{24,16},{1,9},{9,1},{17,25},{25,17},{2,10},{10... | collective-permute-start | bytes 196616 | tf_op jit(solution)/shard_map/ppermute | solution.py:655
  21.6 324.7 %all-gather.15.cloned.1.call-start = ((), (), s32[]{:S(2)}) async-start(), calls=%async_computation.16 | async-start | bytes 9437184 | tf_op jit(solution)/shard_map/all_gather | solution.py:710
  107.4 260.4 %all-gather.13.cloned.1.call-start = ((), (), s32[]{:S(2)}) async-start(), calls=%async_computation.12 | async-start | bytes 10485760 | tf_op jit(solution)/shard_map/all_gather | solution.py:663
  193.2 65.1 %all-to-all-start = ((bf16[4,512,512]{2,1,0:T(8,128)(2,1)}), bf16[4,512,512]{2,1,0:T(8,128)(2,1)S(1)}, u32[]{:S(2)}, u32[]{:S(2)}) async-start(bf16[4,512,512]{2,1,0:T(8,128)(2,1)} %pack_heads.2), calls=%async_computation | async-start | bytes 4194304 | tf_op jit(solution)/shard_map/all_to_all | solution.py:648
  201.1 20.4 %collective-permute-start.1 = (bf16[256,1536]{1,0:T(8,128)(2,1)S(1)}, bf16[256,1536]{1,0:T(8,128)(2,1)S(1)}, u32[]{:S(2)}, u32[]{:S(2)}) collective-permute-start(bf16[256,1536]{1,0:T(8,128)(2,1)S(1)} %get-tuple-element.266), channel_id=1, source_target_pairs={{0,8},{8,0},{16,24},{24,16},{1,9},{9,1},{17,25},{25,17},{2,10},{10... | collective-permute-start | bytes 2359304 | tf_op jit(solution)/shard_map/ppermute | solution.py:681
  203.1 53.3 %collective-permute-start.2 = (bf16[256,1536]{1,0:T(8,128)(2,1)S(1)}, bf16[256,1536]{1,0:T(8,128)(2,1)S(1)}, u32[]{:S(2)}, u32[]{:S(2)}) collective-permute-start(bf16[256,1536]{1,0:T(8,128)(2,1)S(1)} %get-tuple-element.265), channel_id=1, source_target_pairs={{0,16},{8,24},{16,0},{24,8},{1,17},{9,25},{17,1},{25,9},{2,18},{10... | collective-permute-start | bytes 2359304 | tf_op jit(solution)/shard_map/ppermute | solution.py:681
  204.3 53.1 %collective-permute-start.3 = (bf16[256,1536]{1,0:T(8,128)(2,1)S(1)}, bf16[256,1536]{1,0:T(8,128)(2,1)S(1)}, u32[]{:S(2)}, u32[]{:S(2)}) collective-permute-start(bf16[256,1536]{1,0:T(8,128)(2,1)S(1)} %get-tuple-element.264), channel_id=1, source_target_pairs={{0,24},{8,16},{16,8},{24,0},{1,25},{9,17},{17,9},{25,1},{2,26},{10... | collective-permute-start | bytes 2359304 | tf_op jit(solution)/shard_map/ppermute | solution.py:681
  270.4 28.5 %all-to-all-start.1 = ((bf16[4,512,256]{2,1,0:T(8,128)(2,1)}), bf16[4,512,256]{2,1,0:T(8,128)(2,1)S(1)}, u32[]{:S(2)}, u32[]{:S(2)}) async-start(bf16[4,512,256]{2,1,0:T(8,128)(2,1)} %get-tuple-element.122.res_ref), calls=%async_computation.1 | async-start | bytes 2097152 | tf_op jit(solution)/shard_map/all_to_all | solution.py:648
  298.8 28.7 %all-to-all-start.3 = ((bf16[4,512,256]{2,1,0:T(8,128)(2,1)}), bf16[4,512,256]{2,1,0:T(8,128)(2,1)S(1)}, u32[]{:S(2)}, u32[]{:S(2)}) async-start(bf16[4,512,256]{2,1,0:T(8,128)(2,1)} %get-tuple-element.126.res_ref), calls=%async_computation.3 | async-start | bytes 2097152 | tf_op jit(solution)/shard_map/all_to_all | solution.py:648
  302.4 155.2 %all-gather.11.cloned.1.call-start = ((), (), s32[]{:S(2)}) async-start(), calls=%async_computation.11 | async-start | bytes 10485760 | tf_op jit(solution)/shard_map/all_gather | solution.py:663
  311.0 25.2 %collective-permute-start.6 = (bf16[256,2048]{1,0:T(8,128)(2,1)}, bf16[256,2048]{1,0:T(8,128)(2,1)}, u32[]{:S(2)}, u32[]{:S(2)}) collective-permute-start(bf16[256,2048]{1,0:T(8,128)(2,1)} %broadcast_select_fusion.23), channel_id=1, source_target_pairs={{0,1},{1,0},{2,3},{3,2},{4,5},{5,4},{6,7},{7,6},{8,9},{9,8},{10,11... | collective-permute-start | bytes 3145736 | tf_op jit(solution)/shard_map/ppermute | solution.py:638
  345.6 291.5 %reduce-scatter.2.cloned.1.call-start = ((), (), s32[]{:S(2)}) async-start(), calls=%async_computation.13 | async-start | bytes 10485760 | tf_op jit(solution)/shard_map/reduce_scatter | solution.py:660
  550.7 266.7 %all-reduce.5.cloned.1.call-start = ((), (), s32[]{:S(2)}) async-start(), calls=%async_computation.14 | async-start | bytes 6291456 | tf_op jit(solution)/shard_map/psum | solution.py:792
  571.8 39.9 %collective-permute-start.10 = (bf16[768,2048]{1,0:T(8,128)(2,1)S(1)}, bf16[768,2048]{1,0:T(8,128)(2,1)S(1)}, u32[]{:S(2)}, u32[]{:S(2)}) collective-permute-start(bf16[768,2048]{1,0:T(8,128)(2,1)S(1)} %slice_select_fusion.3), channel_id=1, source_target_pairs={{0,1},{1,0},{2,3},{3,2},{4,5},{5,4},{6,7},{7,6},{8,9},{9,8},{10,11... | collective-permute-start | bytes 9437192 | tf_op jit(solution)/shard_map/ppermute | solution.py:638
  593.2 20.2 %collective-permute-start.11 = (bf16[768,2048]{1,0:T(8,128)(2,1)S(1)}, bf16[768,2048]{1,0:T(8,128)(2,1)}, u32[]{:S(2)}, u32[]{:S(2)}) collective-permute-start(bf16[768,2048]{1,0:T(8,128)(2,1)S(1)} %slice_select_fusion.2), channel_id=1, source_target_pairs={{0,1},{1,0},{2,3},{3,2},{4,5},{5,4},{6,7},{7,6},{8,9},{9,8},{10,11... | collective-permute-start | bytes 9437192 | tf_op jit(solution)/shard_map/ppermute | solution.py:638
  611.6 44.6 %collective-permute-start.13 = (bf16[4,256,1536]{2,1,0:T(8,128)(2,1)}, bf16[4,256,1536]{2,1,0:T(8,128)(2,1)}, u32[]{:S(2)}, u32[]{:S(2)}) collective-permute-start(bf16[4,256,1536]{2,1,0:T(8,128)(2,1)} %fusion.27), channel_id=1, source_target_pairs={{0,1},{1,0},{2,3},{3,2},{4,5},{5,4},{6,7},{7,6},{8,9},{9,8},{10,11... | collective-permute-start | bytes 9437192 | tf_op jit(solution)/shard_map/ppermute | solution.py:638
  695.1 43.1 %all-to-all-start.4 = ((bf16[4,512,256]{2,1,0:T(8,128)(2,1)}), bf16[4,512,256]{2,1,0:T(8,128)(2,1)S(1)}, u32[]{:S(2)}, u32[]{:S(2)}) async-start(bf16[4,512,256]{2,1,0:T(8,128)(2,1)} %get-tuple-element.143), calls=%async_computation.5 | async-start | bytes 2097152 | tf_op jit(solution)/shard_map/all_to_all | solution.py:648
  739.1 78.2 %all-to-all-start.6 = ((bf16[4,512,256]{2,1,0:T(8,128)(2,1)}), bf16[4,512,256]{2,1,0:T(8,128)(2,1)S(1)}, u32[]{:S(2)}, u32[]{:S(2)}) async-start(bf16[4,512,256]{2,1,0:T(8,128)(2,1)} %get-tuple-element.151), calls=%async_computation.7 | async-start | bytes 2097152 | tf_op jit(solution)/shard_map/all_to_all | solution.py:648
  817.3 81.0 %all-to-all-start.5 = ((bf16[4,512,512]{2,1,0:T(8,128)(2,1)}), bf16[4,512,512]{2,1,0:T(8,128)(2,1)}, u32[]{:S(2)}, u32[]{:S(2)}) async-start(bf16[4,512,512]{2,1,0:T(8,128)(2,1)} %attend_back.2), calls=%async_computation.6 | async-start | bytes 4194304 | tf_op jit(solution)/shard_map/all_to_all | solution.py:648
  821.8 263.5 %all-reduce.7.cloned.1.call-start = ((), (), s32[]{:S(2)}) async-start(), calls=%async_computation.15 | async-start | bytes 6291456 | tf_op jit(solution)/shard_map/psum | solution.py:835
  827.3 169.7 %collective-permute-start.14 = (bf16[2,512,1024]{2,1,0:T(8,128)(2,1)}, bf16[2,512,1024]{2,1,0:T(8,128)(2,1)}, u32[]{:S(2)}, u32[]{:S(2)}) collective-permute-start(bf16[2,512,1024]{2,1,0:T(8,128)(2,1)} %select_bitcast_fusion.2), channel_id=1, source_target_pairs={{0,8},{8,0},{16,24},{24,16},{1,9},{9,1},{17,25},{25,17},{2,10},{10... | collective-permute-start | bytes 6291464 | tf_op jit(solution)/shard_map/ppermute | solution.py:533
  831.0 165.9 %collective-permute-start.15 = (bf16[2,512,1024]{2,1,0:T(8,128)(2,1)}, bf16[2,512,1024]{2,1,0:T(8,128)(2,1)}, u32[]{:S(2)}, u32[]{:S(2)}) collective-permute-start(bf16[2,512,1024]{2,1,0:T(8,128)(2,1)} %bitcast.30), channel_id=1, source_target_pairs={{0,16},{8,24},{16,0},{24,8},{1,17},{9,25},{17,1},{25,9},{2,18},{10... | collective-permute-start | bytes 6291464 | tf_op jit(solution)/shard_map/ppermute | solution.py:533
  835.3 160.5 %collective-permute-start.16 = (bf16[2,512,512]{2,1,0:T(8,128)(2,1)}, bf16[2,512,512]{2,1,0:T(8,128)(2,1)}, u32[]{:S(2)}, u32[]{:S(2)}) collective-permute-start(bf16[2,512,512]{2,1,0:T(8,128)(2,1)} %select_bitcast_fusion.7), channel_id=1, source_target_pairs={{0,8},{8,0},{16,24},{24,16},{1,9},{9,1},{17,25},{25,17},{2,10},{10... | collective-permute-start | bytes 3145736 | tf_op jit(solution)/shard_map/ppermute | solution.py:533
  840.5 155.9 %collective-permute-start.17 = (bf16[2,512,512]{2,1,0:T(8,128)(2,1)}, bf16[2,512,512]{2,1,0:T(8,128)(2,1)}, u32[]{:S(2)}, u32[]{:S(2)}) collective-permute-start(bf16[2,512,512]{2,1,0:T(8,128)(2,1)} %bitcast.33), channel_id=1, source_target_pairs={{0,16},{8,24},{16,0},{24,8},{1,17},{9,25},{17,1},{25,9},{2,18},{10... | collective-permute-start | bytes 3145736 | tf_op jit(solution)/shard_map/ppermute | solution.py:533
  841.9 65.4 %collective-permute-start.26 = (f32[24,2048]{1,0:T(8,128)S(1)}, f32[24,2048]{1,0:T(8,128)S(1)}, u32[]{:S(2)}, u32[]{:S(2)}) collective-permute-start(f32[24,2048]{1,0:T(8,128)S(1)} %fusion.58), channel_id=1, source_target_pairs={{0,2},{1,3},{2,0},{3,1},{4,6},{5,7},{6,4},{7,5},{8,10},{9,11},{10,... | collective-permute-start | bytes 589832 | tf_op jit(solution)/shard_map/ppermute | solution.py:655
  898.3 174.6 %all-to-all-start.7 = ((bf16[4,512,512]{2,1,0:T(8,128)(2,1)}), bf16[4,512,512]{2,1,0:T(8,128)(2,1)}, u32[]{:S(2)}, u32[]{:S(2)}) async-start(bf16[4,512,512]{2,1,0:T(8,128)(2,1)} %attend_back.3), calls=%async_computation.8 | async-start | bytes 4194304 | tf_op jit(solution)/shard_map/all_to_all | solution.py:648
  907.4 86.0 %collective-permute-start.27 = (f32[24,2048]{1,0:T(8,128)S(1)}, f32[24,2048]{1,0:T(8,128)S(1)}, u32[]{:S(2)}, u32[]{:S(2)}) collective-permute-start(f32[24,2048]{1,0:T(8,128)S(1)} %add.289), channel_id=1, source_target_pairs={{0,4},{1,5},{2,6},{3,7},{4,0},{5,1},{6,2},{7,3},{8,12},{9,13},{10,... | collective-permute-start | bytes 589832 | tf_op jit(solution)/shard_map/ppermute | solution.py:655
  993.4 21.3 %collective-permute-start.24 = (bf16[256,1536]{1,0:T(8,128)(2,1)S(1)}, bf16[256,1536]{1,0:T(8,128)(2,1)S(1)}, u32[]{:S(2)}, u32[]{:S(2)}) collective-permute-start(bf16[256,1536]{1,0:T(8,128)(2,1)S(1)} %get-tuple-element.261), channel_id=1, source_target_pairs={{0,24},{8,16},{16,8},{24,0},{1,25},{9,17},{17,9},{25,1},{2,26},{10... | collective-permute-start | bytes 2359304 | tf_op jit(solution)/shard_map/ppermute | solution.py:681
  995.8 31.1 %collective-permute-start.23 = (bf16[256,1536]{1,0:T(8,128)(2,1)S(1)}, bf16[256,1536]{1,0:T(8,128)(2,1)S(1)}, u32[]{:S(2)}, u32[]{:S(2)}) collective-permute-start(bf16[256,1536]{1,0:T(8,128)(2,1)S(1)} %get-tuple-element.262), channel_id=1, source_target_pairs={{0,16},{8,24},{16,0},{24,8},{1,17},{9,25},{17,1},{25,9},{2,18},{10... | collective-permute-start | bytes 2359304 | tf_op jit(solution)/shard_map/ppermute | solution.py:681
  996.4 60.3 %collective-permute-start.22 = (bf16[256,1536]{1,0:T(8,128)(2,1)S(1)}, bf16[256,1536]{1,0:T(8,128)(2,1)S(1)}, u32[]{:S(2)}, u32[]{:S(2)}) collective-permute-start(bf16[256,1536]{1,0:T(8,128)(2,1)S(1)} %get-tuple-element.263), channel_id=1, source_target_pairs={{0,8},{8,0},{16,24},{24,16},{1,9},{9,1},{17,25},{25,17},{2,10},{10... | collective-permute-start | bytes 2359304 | tf_op jit(solution)/shard_map/ppermute | solution.py:681
  1000.2 72.7 %collective-permute-start.18 = (bf16[512,1024]{1,0:T(8,128)(2,1)}, bf16[512,1024]{1,0:T(8,128)(2,1)}, u32[]{:S(2)}, u32[]{:S(2)}) collective-permute-start(bf16[512,1024]{1,0:T(8,128)(2,1)} %select_bitcast_fusion.6), channel_id=1, source_target_pairs={{0,16},{8,24},{16,0},{24,8},{1,17},{9,25},{17,1},{25,9},{2,18},{10... | collective-permute-start | bytes 3145736 | tf_op jit(solution)/shard_map/ppermute | solution.py:533
  1005.6 67.4 %collective-permute-start.19 = (bf16[512,1024]{1,0:T(8,128)(2,1)}, bf16[512,1024]{1,0:T(8,128)(2,1)}, u32[]{:S(2)}, u32[]{:S(2)}) collective-permute-start(bf16[512,1024]{1,0:T(8,128)(2,1)} %select_bitcast_fusion.5), channel_id=1, source_target_pairs={{0,8},{8,0},{16,24},{24,16},{1,9},{9,1},{17,25},{25,17},{2,10},{10... | collective-permute-start | bytes 3145736 | tf_op jit(solution)/shard_map/ppermute | solution.py:533
  1014.7 40.5 %collective-permute-start.28 = (f32[24,2048]{1,0:T(8,128)S(1)}, f32[24,2048]{1,0:T(8,128)S(1)}, u32[]{:S(2)}, u32[]{:S(2)}) collective-permute-start(f32[24,2048]{1,0:T(8,128)S(1)} %add.290), channel_id=1, source_target_pairs={{0,8},{8,0},{16,24},{24,16},{1,9},{9,1},{17,25},{25,17},{2,10},{10... | collective-permute-start | bytes 589832 | tf_op jit(solution)/shard_map/ppermute | solution.py:655
  1026.9 46.0 %collective-permute-start.20 = (bf16[512,512]{1,0:T(8,128)(2,1)}, bf16[512,512]{1,0:T(8,128)(2,1)}, u32[]{:S(2)}, u32[]{:S(2)}) collective-permute-start(bf16[512,512]{1,0:T(8,128)(2,1)} %select_bitcast_fusion.9), channel_id=1, source_target_pairs={{0,16},{8,24},{16,0},{24,8},{1,17},{9,25},{17,1},{25,9},{2,18},{10... | collective-permute-start | bytes 1572872 | tf_op jit(solution)/shard_map/ppermute | solution.py:533
  1055.2 17.7 %collective-permute-start.21 = (bf16[512,512]{1,0:T(8,128)(2,1)}, bf16[512,512]{1,0:T(8,128)(2,1)}, u32[]{:S(2)}, u32[]{:S(2)}) collective-permute-start(bf16[512,512]{1,0:T(8,128)(2,1)} %select_bitcast_fusion.8), channel_id=1, source_target_pairs={{0,8},{8,0},{16,24},{24,16},{1,9},{9,1},{17,25},{25,17},{2,10},{10... | collective-permute-start | bytes 1572872 | tf_op jit(solution)/shard_map/ppermute | solution.py:533
  1103.4 35.5 %collective-permute-start.30 = (bf16[4,128,1536]{2,1,0:T(8,128)(2,1)S(1)}, bf16[4,128,1536]{2,1,0:T(8,128)(2,1)}, u32[]{:S(2)}, u32[]{:S(2)}) collective-permute-start(bf16[4,128,1536]{2,1,0:T(8,128)(2,1)S(1)} %get-tuple-element.163), channel_id=1, source_target_pairs={{0,2},{1,3},{6,4},{7,5},{8,10},{9,11},{14,12},{15,13},{16,18},{17,... | collective-permute-start | bytes 4718600 | tf_op jit(solution)/shard_map/ppermute | solution.py:550
  1108.7 38.5 %collective-permute-start.33 = (bf16[2,256,2048]{2,1,0:T(8,128)(2,1)}, bf16[2,256,2048]{2,1,0:T(8,128)(2,1)S(1)}, u32[]{:S(2)}, u32[]{:S(2)}) collective-permute-start(bf16[2,256,2048]{2,1,0:T(8,128)(2,1)} %select_bitcast_fusion.1), channel_id=1, source_target_pairs={{0,1},{1,0},{2,3},{3,2},{4,5},{5,4},{6,7},{7,6},{8,9},{9,8},{10,11... | collective-permute-start | bytes 6291464 | tf_op jit(solution)/shard_map/ppermute | solution.py:638
  1109.0 48.1 %collective-permute-start.37 = (bf16[2,512,1024]{2,1,0:T(8,128)(2,1)S(1)}, bf16[2,512,1024]{2,1,0:T(8,128)(2,1)}, u32[]{:S(2)}, u32[]{:S(2)}) collective-permute-start(bf16[2,512,1024]{2,1,0:T(8,128)(2,1)S(1)} %select_bitcast_fusion), channel_id=1, source_target_pairs={{0,8},{8,0},{16,24},{24,16},{1,9},{9,1},{17,25},{25,17},{2,10},{10... | collective-permute-start | bytes 6291464 | tf_op jit(solution)/shard_map/ppermute | solution.py:533
  1115.8 77.1 %collective-permute-start.42 = (bf16[2,512,1024]{2,1,0:T(8,128)(2,1)S(1)}, bf16[2,512,1024]{2,1,0:T(8,128)(2,1)S(1)}, u32[]{:S(2)}, u32[]{:S(2)}) collective-permute-start(bf16[2,512,1024]{2,1,0:T(8,128)(2,1)S(1)} %bitcast.270), channel_id=1, source_target_pairs={{0,16},{8,24},{16,0},{24,8},{1,17},{9,25},{17,1},{25,9},{2,18},{10... | collective-permute-start | bytes 6291464 | tf_op jit(solution)/shard_map/ppermute | solution.py:533
  1140.7 21.1 %collective-permute-start.31 = (bf16[4,128,1536]{2,1,0:T(8,128)(2,1)S(1)}, bf16[4,128,1536]{2,1,0:T(8,128)(2,1)S(1)}, u32[]{:S(2)}, u32[]{:S(2)}) collective-permute-start(bf16[4,128,1536]{2,1,0:T(8,128)(2,1)S(1)} %add.296), channel_id=1, source_target_pairs={{2,4},{3,5},{4,2},{5,3},{10,12},{11,13},{12,10},{13,11},{18,20},{1... | collective-permute-start | bytes 4718600 | tf_op jit(solution)/shard_map/ppermute | solution.py:550
  1141.4 39.0 %collective-permute-start.32 = (bf16[4,128,1536]{2,1,0:T(8,128)(2,1)S(1)}, bf16[4,128,1536]{2,1,0:T(8,128)(2,1)S(1)}, u32[]{:S(2)}, u32[]{:S(2)}) collective-permute-start(bf16[4,128,1536]{2,1,0:T(8,128)(2,1)S(1)} %get-tuple-element.177), channel_id=1, source_target_pairs={{0,2},{1,3},{6,4},{7,5},{8,10},{9,11},{14,12},{15,13},{16,18},{17,... | collective-permute-start | bytes 4718600 | tf_op jit(solution)/shard_map/ppermute | solution.py:550
  1180.9 37.3 %collective-permute-start.34 = (bf16[4,128,1536]{2,1,0:T(8,128)(2,1)S(1)}, bf16[4,128,1536]{2,1,0:T(8,128)(2,1)S(1)}, u32[]{:S(2)}, u32[]{:S(2)}) collective-permute-start(bf16[4,128,1536]{2,1,0:T(8,128)(2,1)S(1)} %add.304), channel_id=1, source_target_pairs={{2,0},{3,1},{4,6},{5,7},{10,8},{11,9},{12,14},{13,15},{18,16},{19,... | collective-permute-start | bytes 4718600 | tf_op jit(solution)/shard_map/ppermute | solution.py:550
  1183.0 35.2 %collective-permute-start.35 = (bf16[4,128,1536]{2,1,0:T(8,128)(2,1)S(1)}, bf16[4,128,1536]{2,1,0:T(8,128)(2,1)S(1)}, u32[]{:S(2)}, u32[]{:S(2)}) collective-permute-start(bf16[4,128,1536]{2,1,0:T(8,128)(2,1)S(1)} %add.305), channel_id=1, source_target_pairs={{2,4},{3,5},{4,2},{5,3},{10,12},{11,13},{12,10},{13,11},{18,20},{1... | collective-permute-start | bytes 4718600 | tf_op jit(solution)/shard_map/ppermute | solution.py:550
  1183.9 26.1 %collective-permute-start.38 = (bf16[512,1024]{1,0:T(8,128)(2,1)S(1)}, bf16[512,1024]{1,0:T(8,128)(2,1)S(1)}, u32[]{:S(2)}, u32[]{:S(2)}) collective-permute-start(bf16[512,1024]{1,0:T(8,128)(2,1)S(1)} %select_bitcast_fusion.4), channel_id=1, source_target_pairs={{0,16},{8,24},{16,0},{24,8},{1,17},{9,25},{17,1},{25,9},{2,18},{10... | collective-permute-start | bytes 3145736 | tf_op jit(solution)/shard_map/ppermute | solution.py:533
  1185.3 30.5 %collective-permute-start.36 = (bf16[512,1024]{1,0:T(8,128)(2,1)S(1)}, bf16[512,1024]{1,0:T(8,128)(2,1)S(1)}, u32[]{:S(2)}, u32[]{:S(2)}) collective-permute-start(bf16[512,1024]{1,0:T(8,128)(2,1)S(1)} %pad_maximum_fusion.9), channel_id=1, source_target_pairs={{0,2},{1,3},{6,4},{7,5},{8,10},{9,11},{14,12},{15,13},{16,18},{17,... | collective-permute-start | bytes 3145736 | tf_op jit(solution)/shard_map/ppermute | solution.py:550
  1194.2 121.4 %collective-permute-start.55 = (bf16[768,2048]{1,0:T(8,128)(2,1)}, bf16[768,2048]{1,0:T(8,128)(2,1)}, u32[]{:S(2)}, u32[]{:S(2)}) collective-permute-start(bf16[768,2048]{1,0:T(8,128)(2,1)} %all-reduce.7.cloned.1.call-done), channel_id=1, source_target_pairs={{0,16},{8,24},{16,0},{24,8},{1,17},{9,25},{17,1},{25,9},{2,18},{10... | collective-permute-start | bytes 9437192 | tf_op jit(solution)/shard_map/ppermute | solution.py:903
  1218.6 83.4 %collective-permute-start.39 = (bf16[4,128,1536]{2,1,0:T(8,128)(2,1)S(1)}, bf16[4,128,1536]{2,1,0:T(8,128)(2,1)S(1)}, u32[]{:S(2)}, u32[]{:S(2)}) collective-permute-start(bf16[4,128,1536]{2,1,0:T(8,128)(2,1)S(1)} %add.308), channel_id=1, source_target_pairs={{2,0},{3,1},{4,6},{5,7},{10,8},{11,9},{12,14},{13,15},{18,16},{19,... | collective-permute-start | bytes 4718600 | tf_op jit(solution)/shard_map/ppermute | solution.py:550
  1220.1 62.3 %collective-permute-start.43 = (bf16[512,1024]{1,0:T(8,128)(2,1)S(1)}, bf16[512,1024]{1,0:T(8,128)(2,1)S(1)}, u32[]{:S(2)}, u32[]{:S(2)}) collective-permute-start(bf16[512,1024]{1,0:T(8,128)(2,1)S(1)} %select_bitcast_fusion.3), channel_id=1, source_target_pairs={{0,8},{8,0},{16,24},{24,16},{1,9},{9,1},{17,25},{25,17},{2,10},{10... | collective-permute-start | bytes 3145736 | tf_op jit(solution)/shard_map/ppermute | solution.py:533
  1228.8 14.7 %collective-permute-start.47 = (f32[2,2048]{1,0:T(2,128)S(1)}, f32[2,2048]{1,0:T(2,128)S(1)}, u32[]{:S(2)}, u32[]{:S(2)}) collective-permute-start(f32[2,2048]{1,0:T(2,128)S(1)} %add.316), channel_id=1, source_target_pairs={{0,8},{8,0},{16,24},{24,16},{1,9},{9,1},{17,25},{25,17},{2,10},{10... | collective-permute-start | bytes 49160 | tf_op jit(solution)/shard_map/ppermute | solution.py:655
  1243.4 32.0 %collective-permute-start.48 = (f32[2,2048]{1,0:T(2,128)S(1)}, f32[2,2048]{1,0:T(2,128)S(1)}, u32[]{:S(2)}, u32[]{:S(2)}) collective-permute-start(f32[2,2048]{1,0:T(2,128)S(1)} %add.317), channel_id=1, source_target_pairs={{0,16},{8,24},{16,0},{24,8},{1,17},{9,25},{17,1},{25,9},{2,18},{10... | collective-permute-start | bytes 49160 | tf_op jit(solution)/shard_map/ppermute | solution.py:655
  1244.9 38.6 %collective-permute-start.40 = (bf16[512,1024]{1,0:T(8,128)(2,1)S(1)}, bf16[512,1024]{1,0:T(8,128)(2,1)S(1)}, u32[]{:S(2)}, u32[]{:S(2)}) collective-permute-start(bf16[512,1024]{1,0:T(8,128)(2,1)S(1)} %add.309), channel_id=1, source_target_pairs={{2,4},{3,5},{4,2},{5,3},{10,12},{11,13},{12,10},{13,11},{18,20},{1... | collective-permute-start | bytes 3145736 | tf_op jit(solution)/shard_map/ppermute | solution.py:550
  1275.5 26.6 %collective-permute-start.41 = (bf16[512,1024]{1,0:T(8,128)(2,1)S(1)}, bf16[512,1024]{1,0:T(8,128)(2,1)S(1)}, u32[]{:S(2)}, u32[]{:S(2)}) collective-permute-start(bf16[512,1024]{1,0:T(8,128)(2,1)S(1)} %bitcast_add_fusion.3), channel_id=1, source_target_pairs={{0,2},{1,3},{6,4},{7,5},{8,10},{9,11},{14,12},{15,13},{16,18},{17,... | collective-permute-start | bytes 3145736 | tf_op jit(solution)/shard_map/ppermute | solution.py:550
  1303.6 23.8 %collective-permute-start.49 = (bf16[512,1024]{1,0:T(8,128)(2,1)}, bf16[512,1024]{1,0:T(8,128)(2,1)}, u32[]{:S(2)}, u32[]{:S(2)}) collective-permute-start(bf16[512,1024]{1,0:T(8,128)(2,1)} %add.319), channel_id=1, source_target_pairs={{2,0},{3,1},{4,6},{5,7},{10,8},{11,9},{12,14},{13,15},{18,16},{19,... | collective-permute-start | bytes 3145736 | tf_op jit(solution)/shard_map/ppermute | solution.py:550
  1306.3 21.1 %collective-permute-start.50 = (bf16[512,1024]{1,0:T(8,128)(2,1)}, bf16[512,1024]{1,0:T(8,128)(2,1)}, u32[]{:S(2)}, u32[]{:S(2)}) collective-permute-start(bf16[512,1024]{1,0:T(8,128)(2,1)} %add.320), channel_id=1, source_target_pairs={{2,4},{3,5},{4,2},{5,3},{10,12},{11,13},{12,10},{13,11},{18,20},{1... | collective-permute-start | bytes 3145736 | tf_op jit(solution)/shard_map/ppermute | solution.py:550
  1307.9 25.8 %collective-permute-start.51 = (bf16[512,1024]{1,0:T(8,128)(2,1)}, bf16[512,1024]{1,0:T(8,128)(2,1)}, u32[]{:S(2)}, u32[]{:S(2)}) collective-permute-start(bf16[512,1024]{1,0:T(8,128)(2,1)} %bitcast_add_fusion.2), channel_id=1, source_target_pairs={{0,2},{1,3},{6,4},{7,5},{8,10},{9,11},{14,12},{15,13},{16,18},{17,... | collective-permute-start | bytes 3145736 | tf_op jit(solution)/shard_map/ppermute | solution.py:550
  1315.6 31.2 %collective-permute-start.54 = (bf16[768,2048]{1,0:T(8,128)(2,1)}, bf16[768,2048]{1,0:T(8,128)(2,1)}, u32[]{:S(2)}, u32[]{:S(2)}) collective-permute-start(bf16[768,2048]{1,0:T(8,128)(2,1)} %all-reduce.5.cloned.1.call-done.keep_ref), channel_id=1, source_target_pairs={{0,1},{1,0},{2,3},{3,2},{4,5},{5,4},{6,7},{7,6},{8,9},{9,8},{10,11... | collective-permute-start | bytes 9437192 | tf_op jit(solution)/shard_map/ppermute | solution.py:638
  1315.6 31.2 %collective-permute-start.56 = (bf16[768,2048]{1,0:T(8,128)(2,1)}, bf16[768,2048]{1,0:T(8,128)(2,1)}, u32[]{:S(2)}, u32[]{:S(2)}) collective-permute-start(bf16[768,2048]{1,0:T(8,128)(2,1)} %collective-permute-done.55.sent_ref), channel_id=1, source_target_pairs={{0,1},{1,0},{2,3},{3,2},{4,5},{5,4},{6,7},{7,6},{8,9},{9,8},{10,11... | collective-permute-start | bytes 9437192 | tf_op jit(solution)/shard_map/ppermute | solution.py:638
  1335.7 27.5 %collective-permute-start.57 = (bf16[4,256,1536]{2,1,0:T(8,128)(2,1)S(1)}, bf16[4,256,1536]{2,1,0:T(8,128)(2,1)}, u32[]{:S(2)}, u32[]{:S(2)}) collective-permute-start(bf16[4,256,1536]{2,1,0:T(8,128)(2,1)S(1)} %pad_maximum_fusion.7.refs_0_), channel_id=1, source_target_pairs={{0,1},{1,0},{2,3},{3,2},{4,5},{5,4},{6,7},{7,6},{8,9},{9,8},{10,11... | collective-permute-start | bytes 9437192 | tf_op jit(solution)/shard_map/ppermute | solution.py:638
  1339.7 35.4 %collective-permute-start.52 = (bf16[512,1024]{1,0:T(8,128)(2,1)}, bf16[512,1024]{1,0:T(8,128)(2,1)}, u32[]{:S(2)}, u32[]{:S(2)}) collective-permute-start(bf16[512,1024]{1,0:T(8,128)(2,1)} %add.321), channel_id=1, source_target_pairs={{2,0},{3,1},{4,6},{5,7},{10,8},{11,9},{12,14},{13,15},{18,16},{19,... | collective-permute-start | bytes 3145736 | tf_op jit(solution)/shard_map/ppermute | solution.py:550
  1343.9 31.2 %collective-permute-start.53 = (bf16[512,1024]{1,0:T(8,128)(2,1)}, bf16[512,1024]{1,0:T(8,128)(2,1)}, u32[]{:S(2)}, u32[]{:S(2)}) collective-permute-start(bf16[512,1024]{1,0:T(8,128)(2,1)} %add.322), channel_id=1, source_target_pairs={{2,4},{3,5},{4,2},{5,3},{10,12},{11,13},{12,10},{13,11},{18,20},{1... | collective-permute-start | bytes 3145736 | tf_op jit(solution)/shard_map/ppermute | solution.py:550
  1379.6 30.0 %collective-permute-start.58 = (bf16[512,1024]{1,0:T(8,128)(2,1)S(1)}, bf16[512,1024]{1,0:T(8,128)(2,1)}, u32[]{:S(2)}, u32[]{:S(2)}) collective-permute-start(bf16[512,1024]{1,0:T(8,128)(2,1)S(1)} %add.323), channel_id=1, source_target_pairs={{2,0},{3,1},{4,6},{5,7},{10,8},{11,9},{12,14},{13,15},{18,16},{19,... | collective-permute-start | bytes 3145736 | tf_op jit(solution)/shard_map/ppermute | solution.py:550
  (102 other events, 1262.3 us)
Sparse Core Ops, SparseCore 0:
  15.7 91.5 all-gather.6
  109.8 52.5 all-gather.8
  164.5 114.0 all-gather.14
  280.3 87.4 all-gather.12
  370.1 87.4 all-gather.10
  550.8 86.2 reduce-scatter.1
  656.3 161.0 all-reduce.4
  844.1 181.3 all-reduce.6

commit v8 on v7

--- a/solution.py
+++ b/solution.py
@@ -593,8 +593,7 @@
 
 
 def tie_all(values, work):
-    *values, work = lax.optimization_barrier((*values, work))
-    return values, work
+    return lax.optimization_barrier((values, work))
 
 
 def tie(value, work):
@@ -788,8 +787,8 @@
     )
     keep_sum = pick(part_keep[:quarter], part_keep[quarter:]) + keep_swap
     recv_sum = pick(part_recv[:quarter], part_recv[quarter:]) + recv_swap
-    d_normed, (keep_sum, recv_sum) = tie(d_normed, (keep_sum, recv_sum))
-    keep = lax.psum(keep_sum, "seq", axis_index_groups=groups)
+    d_normed, gu_sum = tie(d_normed, jnp.concatenate([keep_sum, recv_sum], axis=0))
+    gu_sum = lax.psum(gu_sum, "seq", axis_index_groups=groups)
 
     d_normed = d_normed.astype(F32)
     part_ffn = jnp.sum(d_normed * mid * factor_f, axis=0)
@@ -803,15 +802,6 @@
     down_sum = jnp.stack([moved for _, moved in trade_blocks(down_sum)])
 
     d_mid_low = jnp.concatenate([pick(low_mine, low_other), pick(low_other, low_mine)], axis=1).reshape(tokens, width)
-    def early_sum(d_logit):
-        part_gate = dot_tn(d_logit, normed_a)[:CORE_Q]
-        zero = jnp.zeros_like(part_gate)
-        part_gate = jnp.stack(
-            [pick(part_gate, zero).reshape(-1, GROUP, width), pick(zero, part_gate).reshape(-1, GROUP, width)], 1
-        )
-        part_gate = part_gate.reshape(QUERY_HEADS, width)
-        return total_sum(jnp.concatenate([part_gate, part_ffn[None], jnp.zeros((7, width), F32)], axis=0))
-
     part_out = dot_tn(d_mid_low, gated, BF)
     d_proj, d_logit, d_heads = [], [], []
     q_sum = 0.0
@@ -830,41 +820,19 @@
     back = []
     for row in range(rows):
         grads = attend_back(packed[row], d_heads[row], results[row], logs[row], start[row : row + 1], low[row])
-        if row == 0:
-            grads, (keep, recv_sum) = tie(grads, (keep, recv_sum))
-            recv = lax.psum(recv_sum, "seq", axis_index_groups=groups)
         back.append(exchange(grads))
-    cut = width // 2
-    half_out = part_out.shape[1] // 2
-    trading = [
-        Halving(out_part[:, :cut], dp, False),
-        Halving(out_part[:, cut:], dp, True),
-        Halving(part_out[:, :half_out], dp, False),
-        Halving(part_out[:, half_out:], dp, True),
-    ]
-    moved = [t.send() for t in trading]
-    back[0], moved = tie(back[0], moved)
-    while trading[0].order:
-        for t, m in zip(trading, moved):
-            t.add(m)
-        moved = [t.send() for t in trading]
-    early = early_sum(jnp.concatenate(d_logit, axis=0))
-    back[1], (moved, down_sum, early) = tie(back[1], (moved, down_sum, early))
-    for t, m in zip(trading, moved):
-        t.add(m)
-    out_sum = jnp.concatenate([trading[0].x, trading[1].x], axis=1)
-    shard_out = jnp.concatenate([trading[2].x, trading[3].x], axis=1)
-    output = (mid + out_sum.astype(F32)).astype(BF).reshape(rows, tok, width)
+    shard_out = scatter(part_out)
+    back[1], down_sum = tie(back[1], down_sum)
     for row in range(rows):
         dpr, qs, ks = unpack_heads(back[row], proj, cos, sin, q_gain, k_gain, row, chips, chip_tok)
         d_proj.append(dpr)
         q_sum = q_sum + qs
         k_sum = k_sum + ks
     d_proj = jnp.concatenate(d_proj, axis=0)
-    d_proj, recv = tie(d_proj, recv)
     d_logit = jnp.concatenate(d_logit, axis=0)
     half = width // 2
     part_qkv = [dot_tn(d_proj, normed_a[:, a : a + half], BF) for a in (0, half)]
+    part_qkv, (gu_sum, out_part, d_proj) = tie_all(part_qkv, (gu_sum, out_part, d_proj))
     trading = [Halving(p, dp, flip) for p, flip in zip(part_qkv, (False, True))]
     moved = [t.send() for t in trading]
     while trading[0].order:
@@ -874,6 +842,7 @@
     for t, m in zip(trading, moved):
         t.add(m)
     shard_qkv = [t.x for t in trading]
+    output = (mid + scatter(out_part).astype(F32)).astype(BF).reshape(rows, tok, width)
     d_norm_part = (dot_nn(d_proj, qkv_full) + dot_nn(d_logit, gate_core)).astype(BF)
     d_norm_part = d_norm_part.reshape(rows, CORES, tok, width)
     d_norm_other = swap(pick(d_norm_part[:, 1], d_norm_part[:, 0]))
@@ -893,14 +862,32 @@
     def norm_done(done):
         return [part_attn, grad_input]
 
-    def late_sum(done):
-        return [total_sum(jnp.stack([part_attn, heads]))]
-
-    grad_w_gate = lax.dynamic_slice_in_dim(early, me * gate_count, gate_count, 0)
+    part_gate = dot_tn(d_logit, normed_a)[:CORE_Q]
+    zero = jnp.zeros_like(part_gate)
+    part_gate = jnp.stack(
+        [pick(part_gate, zero).reshape(-1, GROUP, width), pick(zero, part_gate).reshape(-1, GROUP, width)], 1
+    )
+    part_gate = part_gate.reshape(QUERY_HEADS, width)
+    small = jnp.concatenate([part_gate, part_ffn[None], part_attn[None], heads[None], jnp.zeros((5, width), F32)], axis=0)
+    hops = [("dp", 1 << k) for k in range(dp.bit_length() - 1)] + [("seq", 1 << k) for k in range(seq.bit_length() - 1)]
+    near = dp.bit_length()
+    sums_at = [small]
+
+    def hop(some):
+        def work(done):
+            x = sums_at[-1]
+            for name, bit in some:
+                x = x + lax.ppermute(x, name, [(p, p ^ bit) for p in range(lax.axis_size(name))])
+            sums_at.append(x)
+            return [x]
+
+        return work
+
 
     mid_cut = down_sum.shape[1] // 2
     line = Line(chips, chip)
-    sent = lax.ppermute(recv, "dp", trade)
+    keep = gu_sum[:quarter]
+    sent = lax.ppermute(gu_sum[quarter:], "dp", trade)
 
     def join_early(done):
         down_done = jnp.concatenate(done[:2], axis=1)
@@ -911,21 +898,29 @@
         ]
 
     def join_late(done):
-        return [join_cols([done[2]], [swap(done[2])], core, GROUP * HEAD)]
-
-    sums, ((_, grad_input), (late,), (grad_gu, grad_down), (grad_out,)) = line.pipeline(
+        return [join_cols([done[2]], [swap(done[2])], core, GROUP * HEAD), output]
+
+    sums, ((_, grad_input), _, _, (small,), (grad_gu, grad_down), (grad_out, output)) = line.pipeline(
         [down_sum[:, :mid_cut], down_sum[:, mid_cut:], shard_out, *shard_qkv],
-        {1: norm_done, 3: late_sum, 5: join_early, 6: join_late},
+        {
+            1: norm_done,
+            2: hop(hops[:near]),
+            3: hop(hops[near : near + 1]),
+            4: hop(hops[near + 1 :]),
+            5: join_early,
+            6: join_late,
+        },
     )
+    grad_w_gate = lax.dynamic_slice_in_dim(small, me * gate_count, gate_count, 0)
     qkv_sum = sums[3:]
     grad_qkv = join_rows(qkv_sum, [swap(p) for p in qkv_sum], core, jnp.where(q_shard, GROUP, 1), HEAD)
     return (
         output,
         grad_input,
-        late[0],
-        late[1, :HEAD],
-        late[1, HEAD : 2 * HEAD],
-        early[QUERY_HEADS],
+        small[QUERY_HEADS + 1],
+        small[QUERY_HEADS + 2, :HEAD],
+        small[QUERY_HEADS + 2, HEAD : 2 * HEAD],
+        small[QUERY_HEADS],
         grad_qkv,
         grad_w_gate,
         grad_out,

time: 1440 us -> 1430 us (level)
  blocking collectives: 52.5 us -> 112 us
  starting transfers between devices: 125 us -> 88.6 us
  waiting for transfers between devices: 640 us -> 614 us
  other arithmetic: 173 us -> 158 us
    ppermute x12 -> x2, waiting for transfers between devices: 165 us -> 3.66 us  [total_sum(): x = x + lax.ppermute(x, name, [(s, s ^ step) for s in range(size)])]
    ppermute x1 -> x6, waiting for transfers between devices: 0.01 us -> 108 us  [the longest x5 108 us: work(): lax.ppermute(x, name, [(p, p ^ bit) for p in range(lax.axis_size(name))])]
    all_to_all x7 -> x6, waiting for transfers between devices: 84.7 us -> 159 us  [exchange(): return lax.all_to_all(x, 'seq', 0, 0, axis_index_groups=groups, tiled=True)]
    all_to_all x1 -> x2, blocking collectives: 52.5 us -> 112 us  [exchange(): return lax.all_to_all(x, 'seq', 0, 0, axis_index_groups=groups, tiled=True)]
    psum x2 -> x1, waiting for transfers between devices: 54.6 us -> 0.01 us  [shards(): gu_sum = lax.psum(gu_sum, 'seq', axis_index_groups=groups)]
    ppermute x12 -> x2, starting transfers between devices: 24 us -> 4.1 us  [total_sum(): x = x + lax.ppermute(x, name, [(s, s ^ step) for s in range(size)])]
    ppermute x15, waiting for transfers between devices: 92.4 us -> 72.6 us  [send(): return (x, lax.ppermute(x, 'seq', self.stages[stage]))]
    ppermute x6, waiting for transfers between devices: 63.5 us -> 80.7 us  [trade_blocks(): lax.ppermute(out, 'dp', [(d, d ^ k) for d in range(dp)])]
  transfers between devices with their start and end apart: 77 -> 64, of which waited for: 33 -> 27; matrix products, arithmetic and copies ran while one was open for 21% -> 23% of each run, Pallas kernels for 10% -> 10%
where the time goes in v8:
time: 1430 us
  waiting for transfers between devices  614 us (43%)
  matrix products  251 us (18%)
  other arithmetic  158 us (11%)
  Pallas kernels  145 us (10%)
  blocking collectives  112 us (8%)
  starting transfers between devices  88.6 us (6%)
  local copies, waits for them, and re-layouts  43.2 us (3%)
  between operations  15.6 us (1%)
    all_to_all x6, waiting for transfers between devices, exchange(): return lax.all_to_all(x, 'seq', 0, 0, axis_index_groups=groups, tiled=True)  159 us
    all_gather x4, waiting for transfers between devices, gather(): return lax.all_gather(x, 'dp', axis=0, tiled=True)  128 us
    all_to_all x2, blocking collectives, exchange(): return lax.all_to_all(x, 'seq', 0, 0, axis_index_groups=groups, tiled=True)  112 us
    ppermute x5, waiting for transfers between devices, work(): lax.ppermute(x, name, [(p, p ^ bit) for p in range(lax.axis_size(name))])  108 us
    dot_general x7, matrix products, dot_nt(): lax.dot_general(left, right, (((1,), (1,)), ((), ())), preferred_element_...  94.6 us
    dot_general x7, matrix products, dot_nn(): lax.dot_general(left, right, (((1,), (0,)), ((), ())), preferred_element_...  85.8 us
    ppermute x6, waiting for transfers between devices, trade_blocks(): lax.ppermute(out, 'dp', [(d, d ^ k) for d in range(dp)])  80.7 us
    ppermute x15, waiting for transfers between devices, send(): return (x, lax.ppermute(x, 'seq', self.stages[stage]))  72.6 us
  transfers between devices with their start and end apart: 64, of which 27 were waited for; matrix products, arithmetic and copies ran while one was open for 23% of the time, Pallas kernels for 10%

profile of v8, /device:TPU:0, one launch (start us, length us, event | category | flops | bytes accessed | tf_op | source)
XLA Modules:
  0.0 1427.2 jit_solution(12513064749409340300)
XLA Ops:
  30.5 6.6 select_select_fusion
  53.0 54.4 %all-gather.7.cloned.1.call-done = bf16[2048,2048]{1,0:T(8,128)(2,1)} async-done(((bf16[512,2048]{1,0:T(8,128)(2,1)}), bf16[2048,2048]{1,0:T(8,128)(2,1)}) %all-gather.7.cloned.1.call-update) | async-done | bytes 8388624 | tf_op jit(solution)/shard_map/all_gather | solution.py:662
  117.1 11.1 fusion.66.proj_ref
  128.2 6.2 pack_heads.2
  134.4 52.5 %all_to_all.40.q_ref.k_ref.v_ref = bf16[4,512,512]{2,1,0:T(8,128)(2,1)} all-to-all(bf16[4,512,512]{2,1,0:T(8,128)(2,1)} %pack_heads.2), channel_id=1, replica_groups={{0,2,4,6},{1,3,5,7},{8,10,12,14},{9,11,13,15},{16,18,20,22},{17,19,21,2..., dimensions={0} | all-to-all | bytes 4194304 | tf_op jit(solution)/shard_map/all_to_all | solution.py:647
  186.9 6.2 pack_heads.3
  205.7 15.7 %collective-permute-done.3 = bf16[256,1536]{1,0:T(8,128)(2,1)S(1)} collective-permute-done((bf16[256,1536]{1,0:T(8,128)(2,1)S(1)}, bf16[256,1536]{1,0:T(8,128)(2,1)S(1)}, u32[]{:S(2)}, u32[]{:S(2)}) %collective-permute-start.3) | collective-permute-done | bytes 786464 | tf_op jit(solution)/shard_map/ppermute | solution.py:680
  222.3 34.0 %collective-permute-done.4 = bf16[256,1536]{1,0:T(8,128)(2,1)S(1)} collective-permute-done((bf16[256,1536]{1,0:T(8,128)(2,1)S(1)}, bf16[256,1536]{1,0:T(8,128)(2,1)S(1)}, u32[]{:S(2)}, u32[]{:S(2)}) %collective-permute-start.4) | collective-permute-done | bytes 786464 | tf_op jit(solution)/shard_map/ppermute | solution.py:680
  259.5 10.8 attend.2
  270.3 5.2 all-to-all-start.2
  275.5 10.7 attend.3
  286.2 12.5 all-to-all-done.2.res_ref
  305.0 4.9 convolution_convert_fusion.11
  311.2 16.2 %all-to-all-done.3.res_ref = bf16[4,512,256]{2,1,0:T(8,128)(2,1)S(1)} async-done(((bf16[4,512,256]{2,1,0:T(8,128)(2,1)}), bf16[4,512,256]{2,1,0:T(8,128)(2,1)S(1)}, u32[]{:S(2)}, u32[]{:S(2)}) %all-to-all-start.3) | async-done | bytes 1048608 | tf_op jit(solution)/shard_map/all_to_all | solution.py:647
  331.0 5.0 convolution_convert_fusion.10
  345.0 4.8 slice_select_fusion.4
  367.8 18.6 %convolution_convert_fusion.3 = bf16[2048,1536]{1,0:T(8,128)(2,1)} fusion(bf16[2048,2048]{1,0:T(8,128)(2,1)} %all-gather.13.cloned.1.call-done, bf16[2048,1536]{1,0:T(8,128)(2,1)} %bitcast.202), kind=kOutput, calls=%fused_computation.24 | convolution fusion | flops 12888047616 | bytes 20971520 | tf_op jit(solution)/shard_map/dot_general | solution.py:33
  386.4 71.2 %all-gather.11.cloned.1.call-done = bf16[2048,2048]{1,0:T(8,128)(2,1)} async-done(((bf16[512,2048]{1,0:T(8,128)(2,1)}), bf16[2048,2048]{1,0:T(8,128)(2,1)}) %all-gather.11.cloned.1.call-update) | async-done | bytes 8388624 | tf_op jit(solution)/shard_map/all_gather | solution.py:662
  457.6 19.7 %convolution_convert_fusion.1 = bf16[2048,1536]{1,0:T(8,128)(2,1)} fusion(bf16[2048,2048]{1,0:T(8,128)(2,1)} %all-gather.11.cloned.1.call-done, bf16[3072,2048]{1,0:T(8,128)(2,1)} %param.21, pred[]{:T(512)S(6)} %ge.19), kind=kOutput, calls=%fused_computation.22 | convolution fusion | flops 12891193344 | bytes 27262976 | tf_op jit(solution)/shard_map/dot_general | solution.py:29
  477.3 32.2 %select_convert_fusion = (bf16[2048,1536]{1,0:T(8,128)(2,1)}, bf16[2048,1536]{1,0:T(8,128)(2,1)}, bf16[2048,1536]{1,0:T(8,128)(2,1)}) fusion(bf16[2048,1536]{1,0:T(8,128)(2,1)} %convolution_convert_fusion.3, pred[]{:T(512)S(6)} %ge.19, bf16[2048,1536]{1,0:T(8,128)(2,1)} %convolution_convert_fusion.1, bf16[2048,2048]{1,0:T(8,128)(2,1)} %all-gather.11.cloned.1.call-done, ...), kind=kOutput, calls=%fused_computation.14 | convolution fusion | flops 12957253632 | bytes 46137344 | tf_op jit(solution)/shard_map/dot_general | solution.py:29
  509.6 21.8 %fusion.45 = f32[2048,2048]{1,0:T(8,128)} fusion(bf16[2048,1536]{1,0:T(8,128)(2,1)} %get-tuple-element.215, bf16[3072,2048]{1,0:T(8,128)(2,1)} %param.21, pred[]{:T(512)S(6)} %ge.19), kind=kOutput, calls=%fused_computation.140 | convolution fusion | flops 12888047616 | bytes 35651584 | tf_op jit(solution)/shard_map/dot_general | solution.py:33
  531.4 19.1 %add_convert_fusion = bf16[2048,2048]{1,0:T(8,128)(2,1)} fusion(f32[2048,2048]{1,0:T(8,128)} %fusion.45, bf16[2048,1536]{1,0:T(8,128)(2,1)S(1)} %copy-done.75, bf16[1536,2048]{1,0:T(8,128)(2,1)} %pad_maximum_fusion.1), kind=kOutput, calls=%fused_computation.3 | convolution fusion | flops 12893290496 | bytes 37748736 | tf_op jit(solution)/shard_map/dot_general | solution.py:33
  550.6 17.8 %convolution_convert_fusion.6 = bf16[1536,2048]{1,0:T(8,128)(2,1)S(1)} fusion(bf16[2048,1536]{1,0:T(8,128)(2,1)} %get-tuple-element.215, bf16[2048,2048]{1,0:T(8,128)(2,1)} %all-gather.11.cloned.1.call-done), kind=kOutput, calls=%fused_computation.27 | convolution fusion | flops 12888047616 | bytes 20971520 | tf_op jit(solution)/shard_map/dot_general | solution.py:37
  571.7 18.6 %convolution_convert_fusion.5 = bf16[1536,2048]{1,0:T(8,128)(2,1)S(1)} fusion(bf16[2048,1536]{1,0:T(8,128)(2,1)} %get-tuple-element.214, bf16[2048,2048]{1,0:T(8,128)(2,1)} %all-gather.11.cloned.1.call-done), kind=kOutput, calls=%fused_computation.26 | convolution fusion | flops 12888047616 | bytes 20971520 | tf_op jit(solution)/shard_map/dot_general | solution.py:37
  593.4 14.3 %convolution_convert_fusion.4 = bf16[2048,1536]{1,0:T(8,128)(2,1)S(1)} fusion(bf16[2048,2048]{1,0:T(8,128)(2,1)S(1)} %bitcast.222, bf16[2048,1536]{1,0:T(8,128)(2,1)S(1)} %bitcast.224), kind=kOutput, calls=%fused_computation.25 | convolution fusion | flops 12888047616 | bytes 20971520 | tf_op jit(solution)/shard_map/dot_general | solution.py:37
  611.6 25.4 %reduce-scatter.4.cloned.1.call-done = bf16[512,2048]{1,0:T(8,128)(2,1)} async-done(((bf16[2048,2048]{1,0:T(8,128)(2,1)}), bf16[512,2048]{1,0:T(8,128)(2,1)}) %reduce-scatter.4.cloned.1.call-update) | async-done | bytes 2097168 | tf_op jit(solution)/shard_map/reduce_scatter | solution.py:659
  637.0 6.1 select_add_fusion
  655.0 4.5 collective-permute-done.12
  666.2 6.2 convolution_convert_fusion.9
  672.4 6.3 fusion.32.grad_ref
  682.6 19.6 %convolution_convert_fusion = bf16[2048,2048]{1,0:T(8,128)(2,1)} fusion(bf16[2048,1536]{1,0:T(8,128)(2,1)} %get-tuple-element.131, bf16[2048,1536]{1,0:T(8,128)(2,1)} %bitcast.203), kind=kOutput, calls=%fused_computation.21 | convolution fusion | flops 12889096192 | bytes 20971520 | tf_op jit(solution)/shard_map/dot_general | solution.py:29
  702.3 5.9 fusion.67.grad_ref
  712.2 59.2 %all_to_all.41.grad_ref = bf16[4,512,256]{2,1,0:T(8,128)(2,1)} all-to-all(bf16[4,512,256]{2,1,0:T(8,128)(2,1)} %get-tuple-element.133), channel_id=1, replica_groups={{0,2,4,6},{1,3,5,7},{8,10,12,14},{9,11,13,15},{16,18,20,22},{17,19,21,2..., dimensions={0} | all-to-all | bytes 2097152 | tf_op jit(solution)/shard_map/all_to_all | solution.py:647
  775.2 19.7 %attend_back.2 = bf16[4,512,512]{2,1,0:T(8,128)(2,1)} custom-call(s32[4]{0:T(128)} %get-tuple-element.275.low_ref, bf16[4,512,512]{2,1,0:T(8,128)(2,1)} %all_to_all.40.q_ref.k_ref.v_ref, bf16[4,512,512]{2,1,0:T(8,128)(2,1)} %all_to_all.40.q_ref.k_ref.v_ref, bf16[4,512,512]{2,1,0:T(8,128)(2,1)} %all_to_all.40.q_ref.k_ref.v_ref, ...), custom_call_target="tpu_custom_call" | custom-call | tf_op jit(solution)/shard_map/attend_back/pallas_call | solution.py:281
  795.0 14.9 %all-to-all-done.6.grad_ref = bf16[4,512,256]{2,1,0:T(8,128)(2,1)S(1)} async-done(((bf16[4,512,256]{2,1,0:T(8,128)(2,1)}), bf16[4,512,256]{2,1,0:T(8,128)(2,1)S(1)}, u32[]{:S(2)}, u32[]{:S(2)}) %all-to-all-start.6) | async-done | bytes 1048608 | tf_op jit(solution)/shard_map/all_to_all | solution.py:647
  814.3 20.1 %attend_back.3 = bf16[4,512,512]{2,1,0:T(8,128)(2,1)} custom-call(s32[4]{0:T(128)} %get-tuple-element.274.low_ref, bf16[4,512,512]{2,1,0:T(8,128)(2,1)} %copy-done, bf16[4,512,512]{2,1,0:T(8,128)(2,1)} %copy-done, bf16[4,512,512]{2,1,0:T(8,128)(2,1)} %copy-done, bf16[4,512,256]{2,1,0:T(8,128)(2,1)} %copy-done.38, ...), custom_call_target="tpu_custom_call" | custom-call | tf_op jit(solution)/shard_map/attend_back/pallas_call | solution.py:281
  834.4 84.0 %all-to-all-done.5.grad_ref = bf16[4,512,512]{2,1,0:T(8,128)(2,1)S(1)} async-done(((bf16[4,512,512]{2,1,0:T(8,128)(2,1)}), bf16[4,512,512]{2,1,0:T(8,128)(2,1)S(1)}, u32[]{:S(2)}, u32[]{:S(2)}) %all-to-all-start.5) | async-done | bytes 2097184 | tf_op jit(solution)/shard_map/all_to_all | solution.py:647
  922.9 4.8 fusion.25
  933.3 17.6 %collective-permute-done.16 = bf16[256,1536]{1,0:T(8,128)(2,1)} collective-permute-done((bf16[256,1536]{1,0:T(8,128)(2,1)}, bf16[256,1536]{1,0:T(8,128)(2,1)}, u32[]{:S(2)}, u32[]{:S(2)}) %collective-permute-start.16) | collective-permute-done | bytes 786464 | tf_op jit(solution)/shard_map/ppermute | solution.py:680
  950.9 13.3 collective-permute-done.15
  967.5 7.5 unpack_heads.3
  974.9 30.8 %all-to-all-done.7.grad_ref = bf16[4,512,512]{2,1,0:T(8,128)(2,1)} async-done(((bf16[4,512,512]{2,1,0:T(8,128)(2,1)}), bf16[4,512,512]{2,1,0:T(8,128)(2,1)}, u32[]{:S(2)}, u32[]{:S(2)}) %all-to-all-start.7) | async-done | bytes 2097184 | tf_op jit(solution)/shard_map/all_to_all | solution.py:647
  1005.8 7.5 unpack_heads.2
  1016.7 6.3 convolution_convert_fusion.8
  1022.9 6.3 convolution_convert_fusion.7
  1029.3 12.9 fusion.68
  1056.7 4.6 broadcast_select_fusion.6
  1063.0 20.5 %collective-permute-done.17 = bf16[4,128,1536]{2,1,0:T(8,128)(2,1)} collective-permute-done((bf16[4,128,1536]{2,1,0:T(8,128)(2,1)}, bf16[4,128,1536]{2,1,0:T(8,128)(2,1)}, u32[]{:S(2)}, u32[]{:S(2)}) %collective-permute-start.17) | collective-permute-done | bytes 1572896 | tf_op jit(solution)/shard_map/ppermute | solution.py:550
  1088.7 6.8 collective-permute-start.19
  1095.6 5.4 fusion.22
  1102.7 28.5 %collective-permute-done.24 = bf16[2,512,1024]{2,1,0:T(8,128)(2,1)} collective-permute-done((bf16[2,512,1024]{2,1,0:T(8,128)(2,1)}, bf16[2,512,1024]{2,1,0:T(8,128)(2,1)}, u32[]{:S(2)}, u32[]{:S(2)}) %collective-permute-start.24) | collective-permute-done | bytes 2097184 | tf_op jit(solution)/shard_map/ppermute | solution.py:533
  1131.3 4.5 bitcast_add_fusion
  1149.5 43.5 %collective-permute-done.27 = f32[24,2048]{1,0:T(8,128)S(1)} collective-permute-done((f32[24,2048]{1,0:T(8,128)S(1)}, f32[24,2048]{1,0:T(8,128)S(1)}, u32[]{:S(2)}, u32[]{:S(2)}) %collective-permute-start.27) | collective-permute-done | bytes 196640 | tf_op jit(solution)/shard_map/ppermute | solution.py:880
  1193.1 6.0 collective-permute-start.23
  1206.8 15.2 %collective-permute-done.23 = bf16[512,1024]{1,0:T(8,128)(2,1)S(1)} collective-permute-done((bf16[512,1024]{1,0:T(8,128)(2,1)S(1)}, bf16[512,1024]{1,0:T(8,128)(2,1)S(1)}, u32[]{:S(2)}, u32[]{:S(2)}) %collective-permute-start.23) | collective-permute-done | bytes 1048608 | tf_op jit(solution)/shard_map/ppermute | solution.py:550
  1228.4 36.1 %collective-permute-done.34 = f32[24,2048]{1,0:T(8,128)S(1)} collective-permute-done((f32[24,2048]{1,0:T(8,128)S(1)}, f32[24,2048]{1,0:T(8,128)S(1)}, u32[]{:S(2)}, u32[]{:S(2)}) %collective-permute-start.34) | collective-permute-done | bytes 196640 | tf_op jit(solution)/shard_map/ppermute | solution.py:880
  1267.2 20.4 %collective-permute-done.31 = bf16[512,1024]{1,0:T(8,128)(2,1)S(1)} collective-permute-done((bf16[512,1024]{1,0:T(8,128)(2,1)S(1)}, bf16[512,1024]{1,0:T(8,128)(2,1)S(1)}, u32[]{:S(2)}, u32[]{:S(2)}) %collective-permute-start.31) | collective-permute-done | bytes 1048608 | tf_op jit(solution)/shard_map/ppermute | solution.py:550
  1293.6 6.8 collective-permute-start.37
  1300.4 28.3 %collective-permute-done.38 = f32[24,2048]{1,0:T(8,128)S(1)} collective-permute-done((f32[24,2048]{1,0:T(8,128)S(1)}, f32[24,2048]{1,0:T(8,128)S(1)}, u32[]{:S(2)}, u32[]{:S(2)}) %collective-permute-start.38) | collective-permute-done | bytes 196640 | tf_op jit(solution)/shard_map/ppermute | solution.py:880
  1344.0 16.4 %join_units.1 = f32[3072,2048]{1,0:T(8,128)} custom-call(s32[2]{0:T(128)} %pad_add_fusion.which_ref, bf16[768,2048]{1,0:T(8,128)(2,1)} %get-tuple-element.218.keep_ref, bf16[768,2048]{1,0:T(8,128)(2,1)} %collective-permute-done.41.keep_other_ref, bf16[768,2048]{1,0:T(8,128)(2,1)} %collective-permute-done.42.sent_ref, ...), custom_call_target="tpu_custom_call" | custom-call | tf_op jit(solution)/shard_map/join_units/pallas_call | solution.py:478
  1360.5 12.0 join_blocks.1
  1378.1 6.5 join_cols.1
  1388.8 16.4 %collective-permute-done.45 = bf16[512,1024]{1,0:T(8,128)(2,1)} collective-permute-done((bf16[512,1024]{1,0:T(8,128)(2,1)S(1)}, bf16[512,1024]{1,0:T(8,128)(2,1)}, u32[]{:S(2)}, u32[]{:S(2)}) %collective-permute-start.45) | collective-permute-done | bytes 1048608 | tf_op jit(solution)/shard_map/ppermute | solution.py:550
  1412.0 8.4 join_rows.1
  (408 shorter events, 256.0 us)
Async XLA Ops:
  7.2 100.2 %all-gather.7.cloned.1.call-start = ((), (), s32[]{:S(2)}) async-start(), calls=%async_computation.11 | async-start | bytes 10485760 | tf_op jit(solution)/shard_map/all_gather | solution.py:662
  15.6 289.4 %all-gather.9.cloned.1.call-start = ((), (), s32[]{:S(2)}) async-start(), calls=%async_computation.12 | async-start | bytes 5242880 | tf_op jit(solution)/shard_map/all_gather | solution.py:662
  15.7 30.1 %collective-permute-start = (bf16[2,256,2048]{2,1,0:T(8,128)(2,1)S(1)}, bf16[2,256,2048]{2,1,0:T(8,128)(2,1)}, u32[]{:S(2)}, u32[]{:S(2)}) collective-permute-start(bf16[2,256,2048]{2,1,0:T(8,128)(2,1)S(1)} %copy-done.6), channel_id=1, source_target_pairs={{0,1},{1,0},{2,3},{3,2},{4,5},{5,4},{6,7},{7,6},{8,9},{9,8},{10,11... | collective-permute-start | bytes 6291464 | tf_op jit(solution)/shard_map/ppermute | solution.py:637
  16.3 23.2 %collective-permute-start.1 = (bf16[16,2048]{1,0:T(8,128)(2,1)S(1)}, bf16[16,2048]{1,0:T(8,128)(2,1)S(1)}, u32[]{:S(2)}, u32[]{:S(2)}) collective-permute-start(bf16[16,2048]{1,0:T(8,128)(2,1)S(1)} %constant_dynamic-update-slice_fusion.4), channel_id=1, source_target_pairs={{0,8},{8,0},{16,24},{24,16},{1,9},{9,1},{17,25},{25,17},{2,10},{10... | collective-permute-start | bytes 196616 | tf_op jit(solution)/shard_map/ppermute | solution.py:654
  21.6 323.4 %all-gather.15.cloned.1.call-start = ((), (), s32[]{:S(2)}) async-start(), calls=%async_computation.19 | async-start | bytes 9437184 | tf_op jit(solution)/shard_map/all_gather | solution.py:709
  39.5 6.2 collective-permute-start.2
  107.4 260.4 %all-gather.13.cloned.1.call-start = ((), (), s32[]{:S(2)}) async-start(), calls=%async_computation.14 | async-start | bytes 10485760 | tf_op jit(solution)/shard_map/all_gather | solution.py:662
  193.1 65.1 %all-to-all-start.1 = ((bf16[4,512,512]{2,1,0:T(8,128)(2,1)}), bf16[4,512,512]{2,1,0:T(8,128)(2,1)S(1)}, u32[]{:S(2)}, u32[]{:S(2)}) async-start(bf16[4,512,512]{2,1,0:T(8,128)(2,1)} %pack_heads.3), calls=%async_computation.1 | async-start | bytes 4194304 | tf_op jit(solution)/shard_map/all_to_all | solution.py:647
  201.0 20.4 %collective-permute-start.3 = (bf16[256,1536]{1,0:T(8,128)(2,1)S(1)}, bf16[256,1536]{1,0:T(8,128)(2,1)S(1)}, u32[]{:S(2)}, u32[]{:S(2)}) collective-permute-start(bf16[256,1536]{1,0:T(8,128)(2,1)S(1)} %get-tuple-element.243), channel_id=1, source_target_pairs={{0,8},{8,0},{16,24},{24,16},{1,9},{9,1},{17,25},{25,17},{2,10},{10... | collective-permute-start | bytes 2359304 | tf_op jit(solution)/shard_map/ppermute | solution.py:680
  203.1 53.3 %collective-permute-start.4 = (bf16[256,1536]{1,0:T(8,128)(2,1)S(1)}, bf16[256,1536]{1,0:T(8,128)(2,1)S(1)}, u32[]{:S(2)}, u32[]{:S(2)}) collective-permute-start(bf16[256,1536]{1,0:T(8,128)(2,1)S(1)} %get-tuple-element.242), channel_id=1, source_target_pairs={{0,16},{8,24},{16,0},{24,8},{1,17},{9,25},{17,1},{25,9},{2,18},{10... | collective-permute-start | bytes 2359304 | tf_op jit(solution)/shard_map/ppermute | solution.py:680
  204.2 53.1 %collective-permute-start.5 = (bf16[256,1536]{1,0:T(8,128)(2,1)S(1)}, bf16[256,1536]{1,0:T(8,128)(2,1)S(1)}, u32[]{:S(2)}, u32[]{:S(2)}) collective-permute-start(bf16[256,1536]{1,0:T(8,128)(2,1)S(1)} %get-tuple-element.241), channel_id=1, source_target_pairs={{0,24},{8,16},{16,8},{24,0},{1,25},{9,17},{17,9},{25,1},{2,26},{10... | collective-permute-start | bytes 2359304 | tf_op jit(solution)/shard_map/ppermute | solution.py:680
  270.3 28.4 %all-to-all-start.2 = ((bf16[4,512,256]{2,1,0:T(8,128)(2,1)}), bf16[4,512,256]{2,1,0:T(8,128)(2,1)S(1)}, u32[]{:S(2)}, u32[]{:S(2)}) async-start(bf16[4,512,256]{2,1,0:T(8,128)(2,1)} %get-tuple-element.114.res_ref), calls=%async_computation.2 | async-start | bytes 2097152 | tf_op jit(solution)/shard_map/all_to_all | solution.py:647
  298.7 28.7 %all-to-all-start.3 = ((bf16[4,512,256]{2,1,0:T(8,128)(2,1)}), bf16[4,512,256]{2,1,0:T(8,128)(2,1)S(1)}, u32[]{:S(2)}, u32[]{:S(2)}) async-start(bf16[4,512,256]{2,1,0:T(8,128)(2,1)} %get-tuple-element.116.res_ref), calls=%async_computation.3 | async-start | bytes 2097152 | tf_op jit(solution)/shard_map/all_to_all | solution.py:647
  302.2 155.3 %all-gather.11.cloned.1.call-start = ((), (), s32[]{:S(2)}) async-start(), calls=%async_computation.13 | async-start | bytes 10485760 | tf_op jit(solution)/shard_map/all_gather | solution.py:662
  311.2 25.1 %collective-permute-start.6 = (bf16[256,2048]{1,0:T(8,128)(2,1)S(1)}, bf16[256,2048]{1,0:T(8,128)(2,1)S(1)}, u32[]{:S(2)}, u32[]{:S(2)}) collective-permute-start(bf16[256,2048]{1,0:T(8,128)(2,1)S(1)} %broadcast_select_fusion.19), channel_id=1, source_target_pairs={{0,1},{1,0},{2,3},{3,2},{4,5},{5,4},{6,7},{7,6},{8,9},{9,8},{10,11... | collective-permute-start | bytes 3145736 | tf_op jit(solution)/shard_map/ppermute | solution.py:637
  336.2 2.7 collective-permute-start.7
  344.3 292.7 %reduce-scatter.4.cloned.1.call-start = ((), (), s32[]{:S(2)}) async-start(), calls=%async_computation.15 | async-start | bytes 10485760 | tf_op jit(solution)/shard_map/reduce_scatter | solution.py:659
  344.8 6.1 collective-permute-start.8
  349.8 7.9 collective-permute-start.9
  550.5 478.7 %all-reduce.4.cloned.1.call-start = ((), (), s32[]{:S(2)}) async-start(), calls=%async_computation.17 | async-start | bytes 12582912 | tf_op jit(solution)/shard_map/psum | solution.py:791
  571.7 40.0 %collective-permute-start.10 = (bf16[768,2048]{1,0:T(8,128)(2,1)S(1)}, bf16[768,2048]{1,0:T(8,128)(2,1)S(1)}, u32[]{:S(2)}, u32[]{:S(2)}) collective-permute-start(bf16[768,2048]{1,0:T(8,128)(2,1)S(1)} %slice_select_fusion.3), channel_id=1, source_target_pairs={{0,1},{1,0},{2,3},{3,2},{4,5},{5,4},{6,7},{7,6},{8,9},{9,8},{10,11... | collective-permute-start | bytes 9437192 | tf_op jit(solution)/shard_map/ppermute | solution.py:637
  593.0 18.6 %collective-permute-start.11 = (bf16[768,2048]{1,0:T(8,128)(2,1)S(1)}, bf16[768,2048]{1,0:T(8,128)(2,1)}, u32[]{:S(2)}, u32[]{:S(2)}) collective-permute-start(bf16[768,2048]{1,0:T(8,128)(2,1)S(1)} %slice_select_fusion.2), channel_id=1, source_target_pairs={{0,1},{1,0},{2,3},{3,2},{4,5},{5,4},{6,7},{7,6},{8,9},{9,8},{10,11... | collective-permute-start | bytes 9437192 | tf_op jit(solution)/shard_map/ppermute | solution.py:637
  611.4 43.5 %collective-permute-start.13 = (bf16[4,256,1536]{2,1,0:T(8,128)(2,1)}, bf16[4,256,1536]{2,1,0:T(8,128)(2,1)}, u32[]{:S(2)}, u32[]{:S(2)}) collective-permute-start(bf16[4,256,1536]{2,1,0:T(8,128)(2,1)} %fusion.27), channel_id=1, source_target_pairs={{0,1},{1,0},{2,3},{3,2},{4,5},{5,4},{6,7},{7,6},{8,9},{9,8},{10,11... | collective-permute-start | bytes 9437192 | tf_op jit(solution)/shard_map/ppermute | solution.py:637
  654.9 4.5 collective-permute-start.12
  771.4 38.5 %all-to-all-start.6 = ((bf16[4,512,256]{2,1,0:T(8,128)(2,1)}), bf16[4,512,256]{2,1,0:T(8,128)(2,1)S(1)}, u32[]{:S(2)}, u32[]{:S(2)}) async-start(bf16[4,512,256]{2,1,0:T(8,128)(2,1)} %get-tuple-element.142), calls=%async_computation.8 | async-start | bytes 2097152 | tf_op jit(solution)/shard_map/all_to_all | solution.py:647
  809.9 108.5 %all-to-all-start.5 = ((bf16[4,512,512]{2,1,0:T(8,128)(2,1)}), bf16[4,512,512]{2,1,0:T(8,128)(2,1)S(1)}, u32[]{:S(2)}, u32[]{:S(2)}) async-start(bf16[4,512,512]{2,1,0:T(8,128)(2,1)} %attend_back.2), calls=%async_computation.6 | async-start | bytes 4194304 | tf_op jit(solution)/shard_map/all_to_all | solution.py:647
  813.5 326.2 %reduce-scatter.6.cloned.1.call-start = ((), (), s32[]{:S(2)}) async-start(), calls=%async_computation.16 | async-start | bytes 5242880 | tf_op jit(solution)/shard_map/reduce_scatter | solution.py:659
  918.4 87.4 %all-to-all-start.7 = ((bf16[4,512,512]{2,1,0:T(8,128)(2,1)}), bf16[4,512,512]{2,1,0:T(8,128)(2,1)}, u32[]{:S(2)}, u32[]{:S(2)}) async-start(bf16[4,512,512]{2,1,0:T(8,128)(2,1)} %attend_back.3), calls=%async_computation.9 | async-start | bytes 4194304 | tf_op jit(solution)/shard_map/all_to_all | solution.py:647
  922.9 461.7 %reduce-scatter.8.cloned.1.call-start = ((), (), s32[]{:S(2)}) async-start(), calls=%async_computation.18 | async-start | bytes 10485760 | tf_op jit(solution)/shard_map/reduce_scatter | solution.py:659
  929.2 21.6 %collective-permute-start.16 = (bf16[256,1536]{1,0:T(8,128)(2,1)}, bf16[256,1536]{1,0:T(8,128)(2,1)}, u32[]{:S(2)}, u32[]{:S(2)}) collective-permute-start(bf16[256,1536]{1,0:T(8,128)(2,1)} %get-tuple-element.238), channel_id=1, source_target_pairs={{0,24},{8,16},{16,8},{24,0},{1,25},{9,17},{17,9},{25,1},{2,26},{10... | collective-permute-start | bytes 2359304 | tf_op jit(solution)/shard_map/ppermute | solution.py:680
  931.7 32.4 %collective-permute-start.15 = (bf16[256,1536]{1,0:T(8,128)(2,1)}, bf16[256,1536]{1,0:T(8,128)(2,1)}, u32[]{:S(2)}, u32[]{:S(2)}) collective-permute-start(bf16[256,1536]{1,0:T(8,128)(2,1)} %get-tuple-element.239), channel_id=1, source_target_pairs={{0,16},{8,24},{16,0},{24,8},{1,17},{9,25},{17,1},{25,9},{2,18},{10... | collective-permute-start | bytes 2359304 | tf_op jit(solution)/shard_map/ppermute | solution.py:680
  932.2 32.1 %collective-permute-start.14 = (bf16[256,1536]{1,0:T(8,128)(2,1)}, bf16[256,1536]{1,0:T(8,128)(2,1)}, u32[]{:S(2)}, u32[]{:S(2)}) collective-permute-start(bf16[256,1536]{1,0:T(8,128)(2,1)} %get-tuple-element.240), channel_id=1, source_target_pairs={{0,8},{8,0},{16,24},{24,16},{1,9},{9,1},{17,25},{25,17},{2,10},{10... | collective-permute-start | bytes 2359304 | tf_op jit(solution)/shard_map/ppermute | solution.py:680
  1045.0 50.5 %collective-permute-start.20 = (bf16[2,256,2048]{2,1,0:T(8,128)(2,1)}, bf16[2,256,2048]{2,1,0:T(8,128)(2,1)}, u32[]{:S(2)}, u32[]{:S(2)}) collective-permute-start(bf16[2,256,2048]{2,1,0:T(8,128)(2,1)} %select_bitcast_fusion.1), channel_id=1, source_target_pairs={{0,1},{1,0},{2,3},{3,2},{4,5},{5,4},{6,7},{7,6},{8,9},{9,8},{10,11... | collective-permute-start | bytes 6291464 | tf_op jit(solution)/shard_map/ppermute | solution.py:637
  1049.6 33.8 %collective-permute-start.17 = (bf16[4,128,1536]{2,1,0:T(8,128)(2,1)}, bf16[4,128,1536]{2,1,0:T(8,128)(2,1)}, u32[]{:S(2)}, u32[]{:S(2)}) collective-permute-start(bf16[4,128,1536]{2,1,0:T(8,128)(2,1)} %get-tuple-element.138), channel_id=1, source_target_pairs={{0,2},{1,3},{6,4},{7,5},{8,10},{9,11},{14,12},{15,13},{16,18},{17,... | collective-permute-start | bytes 4718600 | tf_op jit(solution)/shard_map/ppermute | solution.py:550
  1053.9 77.4 %collective-permute-start.24 = (bf16[2,512,1024]{2,1,0:T(8,128)(2,1)}, bf16[2,512,1024]{2,1,0:T(8,128)(2,1)}, u32[]{:S(2)}, u32[]{:S(2)}) collective-permute-start(bf16[2,512,1024]{2,1,0:T(8,128)(2,1)} %select_bitcast_fusion), channel_id=1, source_target_pairs={{0,8},{8,0},{16,24},{24,16},{1,9},{9,1},{17,25},{25,17},{2,10},{10... | collective-permute-start | bytes 6291464 | tf_op jit(solution)/shard_map/ppermute | solution.py:533
  1061.3 131.8 %collective-permute-start.32 = (bf16[2,512,1024]{2,1,0:T(8,128)(2,1)}, bf16[2,512,1024]{2,1,0:T(8,128)(2,1)}, u32[]{:S(2)}, u32[]{:S(2)}) collective-permute-start(bf16[2,512,1024]{2,1,0:T(8,128)(2,1)} %bitcast.46), channel_id=1, source_target_pairs={{0,16},{8,24},{16,0},{24,8},{1,17},{9,25},{17,1},{25,9},{2,18},{10... | collective-permute-start | bytes 6291464 | tf_op jit(solution)/shard_map/ppermute | solution.py:533
  1086.9 52.8 %collective-permute-start.18 = (bf16[4,128,1536]{2,1,0:T(8,128)(2,1)}, bf16[4,128,1536]{2,1,0:T(8,128)(2,1)}, u32[]{:S(2)}, u32[]{:S(2)}) collective-permute-start(bf16[4,128,1536]{2,1,0:T(8,128)(2,1)} %add.236), channel_id=1, source_target_pairs={{2,4},{3,5},{4,2},{5,3},{10,12},{11,13},{12,10},{13,11},{18,20},{1... | collective-permute-start | bytes 4718600 | tf_op jit(solution)/shard_map/ppermute | solution.py:550
  1088.7 50.9 %collective-permute-start.19 = (bf16[4,128,1536]{2,1,0:T(8,128)(2,1)}, bf16[4,128,1536]{2,1,0:T(8,128)(2,1)}, u32[]{:S(2)}, u32[]{:S(2)}) collective-permute-start(bf16[4,128,1536]{2,1,0:T(8,128)(2,1)} %get-tuple-element.154), channel_id=1, source_target_pairs={{0,2},{1,3},{6,4},{7,5},{8,10},{9,11},{14,12},{15,13},{16,18},{17,... | collective-permute-start | bytes 4718600 | tf_op jit(solution)/shard_map/ppermute | solution.py:550
  1101.0 47.8 %collective-permute-start.26 = (f32[24,2048]{1,0:T(8,128)S(1)}, f32[24,2048]{1,0:T(8,128)S(1)}, u32[]{:S(2)}, u32[]{:S(2)}) collective-permute-start(f32[24,2048]{1,0:T(8,128)S(1)} %concatenate.70), channel_id=1, source_target_pairs={{0,8},{8,0},{16,24},{24,16},{1,9},{9,1},{17,25},{25,17},{2,10},{10... | collective-permute-start | bytes 589832 | tf_op jit(solution)/shard_map/ppermute | solution.py:880
  1142.4 79.6 %collective-permute-start.21 = (bf16[4,128,1536]{2,1,0:T(8,128)(2,1)S(1)}, bf16[4,128,1536]{2,1,0:T(8,128)(2,1)S(1)}, u32[]{:S(2)}, u32[]{:S(2)}) collective-permute-start(bf16[4,128,1536]{2,1,0:T(8,128)(2,1)S(1)} %add.242), channel_id=1, source_target_pairs={{2,0},{3,1},{4,6},{5,7},{10,8},{11,9},{12,14},{13,15},{18,16},{19,... | collective-permute-start | bytes 4718600 | tf_op jit(solution)/shard_map/ppermute | solution.py:550
  1146.4 75.6 %collective-permute-start.22 = (bf16[4,128,1536]{2,1,0:T(8,128)(2,1)S(1)}, bf16[4,128,1536]{2,1,0:T(8,128)(2,1)S(1)}, u32[]{:S(2)}, u32[]{:S(2)}) collective-permute-start(bf16[4,128,1536]{2,1,0:T(8,128)(2,1)S(1)} %add.243), channel_id=1, source_target_pairs={{2,4},{3,5},{4,2},{5,3},{10,12},{11,13},{12,10},{13,11},{18,20},{1... | collective-permute-start | bytes 4718600 | tf_op jit(solution)/shard_map/ppermute | solution.py:550
  1147.3 59.3 %collective-permute-start.25 = (bf16[512,1024]{1,0:T(8,128)(2,1)S(1)}, bf16[512,1024]{1,0:T(8,128)(2,1)S(1)}, u32[]{:S(2)}, u32[]{:S(2)}) collective-permute-start(bf16[512,1024]{1,0:T(8,128)(2,1)S(1)} %select_bitcast_fusion.3), channel_id=1, source_target_pairs={{0,16},{8,24},{16,0},{24,8},{1,17},{9,25},{17,1},{25,9},{2,18},{10... | collective-permute-start | bytes 3145736 | tf_op jit(solution)/shard_map/ppermute | solution.py:533
  1148.9 44.1 %collective-permute-start.27 = (f32[24,2048]{1,0:T(8,128)S(1)}, f32[24,2048]{1,0:T(8,128)S(1)}, u32[]{:S(2)}, u32[]{:S(2)}) collective-permute-start(f32[24,2048]{1,0:T(8,128)S(1)} %add.250), channel_id=1, source_target_pairs={{0,16},{8,24},{16,0},{24,8},{1,17},{9,25},{17,1},{25,9},{2,18},{10... | collective-permute-start | bytes 589832 | tf_op jit(solution)/shard_map/ppermute | solution.py:880
  1193.0 9.5 collective-permute-start.28
  1193.1 28.9 %collective-permute-start.23 = (bf16[512,1024]{1,0:T(8,128)(2,1)S(1)}, bf16[512,1024]{1,0:T(8,128)(2,1)S(1)}, u32[]{:S(2)}, u32[]{:S(2)}) collective-permute-start(bf16[512,1024]{1,0:T(8,128)(2,1)S(1)} %copy-done.45), channel_id=1, source_target_pairs={{0,2},{1,3},{6,4},{7,5},{8,10},{9,11},{14,12},{15,13},{16,18},{17,... | collective-permute-start | bytes 3145736 | tf_op jit(solution)/shard_map/ppermute | solution.py:550
  1202.5 127.8 %collective-permute-start.42 = (bf16[768,2048]{1,0:T(8,128)(2,1)}, bf16[768,2048]{1,0:T(8,128)(2,1)}, u32[]{:S(2)}, u32[]{:S(2)}) collective-permute-start(bf16[768,2048]{1,0:T(8,128)(2,1)} %get-tuple-element.217), channel_id=1, source_target_pairs={{0,16},{8,24},{16,0},{24,8},{1,17},{9,25},{17,1},{25,9},{2,18},{10... | collective-permute-start | bytes 9437192 | tf_op jit(solution)/shard_map/ppermute | solution.py:890
  1222.4 65.2 %collective-permute-start.29 = (bf16[4,128,1536]{2,1,0:T(8,128)(2,1)S(1)}, bf16[4,128,1536]{2,1,0:T(8,128)(2,1)S(1)}, u32[]{:S(2)}, u32[]{:S(2)}) collective-permute-start(bf16[4,128,1536]{2,1,0:T(8,128)(2,1)S(1)} %add.253), channel_id=1, source_target_pairs={{2,0},{3,1},{4,6},{5,7},{10,8},{11,9},{12,14},{13,15},{18,16},{19,... | collective-permute-start | bytes 4718600 | tf_op jit(solution)/shard_map/ppermute | solution.py:550
  1223.8 42.2 %collective-permute-start.33 = (bf16[512,1024]{1,0:T(8,128)(2,1)S(1)}, bf16[512,1024]{1,0:T(8,128)(2,1)S(1)}, u32[]{:S(2)}, u32[]{:S(2)}) collective-permute-start(bf16[512,1024]{1,0:T(8,128)(2,1)S(1)} %select_bitcast_fusion.2), channel_id=1, source_target_pairs={{0,8},{8,0},{16,24},{24,16},{1,9},{9,1},{17,25},{25,17},{2,10},{10... | collective-permute-start | bytes 3145736 | tf_op jit(solution)/shard_map/ppermute | solution.py:533
  1224.6 40.0 %collective-permute-start.34 = (f32[24,2048]{1,0:T(8,128)S(1)}, f32[24,2048]{1,0:T(8,128)S(1)}, u32[]{:S(2)}, u32[]{:S(2)}) collective-permute-start(f32[24,2048]{1,0:T(8,128)S(1)} %add.252), channel_id=1, source_target_pairs={{0,2},{1,3},{2,0},{3,1},{4,6},{5,7},{6,4},{7,5},{8,10},{9,11},{10,... | collective-permute-start | bytes 589832 | tf_op jit(solution)/shard_map/ppermute | solution.py:880
  1227.7 39.5 %collective-permute-start.30 = (bf16[512,1024]{1,0:T(8,128)(2,1)S(1)}, bf16[512,1024]{1,0:T(8,128)(2,1)S(1)}, u32[]{:S(2)}, u32[]{:S(2)}) collective-permute-start(bf16[512,1024]{1,0:T(8,128)(2,1)S(1)} %add.254), channel_id=1, source_target_pairs={{2,4},{3,5},{4,2},{5,3},{10,12},{11,13},{12,10},{13,11},{18,20},{1... | collective-permute-start | bytes 3145736 | tf_op jit(solution)/shard_map/ppermute | solution.py:550
  1264.5 23.1 %collective-permute-start.31 = (bf16[512,1024]{1,0:T(8,128)(2,1)S(1)}, bf16[512,1024]{1,0:T(8,128)(2,1)S(1)}, u32[]{:S(2)}, u32[]{:S(2)}) collective-permute-start(bf16[512,1024]{1,0:T(8,128)(2,1)S(1)} %bitcast_add_fusion.2), channel_id=1, source_target_pairs={{0,2},{1,3},{6,4},{7,5},{8,10},{9,11},{14,12},{15,13},{16,18},{17,... | collective-permute-start | bytes 3145736 | tf_op jit(solution)/shard_map/ppermute | solution.py:550
  1289.2 41.8 %collective-permute-start.35 = (bf16[512,1024]{1,0:T(8,128)(2,1)}, bf16[512,1024]{1,0:T(8,128)(2,1)}, u32[]{:S(2)}, u32[]{:S(2)}) collective-permute-start(bf16[512,1024]{1,0:T(8,128)(2,1)} %add.258), channel_id=1, source_target_pairs={{2,0},{3,1},{4,6},{5,7},{10,8},{11,9},{12,14},{13,15},{18,16},{19,... | collective-permute-start | bytes 3145736 | tf_op jit(solution)/shard_map/ppermute | solution.py:550
  1292.0 38.9 %collective-permute-start.36 = (bf16[512,1024]{1,0:T(8,128)(2,1)}, bf16[512,1024]{1,0:T(8,128)(2,1)}, u32[]{:S(2)}, u32[]{:S(2)}) collective-permute-start(bf16[512,1024]{1,0:T(8,128)(2,1)} %add.259), channel_id=1, source_target_pairs={{2,4},{3,5},{4,2},{5,3},{10,12},{11,13},{12,10},{13,11},{18,20},{1... | collective-permute-start | bytes 3145736 | tf_op jit(solution)/shard_map/ppermute | solution.py:550
  1293.6 37.3 %collective-permute-start.37 = (bf16[512,1024]{1,0:T(8,128)(2,1)}, bf16[512,1024]{1,0:T(8,128)(2,1)}, u32[]{:S(2)}, u32[]{:S(2)}) collective-permute-start(bf16[512,1024]{1,0:T(8,128)(2,1)} %bitcast_add_fusion.1), channel_id=1, source_target_pairs={{0,2},{1,3},{6,4},{7,5},{8,10},{9,11},{14,12},{15,13},{16,18},{17,... | collective-permute-start | bytes 3145736 | tf_op jit(solution)/shard_map/ppermute | solution.py:550
  1300.4 28.3 %collective-permute-start.38 = (f32[24,2048]{1,0:T(8,128)S(1)}, f32[24,2048]{1,0:T(8,128)S(1)}, u32[]{:S(2)}, u32[]{:S(2)}) collective-permute-start(f32[24,2048]{1,0:T(8,128)S(1)} %add.257), channel_id=1, source_target_pairs={{0,4},{1,5},{2,6},{3,7},{4,0},{5,1},{6,2},{7,3},{8,12},{9,13},{10,... | collective-permute-start | bytes 589832 | tf_op jit(solution)/shard_map/ppermute | solution.py:880
  1329.4 14.7 %collective-permute-start.41 = (bf16[768,2048]{1,0:T(8,128)(2,1)}, bf16[768,2048]{1,0:T(8,128)(2,1)}, u32[]{:S(2)}, u32[]{:S(2)}) collective-permute-start(bf16[768,2048]{1,0:T(8,128)(2,1)} %get-tuple-element.218.keep_ref), channel_id=1, source_target_pairs={{0,1},{1,0},{2,3},{3,2},{4,5},{5,4},{6,7},{7,6},{8,9},{9,8},{10,11... | collective-permute-start | bytes 9437192 | tf_op jit(solution)/shard_map/ppermute | solution.py:637
  1330.3 13.7 collective-permute-start.43
  1333.0 27.5 %collective-permute-start.44 = (bf16[4,256,1536]{2,1,0:T(8,128)(2,1)S(1)}, bf16[4,256,1536]{2,1,0:T(8,128)(2,1)}, u32[]{:S(2)}, u32[]{:S(2)}) collective-permute-start(bf16[4,256,1536]{2,1,0:T(8,128)(2,1)S(1)} %pad_maximum_fusion.7.refs_0_), channel_id=1, source_target_pairs={{0,1},{1,0},{2,3},{3,2},{4,5},{5,4},{6,7},{7,6},{8,9},{9,8},{10,11... | collective-permute-start | bytes 9437192 | tf_op jit(solution)/shard_map/ppermute | solution.py:637
  1337.0 35.4 %collective-permute-start.39 = (bf16[512,1024]{1,0:T(8,128)(2,1)}, bf16[512,1024]{1,0:T(8,128)(2,1)}, u32[]{:S(2)}, u32[]{:S(2)}) collective-permute-start(bf16[512,1024]{1,0:T(8,128)(2,1)} %add.261), channel_id=1, source_target_pairs={{2,0},{3,1},{4,6},{5,7},{10,8},{11,9},{12,14},{13,15},{18,16},{19,... | collective-permute-start | bytes 3145736 | tf_op jit(solution)/shard_map/ppermute | solution.py:550
  1341.2 31.2 %collective-permute-start.40 = (bf16[512,1024]{1,0:T(8,128)(2,1)}, bf16[512,1024]{1,0:T(8,128)(2,1)}, u32[]{:S(2)}, u32[]{:S(2)}) collective-permute-start(bf16[512,1024]{1,0:T(8,128)(2,1)} %add.262), channel_id=1, source_target_pairs={{2,4},{3,5},{4,2},{5,3},{10,12},{11,13},{12,10},{13,11},{18,20},{1... | collective-permute-start | bytes 3145736 | tf_op jit(solution)/shard_map/ppermute | solution.py:550
  1373.8 4.2 collective-permute-start.46
  1376.8 28.5 %collective-permute-start.45 = (bf16[512,1024]{1,0:T(8,128)(2,1)S(1)}, bf16[512,1024]{1,0:T(8,128)(2,1)}, u32[]{:S(2)}, u32[]{:S(2)}) collective-permute-start(bf16[512,1024]{1,0:T(8,128)(2,1)S(1)} %add.263), channel_id=1, source_target_pairs={{2,0},{3,1},{4,6},{5,7},{10,8},{11,9},{12,14},{13,15},{18,16},{19,... | collective-permute-start | bytes 3145736 | tf_op jit(solution)/shard_map/ppermute | solution.py:550
  1406.6 4.4 collective-permute-start.47
  1408.3 2.7 collective-permute-start.48
  (84 other events, 1157.8 us)
Sparse Core Ops, SparseCore 0:
  15.7 91.5 all-gather.6
  109.8 52.5 all-gather.8
  164.5 114.0 all-gather.14
  280.3 87.4 all-gather.12
  370.1 87.4 all-gather.10
  550.7 86.3 reduce-scatter.3
  655.1 353.4 all-reduce.3
  1011.6 58.5 reduce-scatter.5
  1073.2 129.3 reduce-scatter.7

commit v9 on v8

--- a/solution.py
+++ b/solution.py
@@ -565,7 +565,10 @@
     def pipeline(self, parts, fillers):
         if self.chips != 4:
             done = lax.psum(parts, "seq", axis_index_groups=self.groups)
-            return done, [filler(done) for filler in fillers.values()]
+            made = []
+            for filler in fillers.values():
+                made.append(filler(done, made))
+            return done, made
         count = len(parts)
         states = [None] * count
         made = []
@@ -576,7 +579,7 @@
                 elif k < step <= k + 2:
                     states[k] = self.next(states[k])
             done = [self.end(states[k]) if k + 3 <= step else None for k in range(count)]
-            extra = fillers[step](done) if step in fillers else []
+            extra = fillers[step](done, made) if step in fillers else []
             live = [k for k in range(count) if states[k] is not None]
             later = [k for k in range(step + 1, min(step + 2, count))]
             moved, extra = lax.optimization_barrier(
@@ -788,7 +791,9 @@
     keep_sum = pick(part_keep[:quarter], part_keep[quarter:]) + keep_swap
     recv_sum = pick(part_recv[:quarter], part_recv[quarter:]) + recv_swap
     d_normed, gu_sum = tie(d_normed, jnp.concatenate([keep_sum, recv_sum], axis=0))
-    gu_sum = lax.psum(gu_sum, "seq", axis_index_groups=groups)
+    third = gu_sum.shape[0] // 3
+    gu_first = lax.psum(gu_sum[:third], "seq", axis_index_groups=groups)
+    gu_sum = gu_sum[third:]
 
     d_normed = d_normed.astype(F32)
     part_ffn = jnp.sum(d_normed * mid * factor_f, axis=0)
@@ -817,6 +822,8 @@
             d_attn, hidden = tie(d_attn, hidden)
         d_logit.append(dl)
         d_heads.append(exchange(d_attn))
+    d_heads[0], (gu_first, gu_sum) = tie(d_heads[0], (gu_first, gu_sum))
+    gu_sum = lax.psum(gu_sum, "seq", axis_index_groups=groups)
     back = []
     for row in range(rows):
         grads = attend_back(packed[row], d_heads[row], results[row], logs[row], start[row : row + 1], low[row])
@@ -832,7 +839,7 @@
     d_logit = jnp.concatenate(d_logit, axis=0)
     half = width // 2
     part_qkv = [dot_tn(d_proj, normed_a[:, a : a + half], BF) for a in (0, half)]
-    part_qkv, (gu_sum, out_part, d_proj) = tie_all(part_qkv, (gu_sum, out_part, d_proj))
+    part_qkv, (gu_sum, out_part, d_proj, down_sum) = tie_all(part_qkv, (gu_sum, out_part, d_proj, down_sum))
     trading = [Halving(p, dp, flip) for p, flip in zip(part_qkv, (False, True))]
     moved = [t.send() for t in trading]
     while trading[0].order:
@@ -842,7 +849,6 @@
     for t, m in zip(trading, moved):
         t.add(m)
     shard_qkv = [t.x for t in trading]
-    output = (mid + scatter(out_part).astype(F32)).astype(BF).reshape(rows, tok, width)
     d_norm_part = (dot_nn(d_proj, qkv_full) + dot_nn(d_logit, gate_core)).astype(BF)
     d_norm_part = d_norm_part.reshape(rows, CORES, tok, width)
     d_norm_other = swap(pick(d_norm_part[:, 1], d_norm_part[:, 0]))
@@ -859,7 +865,7 @@
     heads = jnp.concatenate([jnp.sum(q_sum, axis=0), jnp.sum(k_sum, axis=0)])
     heads = jnp.pad(heads, (0, width - heads.shape[0]))
 
-    def norm_done(done):
+    def norm_done(done, made):
         return [part_attn, grad_input]
 
     part_gate = dot_tn(d_logit, normed_a)[:CORE_Q]
@@ -869,27 +875,32 @@
     )
     part_gate = part_gate.reshape(QUERY_HEADS, width)
     small = jnp.concatenate([part_gate, part_ffn[None], part_attn[None], heads[None], jnp.zeros((5, width), F32)], axis=0)
-    hops = [("dp", 1 << k) for k in range(dp.bit_length() - 1)] + [("seq", 1 << k) for k in range(seq.bit_length() - 1)]
-    near = dp.bit_length()
-    sums_at = [small]
-
-    def hop(some):
-        def work(done):
-            x = sums_at[-1]
-            for name, bit in some:
-                x = x + lax.ppermute(x, name, [(p, p ^ bit) for p in range(lax.axis_size(name))])
-            sums_at.append(x)
-            return [x]
-
-        return work
-
-
+    hops = [("seq", 1)] + [("dp", 1 << k) for k in range(dp.bit_length() - 1)]
     mid_cut = down_sum.shape[1] // 2
+    parts = [down_sum[:, :mid_cut], down_sum[:, mid_cut:], shard_out, *shard_qkv]
+
+    def hop(x, some):
+        for name, bit in some:
+            x = x + lax.ppermute(x, name, [(p, p ^ bit) for p in range(lax.axis_size(name))])
+        return x
+
+    def near_sum(done, made):
+        return [hop(small, hops[:2]), out_part]
+
+    def far_sum(done, made):
+        total = hop(made[-1][0], hops[2:])
+        if chips == 4:
+            wide = total.astype(BF)
+            parts[4] = jnp.concatenate([parts[4], wide[:, :half], wide[:, half:]], axis=0)
+        else:
+            total = lax.psum(total, "seq", axis_index_groups=groups)
+        return [total, made[-1][1]]
+
     line = Line(chips, chip)
-    keep = gu_sum[:quarter]
-    sent = lax.ppermute(gu_sum[quarter:], "dp", trade)
-
-    def join_early(done):
+    keep = jnp.concatenate([gu_first, gu_sum[: quarter - third]], axis=0)
+    sent = lax.ppermute(gu_sum[quarter - third :], "dp", trade)
+
+    def join_early(done, made):
         down_done = jnp.concatenate(done[:2], axis=1)
         places = [unit_block.index(b) ^ me for b in range(dp)]
         return [
@@ -897,20 +908,17 @@
             join_blocks(down_done, swap(down_done), core, places),
         ]
 
-    def join_late(done):
+    def join_late(done, made):
+        output = (mid + scatter(made[2][1]).astype(F32)).astype(BF).reshape(rows, tok, width)
         return [join_cols([done[2]], [swap(done[2])], core, GROUP * HEAD), output]
 
-    sums, ((_, grad_input), _, _, (small,), (grad_gu, grad_down), (grad_out, output)) = line.pipeline(
-        [down_sum[:, :mid_cut], down_sum[:, mid_cut:], shard_out, *shard_qkv],
-        {
-            1: norm_done,
-            2: hop(hops[:near]),
-            3: hop(hops[near : near + 1]),
-            4: hop(hops[near + 1 :]),
-            5: join_early,
-            6: join_late,
-        },
+    sums, ((_, grad_input), _, (small, _), (grad_gu, grad_down), (grad_out, output)) = line.pipeline(
+        parts, {1: norm_done, 2: near_sum, 3: far_sum, 5: join_early, 6: join_late}
     )
+    if chips == 4:
+        body = shard_qkv[0].shape[0]
+        count = (sums[4].shape[0] - body) // 2
+        small = jnp.concatenate([sums[4][body : body + count], sums[4][body + count :]], axis=1).astype(F32)
     grad_w_gate = lax.dynamic_slice_in_dim(small, me * gate_count, gate_count, 0)
     qkv_sum = sums[3:]
     grad_qkv = join_rows(qkv_sum, [swap(p) for p in qkv_sum], core, jnp.where(q_shard, GROUP, 1), HEAD)

time: 1430 us -> 1470 us (1.028)
  blocking collectives: 112 us -> 52.5 us
  waiting for transfers between devices: 614 us -> 667 us
  local copies, waits for them, and re-layouts: 43.2 us -> 60 us
  other arithmetic: 158 us -> 173 us
    all_to_all x2 -> x1, blocking collectives: 112 us -> 52.5 us  [exchange(): return lax.all_to_all(x, 'seq', 0, 0, axis_index_groups=groups, tiled=True)]
    psum x0 -> x1, waiting for transfers between devices: none -> 55 us  [shards(): gu_first = lax.psum(gu_sum[:third], 'seq', axis_index_groups=groups)]
    all_to_all x6 -> x7, waiting for transfers between devices: 159 us -> 118 us  [exchange(): return lax.all_to_all(x, 'seq', 0, 0, axis_index_groups=groups, tiled=True)]
    psum x1, waiting for transfers between devices: 0.01 us -> 38.2 us  [shards(): gu_sum = lax.psum(gu_sum, 'seq', axis_index_groups=groups)]
    ppermute x15, waiting for transfers between devices: 72.6 us -> 49.8 us  [send(): return (x, lax.ppermute(x, 'seq', self.stages[stage]))]
    ppermute x6 -> x4, waiting for transfers between devices: 108 us -> 125 us  [the longest x1 114 us: shards(): sent = lax.ppermute(gu_sum[quarter - third:], 'dp', trade)]
    unnamed x173 -> x167, local copies, waits for them, and re-layouts: 27 us -> 30.1 us
  transfers between devices with their start and end apart: 64 -> 64, of which waited for: 27 -> 31; matrix products, arithmetic and copies ran while one was open for 23% -> 24% of each run, Pallas kernels for 10% -> 9%
where the time goes in v9:
time: 1470 us; the launch traced here: 1460 us
  waiting for transfers between devices  667 us (45%)
  matrix products  249 us (17%)
  other arithmetic  173 us (12%)
  Pallas kernels  145 us (10%)
  starting transfers between devices  100 us (7%)
  local copies, waits for them, and re-layouts  60 us (4%)
  blocking collectives  52.5 us (4%)
  between operations  15.9 us (1%)
    all_gather x4, waiting for transfers between devices, gather(): return lax.all_gather(x, 'dp', axis=0, tiled=True)  127 us
    all_to_all x7, waiting for transfers between devices, exchange(): return lax.all_to_all(x, 'seq', 0, 0, axis_index_groups=groups, tiled=True)  118 us
    ppermute x1, waiting for transfers between devices, shards(): sent = lax.ppermute(gu_sum[quarter - third:], 'dp', trade)  114 us
    dot_general x7, matrix products, dot_nt(): lax.dot_general(left, right, (((1,), (1,)), ((), ())), preferred_element_...  94.2 us
    dot_general x7, matrix products, dot_nn(): lax.dot_general(left, right, (((1,), (0,)), ((), ())), preferred_element_...  81.7 us
    ppermute x6, waiting for transfers between devices, trade_blocks(): lax.ppermute(out, 'dp', [(d, d ^ k) for d in range(dp)])  79.6 us
    dot_general x7, matrix products, dot_tn(): lax.dot_general(left, right, (((0,), (0,)), ((), ())), preferred_element_...  72.8 us
    psum x1, waiting for transfers between devices, shards(): gu_first = lax.psum(gu_sum[:third], 'seq', axis_index_groups=groups)  55 us
  transfers between devices with their start and end apart: 64, of which 31 were waited for; matrix products, arithmetic and copies ran while one was open for 24% of the time, Pallas kernels for 9%

profile of v9, /device:TPU:0, one launch (start us, length us, event | category | flops | bytes accessed | tf_op | source)
XLA Modules:
  0.0 1461.9 jit_solution(6760195362165599768)
XLA Ops:
  30.5 6.6 select_select_fusion
  53.0 54.4 %all-gather.7.cloned.1.call-done = bf16[2048,2048]{1,0:T(8,128)(2,1)} async-done(((bf16[512,2048]{1,0:T(8,128)(2,1)}), bf16[2048,2048]{1,0:T(8,128)(2,1)}) %all-gather.7.cloned.1.call-update) | async-done | bytes 8388624 | tf_op jit(solution)/shard_map/all_gather | solution.py:665
  117.2 11.1 fusion.67.proj_ref
  128.3 6.2 pack_heads.3
  134.4 52.5 %all_to_all.40.q_ref.k_ref.v_ref = bf16[4,512,512]{2,1,0:T(8,128)(2,1)} all-to-all(bf16[4,512,512]{2,1,0:T(8,128)(2,1)} %pack_heads.3), channel_id=1, replica_groups={{0,2,4,6},{1,3,5,7},{8,10,12,14},{9,11,13,15},{16,18,20,22},{17,19,21,2..., dimensions={0} | all-to-all | bytes 4194304 | tf_op jit(solution)/shard_map/all_to_all | solution.py:650
  187.0 6.2 pack_heads.2
  205.8 15.7 %collective-permute-done.1 = bf16[256,1536]{1,0:T(8,128)(2,1)S(1)} collective-permute-done((bf16[256,1536]{1,0:T(8,128)(2,1)S(1)}, bf16[256,1536]{1,0:T(8,128)(2,1)S(1)}, u32[]{:S(2)}, u32[]{:S(2)}) %collective-permute-start.1) | collective-permute-done | bytes 786464 | tf_op jit(solution)/shard_map/ppermute | solution.py:683
  222.4 34.0 %collective-permute-done.2 = bf16[256,1536]{1,0:T(8,128)(2,1)S(1)} collective-permute-done((bf16[256,1536]{1,0:T(8,128)(2,1)S(1)}, bf16[256,1536]{1,0:T(8,128)(2,1)S(1)}, u32[]{:S(2)}, u32[]{:S(2)}) %collective-permute-start.2) | collective-permute-done | bytes 786464 | tf_op jit(solution)/shard_map/ppermute | solution.py:683
  259.6 10.8 attend.2
  270.3 5.2 all-to-all-start.1
  275.6 10.8 attend.3
  286.3 12.5 all-to-all-done.1.res_ref
  305.0 4.9 convolution_convert_fusion.11
  311.0 16.5 %all-to-all-done.3.res_ref = bf16[4,512,256]{2,1,0:T(8,128)(2,1)S(1)} async-done(((bf16[4,512,256]{2,1,0:T(8,128)(2,1)}), bf16[4,512,256]{2,1,0:T(8,128)(2,1)S(1)}, u32[]{:S(2)}, u32[]{:S(2)}) %all-to-all-start.3) | async-done | bytes 1048608 | tf_op jit(solution)/shard_map/all_to_all | solution.py:650
  331.1 4.9 convolution_convert_fusion.10
  346.2 4.8 slice_select_fusion.4
  367.8 18.6 %convolution_convert_fusion.3 = bf16[2048,1536]{1,0:T(8,128)(2,1)} fusion(bf16[2048,2048]{1,0:T(8,128)(2,1)} %all-gather.13.cloned.1.call-done, bf16[2048,1536]{1,0:T(8,128)(2,1)} %bitcast.202), kind=kOutput, calls=%fused_computation.24 | convolution fusion | flops 12888047616 | bytes 20971520 | tf_op jit(solution)/shard_map/dot_general | solution.py:33
  386.4 71.2 %all-gather.11.cloned.1.call-done = bf16[2048,2048]{1,0:T(8,128)(2,1)} async-done(((bf16[512,2048]{1,0:T(8,128)(2,1)}), bf16[2048,2048]{1,0:T(8,128)(2,1)}) %all-gather.11.cloned.1.call-update) | async-done | bytes 8388624 | tf_op jit(solution)/shard_map/all_gather | solution.py:665
  457.6 19.7 %convolution_convert_fusion.1 = bf16[2048,1536]{1,0:T(8,128)(2,1)} fusion(bf16[2048,2048]{1,0:T(8,128)(2,1)} %all-gather.11.cloned.1.call-done, bf16[3072,2048]{1,0:T(8,128)(2,1)} %param.21, pred[]{:T(512)S(6)} %ge.19), kind=kOutput, calls=%fused_computation.22 | convolution fusion | flops 12891193344 | bytes 27262976 | tf_op jit(solution)/shard_map/dot_general | solution.py:29
  477.3 32.3 %select_convert_fusion = (bf16[2048,1536]{1,0:T(8,128)(2,1)}, bf16[2048,1536]{1,0:T(8,128)(2,1)}, bf16[2048,1536]{1,0:T(8,128)(2,1)}) fusion(bf16[2048,1536]{1,0:T(8,128)(2,1)} %convolution_convert_fusion.3, pred[]{:T(512)S(6)} %ge.19, bf16[2048,1536]{1,0:T(8,128)(2,1)} %convolution_convert_fusion.1, bf16[2048,2048]{1,0:T(8,128)(2,1)} %all-gather.11.cloned.1.call-done, ...), kind=kOutput, calls=%fused_computation.14 | convolution fusion | flops 12957253632 | bytes 46137344 | tf_op jit(solution)/shard_map/dot_general | solution.py:29
  509.6 21.9 %fusion.45 = f32[2048,2048]{1,0:T(8,128)} fusion(bf16[2048,1536]{1,0:T(8,128)(2,1)} %get-tuple-element.227, bf16[3072,2048]{1,0:T(8,128)(2,1)} %param.21, pred[]{:T(512)S(6)} %ge.19), kind=kOutput, calls=%fused_computation.142 | convolution fusion | flops 12888047616 | bytes 35651584 | tf_op jit(solution)/shard_map/dot_general | solution.py:33
  531.5 19.1 %add_convert_fusion = bf16[2048,2048]{1,0:T(8,128)(2,1)} fusion(f32[2048,2048]{1,0:T(8,128)} %fusion.45, bf16[2048,1536]{1,0:T(8,128)(2,1)S(1)} %copy-done.74, bf16[1536,2048]{1,0:T(8,128)(2,1)} %pad_maximum_fusion.1), kind=kOutput, calls=%fused_computation.3 | convolution fusion | flops 12893290496 | bytes 37748736 | tf_op jit(solution)/shard_map/dot_general | solution.py:33
  550.7 17.9 %convolution_convert_fusion.6 = bf16[1536,2048]{1,0:T(8,128)(2,1)S(1)} fusion(bf16[2048,1536]{1,0:T(8,128)(2,1)} %get-tuple-element.227, bf16[2048,2048]{1,0:T(8,128)(2,1)} %all-gather.11.cloned.1.call-done), kind=kOutput, calls=%fused_computation.27 | convolution fusion | flops 12888047616 | bytes 20971520 | tf_op jit(solution)/shard_map/dot_general | solution.py:37
  571.8 18.6 %convolution_convert_fusion.5 = bf16[1536,2048]{1,0:T(8,128)(2,1)S(1)} fusion(bf16[2048,1536]{1,0:T(8,128)(2,1)} %get-tuple-element.226, bf16[2048,2048]{1,0:T(8,128)(2,1)} %all-gather.11.cloned.1.call-done), kind=kOutput, calls=%fused_computation.26 | convolution fusion | flops 12888047616 | bytes 20971520 | tf_op jit(solution)/shard_map/dot_general | solution.py:37
  593.5 14.3 convolution_convert_fusion.4
  611.7 25.4 %reduce-scatter.4.cloned.1.call-done = bf16[512,2048]{1,0:T(8,128)(2,1)} async-done(((bf16[2048,2048]{1,0:T(8,128)(2,1)}), bf16[512,2048]{1,0:T(8,128)(2,1)}) %reduce-scatter.4.cloned.1.call-update) | async-done | bytes 2097168 | tf_op jit(solution)/shard_map/reduce_scatter | solution.py:662
  637.1 8.9 select_add_fusion
  676.8 4.6 all-to-all-start.4
  681.4 19.3 %convolution_convert_fusion = bf16[2048,2048]{1,0:T(8,128)(2,1)} fusion(bf16[2048,1536]{1,0:T(8,128)(2,1)} %get-tuple-element.142, bf16[2048,1536]{1,0:T(8,128)(2,1)} %bitcast.203), kind=kOutput, calls=%fused_computation.21 | convolution fusion | flops 12889096192 | bytes 20971520 | tf_op jit(solution)/shard_map/dot_general | solution.py:29
  704.6 6.4 convolution_convert_fusion.9
  711.0 5.8 fusion.68.grad_ref
  728.0 5.1 slice.370
  733.1 55.0 %all-reduce.5.cloned.1.call-done = bf16[512,2048]{1,0:T(8,128)(2,1)} async-done(((bf16[512,2048]{1,0:T(8,128)(2,1)}), bf16[512,2048]{1,0:T(8,128)(2,1)}) %all-reduce.5.cloned.1.call-update) | async-done | bytes 2097168 | tf_op jit(solution)/shard_map/psum | solution.py:795
  788.1 19.8 %attend_back.2 = bf16[4,512,512]{2,1,0:T(8,128)(2,1)} custom-call(s32[4]{0:T(128)} %get-tuple-element.289.low_ref, bf16[4,512,512]{2,1,0:T(8,128)(2,1)} %copy-done, bf16[4,512,512]{2,1,0:T(8,128)(2,1)} %copy-done, bf16[4,512,512]{2,1,0:T(8,128)(2,1)} %copy-done, bf16[4,512,256]{2,1,0:T(8,128)(2,1)} %copy-done.36, ...), custom_call_target="tpu_custom_call" | custom-call | tf_op jit(solution)/shard_map/attend_back/pallas_call | solution.py:281
  813.2 19.8 %attend_back.3 = bf16[4,512,512]{2,1,0:T(8,128)(2,1)} custom-call(s32[4]{0:T(128)} %get-tuple-element.288.low_ref, bf16[4,512,512]{2,1,0:T(8,128)(2,1)} %all_to_all.40.q_ref.k_ref.v_ref, bf16[4,512,512]{2,1,0:T(8,128)(2,1)} %all_to_all.40.q_ref.k_ref.v_ref, bf16[4,512,512]{2,1,0:T(8,128)(2,1)} %all_to_all.40.q_ref.k_ref.v_ref, ...), custom_call_target="tpu_custom_call" | custom-call | tf_op jit(solution)/shard_map/attend_back/pallas_call | solution.py:281
  832.9 75.9 %all-to-all-done.5.grad_ref = bf16[4,512,512]{2,1,0:T(8,128)(2,1)S(1)} async-done(((bf16[4,512,512]{2,1,0:T(8,128)(2,1)}), bf16[4,512,512]{2,1,0:T(8,128)(2,1)S(1)}, u32[]{:S(2)}, u32[]{:S(2)}) %all-to-all-start.5) | async-done | bytes 2097184 | tf_op jit(solution)/shard_map/all_to_all | solution.py:650
  908.8 4.5 all-to-all-start.7
  913.3 4.4 fusion.25
  923.7 17.0 %collective-permute-done.16 = bf16[256,1536]{1,0:T(8,128)(2,1)S(1)} collective-permute-done((bf16[256,1536]{1,0:T(8,128)(2,1)}, bf16[256,1536]{1,0:T(8,128)(2,1)S(1)}, u32[]{:S(2)}, u32[]{:S(2)}) %collective-permute-start.16) | collective-permute-done | bytes 786464 | tf_op jit(solution)/shard_map/ppermute | solution.py:683
  940.7 12.8 collective-permute-done.15
  956.9 7.5 unpack_heads.2
  967.5 10.3 all-to-all-done.7.grad_ref
  977.8 7.5 unpack_heads.3
  988.6 8.6 convolution_convert_fusion.8
  997.2 6.2 convolution_convert_fusion.7
  1003.5 38.2 %all-reduce.7.cloned.1.call-done = bf16[1024,2048]{1,0:T(8,128)(2,1)} async-done(((bf16[1024,2048]{1,0:T(8,128)(2,1)}), bf16[1024,2048]{1,0:T(8,128)(2,1)}) %all-reduce.7.cloned.1.call-update) | async-done | bytes 4194320 | tf_op jit(solution)/shard_map/psum | solution.py:826
  1049.5 11.5 fusion.69
  1066.5 4.5 broadcast_select_fusion.6
  1072.4 7.1 collective-permute-done.17
  1084.9 7.2 collective-permute-start.19
  1092.0 37.4 %collective-permute-done.24 = bf16[2,512,1024]{2,1,0:T(8,128)(2,1)} collective-permute-done((bf16[2,512,1024]{2,1,0:T(8,128)(2,1)}, bf16[2,512,1024]{2,1,0:T(8,128)(2,1)}, u32[]{:S(2)}, u32[]{:S(2)}) %collective-permute-start.24) | collective-permute-done | bytes 2097184 | tf_op jit(solution)/shard_map/ppermute | solution.py:533
  1134.1 4.6 fusion.22
  1153.9 8.4 collective-permute-start.23
  1169.5 5.9 collective-permute-done.27
  1189.9 12.8 collective-permute-start.30
  1203.7 4.8 collective-permute-done.33
  1209.6 13.3 collective-permute-done.30
  1222.9 5.4 collective-permute-done.28
  1244.6 114.1 %collective-permute-done.40.sent_ref = bf16[768,2048]{1,0:T(8,128)(2,1)} collective-permute-done((bf16[768,2048]{1,0:T(8,128)(2,1)}, bf16[768,2048]{1,0:T(8,128)(2,1)}, u32[]{:S(2)}, u32[]{:S(2)}) %collective-permute-start.40) | collective-permute-done | bytes 3145760 | tf_op jit(solution)/shard_map/ppermute | solution.py:901
  1374.5 16.5 %join_units.1 = f32[3072,2048]{1,0:T(8,128)} custom-call(s32[2]{0:T(128)} %pad_add_fusion.which_ref, bf16[768,2048]{1,0:T(8,128)(2,1)} %copy-done.25, bf16[768,2048]{1,0:T(8,128)(2,1)} %collective-permute-done.39.keep_other_ref, bf16[768,2048]{1,0:T(8,128)(2,1)} %collective-permute-done.40.sent_ref, bf16[768,2048]{1,0:T(8,128)(2,1)} %collective-permute-done.41.sent_other_ref), custom_call_target="tpu_custom_call" | custom-call | tf_op jit(solution)/shard_map/join_units/pallas_call | solution.py:478
  1391.0 11.9 join_blocks.1
  1409.4 6.4 join_cols.1
  1420.1 18.1 %collective-permute-done.43 = bf16[560,1024]{1,0:T(8,128)(2,1)} collective-permute-done((bf16[560,1024]{1,0:T(8,128)(2,1)S(1)}, bf16[560,1024]{1,0:T(8,128)(2,1)}, u32[]{:S(2)}, u32[]{:S(2)}) %collective-permute-start.43) | collective-permute-done | bytes 1146912 | tf_op jit(solution)/shard_map/ppermute | solution.py:550
  1446.2 8.4 join_rows.1
  (406 shorter events, 294.1 us)
Async XLA Ops:
  7.2 100.2 %all-gather.7.cloned.1.call-start = ((), (), s32[]{:S(2)}) async-start(), calls=%async_computation.11 | async-start | bytes 10485760 | tf_op jit(solution)/shard_map/all_gather | solution.py:665
  15.6 289.4 %all-gather.9.cloned.1.call-start = ((), (), s32[]{:S(2)}) async-start(), calls=%async_computation.12 | async-start | bytes 5242880 | tf_op jit(solution)/shard_map/all_gather | solution.py:665
  15.7 30.2 %collective-permute-start = (bf16[2,256,2048]{2,1,0:T(8,128)(2,1)S(1)}, bf16[2,256,2048]{2,1,0:T(8,128)(2,1)}, u32[]{:S(2)}, u32[]{:S(2)}) collective-permute-start(bf16[2,256,2048]{2,1,0:T(8,128)(2,1)S(1)} %copy-done.6), channel_id=1, source_target_pairs={{0,1},{1,0},{2,3},{3,2},{4,5},{5,4},{6,7},{7,6},{8,9},{9,8},{10,11... | collective-permute-start | bytes 6291464 | tf_op jit(solution)/shard_map/ppermute | solution.py:640
  16.3 23.2 %collective-permute-start.4 = (bf16[16,2048]{1,0:T(8,128)(2,1)S(1)}, bf16[16,2048]{1,0:T(8,128)(2,1)S(1)}, u32[]{:S(2)}, u32[]{:S(2)}) collective-permute-start(bf16[16,2048]{1,0:T(8,128)(2,1)S(1)} %constant_dynamic-update-slice_fusion.4), channel_id=1, source_target_pairs={{0,8},{8,0},{16,24},{24,16},{1,9},{9,1},{17,25},{25,17},{2,10},{10... | collective-permute-start | bytes 196616 | tf_op jit(solution)/shard_map/ppermute | solution.py:657
  21.6 324.6 %all-gather.15.cloned.1.call-start = ((), (), s32[]{:S(2)}) async-start(), calls=%async_computation.20 | async-start | bytes 9437184 | tf_op jit(solution)/shard_map/all_gather | solution.py:712
  39.5 6.2 collective-permute-start.5
  107.4 260.4 %all-gather.13.cloned.1.call-start = ((), (), s32[]{:S(2)}) async-start(), calls=%async_computation.14 | async-start | bytes 10485760 | tf_op jit(solution)/shard_map/all_gather | solution.py:665
  193.2 65.1 %all-to-all-start = ((bf16[4,512,512]{2,1,0:T(8,128)(2,1)}), bf16[4,512,512]{2,1,0:T(8,128)(2,1)S(1)}, u32[]{:S(2)}, u32[]{:S(2)}) async-start(bf16[4,512,512]{2,1,0:T(8,128)(2,1)} %pack_heads.2), calls=%async_computation | async-start | bytes 4194304 | tf_op jit(solution)/shard_map/all_to_all | solution.py:650
  201.0 20.4 %collective-permute-start.1 = (bf16[256,1536]{1,0:T(8,128)(2,1)S(1)}, bf16[256,1536]{1,0:T(8,128)(2,1)S(1)}, u32[]{:S(2)}, u32[]{:S(2)}) collective-permute-start(bf16[256,1536]{1,0:T(8,128)(2,1)S(1)} %get-tuple-element.253), channel_id=1, source_target_pairs={{0,8},{8,0},{16,24},{24,16},{1,9},{9,1},{17,25},{25,17},{2,10},{10... | collective-permute-start | bytes 2359304 | tf_op jit(solution)/shard_map/ppermute | solution.py:683
  203.1 53.3 %collective-permute-start.2 = (bf16[256,1536]{1,0:T(8,128)(2,1)S(1)}, bf16[256,1536]{1,0:T(8,128)(2,1)S(1)}, u32[]{:S(2)}, u32[]{:S(2)}) collective-permute-start(bf16[256,1536]{1,0:T(8,128)(2,1)S(1)} %get-tuple-element.252), channel_id=1, source_target_pairs={{0,16},{8,24},{16,0},{24,8},{1,17},{9,25},{17,1},{25,9},{2,18},{10... | collective-permute-start | bytes 2359304 | tf_op jit(solution)/shard_map/ppermute | solution.py:683
  204.3 53.0 %collective-permute-start.3 = (bf16[256,1536]{1,0:T(8,128)(2,1)S(1)}, bf16[256,1536]{1,0:T(8,128)(2,1)S(1)}, u32[]{:S(2)}, u32[]{:S(2)}) collective-permute-start(bf16[256,1536]{1,0:T(8,128)(2,1)S(1)} %get-tuple-element.251), channel_id=1, source_target_pairs={{0,24},{8,16},{16,8},{24,0},{1,25},{9,17},{17,9},{25,1},{2,26},{10... | collective-permute-start | bytes 2359304 | tf_op jit(solution)/shard_map/ppermute | solution.py:683
  270.3 28.5 %all-to-all-start.1 = ((bf16[4,512,256]{2,1,0:T(8,128)(2,1)}), bf16[4,512,256]{2,1,0:T(8,128)(2,1)S(1)}, u32[]{:S(2)}, u32[]{:S(2)}) async-start(bf16[4,512,256]{2,1,0:T(8,128)(2,1)} %get-tuple-element.118.res_ref), calls=%async_computation.1 | async-start | bytes 2097152 | tf_op jit(solution)/shard_map/all_to_all | solution.py:650
  298.8 28.7 %all-to-all-start.3 = ((bf16[4,512,256]{2,1,0:T(8,128)(2,1)}), bf16[4,512,256]{2,1,0:T(8,128)(2,1)S(1)}, u32[]{:S(2)}, u32[]{:S(2)}) async-start(bf16[4,512,256]{2,1,0:T(8,128)(2,1)} %get-tuple-element.122.res_ref), calls=%async_computation.3 | async-start | bytes 2097152 | tf_op jit(solution)/shard_map/all_to_all | solution.py:650
  302.3 155.2 %all-gather.11.cloned.1.call-start = ((), (), s32[]{:S(2)}) async-start(), calls=%async_computation.13 | async-start | bytes 10485760 | tf_op jit(solution)/shard_map/all_gather | solution.py:665
  311.0 25.2 %collective-permute-start.6 = (bf16[256,2048]{1,0:T(8,128)(2,1)}, bf16[256,2048]{1,0:T(8,128)(2,1)}, u32[]{:S(2)}, u32[]{:S(2)}) collective-permute-start(bf16[256,2048]{1,0:T(8,128)(2,1)} %broadcast_select_fusion.19), channel_id=1, source_target_pairs={{0,1},{1,0},{2,3},{3,2},{4,5},{5,4},{6,7},{7,6},{8,9},{9,8},{10,11... | collective-permute-start | bytes 3145736 | tf_op jit(solution)/shard_map/ppermute | solution.py:640
  336.1 2.7 collective-permute-start.7
  345.5 291.6 %reduce-scatter.4.cloned.1.call-start = ((), (), s32[]{:S(2)}) async-start(), calls=%async_computation.15 | async-start | bytes 10485760 | tf_op jit(solution)/shard_map/reduce_scatter | solution.py:662
  346.0 6.1 collective-permute-start.8
  351.0 7.9 collective-permute-start.9
  550.6 237.4 %all-reduce.5.cloned.1.call-start = ((), (), s32[]{:S(2)}) async-start(), calls=%async_computation.16 | async-start | bytes 4194304 | tf_op jit(solution)/shard_map/psum | solution.py:795
  571.8 39.9 %collective-permute-start.10 = (bf16[768,2048]{1,0:T(8,128)(2,1)S(1)}, bf16[768,2048]{1,0:T(8,128)(2,1)S(1)}, u32[]{:S(2)}, u32[]{:S(2)}) collective-permute-start(bf16[768,2048]{1,0:T(8,128)(2,1)S(1)} %slice_select_fusion.3), channel_id=1, source_target_pairs={{0,1},{1,0},{2,3},{3,2},{4,5},{5,4},{6,7},{7,6},{8,9},{9,8},{10,11... | collective-permute-start | bytes 9437192 | tf_op jit(solution)/shard_map/ppermute | solution.py:640
  593.2 18.6 %collective-permute-start.11 = (bf16[768,2048]{1,0:T(8,128)(2,1)S(1)}, bf16[768,2048]{1,0:T(8,128)(2,1)}, u32[]{:S(2)}, u32[]{:S(2)}) collective-permute-start(bf16[768,2048]{1,0:T(8,128)(2,1)S(1)} %slice_select_fusion.2), channel_id=1, source_target_pairs={{0,1},{1,0},{2,3},{3,2},{4,5},{5,4},{6,7},{7,6},{8,9},{9,8},{10,11... | collective-permute-start | bytes 9437192 | tf_op jit(solution)/shard_map/ppermute | solution.py:640
  611.6 47.7 %collective-permute-start.13 = (bf16[4,256,1536]{2,1,0:T(8,128)(2,1)}, bf16[4,256,1536]{2,1,0:T(8,128)(2,1)}, u32[]{:S(2)}, u32[]{:S(2)}) collective-permute-start(bf16[4,256,1536]{2,1,0:T(8,128)(2,1)} %fusion.27), channel_id=1, source_target_pairs={{0,1},{1,0},{2,3},{3,2},{4,5},{5,4},{6,7},{7,6},{8,9},{9,8},{10,11... | collective-permute-start | bytes 9437192 | tf_op jit(solution)/shard_map/ppermute | solution.py:640
  657.6 4.5 collective-permute-start.12
  676.8 47.3 %all-to-all-start.4 = ((bf16[4,512,256]{2,1,0:T(8,128)(2,1)}), bf16[4,512,256]{2,1,0:T(8,128)(2,1)S(1)}, u32[]{:S(2)}, u32[]{:S(2)}) async-start(bf16[4,512,256]{2,1,0:T(8,128)(2,1)} %get-tuple-element.137), calls=%async_computation.5 | async-start | bytes 2097152 | tf_op jit(solution)/shard_map/all_to_all | solution.py:650
  724.1 83.8 %all-to-all-start.6 = ((bf16[4,512,256]{2,1,0:T(8,128)(2,1)}), bf16[4,512,256]{2,1,0:T(8,128)(2,1)S(1)}, u32[]{:S(2)}, u32[]{:S(2)}) async-start(bf16[4,512,256]{2,1,0:T(8,128)(2,1)} %get-tuple-element.144), calls=%async_computation.7 | async-start | bytes 2097152 | tf_op jit(solution)/shard_map/all_to_all | solution.py:650
  808.8 100.0 %all-to-all-start.5 = ((bf16[4,512,512]{2,1,0:T(8,128)(2,1)}), bf16[4,512,512]{2,1,0:T(8,128)(2,1)S(1)}, u32[]{:S(2)}, u32[]{:S(2)}) async-start(bf16[4,512,512]{2,1,0:T(8,128)(2,1)} %attend_back.2), calls=%async_computation.6 | async-start | bytes 4194304 | tf_op jit(solution)/shard_map/all_to_all | solution.py:650
  812.4 229.2 %all-reduce.7.cloned.1.call-start = ((), (), s32[]{:S(2)}) async-start(), calls=%async_computation.17 | async-start | bytes 8388608 | tf_op jit(solution)/shard_map/psum | solution.py:826
  908.8 69.0 %all-to-all-start.7 = ((bf16[4,512,512]{2,1,0:T(8,128)(2,1)}), bf16[4,512,512]{2,1,0:T(8,128)(2,1)}, u32[]{:S(2)}, u32[]{:S(2)}) async-start(bf16[4,512,512]{2,1,0:T(8,128)(2,1)} %attend_back.3), calls=%async_computation.8 | async-start | bytes 4194304 | tf_op jit(solution)/shard_map/all_to_all | solution.py:650
  913.3 229.3 %reduce-scatter.6.cloned.1.call-start = ((), (), s32[]{:S(2)}) async-start(), calls=%async_computation.18 | async-start | bytes 5242880 | tf_op jit(solution)/shard_map/reduce_scatter | solution.py:662
  919.2 21.5 %collective-permute-start.16 = (bf16[256,1536]{1,0:T(8,128)(2,1)}, bf16[256,1536]{1,0:T(8,128)(2,1)S(1)}, u32[]{:S(2)}, u32[]{:S(2)}) collective-permute-start(bf16[256,1536]{1,0:T(8,128)(2,1)} %get-tuple-element.248), channel_id=1, source_target_pairs={{0,24},{8,16},{16,8},{24,0},{1,25},{9,17},{17,9},{25,1},{2,26},{10... | collective-permute-start | bytes 2359304 | tf_op jit(solution)/shard_map/ppermute | solution.py:683
  919.2 34.3 %collective-permute-start.15 = (bf16[256,1536]{1,0:T(8,128)(2,1)}, bf16[256,1536]{1,0:T(8,128)(2,1)S(1)}, u32[]{:S(2)}, u32[]{:S(2)}) collective-permute-start(bf16[256,1536]{1,0:T(8,128)(2,1)} %get-tuple-element.249), channel_id=1, source_target_pairs={{0,16},{8,24},{16,0},{24,8},{1,17},{9,25},{17,1},{25,9},{2,18},{10... | collective-permute-start | bytes 2359304 | tf_op jit(solution)/shard_map/ppermute | solution.py:683
  922.1 31.5 %collective-permute-start.14 = (bf16[256,1536]{1,0:T(8,128)(2,1)S(1)}, bf16[256,1536]{1,0:T(8,128)(2,1)S(1)}, u32[]{:S(2)}, u32[]{:S(2)}) collective-permute-start(bf16[256,1536]{1,0:T(8,128)(2,1)S(1)} %get-tuple-element.250), channel_id=1, source_target_pairs={{0,8},{8,0},{16,24},{24,16},{1,9},{9,1},{17,25},{25,17},{2,10},{10... | collective-permute-start | bytes 2359304 | tf_op jit(solution)/shard_map/ppermute | solution.py:683
  922.7 493.2 %reduce-scatter.8.cloned.1.call-start = ((), (), s32[]{:S(2)}) async-start(), calls=%async_computation.19 | async-start | bytes 10485760 | tf_op jit(solution)/shard_map/reduce_scatter | solution.py:662
  1043.6 35.8 %collective-permute-start.17 = (bf16[4,128,1536]{2,1,0:T(8,128)(2,1)}, bf16[4,128,1536]{2,1,0:T(8,128)(2,1)}, u32[]{:S(2)}, u32[]{:S(2)}) collective-permute-start(bf16[4,128,1536]{2,1,0:T(8,128)(2,1)} %get-tuple-element.154), channel_id=1, source_target_pairs={{0,2},{1,3},{6,4},{7,5},{8,10},{9,11},{14,12},{15,13},{16,18},{17,... | collective-permute-start | bytes 4718600 | tf_op jit(solution)/shard_map/ppermute | solution.py:550
  1047.9 81.5 %collective-permute-start.24 = (bf16[2,512,1024]{2,1,0:T(8,128)(2,1)}, bf16[2,512,1024]{2,1,0:T(8,128)(2,1)}, u32[]{:S(2)}, u32[]{:S(2)}) collective-permute-start(bf16[2,512,1024]{2,1,0:T(8,128)(2,1)} %select_bitcast_fusion), channel_id=1, source_target_pairs={{0,8},{8,0},{16,24},{24,16},{1,9},{9,1},{17,25},{25,17},{2,10},{10... | collective-permute-start | bytes 6291464 | tf_op jit(solution)/shard_map/ppermute | solution.py:533
  1066.0 68.1 %collective-permute-start.20 = (bf16[2,256,2048]{2,1,0:T(8,128)(2,1)}, bf16[2,256,2048]{2,1,0:T(8,128)(2,1)}, u32[]{:S(2)}, u32[]{:S(2)}) collective-permute-start(bf16[2,256,2048]{2,1,0:T(8,128)(2,1)} %select_bitcast_fusion.1), channel_id=1, source_target_pairs={{0,1},{1,0},{2,3},{3,2},{4,5},{5,4},{6,7},{7,6},{8,9},{9,8},{10,11... | collective-permute-start | bytes 6291464 | tf_op jit(solution)/shard_map/ppermute | solution.py:640
  1071.0 94.2 %collective-permute-start.31 = (bf16[2,512,1024]{2,1,0:T(8,128)(2,1)}, bf16[2,512,1024]{2,1,0:T(8,128)(2,1)}, u32[]{:S(2)}, u32[]{:S(2)}) collective-permute-start(bf16[2,512,1024]{2,1,0:T(8,128)(2,1)} %bitcast.48), channel_id=1, source_target_pairs={{0,16},{8,24},{16,0},{24,8},{1,17},{9,25},{17,1},{25,9},{2,18},{10... | collective-permute-start | bytes 6291464 | tf_op jit(solution)/shard_map/ppermute | solution.py:533
  1082.9 59.7 %collective-permute-start.18 = (bf16[4,128,1536]{2,1,0:T(8,128)(2,1)}, bf16[4,128,1536]{2,1,0:T(8,128)(2,1)}, u32[]{:S(2)}, u32[]{:S(2)}) collective-permute-start(bf16[4,128,1536]{2,1,0:T(8,128)(2,1)} %add.232), channel_id=1, source_target_pairs={{2,4},{3,5},{4,2},{5,3},{10,12},{11,13},{12,10},{13,11},{18,20},{1... | collective-permute-start | bytes 4718600 | tf_op jit(solution)/shard_map/ppermute | solution.py:550
  1084.9 57.7 %collective-permute-start.19 = (bf16[4,128,1536]{2,1,0:T(8,128)(2,1)}, bf16[4,128,1536]{2,1,0:T(8,128)(2,1)}, u32[]{:S(2)}, u32[]{:S(2)}) collective-permute-start(bf16[4,128,1536]{2,1,0:T(8,128)(2,1)} %get-tuple-element.163), channel_id=1, source_target_pairs={{0,2},{1,3},{6,4},{7,5},{8,10},{9,11},{14,12},{15,13},{16,18},{17,... | collective-permute-start | bytes 4718600 | tf_op jit(solution)/shard_map/ppermute | solution.py:550
  1132.6 44.1 %collective-permute-start.25 = (bf16[512,1024]{1,0:T(8,128)(2,1)}, bf16[512,1024]{1,0:T(8,128)(2,1)}, u32[]{:S(2)}, u32[]{:S(2)}) collective-permute-start(bf16[512,1024]{1,0:T(8,128)(2,1)} %select_bitcast_fusion.3), channel_id=1, source_target_pairs={{0,16},{8,24},{16,0},{24,8},{1,17},{9,25},{17,1},{25,9},{2,18},{10... | collective-permute-start | bytes 3145736 | tf_op jit(solution)/shard_map/ppermute | solution.py:533
  1146.2 37.8 %collective-permute-start.21 = (bf16[4,128,1536]{2,1,0:T(8,128)(2,1)}, bf16[4,128,1536]{2,1,0:T(8,128)(2,1)}, u32[]{:S(2)}, u32[]{:S(2)}) collective-permute-start(bf16[4,128,1536]{2,1,0:T(8,128)(2,1)} %add.238), channel_id=1, source_target_pairs={{2,0},{3,1},{4,6},{5,7},{10,8},{11,9},{12,14},{13,15},{18,16},{19,... | collective-permute-start | bytes 4718600 | tf_op jit(solution)/shard_map/ppermute | solution.py:550
  1151.1 32.9 %collective-permute-start.22 = (bf16[4,128,1536]{2,1,0:T(8,128)(2,1)}, bf16[4,128,1536]{2,1,0:T(8,128)(2,1)}, u32[]{:S(2)}, u32[]{:S(2)}) collective-permute-start(bf16[4,128,1536]{2,1,0:T(8,128)(2,1)} %add.239), channel_id=1, source_target_pairs={{2,4},{3,5},{4,2},{5,3},{10,12},{11,13},{12,10},{13,11},{18,20},{1... | collective-permute-start | bytes 4718600 | tf_op jit(solution)/shard_map/ppermute | solution.py:550
  1153.9 27.1 %collective-permute-start.23 = (bf16[512,1024]{1,0:T(8,128)(2,1)S(1)}, bf16[512,1024]{1,0:T(8,128)(2,1)}, u32[]{:S(2)}, u32[]{:S(2)}) collective-permute-start(bf16[512,1024]{1,0:T(8,128)(2,1)S(1)} %copy-done.42), channel_id=1, source_target_pairs={{0,2},{1,3},{6,4},{7,5},{8,10},{9,11},{14,12},{15,13},{16,18},{17,... | collective-permute-start | bytes 3145736 | tf_op jit(solution)/shard_map/ppermute | solution.py:550
  1165.2 2.8 collective-permute-start.26
  1168.0 7.3 collective-permute-start.27
  1175.4 28.0 %collective-permute-start.32 = (bf16[512,1024]{1,0:T(8,128)(2,1)S(1)}, bf16[512,1024]{1,0:T(8,128)(2,1)S(1)}, u32[]{:S(2)}, u32[]{:S(2)}) collective-permute-start(bf16[512,1024]{1,0:T(8,128)(2,1)S(1)} %select_bitcast_fusion.2), channel_id=1, source_target_pairs={{0,8},{8,0},{16,24},{24,16},{1,9},{9,1},{17,25},{25,17},{2,10},{10... | collective-permute-start | bytes 3145736 | tf_op jit(solution)/shard_map/ppermute | solution.py:533
  1186.3 42.1 %collective-permute-start.28 = (bf16[4,128,1536]{2,1,0:T(8,128)(2,1)S(1)}, bf16[4,128,1536]{2,1,0:T(8,128)(2,1)}, u32[]{:S(2)}, u32[]{:S(2)}) collective-permute-start(bf16[4,128,1536]{2,1,0:T(8,128)(2,1)S(1)} %add.248), channel_id=1, source_target_pairs={{2,0},{3,1},{4,6},{5,7},{10,8},{11,9},{12,14},{13,15},{18,16},{19,... | collective-permute-start | bytes 4718600 | tf_op jit(solution)/shard_map/ppermute | solution.py:550
  1189.2 20.4 %collective-permute-start.29 = (bf16[512,1024]{1,0:T(8,128)(2,1)S(1)}, bf16[512,1024]{1,0:T(8,128)(2,1)S(1)}, u32[]{:S(2)}, u32[]{:S(2)}) collective-permute-start(bf16[512,1024]{1,0:T(8,128)(2,1)S(1)} %add.249), channel_id=1, source_target_pairs={{2,4},{3,5},{4,2},{5,3},{10,12},{11,13},{12,10},{13,11},{18,20},{1... | collective-permute-start | bytes 3145736 | tf_op jit(solution)/shard_map/ppermute | solution.py:550
  1189.9 33.0 %collective-permute-start.30 = (bf16[512,1024]{1,0:T(8,128)(2,1)S(1)}, bf16[512,1024]{1,0:T(8,128)(2,1)S(1)}, u32[]{:S(2)}, u32[]{:S(2)}) collective-permute-start(bf16[512,1024]{1,0:T(8,128)(2,1)S(1)} %bitcast_add_fusion.2), channel_id=1, source_target_pairs={{0,2},{1,3},{6,4},{7,5},{8,10},{9,11},{14,12},{15,13},{16,18},{17,... | collective-permute-start | bytes 3145736 | tf_op jit(solution)/shard_map/ppermute | solution.py:550
  1202.8 5.7 collective-permute-start.33
  1232.5 126.2 %collective-permute-start.40 = (bf16[768,2048]{1,0:T(8,128)(2,1)}, bf16[768,2048]{1,0:T(8,128)(2,1)}, u32[]{:S(2)}, u32[]{:S(2)}) collective-permute-start(bf16[768,2048]{1,0:T(8,128)(2,1)} %slice.393), channel_id=1, source_target_pairs={{0,16},{8,24},{16,0},{24,8},{1,17},{9,25},{17,1},{25,9},{2,18},{10... | collective-permute-start | bytes 9437192 | tf_op jit(solution)/shard_map/ppermute | solution.py:901
  1233.0 125.7 %collective-permute-start.36 = (bf16[560,1024]{1,0:T(8,128)(2,1)}, bf16[560,1024]{1,0:T(8,128)(2,1)}, u32[]{:S(2)}, u32[]{:S(2)}) collective-permute-start(bf16[560,1024]{1,0:T(8,128)(2,1)} %pad_maximum_fusion.9), channel_id=1, source_target_pairs={{0,2},{1,3},{6,4},{7,5},{8,10},{9,11},{14,12},{15,13},{16,18},{17,... | collective-permute-start | bytes 3440648 | tf_op jit(solution)/shard_map/ppermute | solution.py:550
  1236.8 121.9 %collective-permute-start.34 = (bf16[512,1024]{1,0:T(8,128)(2,1)}, bf16[512,1024]{1,0:T(8,128)(2,1)}, u32[]{:S(2)}, u32[]{:S(2)}) collective-permute-start(bf16[512,1024]{1,0:T(8,128)(2,1)} %add.253), channel_id=1, source_target_pairs={{2,0},{3,1},{4,6},{5,7},{10,8},{11,9},{12,14},{13,15},{18,16},{19,... | collective-permute-start | bytes 3145736 | tf_op jit(solution)/shard_map/ppermute | solution.py:550
  1239.5 119.2 %collective-permute-start.35 = (bf16[512,1024]{1,0:T(8,128)(2,1)}, bf16[512,1024]{1,0:T(8,128)(2,1)}, u32[]{:S(2)}, u32[]{:S(2)}) collective-permute-start(bf16[512,1024]{1,0:T(8,128)(2,1)} %add.254), channel_id=1, source_target_pairs={{2,4},{3,5},{4,2},{5,3},{10,12},{11,13},{12,10},{13,11},{18,20},{1... | collective-permute-start | bytes 3145736 | tf_op jit(solution)/shard_map/ppermute | solution.py:550
  1244.5 130.0 %collective-permute-start.39 = (bf16[768,2048]{1,0:T(8,128)(2,1)S(1)}, bf16[768,2048]{1,0:T(8,128)(2,1)}, u32[]{:S(2)}, u32[]{:S(2)}) collective-permute-start(bf16[768,2048]{1,0:T(8,128)(2,1)S(1)} %pad_maximum_fusion.7.keep_ref), channel_id=1, source_target_pairs={{0,1},{1,0},{2,3},{3,2},{4,5},{5,4},{6,7},{7,6},{8,9},{9,8},{10,11... | collective-permute-start | bytes 9437192 | tf_op jit(solution)/shard_map/ppermute | solution.py:640
  1358.7 15.8 %collective-permute-start.41 = (bf16[768,2048]{1,0:T(8,128)(2,1)}, bf16[768,2048]{1,0:T(8,128)(2,1)}, u32[]{:S(2)}, u32[]{:S(2)}) collective-permute-start(bf16[768,2048]{1,0:T(8,128)(2,1)} %collective-permute-done.40.sent_ref), channel_id=1, source_target_pairs={{0,1},{1,0},{2,3},{3,2},{4,5},{5,4},{6,7},{7,6},{8,9},{9,8},{10,11... | collective-permute-start | bytes 9437192 | tf_op jit(solution)/shard_map/ppermute | solution.py:640
  1363.8 27.1 %collective-permute-start.42 = (bf16[4,256,1536]{2,1,0:T(8,128)(2,1)}, bf16[4,256,1536]{2,1,0:T(8,128)(2,1)}, u32[]{:S(2)}, u32[]{:S(2)}) collective-permute-start(bf16[4,256,1536]{2,1,0:T(8,128)(2,1)} %pad_maximum_fusion.8.refs_0_), channel_id=1, source_target_pairs={{0,1},{1,0},{2,3},{3,2},{4,5},{5,4},{6,7},{7,6},{8,9},{9,8},{10,11... | collective-permute-start | bytes 9437192 | tf_op jit(solution)/shard_map/ppermute | solution.py:640
  1367.4 35.5 %collective-permute-start.38 = (bf16[560,1024]{1,0:T(8,128)(2,1)}, bf16[560,1024]{1,0:T(8,128)(2,1)}, u32[]{:S(2)}, u32[]{:S(2)}) collective-permute-start(bf16[560,1024]{1,0:T(8,128)(2,1)} %add.256), channel_id=1, source_target_pairs={{2,4},{3,5},{4,2},{5,3},{10,12},{11,13},{12,10},{13,11},{18,20},{1... | collective-permute-start | bytes 3440648 | tf_op jit(solution)/shard_map/ppermute | solution.py:550
  1372.0 30.9 %collective-permute-start.37 = (bf16[512,1024]{1,0:T(8,128)(2,1)}, bf16[512,1024]{1,0:T(8,128)(2,1)}, u32[]{:S(2)}, u32[]{:S(2)}) collective-permute-start(bf16[512,1024]{1,0:T(8,128)(2,1)} %add.255), channel_id=1, source_target_pairs={{2,0},{3,1},{4,6},{5,7},{10,8},{11,9},{12,14},{13,15},{18,16},{19,... | collective-permute-start | bytes 3145736 | tf_op jit(solution)/shard_map/ppermute | solution.py:550
  1405.2 4.2 collective-permute-start.44
  1407.5 30.8 %collective-permute-start.43 = (bf16[560,1024]{1,0:T(8,128)(2,1)S(1)}, bf16[560,1024]{1,0:T(8,128)(2,1)}, u32[]{:S(2)}, u32[]{:S(2)}) collective-permute-start(bf16[560,1024]{1,0:T(8,128)(2,1)S(1)} %add.257), channel_id=1, source_target_pairs={{2,0},{3,1},{4,6},{5,7},{10,8},{11,9},{12,14},{13,15},{18,16},{19,... | collective-permute-start | bytes 3440648 | tf_op jit(solution)/shard_map/ppermute | solution.py:550
  1439.6 5.5 collective-permute-start.46
  1441.4 2.7 collective-permute-start.45
  (81 other events, 1219.9 us)
Sparse Core Ops, SparseCore 0:
  15.7 91.5 all-gather.6
  109.8 52.5 all-gather.8
  164.5 114.0 all-gather.14
  280.3 87.4 all-gather.12
  370.1 87.4 all-gather.10
  550.7 86.3 reduce-scatter.3
  659.4 128.6 all-reduce.4
  815.6 225.9 all-reduce.6
  1044.6 84.6 reduce-scatter.5
  1228.5 140.4 reduce-scatter.7

commit v10 on v9

--- a/solution.py
+++ b/solution.py
@@ -884,6 +884,9 @@
             x = x + lax.ppermute(x, name, [(p, p ^ bit) for p in range(lax.axis_size(name))])
         return x
 
+    keep = jnp.concatenate([gu_first, gu_sum[: quarter - third]], axis=0)
+    sent = lax.ppermute(gu_sum[quarter - third :], "dp", trade)
+
     def near_sum(done, made):
         return [hop(small, hops[:2]), out_part]
 
@@ -894,14 +897,12 @@
             parts[4] = jnp.concatenate([parts[4], wide[:, :half], wide[:, half:]], axis=0)
         else:
             total = lax.psum(total, "seq", axis_index_groups=groups)
-        return [total, made[-1][1]]
+        return [total, made[-1][1], sent]
 
     line = Line(chips, chip)
-    keep = jnp.concatenate([gu_first, gu_sum[: quarter - third]], axis=0)
-    sent = lax.ppermute(gu_sum[quarter - third :], "dp", trade)
-
     def join_early(done, made):
         down_done = jnp.concatenate(done[:2], axis=1)
+        sent = made[2][2]
         places = [unit_block.index(b) ^ me for b in range(dp)]
         return [
             join_units([keep, sent], [swap(keep), swap(sent)], core, upper.astype(jnp.int32)),
@@ -912,7 +913,7 @@
         output = (mid + scatter(made[2][1]).astype(F32)).astype(BF).reshape(rows, tok, width)
         return [join_cols([done[2]], [swap(done[2])], core, GROUP * HEAD), output]
 
-    sums, ((_, grad_input), _, (small, _), (grad_gu, grad_down), (grad_out, output)) = line.pipeline(
+    sums, ((_, grad_input), _, (small, *_), (grad_gu, grad_down), (grad_out, output)) = line.pipeline(
         parts, {1: norm_done, 2: near_sum, 3: far_sum, 5: join_early, 6: join_late}
     )
     if chips == 4:

time: 1470 us -> 1400 us (0.952)
  waiting for transfers between devices: 667 us -> 613 us
    ppermute x1, waiting for transfers between devices: 114 us -> 0.01 us  [shards(): sent = lax.ppermute(gu_sum[quarter - third:], 'dp', trade)]
    ppermute x4, waiting for transfers between devices: 37.4 us -> 81.2 us  [send(): return lax.ppermute(jnp.where(mark, low, high), 'dp', pairs)]
    ppermute x15, waiting for transfers between devices: 49.8 us -> 67.1 us  [send(): return (x, lax.ppermute(x, 'seq', self.stages[stage]))]
    unnamed x167 -> x181, local copies, waits for them, and re-layouts: 30.1 us -> 30.5 us
  transfers between devices with their start and end apart: 64 -> 64, of which waited for: 31 -> 34; matrix products, arithmetic and copies ran while one was open for 24% -> 25% of each run, Pallas kernels for 9% -> 10%
where the time goes in v10:
time: 1400 us
  waiting for transfers between devices  613 us (44%)
  matrix products  250 us (18%)
  other arithmetic  168 us (12%)
  Pallas kernels  145 us (10%)
  starting transfers between devices  94.7 us (7%)
  local copies, waits for them, and re-layouts  56.9 us (4%)
  blocking collectives  52.5 us (4%)
  between operations  16 us (1%)
    all_gather x4, waiting for transfers between devices, gather(): return lax.all_gather(x, 'dp', axis=0, tiled=True)  127 us
    all_to_all x7, waiting for transfers between devices, exchange(): return lax.all_to_all(x, 'seq', 0, 0, axis_index_groups=groups, tiled=True)  117 us
    dot_general x7, matrix products, dot_nt(): lax.dot_general(left, right, (((1,), (1,)), ((), ())), preferred_element_...  94.2 us
    dot_general x7, matrix products, dot_nn(): lax.dot_general(left, right, (((1,), (0,)), ((), ())), preferred_element_...  83 us
    ppermute x4, waiting for transfers between devices, send(): return lax.ppermute(jnp.where(mark, low, high), 'dp', pairs)  81.2 us
    ppermute x6, waiting for transfers between devices, trade_blocks(): lax.ppermute(out, 'dp', [(d, d ^ k) for d in range(dp)])  77.5 us
    dot_general x7, matrix products, dot_tn(): lax.dot_general(left, right, (((0,), (0,)), ((), ())), preferred_element_...  72.8 us
    ppermute x15, waiting for transfers between devices, send(): return (x, lax.ppermute(x, 'seq', self.stages[stage]))  67.1 us
  transfers between devices with their start and end apart: 64, of which 34 were waited for; matrix products, arithmetic and copies ran while one was open for 25% of the time, Pallas kernels for 10%

profile of v10, /device:TPU:0, one launch (start us, length us, event | category | flops | bytes accessed | tf_op | source)
XLA Modules:
  0.0 1396.4 jit_solution(4721510992868949028)
XLA Ops:
  30.5 6.6 select_select_fusion
  48.7 4.3 maximum_convert_fusion
  53.0 54.4 %all-gather.7.cloned.1.call-done = bf16[2048,2048]{1,0:T(8,128)(2,1)} async-done(((bf16[512,2048]{1,0:T(8,128)(2,1)}), bf16[2048,2048]{1,0:T(8,128)(2,1)}) %all-gather.7.cloned.1.call-update) | async-done | bytes 8388624 | tf_op jit(solution)/shard_map/all_gather | solution.py:665
  117.2 11.1 fusion.67.proj_ref
  128.3 6.2 pack_heads.3
  134.4 52.5 %all_to_all.40.q_ref.k_ref.v_ref = bf16[4,512,512]{2,1,0:T(8,128)(2,1)} all-to-all(bf16[4,512,512]{2,1,0:T(8,128)(2,1)} %pack_heads.3), channel_id=1, replica_groups={{0,2,4,6},{1,3,5,7},{8,10,12,14},{9,11,13,15},{16,18,20,22},{17,19,21,2..., dimensions={0} | all-to-all | bytes 4194304 | tf_op jit(solution)/shard_map/all_to_all | solution.py:650
  187.0 6.2 pack_heads.2
  205.7 15.7 %collective-permute-done.1 = bf16[256,1536]{1,0:T(8,128)(2,1)S(1)} collective-permute-done((bf16[256,1536]{1,0:T(8,128)(2,1)S(1)}, bf16[256,1536]{1,0:T(8,128)(2,1)S(1)}, u32[]{:S(2)}, u32[]{:S(2)}) %collective-permute-start.1) | collective-permute-done | bytes 786464 | tf_op jit(solution)/shard_map/ppermute | solution.py:683
  222.4 34.0 %collective-permute-done.2 = bf16[256,1536]{1,0:T(8,128)(2,1)S(1)} collective-permute-done((bf16[256,1536]{1,0:T(8,128)(2,1)S(1)}, bf16[256,1536]{1,0:T(8,128)(2,1)S(1)}, u32[]{:S(2)}, u32[]{:S(2)}) %collective-permute-start.2) | collective-permute-done | bytes 786464 | tf_op jit(solution)/shard_map/ppermute | solution.py:683
  259.6 10.8 attend.2
  270.3 5.2 all-to-all-start.1
  275.5 10.8 attend.3
  286.3 12.5 all-to-all-done.1.res_ref
  305.0 4.9 convolution_convert_fusion.11
  311.0 16.5 %all-to-all-done.3.res_ref = bf16[4,512,256]{2,1,0:T(8,128)(2,1)S(1)} async-done(((bf16[4,512,256]{2,1,0:T(8,128)(2,1)}), bf16[4,512,256]{2,1,0:T(8,128)(2,1)S(1)}, u32[]{:S(2)}, u32[]{:S(2)}) %all-to-all-start.3) | async-done | bytes 1048608 | tf_op jit(solution)/shard_map/all_to_all | solution.py:650
  331.1 4.9 convolution_convert_fusion.10
  346.2 4.8 slice_select_fusion.4
  367.8 18.6 %convolution_convert_fusion.3 = bf16[2048,1536]{1,0:T(8,128)(2,1)} fusion(bf16[2048,2048]{1,0:T(8,128)(2,1)} %all-gather.13.cloned.1.call-done, bf16[2048,1536]{1,0:T(8,128)(2,1)} %bitcast.202), kind=kOutput, calls=%fused_computation.24 | convolution fusion | flops 12888047616 | bytes 20971520 | tf_op jit(solution)/shard_map/dot_general | solution.py:33
  386.4 71.1 %all-gather.11.cloned.1.call-done = bf16[2048,2048]{1,0:T(8,128)(2,1)} async-done(((bf16[512,2048]{1,0:T(8,128)(2,1)}), bf16[2048,2048]{1,0:T(8,128)(2,1)}) %all-gather.11.cloned.1.call-update) | async-done | bytes 8388624 | tf_op jit(solution)/shard_map/all_gather | solution.py:665
  457.6 19.7 %convolution_convert_fusion.1 = bf16[2048,1536]{1,0:T(8,128)(2,1)} fusion(bf16[2048,2048]{1,0:T(8,128)(2,1)} %all-gather.11.cloned.1.call-done, bf16[3072,2048]{1,0:T(8,128)(2,1)} %param.21, pred[]{:T(512)S(6)} %ge.19), kind=kOutput, calls=%fused_computation.22 | convolution fusion | flops 12891193344 | bytes 27262976 | tf_op jit(solution)/shard_map/dot_general | solution.py:29
  477.3 32.3 %select_convert_fusion = (bf16[2048,1536]{1,0:T(8,128)(2,1)}, bf16[2048,1536]{1,0:T(8,128)(2,1)}, bf16[2048,1536]{1,0:T(8,128)(2,1)}) fusion(bf16[2048,1536]{1,0:T(8,128)(2,1)} %convolution_convert_fusion.3, pred[]{:T(512)S(6)} %ge.19, bf16[2048,1536]{1,0:T(8,128)(2,1)} %convolution_convert_fusion.1, bf16[2048,2048]{1,0:T(8,128)(2,1)} %all-gather.11.cloned.1.call-done, ...), kind=kOutput, calls=%fused_computation.14 | convolution fusion | flops 12957253632 | bytes 46137344 | tf_op jit(solution)/shard_map/dot_general | solution.py:29
  509.7 21.9 %fusion.45 = f32[2048,2048]{1,0:T(8,128)} fusion(bf16[2048,1536]{1,0:T(8,128)(2,1)} %get-tuple-element.229, bf16[3072,2048]{1,0:T(8,128)(2,1)} %param.21, pred[]{:T(512)S(6)} %ge.19), kind=kOutput, calls=%fused_computation.142 | convolution fusion | flops 12888047616 | bytes 35651584 | tf_op jit(solution)/shard_map/dot_general | solution.py:33
  531.5 19.1 %add_convert_fusion = bf16[2048,2048]{1,0:T(8,128)(2,1)} fusion(f32[2048,2048]{1,0:T(8,128)} %fusion.45, bf16[2048,1536]{1,0:T(8,128)(2,1)S(1)} %copy-done.81, bf16[1536,2048]{1,0:T(8,128)(2,1)} %pad_maximum_fusion.1), kind=kOutput, calls=%fused_computation.3 | convolution fusion | flops 12893290496 | bytes 37748736 | tf_op jit(solution)/shard_map/dot_general | solution.py:33
  550.7 17.9 %convolution_convert_fusion.6 = bf16[1536,2048]{1,0:T(8,128)(2,1)S(1)} fusion(bf16[2048,1536]{1,0:T(8,128)(2,1)} %get-tuple-element.229, bf16[2048,2048]{1,0:T(8,128)(2,1)} %all-gather.11.cloned.1.call-done), kind=kOutput, calls=%fused_computation.27 | convolution fusion | flops 12888047616 | bytes 20971520 | tf_op jit(solution)/shard_map/dot_general | solution.py:37
  571.8 18.6 %convolution_convert_fusion.5 = bf16[1536,2048]{1,0:T(8,128)(2,1)S(1)} fusion(bf16[2048,1536]{1,0:T(8,128)(2,1)} %get-tuple-element.228, bf16[2048,2048]{1,0:T(8,128)(2,1)} %all-gather.11.cloned.1.call-done), kind=kOutput, calls=%fused_computation.26 | convolution fusion | flops 12888047616 | bytes 20971520 | tf_op jit(solution)/shard_map/dot_general | solution.py:37
  593.5 14.3 %convolution_convert_fusion.4 = bf16[2048,1536]{1,0:T(8,128)(2,1)S(1)} fusion(bf16[2048,2048]{1,0:T(8,128)(2,1)S(1)} %bitcast.224, bf16[2048,1536]{1,0:T(8,128)(2,1)S(1)} %bitcast.226), kind=kOutput, calls=%fused_computation.25 | convolution fusion | flops 12888047616 | bytes 20971520 | tf_op jit(solution)/shard_map/dot_general | solution.py:37
  611.7 25.4 %reduce-scatter.4.cloned.1.call-done = bf16[512,2048]{1,0:T(8,128)(2,1)} async-done(((bf16[2048,2048]{1,0:T(8,128)(2,1)}), bf16[512,2048]{1,0:T(8,128)(2,1)}) %reduce-scatter.4.cloned.1.call-update) | async-done | bytes 2097168 | tf_op jit(solution)/shard_map/reduce_scatter | solution.py:662
  637.1 8.9 select_add_fusion
  676.8 4.7 all-to-all-start.4
  681.5 19.3 %convolution_convert_fusion = bf16[2048,2048]{1,0:T(8,128)(2,1)} fusion(bf16[2048,1536]{1,0:T(8,128)(2,1)} %get-tuple-element.143, bf16[2048,1536]{1,0:T(8,128)(2,1)} %bitcast.203), kind=kOutput, calls=%fused_computation.21 | convolution fusion | flops 12889096192 | bytes 20971520 | tf_op jit(solution)/shard_map/dot_general | solution.py:29
  704.6 6.4 convolution_convert_fusion.9
  711.1 5.8 fusion.68.grad_ref
  728.0 5.1 slice.370
  733.1 55.0 %all-reduce.5.cloned.1.call-done = bf16[512,2048]{1,0:T(8,128)(2,1)} async-done(((bf16[512,2048]{1,0:T(8,128)(2,1)}), bf16[512,2048]{1,0:T(8,128)(2,1)}) %all-reduce.5.cloned.1.call-update) | async-done | bytes 2097168 | tf_op jit(solution)/shard_map/psum | solution.py:795
  788.1 19.8 %attend_back.2 = bf16[4,512,512]{2,1,0:T(8,128)(2,1)} custom-call(s32[4]{0:T(128)} %get-tuple-element.291.low_ref, bf16[4,512,512]{2,1,0:T(8,128)(2,1)} %copy-done, bf16[4,512,512]{2,1,0:T(8,128)(2,1)} %copy-done, bf16[4,512,512]{2,1,0:T(8,128)(2,1)} %copy-done, bf16[4,512,256]{2,1,0:T(8,128)(2,1)} %copy-done.38, ...), custom_call_target="tpu_custom_call" | custom-call | tf_op jit(solution)/shard_map/attend_back/pallas_call | solution.py:281
  813.2 19.8 %attend_back.3 = bf16[4,512,512]{2,1,0:T(8,128)(2,1)} custom-call(s32[4]{0:T(128)} %get-tuple-element.290.low_ref, bf16[4,512,512]{2,1,0:T(8,128)(2,1)} %all_to_all.40.q_ref.k_ref.v_ref, bf16[4,512,512]{2,1,0:T(8,128)(2,1)} %all_to_all.40.q_ref.k_ref.v_ref, bf16[4,512,512]{2,1,0:T(8,128)(2,1)} %all_to_all.40.q_ref.k_ref.v_ref, ...), custom_call_target="tpu_custom_call" | custom-call | tf_op jit(solution)/shard_map/attend_back/pallas_call | solution.py:281
  833.0 75.9 %all-to-all-done.5.grad_ref = bf16[4,512,512]{2,1,0:T(8,128)(2,1)S(1)} async-done(((bf16[4,512,512]{2,1,0:T(8,128)(2,1)}), bf16[4,512,512]{2,1,0:T(8,128)(2,1)S(1)}, u32[]{:S(2)}, u32[]{:S(2)}) %all-to-all-start.5) | async-done | bytes 2097184 | tf_op jit(solution)/shard_map/all_to_all | solution.py:650
  908.8 4.5 all-to-all-start.7
  913.4 4.4 fusion.25
  923.4 17.5 %collective-permute-done.16 = bf16[256,1536]{1,0:T(8,128)(2,1)} collective-permute-done((bf16[256,1536]{1,0:T(8,128)(2,1)}, bf16[256,1536]{1,0:T(8,128)(2,1)}, u32[]{:S(2)}, u32[]{:S(2)}) %collective-permute-start.16) | collective-permute-done | bytes 786464 | tf_op jit(solution)/shard_map/ppermute | solution.py:683
  940.9 10.2 collective-permute-done.15
  954.4 7.5 unpack_heads.2
  965.0 8.5 all-to-all-done.7.grad_ref
  973.5 7.5 unpack_heads.3
  984.4 8.6 convolution_convert_fusion.8
  993.0 6.3 convolution_convert_fusion.7
  999.2 43.5 %all-reduce.7.cloned.1.call-done = bf16[1024,2048]{1,0:T(8,128)(2,1)} async-done(((bf16[1024,2048]{1,0:T(8,128)(2,1)}), bf16[1024,2048]{1,0:T(8,128)(2,1)}) %all-reduce.7.cloned.1.call-update) | async-done | bytes 4194320 | tf_op jit(solution)/shard_map/psum | solution.py:826
  1042.8 12.7 fusion.69
  1070.1 4.7 broadcast_select_fusion.6
  1078.9 19.7 %collective-permute-done.17 = bf16[4,128,1536]{2,1,0:T(8,128)(2,1)} collective-permute-done((bf16[4,128,1536]{2,1,0:T(8,128)(2,1)}, bf16[4,128,1536]{2,1,0:T(8,128)(2,1)}, u32[]{:S(2)}, u32[]{:S(2)}) %collective-permute-start.17) | collective-permute-done | bytes 1572896 | tf_op jit(solution)/shard_map/ppermute | solution.py:550
  1103.9 7.9 collective-permute-start.19
  1111.8 5.4 fusion.22
  1117.2 14.8 %collective-permute-done.24 = bf16[2,512,1024]{2,1,0:T(8,128)(2,1)} collective-permute-done((bf16[2,512,1024]{2,1,0:T(8,128)(2,1)}, bf16[2,512,1024]{2,1,0:T(8,128)(2,1)}, u32[]{:S(2)}, u32[]{:S(2)}) %collective-permute-start.24) | collective-permute-done | bytes 2097184 | tf_op jit(solution)/shard_map/ppermute | solution.py:533
  1132.0 4.5 bitcast_add_fusion
  1157.7 6.3 collective-permute-start.23
  1166.7 56.1 %collective-permute-done.25 = bf16[512,1024]{1,0:T(8,128)(2,1)S(1)} collective-permute-done((bf16[512,1024]{1,0:T(8,128)(2,1)S(1)}, bf16[512,1024]{1,0:T(8,128)(2,1)S(1)}, u32[]{:S(2)}, u32[]{:S(2)}) %collective-permute-start.25) | collective-permute-done | bytes 1048608 | tf_op jit(solution)/shard_map/ppermute | solution.py:533
  1226.4 9.5 collective-permute-start.30
  1236.0 10.3 collective-permute-done.32
  1274.1 16.5 %collective-permute-done.35 = bf16[512,1024]{1,0:T(8,128)(2,1)} collective-permute-done((bf16[512,1024]{1,0:T(8,128)(2,1)}, bf16[512,1024]{1,0:T(8,128)(2,1)}, u32[]{:S(2)}, u32[]{:S(2)}) %collective-permute-start.35) | collective-permute-done | bytes 1048608 | tf_op jit(solution)/shard_map/ppermute | solution.py:550
  1304.8 16.5 %join_units.1 = f32[3072,2048]{1,0:T(8,128)} custom-call(s32[2]{0:T(128)} %pad_add_fusion.which_ref, bf16[768,2048]{1,0:T(8,128)(2,1)} %copy-done.23, bf16[768,2048]{1,0:T(8,128)(2,1)} %collective-permute-done.40.keep_other_ref, bf16[768,2048]{1,0:T(8,128)(2,1)} %collective-permute-done.34.sent_ref, bf16[768,2048]{1,0:T(8,128)(2,1)} %collective-permute-done.41.sent_other_ref), custom_call_target="tpu_custom_call" | custom-call | tf_op jit(solution)/shard_map/join_units/pallas_call | solution.py:478
  1321.2 12.2 join_blocks.1
  1340.4 6.5 join_cols.1
  1351.9 20.9 %collective-permute-done.43 = bf16[560,1024]{1,0:T(8,128)(2,1)} collective-permute-done((bf16[560,1024]{1,0:T(8,128)(2,1)S(1)}, bf16[560,1024]{1,0:T(8,128)(2,1)}, u32[]{:S(2)}, u32[]{:S(2)}) %collective-permute-start.43) | collective-permute-done | bytes 1146912 | tf_op jit(solution)/shard_map/ppermute | solution.py:550
  1380.7 8.4 join_rows.1
  (420 shorter events, 288.2 us)
Async XLA Ops:
  7.2 100.2 %all-gather.7.cloned.1.call-start = ((), (), s32[]{:S(2)}) async-start(), calls=%async_computation.11 | async-start | bytes 10485760 | tf_op jit(solution)/shard_map/all_gather | solution.py:665
  15.6 289.4 %all-gather.9.cloned.1.call-start = ((), (), s32[]{:S(2)}) async-start(), calls=%async_computation.12 | async-start | bytes 5242880 | tf_op jit(solution)/shard_map/all_gather | solution.py:665
  15.7 30.2 %collective-permute-start = (bf16[2,256,2048]{2,1,0:T(8,128)(2,1)S(1)}, bf16[2,256,2048]{2,1,0:T(8,128)(2,1)}, u32[]{:S(2)}, u32[]{:S(2)}) collective-permute-start(bf16[2,256,2048]{2,1,0:T(8,128)(2,1)S(1)} %copy-done.6), channel_id=1, source_target_pairs={{0,1},{1,0},{2,3},{3,2},{4,5},{5,4},{6,7},{7,6},{8,9},{9,8},{10,11... | collective-permute-start | bytes 6291464 | tf_op jit(solution)/shard_map/ppermute | solution.py:640
  16.3 23.2 %collective-permute-start.4 = (bf16[16,2048]{1,0:T(8,128)(2,1)S(1)}, bf16[16,2048]{1,0:T(8,128)(2,1)S(1)}, u32[]{:S(2)}, u32[]{:S(2)}) collective-permute-start(bf16[16,2048]{1,0:T(8,128)(2,1)S(1)} %constant_dynamic-update-slice_fusion.4), channel_id=1, source_target_pairs={{0,8},{8,0},{16,24},{24,16},{1,9},{9,1},{17,25},{25,17},{2,10},{10... | collective-permute-start | bytes 196616 | tf_op jit(solution)/shard_map/ppermute | solution.py:657
  21.6 324.6 %all-gather.15.cloned.1.call-start = ((), (), s32[]{:S(2)}) async-start(), calls=%async_computation.20 | async-start | bytes 9437184 | tf_op jit(solution)/shard_map/all_gather | solution.py:712
  39.5 6.2 collective-permute-start.5
  107.4 260.4 %all-gather.13.cloned.1.call-start = ((), (), s32[]{:S(2)}) async-start(), calls=%async_computation.14 | async-start | bytes 10485760 | tf_op jit(solution)/shard_map/all_gather | solution.py:665
  193.2 65.1 %all-to-all-start = ((bf16[4,512,512]{2,1,0:T(8,128)(2,1)}), bf16[4,512,512]{2,1,0:T(8,128)(2,1)S(1)}, u32[]{:S(2)}, u32[]{:S(2)}) async-start(bf16[4,512,512]{2,1,0:T(8,128)(2,1)} %pack_heads.2), calls=%async_computation | async-start | bytes 4194304 | tf_op jit(solution)/shard_map/all_to_all | solution.py:650
  201.0 20.4 %collective-permute-start.1 = (bf16[256,1536]{1,0:T(8,128)(2,1)S(1)}, bf16[256,1536]{1,0:T(8,128)(2,1)S(1)}, u32[]{:S(2)}, u32[]{:S(2)}) collective-permute-start(bf16[256,1536]{1,0:T(8,128)(2,1)S(1)} %get-tuple-element.255), channel_id=1, source_target_pairs={{0,8},{8,0},{16,24},{24,16},{1,9},{9,1},{17,25},{25,17},{2,10},{10... | collective-permute-start | bytes 2359304 | tf_op jit(solution)/shard_map/ppermute | solution.py:683
  203.1 53.3 %collective-permute-start.2 = (bf16[256,1536]{1,0:T(8,128)(2,1)S(1)}, bf16[256,1536]{1,0:T(8,128)(2,1)S(1)}, u32[]{:S(2)}, u32[]{:S(2)}) collective-permute-start(bf16[256,1536]{1,0:T(8,128)(2,1)S(1)} %get-tuple-element.254), channel_id=1, source_target_pairs={{0,16},{8,24},{16,0},{24,8},{1,17},{9,25},{17,1},{25,9},{2,18},{10... | collective-permute-start | bytes 2359304 | tf_op jit(solution)/shard_map/ppermute | solution.py:683
  204.2 53.1 %collective-permute-start.3 = (bf16[256,1536]{1,0:T(8,128)(2,1)S(1)}, bf16[256,1536]{1,0:T(8,128)(2,1)S(1)}, u32[]{:S(2)}, u32[]{:S(2)}) collective-permute-start(bf16[256,1536]{1,0:T(8,128)(2,1)S(1)} %get-tuple-element.253), channel_id=1, source_target_pairs={{0,24},{8,16},{16,8},{24,0},{1,25},{9,17},{17,9},{25,1},{2,26},{10... | collective-permute-start | bytes 2359304 | tf_op jit(solution)/shard_map/ppermute | solution.py:683
  270.3 28.5 %all-to-all-start.1 = ((bf16[4,512,256]{2,1,0:T(8,128)(2,1)}), bf16[4,512,256]{2,1,0:T(8,128)(2,1)S(1)}, u32[]{:S(2)}, u32[]{:S(2)}) async-start(bf16[4,512,256]{2,1,0:T(8,128)(2,1)} %get-tuple-element.119.res_ref), calls=%async_computation.1 | async-start | bytes 2097152 | tf_op jit(solution)/shard_map/all_to_all | solution.py:650
  298.8 28.7 %all-to-all-start.3 = ((bf16[4,512,256]{2,1,0:T(8,128)(2,1)}), bf16[4,512,256]{2,1,0:T(8,128)(2,1)S(1)}, u32[]{:S(2)}, u32[]{:S(2)}) async-start(bf16[4,512,256]{2,1,0:T(8,128)(2,1)} %get-tuple-element.123.res_ref), calls=%async_computation.3 | async-start | bytes 2097152 | tf_op jit(solution)/shard_map/all_to_all | solution.py:650
  302.3 155.3 %all-gather.11.cloned.1.call-start = ((), (), s32[]{:S(2)}) async-start(), calls=%async_computation.13 | async-start | bytes 10485760 | tf_op jit(solution)/shard_map/all_gather | solution.py:665
  311.0 25.2 %collective-permute-start.6 = (bf16[256,2048]{1,0:T(8,128)(2,1)}, bf16[256,2048]{1,0:T(8,128)(2,1)}, u32[]{:S(2)}, u32[]{:S(2)}) collective-permute-start(bf16[256,2048]{1,0:T(8,128)(2,1)} %broadcast_select_fusion.19), channel_id=1, source_target_pairs={{0,1},{1,0},{2,3},{3,2},{4,5},{5,4},{6,7},{7,6},{8,9},{9,8},{10,11... | collective-permute-start | bytes 3145736 | tf_op jit(solution)/shard_map/ppermute | solution.py:640
  336.1 2.7 collective-permute-start.7
  345.5 291.7 %reduce-scatter.4.cloned.1.call-start = ((), (), s32[]{:S(2)}) async-start(), calls=%async_computation.15 | async-start | bytes 10485760 | tf_op jit(solution)/shard_map/reduce_scatter | solution.py:662
  346.0 6.1 collective-permute-start.8
  351.0 7.9 collective-permute-start.9
  550.6 237.5 %all-reduce.5.cloned.1.call-start = ((), (), s32[]{:S(2)}) async-start(), calls=%async_computation.16 | async-start | bytes 4194304 | tf_op jit(solution)/shard_map/psum | solution.py:795
  571.8 39.9 %collective-permute-start.10 = (bf16[768,2048]{1,0:T(8,128)(2,1)S(1)}, bf16[768,2048]{1,0:T(8,128)(2,1)S(1)}, u32[]{:S(2)}, u32[]{:S(2)}) collective-permute-start(bf16[768,2048]{1,0:T(8,128)(2,1)S(1)} %slice_select_fusion.3), channel_id=1, source_target_pairs={{0,1},{1,0},{2,3},{3,2},{4,5},{5,4},{6,7},{7,6},{8,9},{9,8},{10,11... | collective-permute-start | bytes 9437192 | tf_op jit(solution)/shard_map/ppermute | solution.py:640
  593.2 18.5 %collective-permute-start.11 = (bf16[768,2048]{1,0:T(8,128)(2,1)S(1)}, bf16[768,2048]{1,0:T(8,128)(2,1)}, u32[]{:S(2)}, u32[]{:S(2)}) collective-permute-start(bf16[768,2048]{1,0:T(8,128)(2,1)S(1)} %slice_select_fusion.2), channel_id=1, source_target_pairs={{0,1},{1,0},{2,3},{3,2},{4,5},{5,4},{6,7},{7,6},{8,9},{9,8},{10,11... | collective-permute-start | bytes 9437192 | tf_op jit(solution)/shard_map/ppermute | solution.py:640
  611.6 47.7 %collective-permute-start.13 = (bf16[4,256,1536]{2,1,0:T(8,128)(2,1)}, bf16[4,256,1536]{2,1,0:T(8,128)(2,1)}, u32[]{:S(2)}, u32[]{:S(2)}) collective-permute-start(bf16[4,256,1536]{2,1,0:T(8,128)(2,1)} %fusion.27), channel_id=1, source_target_pairs={{0,1},{1,0},{2,3},{3,2},{4,5},{5,4},{6,7},{7,6},{8,9},{9,8},{10,11... | collective-permute-start | bytes 9437192 | tf_op jit(solution)/shard_map/ppermute | solution.py:640
  657.7 4.5 collective-permute-start.12
  676.8 47.3 %all-to-all-start.4 = ((bf16[4,512,256]{2,1,0:T(8,128)(2,1)}), bf16[4,512,256]{2,1,0:T(8,128)(2,1)S(1)}, u32[]{:S(2)}, u32[]{:S(2)}) async-start(bf16[4,512,256]{2,1,0:T(8,128)(2,1)} %get-tuple-element.138), calls=%async_computation.5 | async-start | bytes 2097152 | tf_op jit(solution)/shard_map/all_to_all | solution.py:650
  724.1 83.8 %all-to-all-start.6 = ((bf16[4,512,256]{2,1,0:T(8,128)(2,1)}), bf16[4,512,256]{2,1,0:T(8,128)(2,1)S(1)}, u32[]{:S(2)}, u32[]{:S(2)}) async-start(bf16[4,512,256]{2,1,0:T(8,128)(2,1)} %get-tuple-element.145), calls=%async_computation.7 | async-start | bytes 2097152 | tf_op jit(solution)/shard_map/all_to_all | solution.py:650
  808.9 100.0 %all-to-all-start.5 = ((bf16[4,512,512]{2,1,0:T(8,128)(2,1)}), bf16[4,512,512]{2,1,0:T(8,128)(2,1)S(1)}, u32[]{:S(2)}, u32[]{:S(2)}) async-start(bf16[4,512,512]{2,1,0:T(8,128)(2,1)} %attend_back.2), calls=%async_computation.6 | async-start | bytes 4194304 | tf_op jit(solution)/shard_map/all_to_all | solution.py:650
  812.5 230.3 %all-reduce.7.cloned.1.call-start = ((), (), s32[]{:S(2)}) async-start(), calls=%async_computation.17 | async-start | bytes 8388608 | tf_op jit(solution)/shard_map/psum | solution.py:826
  908.8 64.7 %all-to-all-start.7 = ((bf16[4,512,512]{2,1,0:T(8,128)(2,1)}), bf16[4,512,512]{2,1,0:T(8,128)(2,1)}, u32[]{:S(2)}, u32[]{:S(2)}) async-start(bf16[4,512,512]{2,1,0:T(8,128)(2,1)} %attend_back.3), calls=%async_computation.8 | async-start | bytes 4194304 | tf_op jit(solution)/shard_map/all_to_all | solution.py:650
  913.3 227.0 %reduce-scatter.6.cloned.1.call-start = ((), (), s32[]{:S(2)}) async-start(), calls=%async_computation.18 | async-start | bytes 5242880 | tf_op jit(solution)/shard_map/reduce_scatter | solution.py:662
  919.3 21.6 %collective-permute-start.16 = (bf16[256,1536]{1,0:T(8,128)(2,1)}, bf16[256,1536]{1,0:T(8,128)(2,1)}, u32[]{:S(2)}, u32[]{:S(2)}) collective-permute-start(bf16[256,1536]{1,0:T(8,128)(2,1)} %get-tuple-element.250), channel_id=1, source_target_pairs={{0,24},{8,16},{16,8},{24,0},{1,25},{9,17},{17,9},{25,1},{2,26},{10... | collective-permute-start | bytes 2359304 | tf_op jit(solution)/shard_map/ppermute | solution.py:683
  921.6 29.4 %collective-permute-start.15 = (bf16[256,1536]{1,0:T(8,128)(2,1)}, bf16[256,1536]{1,0:T(8,128)(2,1)}, u32[]{:S(2)}, u32[]{:S(2)}) collective-permute-start(bf16[256,1536]{1,0:T(8,128)(2,1)} %get-tuple-element.251), channel_id=1, source_target_pairs={{0,16},{8,24},{16,0},{24,8},{1,17},{9,25},{17,1},{25,9},{2,18},{10... | collective-permute-start | bytes 2359304 | tf_op jit(solution)/shard_map/ppermute | solution.py:683
  922.2 28.9 %collective-permute-start.14 = (bf16[256,1536]{1,0:T(8,128)(2,1)}, bf16[256,1536]{1,0:T(8,128)(2,1)}, u32[]{:S(2)}, u32[]{:S(2)}) collective-permute-start(bf16[256,1536]{1,0:T(8,128)(2,1)} %get-tuple-element.252), channel_id=1, source_target_pairs={{0,8},{8,0},{16,24},{24,16},{1,9},{9,1},{17,25},{25,17},{2,10},{10... | collective-permute-start | bytes 2359304 | tf_op jit(solution)/shard_map/ppermute | solution.py:683
  923.3 424.4 %reduce-scatter.8.cloned.1.call-start = ((), (), s32[]{:S(2)}) async-start(), calls=%async_computation.19 | async-start | bytes 10485760 | tf_op jit(solution)/shard_map/reduce_scatter | solution.py:662
  1058.3 45.6 %collective-permute-start.20 = (bf16[2,256,2048]{2,1,0:T(8,128)(2,1)}, bf16[2,256,2048]{2,1,0:T(8,128)(2,1)}, u32[]{:S(2)}, u32[]{:S(2)}) collective-permute-start(bf16[2,256,2048]{2,1,0:T(8,128)(2,1)} %select_bitcast_fusion.1), channel_id=1, source_target_pairs={{0,1},{1,0},{2,3},{3,2},{4,5},{5,4},{6,7},{7,6},{8,9},{9,8},{10,11... | collective-permute-start | bytes 6291464 | tf_op jit(solution)/shard_map/ppermute | solution.py:640
  1063.0 35.7 %collective-permute-start.17 = (bf16[4,128,1536]{2,1,0:T(8,128)(2,1)}, bf16[4,128,1536]{2,1,0:T(8,128)(2,1)}, u32[]{:S(2)}, u32[]{:S(2)}) collective-permute-start(bf16[4,128,1536]{2,1,0:T(8,128)(2,1)} %get-tuple-element.155), channel_id=1, source_target_pairs={{0,2},{1,3},{6,4},{7,5},{8,10},{9,11},{14,12},{15,13},{16,18},{17,... | collective-permute-start | bytes 4718600 | tf_op jit(solution)/shard_map/ppermute | solution.py:550
  1067.3 64.7 %collective-permute-start.24 = (bf16[2,512,1024]{2,1,0:T(8,128)(2,1)}, bf16[2,512,1024]{2,1,0:T(8,128)(2,1)}, u32[]{:S(2)}, u32[]{:S(2)}) collective-permute-start(bf16[2,512,1024]{2,1,0:T(8,128)(2,1)} %select_bitcast_fusion), channel_id=1, source_target_pairs={{0,8},{8,0},{16,24},{24,16},{1,9},{9,1},{17,25},{25,17},{2,10},{10... | collective-permute-start | bytes 6291464 | tf_op jit(solution)/shard_map/ppermute | solution.py:533
  1074.8 77.1 %collective-permute-start.31 = (bf16[2,512,1024]{2,1,0:T(8,128)(2,1)}, bf16[2,512,1024]{2,1,0:T(8,128)(2,1)}, u32[]{:S(2)}, u32[]{:S(2)}) collective-permute-start(bf16[2,512,1024]{2,1,0:T(8,128)(2,1)} %bitcast.48), channel_id=1, source_target_pairs={{0,16},{8,24},{16,0},{24,8},{1,17},{9,25},{17,1},{25,9},{2,18},{10... | collective-permute-start | bytes 6291464 | tf_op jit(solution)/shard_map/ppermute | solution.py:533
  1078.4 174.7 %collective-permute-start.34 = (bf16[768,2048]{1,0:T(8,128)(2,1)}, bf16[768,2048]{1,0:T(8,128)(2,1)}, u32[]{:S(2)}, u32[]{:S(2)}) collective-permute-start(bf16[768,2048]{1,0:T(8,128)(2,1)} %slice.392), channel_id=1, source_target_pairs={{0,16},{8,24},{16,0},{24,8},{1,17},{9,25},{17,1},{25,9},{2,18},{10... | collective-permute-start | bytes 9437192 | tf_op jit(solution)/shard_map/ppermute | solution.py:888
  1102.1 38.3 %collective-permute-start.18 = (bf16[4,128,1536]{2,1,0:T(8,128)(2,1)}, bf16[4,128,1536]{2,1,0:T(8,128)(2,1)}, u32[]{:S(2)}, u32[]{:S(2)}) collective-permute-start(bf16[4,128,1536]{2,1,0:T(8,128)(2,1)} %add.232), channel_id=1, source_target_pairs={{2,4},{3,5},{4,2},{5,3},{10,12},{11,13},{12,10},{13,11},{18,20},{1... | collective-permute-start | bytes 4718600 | tf_op jit(solution)/shard_map/ppermute | solution.py:550
  1103.9 39.4 %collective-permute-start.19 = (bf16[4,128,1536]{2,1,0:T(8,128)(2,1)}, bf16[4,128,1536]{2,1,0:T(8,128)(2,1)}, u32[]{:S(2)}, u32[]{:S(2)}) collective-permute-start(bf16[4,128,1536]{2,1,0:T(8,128)(2,1)} %get-tuple-element.164), channel_id=1, source_target_pairs={{0,2},{1,3},{6,4},{7,5},{8,10},{9,11},{14,12},{15,13},{16,18},{17,... | collective-permute-start | bytes 4718600 | tf_op jit(solution)/shard_map/ppermute | solution.py:550
  1132.0 18.3 %collective-permute-start.26 = (f32[24,2048]{1,0:T(8,128)S(1)}, f32[24,2048]{1,0:T(8,128)S(1)}, u32[]{:S(2)}, u32[]{:S(2)}) collective-permute-start(f32[24,2048]{1,0:T(8,128)S(1)} %concatenate.79), channel_id=1, source_target_pairs={{0,1},{1,0},{2,3},{3,2},{4,5},{5,4},{6,7},{7,6},{8,9},{9,8},{10,11... | collective-permute-start | bytes 589832 | tf_op jit(solution)/shard_map/ppermute | solution.py:884
  1145.6 78.0 %collective-permute-start.21 = (bf16[4,128,1536]{2,1,0:T(8,128)(2,1)S(1)}, bf16[4,128,1536]{2,1,0:T(8,128)(2,1)S(1)}, u32[]{:S(2)}, u32[]{:S(2)}) collective-permute-start(bf16[4,128,1536]{2,1,0:T(8,128)(2,1)S(1)} %add.238), channel_id=1, source_target_pairs={{2,0},{3,1},{4,6},{5,7},{10,8},{11,9},{12,14},{13,15},{18,16},{19,... | collective-permute-start | bytes 4718600 | tf_op jit(solution)/shard_map/ppermute | solution.py:550
  1149.4 74.1 %collective-permute-start.22 = (bf16[4,128,1536]{2,1,0:T(8,128)(2,1)S(1)}, bf16[4,128,1536]{2,1,0:T(8,128)(2,1)S(1)}, u32[]{:S(2)}, u32[]{:S(2)}) collective-permute-start(bf16[4,128,1536]{2,1,0:T(8,128)(2,1)S(1)} %add.239), channel_id=1, source_target_pairs={{2,4},{3,5},{4,2},{5,3},{10,12},{11,13},{12,10},{13,11},{18,20},{1... | collective-permute-start | bytes 4718600 | tf_op jit(solution)/shard_map/ppermute | solution.py:550
  1150.3 72.5 %collective-permute-start.25 = (bf16[512,1024]{1,0:T(8,128)(2,1)S(1)}, bf16[512,1024]{1,0:T(8,128)(2,1)S(1)}, u32[]{:S(2)}, u32[]{:S(2)}) collective-permute-start(bf16[512,1024]{1,0:T(8,128)(2,1)S(1)} %select_bitcast_fusion.3), channel_id=1, source_target_pairs={{0,16},{8,24},{16,0},{24,8},{1,17},{9,25},{17,1},{25,9},{2,18},{10... | collective-permute-start | bytes 3145736 | tf_op jit(solution)/shard_map/ppermute | solution.py:533
  1151.9 5.7 collective-permute-start.27
  1157.7 65.9 %collective-permute-start.23 = (bf16[512,1024]{1,0:T(8,128)(2,1)S(1)}, bf16[512,1024]{1,0:T(8,128)(2,1)S(1)}, u32[]{:S(2)}, u32[]{:S(2)}) collective-permute-start(bf16[512,1024]{1,0:T(8,128)(2,1)S(1)} %copy-done.47), channel_id=1, source_target_pairs={{0,2},{1,3},{6,4},{7,5},{8,10},{9,11},{14,12},{15,13},{16,18},{17,... | collective-permute-start | bytes 3145736 | tf_op jit(solution)/shard_map/ppermute | solution.py:550
  1222.9 23.4 %collective-permute-start.32 = (bf16[512,1024]{1,0:T(8,128)(2,1)S(1)}, bf16[512,1024]{1,0:T(8,128)(2,1)S(1)}, u32[]{:S(2)}, u32[]{:S(2)}) collective-permute-start(bf16[512,1024]{1,0:T(8,128)(2,1)S(1)} %select_bitcast_fusion.2), channel_id=1, source_target_pairs={{0,8},{8,0},{16,24},{24,16},{1,9},{9,1},{17,25},{25,17},{2,10},{10... | collective-permute-start | bytes 3145736 | tf_op jit(solution)/shard_map/ppermute | solution.py:533
  1224.0 36.7 %collective-permute-start.28 = (bf16[4,128,1536]{2,1,0:T(8,128)(2,1)S(1)}, bf16[4,128,1536]{2,1,0:T(8,128)(2,1)}, u32[]{:S(2)}, u32[]{:S(2)}) collective-permute-start(bf16[4,128,1536]{2,1,0:T(8,128)(2,1)S(1)} %add.248), channel_id=1, source_target_pairs={{2,0},{3,1},{4,6},{5,7},{10,8},{11,9},{12,14},{13,15},{18,16},{19,... | collective-permute-start | bytes 4718600 | tf_op jit(solution)/shard_map/ppermute | solution.py:550
  1225.7 27.4 %collective-permute-start.29 = (bf16[512,1024]{1,0:T(8,128)(2,1)S(1)}, bf16[512,1024]{1,0:T(8,128)(2,1)S(1)}, u32[]{:S(2)}, u32[]{:S(2)}) collective-permute-start(bf16[512,1024]{1,0:T(8,128)(2,1)S(1)} %add.249), channel_id=1, source_target_pairs={{2,4},{3,5},{4,2},{5,3},{10,12},{11,13},{12,10},{13,11},{18,20},{1... | collective-permute-start | bytes 3145736 | tf_op jit(solution)/shard_map/ppermute | solution.py:550
  1226.4 29.3 %collective-permute-start.30 = (bf16[512,1024]{1,0:T(8,128)(2,1)S(1)}, bf16[512,1024]{1,0:T(8,128)(2,1)S(1)}, u32[]{:S(2)}, u32[]{:S(2)}) collective-permute-start(bf16[512,1024]{1,0:T(8,128)(2,1)S(1)} %bitcast_add_fusion.2), channel_id=1, source_target_pairs={{0,2},{1,3},{6,4},{7,5},{8,10},{9,11},{14,12},{15,13},{16,18},{17,... | collective-permute-start | bytes 3145736 | tf_op jit(solution)/shard_map/ppermute | solution.py:550
  1246.3 5.7 collective-permute-start.33
  1260.7 29.9 %collective-permute-start.37 = (bf16[560,1024]{1,0:T(8,128)(2,1)}, bf16[560,1024]{1,0:T(8,128)(2,1)}, u32[]{:S(2)}, u32[]{:S(2)}) collective-permute-start(bf16[560,1024]{1,0:T(8,128)(2,1)} %pad_maximum_fusion.9), channel_id=1, source_target_pairs={{0,2},{1,3},{6,4},{7,5},{8,10},{9,11},{14,12},{15,13},{16,18},{17,... | collective-permute-start | bytes 3440648 | tf_op jit(solution)/shard_map/ppermute | solution.py:550
  1265.8 24.8 %collective-permute-start.35 = (bf16[512,1024]{1,0:T(8,128)(2,1)}, bf16[512,1024]{1,0:T(8,128)(2,1)}, u32[]{:S(2)}, u32[]{:S(2)}) collective-permute-start(bf16[512,1024]{1,0:T(8,128)(2,1)} %add.253), channel_id=1, source_target_pairs={{2,0},{3,1},{4,6},{5,7},{10,8},{11,9},{12,14},{13,15},{18,16},{19,... | collective-permute-start | bytes 3145736 | tf_op jit(solution)/shard_map/ppermute | solution.py:550
  1268.5 22.1 %collective-permute-start.36 = (bf16[512,1024]{1,0:T(8,128)(2,1)}, bf16[512,1024]{1,0:T(8,128)(2,1)}, u32[]{:S(2)}, u32[]{:S(2)}) collective-permute-start(bf16[512,1024]{1,0:T(8,128)(2,1)} %add.254), channel_id=1, source_target_pairs={{2,4},{3,5},{4,2},{5,3},{10,12},{11,13},{12,10},{13,11},{18,20},{1... | collective-permute-start | bytes 3145736 | tf_op jit(solution)/shard_map/ppermute | solution.py:550
  1273.5 31.2 %collective-permute-start.40 = (bf16[768,2048]{1,0:T(8,128)(2,1)S(1)}, bf16[768,2048]{1,0:T(8,128)(2,1)}, u32[]{:S(2)}, u32[]{:S(2)}) collective-permute-start(bf16[768,2048]{1,0:T(8,128)(2,1)S(1)} %pad_maximum_fusion.7.keep_ref), channel_id=1, source_target_pairs={{0,1},{1,0},{2,3},{3,2},{4,5},{5,4},{6,7},{7,6},{8,9},{9,8},{10,11... | collective-permute-start | bytes 9437192 | tf_op jit(solution)/shard_map/ppermute | solution.py:640
  1273.6 31.2 %collective-permute-start.41 = (bf16[768,2048]{1,0:T(8,128)(2,1)}, bf16[768,2048]{1,0:T(8,128)(2,1)}, u32[]{:S(2)}, u32[]{:S(2)}) collective-permute-start(bf16[768,2048]{1,0:T(8,128)(2,1)} %collective-permute-done.34.sent_ref), channel_id=1, source_target_pairs={{0,1},{1,0},{2,3},{3,2},{4,5},{5,4},{6,7},{7,6},{8,9},{9,8},{10,11... | collective-permute-start | bytes 9437192 | tf_op jit(solution)/shard_map/ppermute | solution.py:640
  1294.5 26.7 %collective-permute-start.42 = (bf16[4,256,1536]{2,1,0:T(8,128)(2,1)}, bf16[4,256,1536]{2,1,0:T(8,128)(2,1)}, u32[]{:S(2)}, u32[]{:S(2)}) collective-permute-start(bf16[4,256,1536]{2,1,0:T(8,128)(2,1)} %pad_maximum_fusion.8.refs_0_), channel_id=1, source_target_pairs={{0,1},{1,0},{2,3},{3,2},{4,5},{5,4},{6,7},{7,6},{8,9},{9,8},{10,11... | collective-permute-start | bytes 9437192 | tf_op jit(solution)/shard_map/ppermute | solution.py:640
  1297.5 36.3 %collective-permute-start.39 = (bf16[560,1024]{1,0:T(8,128)(2,1)}, bf16[560,1024]{1,0:T(8,128)(2,1)}, u32[]{:S(2)}, u32[]{:S(2)}) collective-permute-start(bf16[560,1024]{1,0:T(8,128)(2,1)} %add.256), channel_id=1, source_target_pairs={{2,4},{3,5},{4,2},{5,3},{10,12},{11,13},{12,10},{13,11},{18,20},{1... | collective-permute-start | bytes 3440648 | tf_op jit(solution)/shard_map/ppermute | solution.py:550
  1302.3 31.6 %collective-permute-start.38 = (bf16[512,1024]{1,0:T(8,128)(2,1)}, bf16[512,1024]{1,0:T(8,128)(2,1)}, u32[]{:S(2)}, u32[]{:S(2)}) collective-permute-start(bf16[512,1024]{1,0:T(8,128)(2,1)} %add.255), channel_id=1, source_target_pairs={{2,0},{3,1},{4,6},{5,7},{10,8},{11,9},{12,14},{13,15},{18,16},{19,... | collective-permute-start | bytes 3145736 | tf_op jit(solution)/shard_map/ppermute | solution.py:550
  1336.2 4.2 collective-permute-start.44
  1338.5 34.3 %collective-permute-start.43 = (bf16[560,1024]{1,0:T(8,128)(2,1)S(1)}, bf16[560,1024]{1,0:T(8,128)(2,1)}, u32[]{:S(2)}, u32[]{:S(2)}) collective-permute-start(bf16[560,1024]{1,0:T(8,128)(2,1)S(1)} %add.257), channel_id=1, source_target_pairs={{2,0},{3,1},{4,6},{5,7},{10,8},{11,9},{12,14},{13,15},{18,16},{19,... | collective-permute-start | bytes 3440648 | tf_op jit(solution)/shard_map/ppermute | solution.py:550
  1374.2 5.5 collective-permute-start.46
  1376.0 2.7 collective-permute-start.45
  (88 other events, 1197.8 us)
Sparse Core Ops, SparseCore 0:
  15.7 91.5 all-gather.6
  109.8 52.5 all-gather.8
  164.5 114.0 all-gather.14
  280.3 87.4 all-gather.12
  370.1 87.4 all-gather.10
  550.8 86.3 reduce-scatter.3
  659.5 128.6 all-reduce.4
  815.6 227.0 all-reduce.6
  1045.7 69.9 reduce-scatter.5
  1260.8 86.7 reduce-scatter.7
